TPU v7x, 256 devices: a whole 4x4x8 slice. The times are simulated.
256 devices in a mesh: row: 16 (over x_lo, y, core), col: 16 (over z, x_hi).
Axes of the slice: x: 4 (x_hi: 2, x_lo: 2; x = x_hi * 2 + x_lo), y: 4, z: 8, core: 2. Of those that a mesh axis runs over, the one named last changes fastest.
Arguments:
- tokens: bfloat16 [1536, 8192], P('row', 'col'), may hold values from -6 to 6
- gate_weight: bfloat16 [8192, 28672], P('col', 'row'), may hold values from -0.0625 to 0.0625
- up_weight: bfloat16 [8192, 28672], P('col', 'row'), may hold values from -0.0625 to 0.0625
- down_weight: bfloat16 [28672, 8192], P('row', 'col'), may hold values from -0.03125 to 0.03125
Outputs:
- mixed: float32 [1536, 8192], P('row', 'col')
All inputs are finite; a program needn't handle non-finite values.
Results may differ from a plain program's by a relative error of at most 0.0029.
Values may be sent and summed in bfloat16 or wider, within the bound.
No kernel may reach another device: no remote copies, remote signals or barrier semaphores. Data moves between devices by JAX's collectives and lax.ppermute only.
A program may use at most 128 MiB of HBM per device.

v0:
```python
import jax
import jax.numpy as jnp
from jax import lax
from jax.sharding import PartitionSpec as P


def shards(tokens, gate_weight, up_weight, down_weight):
    fragment = lax.all_gather(tokens, "row", axis=0, tiled=True)
    gate_part = jnp.dot(fragment, gate_weight, preferred_element_type=jnp.float32)
    up_part = jnp.dot(fragment, up_weight, preferred_element_type=jnp.float32)
    partial_sums = jnp.stack((gate_part, up_part))
    shared = lax.psum_scatter(partial_sums, "col", scatter_dimension=1, tiled=True)
    hidden_share = (jax.nn.silu(shared[0]) * shared[1]).astype(jnp.bfloat16)
    hidden = lax.all_gather(hidden_share, "col", axis=0, tiled=True)
    return lax.psum_scatter(
        jnp.dot(hidden, down_weight, preferred_element_type=jnp.float32),
        "row",
        scatter_dimension=0,
        tiled=True,
    )


def solution(mesh):
    return jax.shard_map(
        shards,
        mesh=mesh,
        in_specs=(P("row", "col"), P("col", "row"), P("col", "row"), P("row", "col")),
        out_specs=P("row", "col"),
        check_vma=False,
    )
```

profile of v0, /device:TPU:2, one launch (start us, length us, event | category | flops | bytes accessed | tf_op | source)
XLA Modules:
  0.0 606.4 jit_solution(4885500907963222633)
XLA Ops:
  6.5 0.0 copy-start
  6.5 0.0 all-gather.3.cloned.1.call-start
  6.5 0.7 all-gather.3.cloned.1.call-update
  7.3 0.0 reduce-scatter.3.cloned.1.call-start
  7.3 40.3 %all-gather.3.cloned.1.call-done = bf16[1536,512]{1,0:T(8,128)(2,1)} async-done(((bf16[96,512]{1,0:T(8,128)(2,1)}), bf16[1536,512]{1,0:T(8,128)(2,1)}) %all-gather.3.cloned.1.call-update) | async-done | bytes 1572880 | tf_op jit(solution)/shard_map/all_gather | solution.py:8
  47.6 0.0 copy-done
  47.6 0.0 copy-start.1
  47.6 0.0 copy-start.2
  47.6 4.6 convolution_bitcast_fusion
  52.3 0.0 copy-done.1
  52.3 0.0 copy-done.2
  52.3 3.0 convolution_bitcast_fusion.1
  55.3 7.8 %pad_maximum_fusion = f32[2,1536,1792]{2,1,0:T(8,128)} fusion(f32[1,1536,1792]{2,1,0:T(8,128)S(1)} %convolution_bitcast_fusion, f32[1,1536,1792]{2,1,0:T(8,128)S(1)} %convolution_bitcast_fusion.1), kind=kLoop, calls=%fused_computation | loop fusion | flops 5505024 | bytes 44040192 | tf_op jit(solution)/shard_map/stack | solution.py:11
  63.1 0.0 reduce-scatter.3.cloned.1.call-update
  63.1 0.0 all-gather.5.cloned.1.call-start
  63.2 355.0 %reduce-scatter.3.cloned.1.call-done = f32[2,96,1792]{2,1,0:T(8,128)} async-done(((f32[2,1536,1792]{2,1,0:T(8,128)}), f32[2,96,1792]{2,1,0:T(8,128)}) %reduce-scatter.3.cloned.1.call-update) | async-done | bytes 1376272 | tf_op jit(solution)/shard_map/reduce_scatter | solution.py:12
  418.2 2.2 fusion.1
  420.4 0.0 all-gather.5.cloned.1.call-update
  420.4 0.0 reduce-scatter.5.cloned.1.call-start
  420.5 107.1 %all-gather.5.cloned.1.call-done = bf16[1536,1792]{1,0:T(8,128)(2,1)} async-done(((bf16[96,1792]{1,0:T(8,128)(2,1)}), bf16[1536,1792]{1,0:T(8,128)(2,1)}) %all-gather.5.cloned.1.call-update) | async-done | bytes 5505040 | tf_op jit(solution)/shard_map/all_gather | solution.py:14
  527.6 7.9 %fusion.2 = f32[1536,512]{1,0:T(8,128)} fusion(bf16[1536,1792]{1,0:T(8,128)(2,1)} %all-gather.5.cloned.1.call-done, bf16[1792,512]{1,0:T(8,128)(2,1)} %param.7), kind=kOutput, calls=%fused_computation.7 | convolution fusion | flops 2818572288 | bytes 10485760 | tf_op jit(solution)/shard_map/dot_general | solution.py:16
  535.4 0.0 reduce-scatter.5.cloned.1.call-update
  535.5 64.4 %reduce-scatter.5.cloned.1.call-done = f32[96,512]{1,0:T(8,128)} async-done(((f32[1536,512]{1,0:T(8,128)}), f32[96,512]{1,0:T(8,128)}) %reduce-scatter.5.cloned.1.call-update) | async-done | bytes 196624 | tf_op jit(solution)/shard_map/reduce_scatter | solution.py:15
Async XLA Ops:
  6.5 41.1 %copy-start = (bf16[512,1792]{1,0:T(8,128)(2,1)S(1)}, bf16[512,1792]{1,0:T(8,128)(2,1)}, u32[]{:S(2)}) copy-start(bf16[512,1792]{1,0:T(8,128)(2,1)} %param.6) | copy-start | bytes 5505028
  6.5 41.1 %all-gather.3.cloned.1.call-start = ((), (), s32[]{:S(2)}) async-start(), calls=%async_computation.2 | async-start | bytes 1671168 | tf_op jit(solution)/shard_map/all_gather | solution.py:8
  7.3 410.9 %reduce-scatter.3.cloned.1.call-start = ((), (), s32[]{:S(2)}) async-start(), calls=%async_computation.3 | async-start | bytes 23396352 | tf_op jit(solution)/shard_map/reduce_scatter | solution.py:12
  47.6 4.7 copy-start.1
  47.6 4.7 copy-start.2
  63.1 464.5 %all-gather.5.cloned.1.call-start = ((), (), s32[]{:S(2)}) async-start(), calls=%async_computation.4 | async-start | bytes 5849088 | tf_op jit(solution)/shard_map/all_gather | solution.py:14
  420.4 179.4 %reduce-scatter.5.cloned.1.call-start = ((), (), s32[]{:S(2)}) async-start(), calls=%async_computation.5 | async-start | bytes 3342336 | tf_op jit(solution)/shard_map/reduce_scatter | solution.py:15
Sparse Core Ops, SparseCore 0:
  9.2 38.3 all-gather.2
  63.2 354.9 reduce-scatter.2
  421.1 106.4 all-gather.4
  535.6 64.2 reduce-scatter.4
where the time goes:
time: 607 us; the launch traced here: 606 us
  waiting for transfers between devices  568 us (94%)
  matrix products  15.5 us (3%)
  between operations  13.2 us (2%)
  other arithmetic  10 us (2%)
    reduce_scatter x1, waiting for transfers between devices, shards(): lax.psum_scatter(partial_sums, 'col', scatter_dimension=1, tiled=True)  355 us
    all_gather x1, waiting for transfers between devices, shards(): hidden = lax.all_gather(hidden_share, 'col', axis=0, tiled=True)  107 us
    reduce_scatter x1, waiting for transfers between devices, shards(): lax.psum_scatter(jnp.dot(hidden, down_weight, preferred_element_type=jnp....  64.4 us
    all_gather x1, waiting for transfers between devices, shards(): fragment = lax.all_gather(tokens, 'row', axis=0, tiled=True)  40.3 us
  transfers between devices with their start and end apart: 4, of which 4 were waited for; matrix products, arithmetic and copies ran while one was open for 0% of the time, Pallas kernels for 0%

commit v1 on v0

v1 whole, which is shorter than its diff:
```python
import functools
import itertools

import jax
import jax.numpy as jnp
from jax import lax
from jax.experimental import pallas as pl
from jax.experimental.pallas import tpu as pltpu
from jax.sharding import Mesh, PartitionSpec as P

AXES = ("xl", "y", "c", "z", "xh")
SIZES = (2, 4, 2, 8, 2)
CHUNKS = 2
F32, BF16 = jnp.float32, jnp.bfloat16
SCALARS = pl.BlockSpec(memory_space=pltpu.SMEM)
WHOLE = pl.BlockSpec(memory_space=pltpu.VMEM)


def send(value, move):
    flat = lambda at: sum(i * k for i, k in zip(at, (128, 32, 16, 2, 1)))
    pairs = []
    for at in itertools.product(*map(range, SIZES)):
        to = move(*at)
        if to is not None:
            pairs.append((flat(at), flat(tuple(i % n for i, n in zip(to, SIZES)))))
    return lax.ppermute(value, AXES, pairs)


def along_z(value, step):
    return send(value, lambda xl, y, c, z, xh: (xl, y, c, z + step, xh))


def along_y(value, step):
    return send(value, lambda xl, y, c, z, xh: (xl, y + step, c, z, xh))


def swap_xl(value):
    return send(value, lambda xl, y, c, z, xh: (1 - xl, y, c, z, xh))


def swap_xh(value):
    return send(value, lambda xl, y, c, z, xh: (xl, y, c, z, 1 - xh))


def swap_core(value):
    return send(value, lambda xl, y, c, z, xh: (xl, y, 1 - c, z, xh))


def together(*values):
    return lax.optimization_barrier(values)


def cost(flops, *arrays):
    size = sum(a.size * a.dtype.itemsize for a in arrays)
    return pl.CostEstimate(flops=flops, bytes_accessed=size, transcendentals=0)


def slice_units(gate, up, nz):
    depth, width = gate.shape
    units = width // nz
    step = 128

    def body(g_ref, u_ref, o_ref):
        o_ref[:, :units] = g_ref[...].T.reshape(nz, units, step)
        o_ref[:, units:] = u_ref[...].T.reshape(nz, units, step)

    out = jax.ShapeDtypeStruct((nz, 2 * units, depth), gate.dtype)
    return pl.pallas_call(
        body,
        grid=(depth // step,),
        in_specs=[pl.BlockSpec((step, width), lambda k: (k, 0))] * 2,
        out_specs=pl.BlockSpec((nz, 2 * units, step), lambda k: (0, 0, k)),
        out_shape=out,
        cost_estimate=cost(0, gate, up, out),
        name="slice_units",
    )(gate, up)


def project(place, weight, pieces, here=None):
    near, far, before, after, across_0, across_1 = pieces
    nz, units, depth = weight.shape
    rows = near.shape[1]
    last = here is not None

    def body(place_ref, w_ref, near_ref, far_ref, before_ref, after_ref, a0_ref, a1_ref, *rest):
        here_ref = rest[0] if last else None
        outs, (t_ref, acc_ref) = rest[last:-2], rest[-2:]
        xl, y = place_ref[0], place_ref[1]
        found = (
            (0, 0, near_ref[0]), (0, 1, far_ref[0]),
            (1, 0, after_ref[0, 0]), (1, 1, after_ref[1, 0]),
            (2, 0, a0_ref[0]), (2, 1, a1_ref[0]),
            (3, 0, before_ref[0, 0]), (3, 1, before_ref[1, 0]),
        )
        for dy, dx, piece in found:
            at = ((y + dy) % 4) * 2 + (xl + dx) % 2
            t_ref[pl.ds(pl.multiple_of(at * rows, rows), rows)] = piece
        k = pl.program_id(0)
        term = lax.dot_general(
            w_ref[0], t_ref[...], (((1,), (1,)), ((), ())), preferred_element_type=F32
        )

        @pl.when(k == 0)
        def _():
            acc_ref[...] = term

        @pl.when(k > 0)
        def _():
            acc_ref[...] += term

        @pl.when(k == nz - 1)
        def _():
            if last:
                same = place_ref[2] == place_ref[4]
                outs[0][...] = jnp.where(same, here_ref[...], acc_ref[...])
                outs[1][...] = jnp.where(same, acc_ref[...], here_ref[...])
            else:
                outs[0][...] = acc_ref[...]

    one = pl.BlockSpec((1, rows, depth), lambda k: (k, 0, 0))
    two = pl.BlockSpec((2, 1, rows, depth), lambda k: (0, k, 0, 0))
    full = pl.BlockSpec((units, 8 * rows), lambda k: (0, 0))
    out = jax.ShapeDtypeStruct((units, 8 * rows), F32)
    args = (weight, *pieces) + ((here,) if last else ())
    return pl.pallas_call(
        body,
        grid=(nz,),
        in_specs=[SCALARS, pl.BlockSpec((1, units, depth), lambda k: (k, 0, 0)), one, one, two, two, one, one]
        + [full] * last,
        out_specs=[full] * (1 + last),
        out_shape=[out] * (1 + last),
        scratch_shapes=[pltpu.VMEM((8 * rows, depth), BF16), pltpu.VMEM((units, 8 * rows), F32)],
        cost_estimate=cost(2 * nz * units * depth * 8 * rows, *args),
        name="project_last" if last else "project",
    )(place, *args)


def activate(keep, got):
    units, rows = keep.shape[0] // 2, keep.shape[1]

    def body(keep_ref, got_ref, o_ref):
        gate = keep_ref[:units] + got_ref[:units]
        up = keep_ref[units:] + got_ref[units:]
        o_ref[...] = (gate / (1 + jnp.exp(-gate)) * up).astype(o_ref.dtype)

    return pl.pallas_call(
        body,
        in_specs=[WHOLE] * 2,
        out_specs=WHOLE,
        out_shape=jax.ShapeDtypeStruct((units, rows), BF16),
        cost_estimate=cost(0, keep, got),
        name="activate",
    )(keep, got)


def mix(place, parts, mine, theirs):
    units, rows = parts[0].shape
    width = mine.shape[1]
    nz = SIZES[3]

    def body(place_ref, mine_ref, theirs_ref, *rest):
        part_refs, (o_ref, h_ref) = rest[:-2], rest[-2:]
        c, z = place_ref[2], place_ref[3]
        at = 0
        for s in range(nz):
            slot = pl.multiple_of(((z + nz - s) % nz) * units, units)
            if s == nz // 2:
                low, high = part_refs[s], part_refs[s + 1]
                h_ref[pl.ds(slot, units // 2)] = low[...]
                h_ref[pl.ds(pl.multiple_of(slot + units // 2, units // 2), units // 2)] = high[...]
            else:
                h_ref[pl.ds(slot, units)] = part_refs[s + (s > nz // 2)][...]
        for side, w_ref in ((c, mine_ref), (1 - c, theirs_ref)):
            o_ref[side] = lax.dot_general(
                h_ref[...], w_ref[...], (((0,), (0,)), ((), ())), preferred_element_type=F32
            ).astype(o_ref.dtype)

    return pl.pallas_call(
        body,
        in_specs=[SCALARS] + [WHOLE] * (2 + len(parts)),
        out_specs=WHOLE,
        out_shape=jax.ShapeDtypeStruct((2, rows, width), BF16),
        scratch_shapes=[pltpu.VMEM((nz * units, rows), BF16)],
        cost_estimate=cost(4 * nz * units * rows * width, mine, theirs, *parts),
        name="mix",
    )(place, mine, theirs, *parts)


def shards(tokens, gate_weight, up_weight, down_weight):
    xl, y, c, z, xh = (lax.axis_index(a) for a in AXES)
    place = jnp.stack([xl, y, c, z, xh]).astype(jnp.int32)
    nz = SIZES[3]
    rows = tokens.shape[0] // CHUNKS

    token = jnp.broadcast_to(tokens[None], (nz, *tokens.shape))
    token = lax.all_to_all(token, "z", 0, 0, tiled=True)

    sliced, token = together(slice_units(gate_weight, up_weight, nz), token)
    weight = lax.all_to_all(sliced, "z", 0, 0, tiled=True)

    nears = [token[:, i * rows : (i + 1) * rows] for i in range(CHUNKS)]
    fars = [swap_xl(near) for near in nears]
    chunks = []
    for near, far in zip(nears, fars):
        pair = jnp.stack([near, far])
        before, after = along_y(pair, 1), along_y(pair, -1)
        across_0, across_1 = along_y(before[0], 1), along_y(after[1], -1)
        chunks.append((near, far, before, after, across_0, across_1))

    down_weight, *fars = together(down_weight, *fars)
    moved = send(
        down_weight,
        lambda xl, y, c, z, xh: (xl, y, 1 - c, z, 1 - xh) if c != xh else None,
    )
    mine = jnp.where(c == xh, down_weight, moved)
    theirs = swap_core(mine)
    weight, mine, theirs, chunks = together(weight, mine, theirs, chunks)
    other = swap_core(weight)

    heres = [project(place, weight, pieces)[0] for pieces in chunks]
    other, heres = together(other, heres)
    sums = [project(place, other, pieces, here) for pieces, here in zip(chunks, heres)]
    gots = [swap_xh(give) for _, give in sums]

    rings, outs = [], []
    ends = 2 * (CHUNKS - 1) + nz // 2
    for step in range(ends + 1):
        for i in range(CHUNKS):
            at = step - 2 * i
            if at == 0:
                hidden = activate(sums[i][0], gots[i])
                rings.append({0: hidden, "up": hidden, "down": hidden})
            if 0 <= at < nz // 2:
                ring = rings[i]
                up, down = ring["up"], ring["down"]
                if at == nz // 2 - 1:
                    half = up.shape[0] // 2
                    up, down = up[:half], down[half:]
                up, down = along_z(up, 1), along_z(down, -1)
                ring.update({"up": up, "down": down, at + 1: up, -at - 1: down})
            if at == nz // 2:
                ring = rings[i]
                parts = [ring[s] for s in (0, 1, 2, 3, 4, -4, -3, -2, -1)]
                out = mix(place, parts, mine, theirs).reshape(16, rows, -1)
                got = lax.all_to_all(out, ("xh", "y", "xl"), 0, 0, tiled=True)
                outs.append(jnp.sum(got.astype(F32), 0))
        live = [i for i in range(CHUNKS) if 0 <= step - 2 * i < nz // 2]
        if len(live) > 1 or step == 1:
            held = [(rings[i]["up"], rings[i]["down"]) for i in live]
            if step == 1:
                held, gots[1] = together(held, gots[1])
            else:
                held = together(*held)
            for i, (up, down) in zip(live, held):
                rings[i].update({"up": up, "down": down})
    return jnp.concatenate(outs)


def solution(mesh):
    split = Mesh(mesh.devices.reshape(SIZES), AXES)
    row, col = ("xl", "y", "c"), ("z", "xh")
    return jax.shard_map(
        shards,
        mesh=split,
        in_specs=(P(row, col), P(col, row), P(col, row), P(row, col)),
        out_specs=P(row, col),
        check_vma=False,
    )
```

time: 607 us -> 269 us (0.44)
  waiting for transfers between devices: 568 us -> 108 us
  starting transfers between devices: 0.12 us -> 94.6 us
  Pallas kernels: 0 us -> 53.8 us
  matrix products: 15.5 us -> 0 us
  between operations: 13.2 us -> 0.29 us
  local copies, waits for them, and re-layouts: 0.01 us -> 8.22 us
  other arithmetic: 10 us -> 2.76 us
    reduce_scatter x2 -> x0, waiting for transfers between devices: 419 us -> none  [the longest x1 355 us: shards(): lax.psum_scatter(partial_sums, 'col', scatter_dimension=1, tiled=True)]
    all_gather x2 -> x0, waiting for transfers between devices: 147 us -> none  [the longest x1 107 us: shards(): hidden = lax.all_gather(hidden_share, 'col', axis=0, tiled=True)]
    ppermute x0 -> x31, waiting for transfers between devices: none -> 79.6 us  [send(): return lax.ppermute(value, AXES, pairs)]
    ppermute x0 -> x31, starting transfers between devices: none -> 66.4 us  [send(): return lax.ppermute(value, AXES, pairs)]
    pallas_call x0 -> x9, Pallas kernels: none -> 53.8 us  [the longest x4 34.4 us: project(): pl.pallas_call(body, grid=(nz,), in_specs=[SCALARS, pl.BlockSpec((1, unit...]
    all_to_all x0 -> x4, waiting for transfers between devices: none -> 28.2 us  [the longest x1 18.1 us: shards(): token = lax.all_to_all(token, 'z', 0, 0, tiled=True)]
    all_to_all x0 -> x4, starting transfers between devices: none -> 28.2 us  [the longest x2 15.2 us: shards(): got = lax.all_to_all(out, ('xh', 'y', 'xl'), 0, 0, tiled=True)]
    dot_general x3 -> x0, matrix products: 15.5 us -> none  [the longest x1 7.85 us: shards(): jnp.dot(hidden, down_weight, preferred_element_type=jnp.float32)]
  transfers between devices with their start and end apart: 4 -> 35, of which waited for: 4 -> 22; matrix products, arithmetic and copies ran while one was open for 0% -> 1% of each run, Pallas kernels for 0% -> 14%
where the time goes in v1:
time: 269 us; the launch traced here: 268 us
  waiting for transfers between devices  108 us (40%)
  starting transfers between devices  94.6 us (35%)
  Pallas kernels  53.8 us (20%)
  local copies, waits for them, and re-layouts  8.22 us (3%)
  other arithmetic  2.76 us (1%)
    ppermute x31, waiting for transfers between devices, send(): return lax.ppermute(value, AXES, pairs)  79.6 us
    ppermute x31, starting transfers between devices, send(): return lax.ppermute(value, AXES, pairs)  66.4 us
    pallas_call x4, Pallas kernels, project(): pl.pallas_call(body, grid=(nz,), in_specs=[SCALARS, pl.BlockSpec((1, unit...  34.4 us
    all_to_all x1, waiting for transfers between devices, shards(): token = lax.all_to_all(token, 'z', 0, 0, tiled=True)  18.1 us
    all_to_all x2, starting transfers between devices, shards(): got = lax.all_to_all(out, ('xh', 'y', 'xl'), 0, 0, tiled=True)  15.2 us
    all_to_all x2, waiting for transfers between devices, shards(): got = lax.all_to_all(out, ('xh', 'y', 'xl'), 0, 0, tiled=True)  10.1 us
    pallas_call x2, Pallas kernels, mix(): pl.pallas_call(body, in_specs=[SCALARS] + [WHOLE] * (2 + len(parts)), out...  10.1 us
    all_to_all x1, starting transfers between devices, shards(): token = lax.all_to_all(token, 'z', 0, 0, tiled=True)  8.47 us
  transfers between devices with their start and end apart: 35, of which 22 were waited for; matrix products, arithmetic and copies ran while one was open for 1% of the time, Pallas kernels for 14%

profile of v1, /device:TPU:2, one launch (start us, length us, event | category | flops | bytes accessed | tf_op | source)
XLA Modules:
  0.0 267.5 jit_solution(1546492529314604130)
XLA Ops:
  1.9 8.5 %all-to-all-start = ((bf16[8,96,512]{2,1,0:T(8,128)(2,1)}), bf16[8,96,512]{2,1,0:T(8,128)(2,1)S(1)}, u32[]{:S(2)}, u32[]{:S(2)}) async-start(bf16[8,96,512]{2,1,0:T(8,128)(2,1)} %broadcast_in_dim.2), calls=%async_computation | async-start | bytes 1572864 | tf_op jit(solution)/shard_map/all_to_all | solution.py:196
  10.3 5.0 %slice_units.1 = bf16[8,448,512]{2,1,0:T(8,128)(2,1)} custom-call(bf16[512,1792]{1,0:T(8,128)(2,1)} %g_ref.1, bf16[512,1792]{1,0:T(8,128)(2,1)} %u_ref.1), custom_call_target="tpu_custom_call" | custom-call | bytes 7340032 | tf_op jit(solution)/shard_map/slice_units/pallas_call | solution.py:68
  15.3 18.1 %all-to-all-done = bf16[8,96,512]{2,1,0:T(8,128)(2,1)S(1)} async-done(((bf16[8,96,512]{2,1,0:T(8,128)(2,1)}), bf16[8,96,512]{2,1,0:T(8,128)(2,1)S(1)}, u32[]{:S(2)}, u32[]{:S(2)}) %all-to-all-start) | async-done | bytes 786464 | tf_op jit(solution)/shard_map/all_to_all | solution.py:196
  33.4 4.5 %all-to-all-start.1 = ((bf16[8,448,512]{2,1,0:T(8,128)(2,1)}), bf16[8,448,512]{2,1,0:T(8,128)(2,1)}, u32[]{:S(2)}, u32[]{:S(2)}) async-start(bf16[8,448,512]{2,1,0:T(8,128)(2,1)} %slice_units.1), calls=%async_computation.1 | async-start | bytes 7340032 | tf_op jit(solution)/shard_map/all_to_all | solution.py:199
  40.9 9.9 %collective-permute-done.far_ref = bf16[8,48,512]{2,1,0:T(8,128)(2,1)S(1)} collective-permute-done((bf16[8,48,512]{2,1,0:T(8,128)(2,1)S(1)}, bf16[8,48,512]{2,1,0:T(8,128)(2,1)S(1)}, u32[]{:S(2)}, u32[]{:S(2)}) %collective-permute-start) | collective-permute-done | bytes 393248 | tf_op jit(solution)/shard_map/ppermute | solution.py:26
  50.9 7.5 %collective-permute-done.1.far_ref = bf16[8,48,512]{2,1,0:T(8,128)(2,1)S(1)} collective-permute-done((bf16[8,48,512]{2,1,0:T(8,128)(2,1)S(1)}, bf16[8,48,512]{2,1,0:T(8,128)(2,1)S(1)}, u32[]{:S(2)}, u32[]{:S(2)}) %collective-permute-start.1) | collective-permute-done | bytes 393248 | tf_op jit(solution)/shard_map/ppermute | solution.py:26
  65.5 20.6 %collective-permute-start.3 = (bf16[1792,512]{1,0:T(8,128)(2,1)S(1)}, bf16[1792,512]{1,0:T(8,128)(2,1)S(1)}, u32[]{:S(2)}, u32[]{:S(2)}) collective-permute-start(bf16[1792,512]{1,0:T(8,128)(2,1)S(1)} %broadcast_select_fusion.mine_ref), channel_id=1, source_target_pairs={{0,16},{1,17},{2,18},{3,19},{4,20},{5,21},{6,22},{7,23},{8,24},{9,... | collective-permute-start | bytes 5505032 | tf_op jit(solution)/shard_map/ppermute | solution.py:26
  90.0 2.9 %collective-permute-start.7 = (bf16[8,48,512]{2,1,0:T(8,128)(2,1)S(1)}, bf16[8,48,512]{2,1,0:T(8,128)(2,1)S(1)}, u32[]{:S(2)}, u32[]{:S(2)}) collective-permute-start(bf16[8,48,512]{2,1,0:T(8,128)(2,1)S(1)} %slice_bitcast_fusion.2), channel_id=1, source_target_pairs={{0,96},{1,97},{2,98},{3,99},{4,100},{5,101},{6,102},{7,103},{8,104... | collective-permute-start | bytes 1179656 | tf_op jit(solution)/shard_map/ppermute | solution.py:26
  93.0 14.9 %collective-permute-done.8.before_ref = bf16[2,8,48,512]{3,2,1,0:T(8,128)(2,1)S(1)} collective-permute-done((bf16[2,8,48,512]{3,2,1,0:T(8,128)(2,1)S(1)}, bf16[2,8,48,512]{3,2,1,0:T(8,128)(2,1)S(1)}, u32[]{:S(2)}, u32[]{:S(2)}) %collective-permute-start.8) | collective-permute-done | bytes 786464 | tf_op jit(solution)/shard_map/ppermute | solution.py:26
  108.4 2.9 %collective-permute-start.11 = (bf16[8,48,512]{2,1,0:T(8,128)(2,1)S(1)}, bf16[8,48,512]{2,1,0:T(8,128)(2,1)S(1)}, u32[]{:S(2)}, u32[]{:S(2)}) collective-permute-start(bf16[8,48,512]{2,1,0:T(8,128)(2,1)S(1)} %slice_bitcast_fusion), channel_id=1, source_target_pairs={{0,96},{1,97},{2,98},{3,99},{4,100},{5,101},{6,102},{7,103},{8,104... | collective-permute-start | bytes 1179656 | tf_op jit(solution)/shard_map/ppermute | solution.py:26
  111.3 5.0 %collective-permute-done.6.a0_ref = bf16[8,48,512]{2,1,0:T(8,128)(2,1)S(1)} collective-permute-done((bf16[8,48,512]{2,1,0:T(8,128)(2,1)S(1)}, bf16[8,48,512]{2,1,0:T(8,128)(2,1)S(1)}, u32[]{:S(2)}, u32[]{:S(2)}) %collective-permute-start.6) | collective-permute-done | bytes 393248 | tf_op jit(solution)/shard_map/ppermute | solution.py:26
  116.7 7.2 %collective-permute-done.10.a0_ref = bf16[8,48,512]{2,1,0:T(8,128)(2,1)S(1)} collective-permute-done((bf16[8,48,512]{2,1,0:T(8,128)(2,1)S(1)}, bf16[8,48,512]{2,1,0:T(8,128)(2,1)S(1)}, u32[]{:S(2)}, u32[]{:S(2)}) %collective-permute-start.10) | collective-permute-done | bytes 393248 | tf_op jit(solution)/shard_map/ppermute | solution.py:26
  126.3 8.3 %project.2.rest_0_ = f32[448,384]{1,0:T(8,128)} custom-call(s32[5]{0:T(128)} %stack.41.place_ref, bf16[8,448,512]{2,1,0:T(8,128)(2,1)} %all-to-all-done.1.w_ref, bf16[8,48,512]{2,1,0:T(8,128)(2,1)} %copy-done.7, bf16[8,48,512]{2,1,0:T(8,128)(2,1)} %copy-done.10, bf16[2,8,48,512]{3,2,1,0:T(8,128)(2,1)} %copy-done.2, bf16[2,8,48,512]{3,2,1,0:T(8,128)(2,1)} %copy-done.3, ...), custom_call_target="tpu_custom_call" | custom-call | flops 1409286144 | bytes 6815744 | tf_op jit(solution)/shard_map/project/pallas_call | solution.py:125
  134.6 8.3 %project.3.rest_0_ = f32[448,384]{1,0:T(8,128)} custom-call(s32[5]{0:T(128)} %stack.41.place_ref, bf16[8,448,512]{2,1,0:T(8,128)(2,1)} %all-to-all-done.1.w_ref, bf16[8,48,512]{2,1,0:T(8,128)(2,1)} %copy-done.6, bf16[8,48,512]{2,1,0:T(8,128)(2,1)} %copy-done.8, bf16[2,8,48,512]{3,2,1,0:T(8,128)(2,1)} %copy-done.4, bf16[2,8,48,512]{3,2,1,0:T(8,128)(2,1)} %copy-done.5, ...), custom_call_target="tpu_custom_call" | custom-call | flops 1409286144 | bytes 6815744 | tf_op jit(solution)/shard_map/project/pallas_call | solution.py:125
  142.9 8.9 %project_last.2 = (f32[448,384]{1,0:T(8,128)}, f32[448,384]{1,0:T(8,128)}) custom-call(s32[5]{0:T(128)} %stack.41.place_ref, bf16[8,448,512]{2,1,0:T(8,128)(2,1)} %collective-permute-done.12.w_ref, bf16[8,48,512]{2,1,0:T(8,128)(2,1)} %copy-done.7, bf16[8,48,512]{2,1,0:T(8,128)(2,1)} %copy-done.10, bf16[2,8,48,512]{3,2,1,0:T(8,128)(2,1)} %copy-done.2, ...), custom_call_target="tpu_custom_call" | custom-call | flops 1409286144 | bytes 7503872 | tf_op jit(solution)/shard_map/project_last/pallas_call | solution.py:125
  151.8 3.0 %collective-permute-start.13 = (f32[448,384]{1,0:T(8,128)}, f32[448,384]{1,0:T(8,128)S(1)}, u32[]{:S(2)}, u32[]{:S(2)}) collective-permute-start(f32[448,384]{1,0:T(8,128)} %get-tuple-element.60), channel_id=1, source_target_pairs={{0,1},{1,0},{2,3},{3,2},{4,5},{5,4},{6,7},{7,6},{8,9},{9,8},{10,11... | collective-permute-start | bytes 2064392 | tf_op jit(solution)/shard_map/ppermute | solution.py:26
  154.8 8.9 %project_last.3 = (f32[448,384]{1,0:T(8,128)}, f32[448,384]{1,0:T(8,128)}) custom-call(s32[5]{0:T(128)} %stack.41.place_ref, bf16[8,448,512]{2,1,0:T(8,128)(2,1)} %collective-permute-done.12.w_ref, bf16[8,48,512]{2,1,0:T(8,128)(2,1)} %copy-done.6, bf16[8,48,512]{2,1,0:T(8,128)(2,1)} %copy-done.8, bf16[2,8,48,512]{3,2,1,0:T(8,128)(2,1)} %copy-done.4, ...), custom_call_target="tpu_custom_call" | custom-call | flops 1409286144 | bytes 7503872 | tf_op jit(solution)/shard_map/project_last/pallas_call | solution.py:125
  164.2 7.6 %collective-permute-done.13.got_ref = f32[448,384]{1,0:T(8,128)S(1)} collective-permute-done((f32[448,384]{1,0:T(8,128)}, f32[448,384]{1,0:T(8,128)S(1)}, u32[]{:S(2)}, u32[]{:S(2)}) %collective-permute-start.13) | collective-permute-done | bytes 688160 | tf_op jit(solution)/shard_map/ppermute | solution.py:26
  178.0 3.6 %collective-permute-done.14.rest_1_ = bf16[224,384]{1,0:T(8,128)(2,1)S(1)} collective-permute-done((bf16[224,384]{1,0:T(8,128)(2,1)}, bf16[224,384]{1,0:T(8,128)(2,1)S(1)}, u32[]{:S(2)}, u32[]{:S(2)}) %collective-permute-start.14) | collective-permute-done | bytes 172064 | tf_op jit(solution)/shard_map/ppermute | solution.py:26
  181.7 3.1 %collective-permute-start.17 = (bf16[224,384]{1,0:T(8,128)(2,1)S(1)}, bf16[224,384]{1,0:T(8,128)(2,1)S(1)}, u32[]{:S(2)}, u32[]{:S(2)}) collective-permute-start(bf16[224,384]{1,0:T(8,128)(2,1)S(1)} %collective-permute-done.16.rest_8_), channel_id=1, source_target_pairs={{0,14},{1,15},{2,0},{3,1},{4,2},{5,3},{6,4},{7,5},{8,6},{9,7},{10,... | collective-permute-start | bytes 516104 | tf_op jit(solution)/shard_map/ppermute | solution.py:26
  190.9 3.2 %collective-permute-start.19 = (bf16[224,384]{1,0:T(8,128)(2,1)S(1)}, bf16[224,384]{1,0:T(8,128)(2,1)S(1)}, u32[]{:S(2)}, u32[]{:S(2)}) collective-permute-start(bf16[224,384]{1,0:T(8,128)(2,1)S(1)} %collective-permute-done.15.rest_2_), channel_id=1, source_target_pairs={{0,2},{1,3},{2,4},{3,5},{4,6},{5,7},{6,8},{7,9},{8,10},{9,11},{10,... | collective-permute-start | bytes 516104 | tf_op jit(solution)/shard_map/ppermute | solution.py:26
  206.2 2.4 collective-permute-done.23.rest_4_
  209.9 5.1 %mix.2 = bf16[2,384,512]{2,1,0:T(8,128)(2,1)} custom-call(s32[5]{0:T(128)} %stack.41.place_ref, bf16[1792,512]{1,0:T(8,128)(2,1)} %copy-done, bf16[1792,512]{1,0:T(8,128)(2,1)} %copy-done.1, bf16[224,384]{1,0:T(8,128)(2,1)} %activate.2.rest_0_, bf16[224,384]{1,0:T(8,128)(2,1)} %copy-done.24, bf16[224,384]{1,0:T(8,128)(2,1)} %copy-done.26, ...), custom_call_target="tpu_custom_call" | custom-call | flops 1409286144 | bytes 5046272 | tf_op jit(solution)/shard_map/mix/pallas_call | solution.py:178
  215.0 8.0 %all-to-all-start.2 = ((bf16[16,48,512]{2,1,0:T(8,128)(2,1)}), bf16[16,48,512]{2,1,0:T(8,128)(2,1)S(1)}, u32[]{:S(2)}, u32[]{:S(2)}) async-start(bf16[16,48,512]{2,1,0:T(8,128)(2,1)} %bitcast.23), calls=%async_computation.2 | async-start | bytes 1572864 | tf_op jit(solution)/shard_map/all_to_all | solution.py:245
  223.5 2.7 %collective-permute-start.26 = (bf16[224,384]{1,0:T(8,128)(2,1)S(1)}, bf16[224,384]{1,0:T(8,128)(2,1)S(1)}, u32[]{:S(2)}, u32[]{:S(2)}) collective-permute-start(bf16[224,384]{1,0:T(8,128)(2,1)S(1)} %collective-permute-done.22.rest_8_), channel_id=1, source_target_pairs={{0,14},{1,15},{2,0},{3,1},{4,2},{5,3},{6,4},{7,5},{8,6},{9,7},{10,... | collective-permute-start | bytes 516104 | tf_op jit(solution)/shard_map/ppermute | solution.py:26
  226.2 3.5 %collective-permute-done.25.rest_2_ = bf16[224,384]{1,0:T(8,128)(2,1)S(1)} collective-permute-done((bf16[224,384]{1,0:T(8,128)(2,1)S(1)}, bf16[224,384]{1,0:T(8,128)(2,1)S(1)}, u32[]{:S(2)}, u32[]{:S(2)}) %collective-permute-start.25) | collective-permute-done | bytes 172064 | tf_op jit(solution)/shard_map/ppermute | solution.py:26
  233.8 3.4 %collective-permute-done.27.rest_3_ = bf16[224,384]{1,0:T(8,128)(2,1)S(1)} collective-permute-done((bf16[224,384]{1,0:T(8,128)(2,1)S(1)}, bf16[224,384]{1,0:T(8,128)(2,1)S(1)}, u32[]{:S(2)}, u32[]{:S(2)}) %collective-permute-start.27) | collective-permute-done | bytes 172064 | tf_op jit(solution)/shard_map/ppermute | solution.py:26
  237.3 3.3 %collective-permute-start.30 = (bf16[112,384]{1,0:T(8,128)(2,1)S(1)}, bf16[112,384]{1,0:T(8,128)(2,1)S(1)}, u32[]{:S(2)}, u32[]{:S(2)}) collective-permute-start(bf16[112,384]{1,0:T(8,128)(2,1)S(1)} %slice.45), channel_id=1, source_target_pairs={{0,14},{1,15},{2,0},{3,1},{4,2},{5,3},{6,4},{7,5},{8,6},{9,7},{10,... | collective-permute-start | bytes 258056 | tf_op jit(solution)/shard_map/ppermute | solution.py:26
  240.6 2.4 collective-permute-done.28.rest_4_
  244.2 5.0 %mix.3 = bf16[2,384,512]{2,1,0:T(8,128)(2,1)} custom-call(s32[5]{0:T(128)} %stack.41.place_ref, bf16[1792,512]{1,0:T(8,128)(2,1)} %copy-done, bf16[1792,512]{1,0:T(8,128)(2,1)} %copy-done.1, bf16[224,384]{1,0:T(8,128)(2,1)} %activate.3.rest_0_, bf16[224,384]{1,0:T(8,128)(2,1)} %copy-done.22, bf16[224,384]{1,0:T(8,128)(2,1)} %copy-done.28, ...), custom_call_target="tpu_custom_call" | custom-call | flops 1409286144 | bytes 5046272 | tf_op jit(solution)/shard_map/mix/pallas_call | solution.py:178
  249.3 7.2 %all-to-all-start.3 = ((bf16[16,48,512]{2,1,0:T(8,128)(2,1)}), bf16[16,48,512]{2,1,0:T(8,128)(2,1)S(1)}, u32[]{:S(2)}, u32[]{:S(2)}) async-start(bf16[16,48,512]{2,1,0:T(8,128)(2,1)} %bitcast.24), calls=%async_computation.3 | async-start | bytes 1572864 | tf_op jit(solution)/shard_map/all_to_all | solution.py:245
  256.6 10.1 %all-to-all-done.3 = bf16[16,48,512]{2,1,0:T(8,128)(2,1)S(1)} async-done(((bf16[16,48,512]{2,1,0:T(8,128)(2,1)}), bf16[16,48,512]{2,1,0:T(8,128)(2,1)S(1)}, u32[]{:S(2)}, u32[]{:S(2)}) %all-to-all-start.3) | async-done | bytes 786464 | tf_op jit(solution)/shard_map/all_to_all | solution.py:245
  (132 shorter events, 52.1 us)
Async XLA Ops:
  1.9 31.6 %all-to-all-start = ((bf16[8,96,512]{2,1,0:T(8,128)(2,1)}), bf16[8,96,512]{2,1,0:T(8,128)(2,1)S(1)}, u32[]{:S(2)}, u32[]{:S(2)}) async-start(bf16[8,96,512]{2,1,0:T(8,128)(2,1)} %broadcast_in_dim.2), calls=%async_computation | async-start | bytes 1572864 | tf_op jit(solution)/shard_map/all_to_all | solution.py:196
  33.4 91.9 %all-to-all-start.1 = ((bf16[8,448,512]{2,1,0:T(8,128)(2,1)}), bf16[8,448,512]{2,1,0:T(8,128)(2,1)}, u32[]{:S(2)}, u32[]{:S(2)}) async-start(bf16[8,448,512]{2,1,0:T(8,128)(2,1)} %slice_units.1), calls=%async_computation.1 | async-start | bytes 7340032 | tf_op jit(solution)/shard_map/all_to_all | solution.py:199
  38.9 12.0 %collective-permute-start = (bf16[8,48,512]{2,1,0:T(8,128)(2,1)S(1)}, bf16[8,48,512]{2,1,0:T(8,128)(2,1)S(1)}, u32[]{:S(2)}, u32[]{:S(2)}) collective-permute-start(bf16[8,48,512]{2,1,0:T(8,128)(2,1)S(1)} %get-tuple-element.45.near_ref), channel_id=1, source_target_pairs={{0,128},{1,129},{2,130},{3,131},{4,132},{5,133},{6,134},{7,135},{8... | collective-permute-start | bytes 1179656 | tf_op jit(solution)/shard_map/ppermute | solution.py:26
  39.7 18.7 %collective-permute-start.1 = (bf16[8,48,512]{2,1,0:T(8,128)(2,1)S(1)}, bf16[8,48,512]{2,1,0:T(8,128)(2,1)S(1)}, u32[]{:S(2)}, u32[]{:S(2)}) collective-permute-start(bf16[8,48,512]{2,1,0:T(8,128)(2,1)S(1)} %get-tuple-element.51.near_ref), channel_id=1, source_target_pairs={{0,128},{1,129},{2,130},{3,131},{4,132},{5,133},{6,134},{7,135},{8... | collective-permute-start | bytes 1179656 | tf_op jit(solution)/shard_map/ppermute | solution.py:26
  60.4 29.1 %collective-permute-start.4 = (bf16[2,8,48,512]{3,2,1,0:T(8,128)(2,1)S(1)}, bf16[2,8,48,512]{3,2,1,0:T(8,128)(2,1)S(1)}, u32[]{:S(2)}, u32[]{:S(2)}) collective-permute-start(bf16[2,8,48,512]{3,2,1,0:T(8,128)(2,1)S(1)} %pad_maximum_fusion), channel_id=1, source_target_pairs={{0,32},{1,33},{2,34},{3,35},{4,36},{5,37},{6,38},{7,39},{8,40},{9,... | collective-permute-start | bytes 2359304 | tf_op jit(solution)/shard_map/ppermute | solution.py:26
  62.1 27.9 %collective-permute-start.5 = (bf16[2,8,48,512]{3,2,1,0:T(8,128)(2,1)S(1)}, bf16[2,8,48,512]{3,2,1,0:T(8,128)(2,1)S(1)}, u32[]{:S(2)}, u32[]{:S(2)}) collective-permute-start(bf16[2,8,48,512]{3,2,1,0:T(8,128)(2,1)S(1)} %pad_maximum_fusion), channel_id=1, source_target_pairs={{0,96},{1,97},{2,98},{3,99},{4,100},{5,101},{6,102},{7,103},{8,104... | collective-permute-start | bytes 2359304 | tf_op jit(solution)/shard_map/ppermute | solution.py:26
  65.5 59.9 %collective-permute-start.3 = (bf16[1792,512]{1,0:T(8,128)(2,1)S(1)}, bf16[1792,512]{1,0:T(8,128)(2,1)S(1)}, u32[]{:S(2)}, u32[]{:S(2)}) collective-permute-start(bf16[1792,512]{1,0:T(8,128)(2,1)S(1)} %broadcast_select_fusion.mine_ref), channel_id=1, source_target_pairs={{0,16},{1,17},{2,18},{3,19},{4,20},{5,21},{6,22},{7,23},{8,24},{9,... | collective-permute-start | bytes 5505032 | tf_op jit(solution)/shard_map/ppermute | solution.py:26
  86.2 21.7 %collective-permute-start.8 = (bf16[2,8,48,512]{3,2,1,0:T(8,128)(2,1)S(1)}, bf16[2,8,48,512]{3,2,1,0:T(8,128)(2,1)S(1)}, u32[]{:S(2)}, u32[]{:S(2)}) collective-permute-start(bf16[2,8,48,512]{3,2,1,0:T(8,128)(2,1)S(1)} %pad_maximum_fusion.1), channel_id=1, source_target_pairs={{0,32},{1,33},{2,34},{3,35},{4,36},{5,37},{6,38},{7,39},{8,40},{9,... | collective-permute-start | bytes 2359304 | tf_op jit(solution)/shard_map/ppermute | solution.py:26
  87.8 20.5 %collective-permute-start.9 = (bf16[2,8,48,512]{3,2,1,0:T(8,128)(2,1)S(1)}, bf16[2,8,48,512]{3,2,1,0:T(8,128)(2,1)S(1)}, u32[]{:S(2)}, u32[]{:S(2)}) collective-permute-start(bf16[2,8,48,512]{3,2,1,0:T(8,128)(2,1)S(1)} %pad_maximum_fusion.1), channel_id=1, source_target_pairs={{0,96},{1,97},{2,98},{3,99},{4,100},{5,101},{6,102},{7,103},{8,104... | collective-permute-start | bytes 2359304 | tf_op jit(solution)/shard_map/ppermute | solution.py:26
  89.5 26.8 %collective-permute-start.6 = (bf16[8,48,512]{2,1,0:T(8,128)(2,1)S(1)}, bf16[8,48,512]{2,1,0:T(8,128)(2,1)S(1)}, u32[]{:S(2)}, u32[]{:S(2)}) collective-permute-start(bf16[8,48,512]{2,1,0:T(8,128)(2,1)S(1)} %slice_bitcast_fusion.3), channel_id=1, source_target_pairs={{0,32},{1,33},{2,34},{3,35},{4,36},{5,37},{6,38},{7,39},{8,40},{9,... | collective-permute-start | bytes 1179656 | tf_op jit(solution)/shard_map/ppermute | solution.py:26
  90.0 26.7 %collective-permute-start.7 = (bf16[8,48,512]{2,1,0:T(8,128)(2,1)S(1)}, bf16[8,48,512]{2,1,0:T(8,128)(2,1)S(1)}, u32[]{:S(2)}, u32[]{:S(2)}) collective-permute-start(bf16[8,48,512]{2,1,0:T(8,128)(2,1)S(1)} %slice_bitcast_fusion.2), channel_id=1, source_target_pairs={{0,96},{1,97},{2,98},{3,99},{4,100},{5,101},{6,102},{7,103},{8,104... | collective-permute-start | bytes 1179656 | tf_op jit(solution)/shard_map/ppermute | solution.py:26
  107.9 16.0 %collective-permute-start.10 = (bf16[8,48,512]{2,1,0:T(8,128)(2,1)S(1)}, bf16[8,48,512]{2,1,0:T(8,128)(2,1)S(1)}, u32[]{:S(2)}, u32[]{:S(2)}) collective-permute-start(bf16[8,48,512]{2,1,0:T(8,128)(2,1)S(1)} %slice_bitcast_fusion.1), channel_id=1, source_target_pairs={{0,32},{1,33},{2,34},{3,35},{4,36},{5,37},{6,38},{7,39},{8,40},{9,... | collective-permute-start | bytes 1179656 | tf_op jit(solution)/shard_map/ppermute | solution.py:26
  108.4 15.5 %collective-permute-start.11 = (bf16[8,48,512]{2,1,0:T(8,128)(2,1)S(1)}, bf16[8,48,512]{2,1,0:T(8,128)(2,1)S(1)}, u32[]{:S(2)}, u32[]{:S(2)}) collective-permute-start(bf16[8,48,512]{2,1,0:T(8,128)(2,1)S(1)} %slice_bitcast_fusion), channel_id=1, source_target_pairs={{0,96},{1,97},{2,98},{3,99},{4,100},{5,101},{6,102},{7,103},{8,104... | collective-permute-start | bytes 1179656 | tf_op jit(solution)/shard_map/ppermute | solution.py:26
  125.4 17.5 %collective-permute-start.12 = (bf16[8,448,512]{2,1,0:T(8,128)(2,1)}, bf16[8,448,512]{2,1,0:T(8,128)(2,1)}, u32[]{:S(2)}, u32[]{:S(2)}) collective-permute-start(bf16[8,448,512]{2,1,0:T(8,128)(2,1)} %all-to-all-done.1.w_ref), channel_id=1, source_target_pairs={{0,16},{1,17},{2,18},{3,19},{4,20},{5,21},{6,22},{7,23},{8,24},{9,... | collective-permute-start | bytes 11010056 | tf_op jit(solution)/shard_map/ppermute | solution.py:26
  151.8 20.0 %collective-permute-start.13 = (f32[448,384]{1,0:T(8,128)}, f32[448,384]{1,0:T(8,128)S(1)}, u32[]{:S(2)}, u32[]{:S(2)}) collective-permute-start(f32[448,384]{1,0:T(8,128)} %get-tuple-element.60), channel_id=1, source_target_pairs={{0,1},{1,0},{2,3},{3,2},{4,5},{5,4},{6,7},{7,6},{8,9},{9,8},{10,11... | collective-permute-start | bytes 2064392 | tf_op jit(solution)/shard_map/ppermute | solution.py:26
  163.7 22.2 %collective-permute-start.18 = (f32[448,384]{1,0:T(8,128)}, f32[448,384]{1,0:T(8,128)S(1)}, u32[]{:S(2)}, u32[]{:S(2)}) collective-permute-start(f32[448,384]{1,0:T(8,128)} %get-tuple-element.62), channel_id=1, source_target_pairs={{0,1},{1,0},{2,3},{3,2},{4,5},{5,4},{6,7},{7,6},{8,9},{9,8},{10,11... | collective-permute-start | bytes 2064392 | tf_op jit(solution)/shard_map/ppermute | solution.py:26
  174.7 6.8 %collective-permute-start.14 = (bf16[224,384]{1,0:T(8,128)(2,1)}, bf16[224,384]{1,0:T(8,128)(2,1)S(1)}, u32[]{:S(2)}, u32[]{:S(2)}) collective-permute-start(bf16[224,384]{1,0:T(8,128)(2,1)} %activate.2.rest_0_), channel_id=1, source_target_pairs={{0,2},{1,3},{2,4},{3,5},{4,6},{5,7},{6,8},{7,9},{8,10},{9,11},{10,... | collective-permute-start | bytes 516104 | tf_op jit(solution)/shard_map/ppermute | solution.py:26
  181.6 6.6 %collective-permute-start.15 = (bf16[224,384]{1,0:T(8,128)(2,1)S(1)}, bf16[224,384]{1,0:T(8,128)(2,1)S(1)}, u32[]{:S(2)}, u32[]{:S(2)}) collective-permute-start(bf16[224,384]{1,0:T(8,128)(2,1)S(1)} %collective-permute-done.14.rest_1_), channel_id=1, source_target_pairs={{0,2},{1,3},{2,4},{3,5},{4,6},{5,7},{6,8},{7,9},{8,10},{9,11},{10,... | collective-permute-start | bytes 516104 | tf_op jit(solution)/shard_map/ppermute | solution.py:26
  181.7 6.5 %collective-permute-start.17 = (bf16[224,384]{1,0:T(8,128)(2,1)S(1)}, bf16[224,384]{1,0:T(8,128)(2,1)S(1)}, u32[]{:S(2)}, u32[]{:S(2)}) collective-permute-start(bf16[224,384]{1,0:T(8,128)(2,1)S(1)} %collective-permute-done.16.rest_8_), channel_id=1, source_target_pairs={{0,14},{1,15},{2,0},{3,1},{4,2},{5,3},{6,4},{7,5},{8,6},{9,7},{10,... | collective-permute-start | bytes 516104 | tf_op jit(solution)/shard_map/ppermute | solution.py:26
  190.4 7.5 %collective-permute-start.21 = (bf16[224,384]{1,0:T(8,128)(2,1)}, bf16[224,384]{1,0:T(8,128)(2,1)S(1)}, u32[]{:S(2)}, u32[]{:S(2)}) collective-permute-start(bf16[224,384]{1,0:T(8,128)(2,1)} %activate.3.rest_0_), channel_id=1, source_target_pairs={{0,2},{1,3},{2,4},{3,5},{4,6},{5,7},{6,8},{7,9},{8,10},{9,11},{10,... | collective-permute-start | bytes 516104 | tf_op jit(solution)/shard_map/ppermute | solution.py:26
  190.9 8.9 %collective-permute-start.19 = (bf16[224,384]{1,0:T(8,128)(2,1)S(1)}, bf16[224,384]{1,0:T(8,128)(2,1)S(1)}, u32[]{:S(2)}, u32[]{:S(2)}) collective-permute-start(bf16[224,384]{1,0:T(8,128)(2,1)S(1)} %collective-permute-done.15.rest_2_), channel_id=1, source_target_pairs={{0,2},{1,3},{2,4},{3,5},{4,6},{5,7},{6,8},{7,9},{8,10},{9,11},{10,... | collective-permute-start | bytes 516104 | tf_op jit(solution)/shard_map/ppermute | solution.py:26
  194.1 6.6 %collective-permute-start.20 = (bf16[224,384]{1,0:T(8,128)(2,1)S(1)}, bf16[224,384]{1,0:T(8,128)(2,1)S(1)}, u32[]{:S(2)}, u32[]{:S(2)}) collective-permute-start(bf16[224,384]{1,0:T(8,128)(2,1)S(1)} %collective-permute-done.17.rest_7_), channel_id=1, source_target_pairs={{0,14},{1,15},{2,0},{3,1},{4,2},{5,3},{6,4},{7,5},{8,6},{9,7},{10,... | collective-permute-start | bytes 516104 | tf_op jit(solution)/shard_map/ppermute | solution.py:26
  194.1 8.6 %collective-permute-start.22 = (bf16[224,384]{1,0:T(8,128)(2,1)}, bf16[224,384]{1,0:T(8,128)(2,1)S(1)}, u32[]{:S(2)}, u32[]{:S(2)}) collective-permute-start(bf16[224,384]{1,0:T(8,128)(2,1)} %activate.3.rest_0_), channel_id=1, source_target_pairs={{0,14},{1,15},{2,0},{3,1},{4,2},{5,3},{6,4},{7,5},{8,6},{9,7},{10,... | collective-permute-start | bytes 516104 | tf_op jit(solution)/shard_map/ppermute | solution.py:26
  202.8 5.8 %collective-permute-start.23 = (bf16[112,384]{1,0:T(8,128)(2,1)S(1)}, bf16[112,384]{1,0:T(8,128)(2,1)S(1)}, u32[]{:S(2)}, u32[]{:S(2)}) collective-permute-start(bf16[112,384]{1,0:T(8,128)(2,1)S(1)} %slice.36), channel_id=1, source_target_pairs={{0,2},{1,3},{2,4},{3,5},{4,6},{5,7},{6,8},{7,9},{8,10},{9,11},{10,... | collective-permute-start | bytes 258056 | tf_op jit(solution)/shard_map/ppermute | solution.py:26
  215.0 34.3 %all-to-all-start.2 = ((bf16[16,48,512]{2,1,0:T(8,128)(2,1)}), bf16[16,48,512]{2,1,0:T(8,128)(2,1)S(1)}, u32[]{:S(2)}, u32[]{:S(2)}) async-start(bf16[16,48,512]{2,1,0:T(8,128)(2,1)} %bitcast.23), calls=%async_computation.2 | async-start | bytes 1572864 | tf_op jit(solution)/shard_map/all_to_all | solution.py:245
  223.0 6.8 %collective-permute-start.25 = (bf16[224,384]{1,0:T(8,128)(2,1)S(1)}, bf16[224,384]{1,0:T(8,128)(2,1)S(1)}, u32[]{:S(2)}, u32[]{:S(2)}) collective-permute-start(bf16[224,384]{1,0:T(8,128)(2,1)S(1)} %collective-permute-done.21.rest_1_), channel_id=1, source_target_pairs={{0,2},{1,3},{2,4},{3,5},{4,6},{5,7},{6,8},{7,9},{8,10},{9,11},{10,... | collective-permute-start | bytes 516104 | tf_op jit(solution)/shard_map/ppermute | solution.py:26
  223.5 7.1 %collective-permute-start.26 = (bf16[224,384]{1,0:T(8,128)(2,1)S(1)}, bf16[224,384]{1,0:T(8,128)(2,1)S(1)}, u32[]{:S(2)}, u32[]{:S(2)}) collective-permute-start(bf16[224,384]{1,0:T(8,128)(2,1)S(1)} %collective-permute-done.22.rest_8_), channel_id=1, source_target_pairs={{0,14},{1,15},{2,0},{3,1},{4,2},{5,3},{6,4},{7,5},{8,6},{9,7},{10,... | collective-permute-start | bytes 516104 | tf_op jit(solution)/shard_map/ppermute | solution.py:26
  230.6 6.6 %collective-permute-start.27 = (bf16[224,384]{1,0:T(8,128)(2,1)S(1)}, bf16[224,384]{1,0:T(8,128)(2,1)S(1)}, u32[]{:S(2)}, u32[]{:S(2)}) collective-permute-start(bf16[224,384]{1,0:T(8,128)(2,1)S(1)} %collective-permute-done.25.rest_2_), channel_id=1, source_target_pairs={{0,2},{1,3},{2,4},{3,5},{4,6},{5,7},{6,8},{7,9},{8,10},{9,11},{10,... | collective-permute-start | bytes 516104 | tf_op jit(solution)/shard_map/ppermute | solution.py:26
  231.5 5.8 %collective-permute-start.29 = (bf16[224,384]{1,0:T(8,128)(2,1)S(1)}, bf16[224,384]{1,0:T(8,128)(2,1)S(1)}, u32[]{:S(2)}, u32[]{:S(2)}) collective-permute-start(bf16[224,384]{1,0:T(8,128)(2,1)S(1)} %collective-permute-done.26.rest_7_), channel_id=1, source_target_pairs={{0,14},{1,15},{2,0},{3,1},{4,2},{5,3},{6,4},{7,5},{8,6},{9,7},{10,... | collective-permute-start | bytes 516104 | tf_op jit(solution)/shard_map/ppermute | solution.py:26
  237.2 5.8 %collective-permute-start.28 = (bf16[112,384]{1,0:T(8,128)(2,1)S(1)}, bf16[112,384]{1,0:T(8,128)(2,1)S(1)}, u32[]{:S(2)}, u32[]{:S(2)}) collective-permute-start(bf16[112,384]{1,0:T(8,128)(2,1)S(1)} %slice.44), channel_id=1, source_target_pairs={{0,2},{1,3},{2,4},{3,5},{4,6},{5,7},{6,8},{7,9},{8,10},{9,11},{10,... | collective-permute-start | bytes 258056 | tf_op jit(solution)/shard_map/ppermute | solution.py:26
  237.3 5.6 %collective-permute-start.30 = (bf16[112,384]{1,0:T(8,128)(2,1)S(1)}, bf16[112,384]{1,0:T(8,128)(2,1)S(1)}, u32[]{:S(2)}, u32[]{:S(2)}) collective-permute-start(bf16[112,384]{1,0:T(8,128)(2,1)S(1)} %slice.45), channel_id=1, source_target_pairs={{0,14},{1,15},{2,0},{3,1},{4,2},{5,3},{6,4},{7,5},{8,6},{9,7},{10,... | collective-permute-start | bytes 258056 | tf_op jit(solution)/shard_map/ppermute | solution.py:26
  249.3 17.4 %all-to-all-start.3 = ((bf16[16,48,512]{2,1,0:T(8,128)(2,1)}), bf16[16,48,512]{2,1,0:T(8,128)(2,1)S(1)}, u32[]{:S(2)}, u32[]{:S(2)}) async-start(bf16[16,48,512]{2,1,0:T(8,128)(2,1)} %bitcast.24), calls=%async_computation.3 | async-start | bytes 1572864 | tf_op jit(solution)/shard_map/all_to_all | solution.py:245
  (37 other events, 498.7 us)

commit v2 on v1

v2 whole, which is shorter than its diff:
```python
import functools
import itertools

import jax
import jax.numpy as jnp
from jax import lax
from jax.experimental import pallas as pl
from jax.experimental.pallas import tpu as pltpu
from jax.sharding import Mesh, PartitionSpec as P

AXES = ("xl", "y", "c", "z", "xh")
SIZES = (2, 4, 2, 8, 2)
CHUNKS = 2
FIRST = 160
TOGETHER = 2
F32, BF16 = jnp.float32, jnp.bfloat16
SCALARS = pl.BlockSpec(memory_space=pltpu.SMEM)
WHOLE = pl.BlockSpec(memory_space=pltpu.VMEM)


def send(value, move):
    flat = lambda at: sum(i * k for i, k in zip(at, (128, 32, 16, 2, 1)))
    pairs = []
    for at in itertools.product(*map(range, SIZES)):
        to = move(*at)
        if to is not None:
            pairs.append((flat(at), flat(tuple(i % n for i, n in zip(to, SIZES)))))
    return lax.ppermute(value, AXES, pairs)


def along_z(value, step):
    return send(value, lambda xl, y, c, z, xh: (xl, y, c, z + step, xh))


def along_y(value, step):
    return send(value, lambda xl, y, c, z, xh: (xl, y + step, c, z, xh))


def swap_xl(value):
    return send(value, lambda xl, y, c, z, xh: (1 - xl, y, c, z, xh))


def swap_xh(value):
    return send(value, lambda xl, y, c, z, xh: (xl, y, c, z, 1 - xh))


def swap_core(value):
    return send(value, lambda xl, y, c, z, xh: (xl, y, 1 - c, z, xh))


def together(*values):
    return lax.optimization_barrier(values)


def cost(flops, *arrays):
    size = sum(a.size * a.dtype.itemsize for a in arrays)
    return pl.CostEstimate(flops=flops // 64, bytes_accessed=size // 64, transcendentals=0)


def regroup(place, parts):
    nz = SIZES[3]

    def body(place_ref, *rest):
        z = place_ref[3]
        for s, part_ref in enumerate(rest[:nz]):
            rest[nz][(z + nz - s) % nz] = part_ref[...]

    return pl.pallas_call(
        body,
        in_specs=[SCALARS] + [WHOLE] * nz,
        out_specs=WHOLE,
        out_shape=jax.ShapeDtypeStruct((nz, *parts[0].shape), BF16),
        cost_estimate=cost(0, *parts, *parts),
        name="regroup",
    )(place, *parts)


def slice_units(gate, up, nz):
    depth, width = gate.shape
    units = width // nz
    step = 256
    cuts = ((0, FIRST), (FIRST, units))

    def body(g_ref, u_ref, *o_refs):
        for w_ref, at in ((g_ref, 0), (u_ref, 1)):
            w = w_ref[...].T.reshape(nz, units, step)
            for (lo, hi), o_ref in zip(cuts, o_refs):
                o_ref[:, at * (hi - lo) : (at + 1) * (hi - lo)] = w[:, lo:hi]

    outs = [jax.ShapeDtypeStruct((nz, 2 * (hi - lo), depth), gate.dtype) for lo, hi in cuts]
    return pl.pallas_call(
        body,
        grid=(depth // step,),
        in_specs=[pl.BlockSpec((step, width), lambda k: (k, 0))] * 2,
        out_specs=[pl.BlockSpec((*o.shape[:2], step), lambda k: (0, 0, k)) for o in outs],
        out_shape=outs,
        cost_estimate=cost(0, gate, up, *outs),
        name="slice_units",
    )(gate, up)


def project(place, weight, pieces, here=None):
    nz, units, depth = weight.shape
    rows = pieces[0].shape[1] // CHUNKS
    width = 8 * rows * CHUNKS
    last = here is not None

    def body(place_ref, w_ref, *rest):
        piece_refs, rest = rest[:8], rest[8:]
        here_ref = rest[0] if last else None
        outs, (t_ref, acc_ref) = rest[last:-2], rest[-2:]
        xl, y = place_ref[0], place_ref[1]
        k = pl.program_id(0)
        term = None
        for j in range(TOGETHER):
            for n, piece_ref in enumerate(piece_refs):
                at = ((y + n // 2) % 4) * 2 + (xl + n % 2) % 2
                for i in range(CHUNKS):
                    to = pl.multiple_of((8 * i + at) * rows, rows)
                    t_ref[j, pl.ds(to, rows)] = piece_ref[j, i * rows : (i + 1) * rows]
            product = lax.dot_general(
                w_ref[j], t_ref[j], (((1,), (1,)), ((), ())), preferred_element_type=F32
            )
            term = product if term is None else term + product

        @pl.when(k == 0)
        def _():
            acc_ref[...] = term

        @pl.when(k > 0)
        def _():
            acc_ref[...] += term

        @pl.when(k == nz // TOGETHER - 1)
        def _():
            if last:
                same = place_ref[2] == place_ref[4]
                outs[0][...] = jnp.where(same, here_ref[...], acc_ref[...])
                outs[1][...] = jnp.where(same, acc_ref[...], here_ref[...])
            else:
                outs[0][...] = acc_ref[...]

    full = pl.BlockSpec((units, width), lambda k: (0, 0))
    out = jax.ShapeDtypeStruct((units, width), F32)
    args = (weight, *pieces) + ((here,) if last else ())
    return pl.pallas_call(
        body,
        grid=(nz // TOGETHER,),
        in_specs=[SCALARS, pl.BlockSpec((TOGETHER, units, depth), lambda k: (k, 0, 0))]
        + [pl.BlockSpec((TOGETHER, CHUNKS * rows, depth), lambda k: (k, 0, 0))] * 8
        + [full] * last,
        out_specs=[full] * (1 + last),
        out_shape=[out] * (1 + last),
        scratch_shapes=[pltpu.VMEM((TOGETHER, width, depth), BF16), pltpu.VMEM((units, width), F32)],
        cost_estimate=cost(2 * nz * units * depth * width, *args),
        name="project_last" if last else "project",
    )(place, *args)


def activate(keep, got):
    units, rows = keep.shape[0] // 2, keep.shape[1]

    def body(keep_ref, got_ref, o_ref):
        gate = keep_ref[:units] + got_ref[:units]
        up = keep_ref[units:] + got_ref[units:]
        o_ref[...] = (gate / (1 + jnp.exp(-gate)) * up).astype(o_ref.dtype)

    return pl.pallas_call(
        body,
        in_specs=[WHOLE] * 2,
        out_specs=WHOLE,
        out_shape=jax.ShapeDtypeStruct((units, rows), BF16),
        cost_estimate=cost(0, keep, got),
        name="activate",
    )(keep, got)


def mix(place, chunk, rings, mine, theirs):
    nz = SIZES[3]
    sizes = [ring[0].shape[0] for ring in rings]
    units, rows = sum(sizes), rings[0][0].shape[1] // CHUNKS
    width = mine.shape[1]
    order = (0, 1, 2, 3, 4, -4, -3, -2, -1)
    parts = [ring[s] for ring in rings for s in order]

    def body(place_ref, mine_ref, theirs_ref, *rest):
        part_refs, (o_ref, h_ref) = list(rest[:-2]), rest[-2:]
        c, z = place_ref[2], place_ref[3]
        first = 0
        for size in sizes:
            for s in order:
                length = size // 2 if abs(s) == nz // 2 else size
                at = ((z - s + nz) % nz) * units + first + (length if s == -nz // 2 else 0)
                h_ref[pl.ds(pl.multiple_of(at, 16), length)] = part_refs.pop(0)[...]
            first += size
        for side, w_ref in ((c, mine_ref), (1 - c, theirs_ref)):
            o_ref[side] = lax.dot_general(
                h_ref[...], w_ref[...], (((0,), (0,)), ((), ())), preferred_element_type=F32
            ).astype(o_ref.dtype)

    return pl.pallas_call(
        body,
        grid=(1,),
        in_specs=[SCALARS]
        + [pl.BlockSpec(mine.shape, lambda k: (0, 0))] * 2
        + [pl.BlockSpec((p.shape[0], rows), lambda k: (0, chunk)) for p in parts],
        out_specs=pl.BlockSpec((2, rows, width), lambda k: (0, 0, 0)),
        out_shape=jax.ShapeDtypeStruct((2, rows, width), BF16),
        scratch_shapes=[pltpu.VMEM((nz * units, rows), BF16)],
        cost_estimate=cost(4 * nz * units * rows * width, mine, theirs, *parts),
        name="mix",
    )(place, mine, theirs, *parts)


def shards(tokens, gate_weight, up_weight, down_weight):
    xl, y, c, z, xh = (lax.axis_index(a) for a in AXES)
    place = jnp.stack([xl, y, c, z, xh]).astype(jnp.int32)
    nz = SIZES[3]
    rows = tokens.shape[0] // CHUNKS

    around = {0: tokens}
    for s in (1, -1, 2, -2, 4):
        around[s] = along_z(tokens, s)
    around[3], around[-3] = along_z(around[2], 1), along_z(around[-2], -1)
    sliced = slice_units(gate_weight, up_weight, nz)
    ready, *around = together(sliced[0], *(around[s] for s in (0, 1, 2, 3, 4, -3, -2, -1)))
    weights = [lax.all_to_all(ready, "z", 0, 0, tiled=True)]

    near = regroup(place, around)
    far = swap_xl(near)
    near_before, near_after = along_y(near, 1), along_y(near, -1)
    far_before, far_after = along_y(far, 1), along_y(far, -1)
    ready, weights[0], near_before, near_after, far_before, far_after = together(
        sliced[1], weights[0], near_before, near_after, far_before, far_after
    )
    weights.append(lax.all_to_all(ready, "z", 0, 0, tiled=True))
    near_across, far_across = along_y(near_before, 1), along_y(far_after, -1)
    pieces = (near, far, near_after, far_after, near_across, far_across, near_before, far_before)

    def sums(weight):
        other = swap_core(weight)
        here = project(place, weight, pieces)[0]
        return project(place, other, pieces, here)

    keep, give = sums(weights[0])
    got = swap_xh(give)
    hiddens = [activate(keep, got)]

    down_weight, _ = together(down_weight, far)
    moved = send(
        down_weight,
        lambda xl, y, c, z, xh: (xl, y, 1 - c, z, 1 - xh) if c != xh else None,
    )
    moved, weights[1], _ = together(moved, weights[1], give)
    mine = jnp.where(c == xh, down_weight, moved)
    keep, give = sums(weights[1])
    hiddens.append(activate(keep, swap_xh(give)))
    mine, _ = together(mine, give)
    theirs = swap_core(mine)

    rings = []
    for hidden in hiddens:
        ring, up, down = {0: hidden}, hidden, hidden
        for at in range(nz // 2):
            if at == nz // 2 - 1:
                half = up.shape[0] // 2
                up, down = up[:half], down[half:]
            up, down = along_z(up, 1), along_z(down, -1)
            ring.update({at + 1: up, -at - 1: down})
        rings.append(ring)

    outs = []
    for i in range(CHUNKS):
        out = mix(place, i, rings, mine, theirs).reshape(16, rows, -1)
        got = lax.all_to_all(out, ("xh", "y", "xl"), 0, 0, tiled=True)
        outs.append(jnp.sum(got.astype(F32), 0))
    return jnp.concatenate(outs)


def solution(mesh):
    split = Mesh(mesh.devices.reshape(SIZES), AXES)
    row, col = ("xl", "y", "c"), ("z", "xh")
    return jax.shard_map(
        shards,
        mesh=split,
        in_specs=(P(row, col), P(col, row), P(col, row), P(row, col)),
        out_specs=P(row, col),
        check_vma=False,
    )
```

time: 269 us -> 249 us (0.926)
  starting transfers between devices: 94.6 us -> 82.7 us
  local copies, waits for them, and re-layouts: 8.22 us -> 3.79 us
  Pallas kernels: 53.8 us -> 49.6 us
    ppermute x31 -> x36, waiting for transfers between devices: 79.6 us -> 72.4 us  [send(): return lax.ppermute(value, AXES, pairs)]
    all_to_all x2, waiting for transfers between devices: 10.1 us -> 15.4 us  [shards(): got = lax.all_to_all(out, ('xh', 'y', 'xl'), 0, 0, tiled=True)]
    ppermute x31 -> x36, starting transfers between devices: 66.4 us -> 61.8 us  [send(): return lax.ppermute(value, AXES, pairs)]
    all_to_all x2, starting transfers between devices: 13 us -> 8.92 us  [the longest x1 4.68 us: shards(): weights = [lax.all_to_all(ready, 'z', 0, 0, tiled=True)]]
    all_to_all x2, starting transfers between devices: 15.2 us -> 12 us  [shards(): got = lax.all_to_all(out, ('xh', 'y', 'xl'), 0, 0, tiled=True)]
    pallas_call x6 -> x7, Pallas kernels: 44.5 us -> 41.6 us  [the longest x4 29.4 us: project(): pl.pallas_call(body, grid=(nz // TOGETHER,), in_specs=[SCALARS, pl.BlockS...]
  transfers between devices with their start and end apart: 35 -> 40, of which waited for: 22 -> 14; matrix products, arithmetic and copies ran while one was open for 1% -> 1% of each run, Pallas kernels for 14% -> 18%
where the time goes in v2:
time: 249 us; the launch traced here: 246 us
  waiting for transfers between devices  107 us (43%)
  starting transfers between devices  82.7 us (33%)
  Pallas kernels  49.6 us (20%)
  local copies, waits for them, and re-layouts  3.79 us (2%)
  other arithmetic  2.61 us (1%)
    ppermute x36, waiting for transfers between devices, send(): return lax.ppermute(value, AXES, pairs)  72.4 us
    ppermute x36, starting transfers between devices, send(): return lax.ppermute(value, AXES, pairs)  61.8 us
    pallas_call x4, Pallas kernels, project(): pl.pallas_call(body, grid=(nz // TOGETHER,), in_specs=[SCALARS, pl.BlockS...  29.4 us
    all_to_all x1, waiting for transfers between devices, shards(): weights = [lax.all_to_all(ready, 'z', 0, 0, tiled=True)]  19.6 us
    all_to_all x2, waiting for transfers between devices, shards(): got = lax.all_to_all(out, ('xh', 'y', 'xl'), 0, 0, tiled=True)  15.4 us
    all_to_all x2, starting transfers between devices, shards(): got = lax.all_to_all(out, ('xh', 'y', 'xl'), 0, 0, tiled=True)  12 us
    pallas_call x2, Pallas kernels, mix(): pl.pallas_call(body, grid=(1,), in_specs=[SCALARS] + [pl.BlockSpec(mine.s...  10 us
  transfers between devices with their start and end apart: 40, of which 14 were waited for; matrix products, arithmetic and copies ran while one was open for 1% of the time, Pallas kernels for 18%

profile of v2, /device:TPU:2, one launch (start us, length us, event | category | flops | bytes accessed | tf_op | source)
XLA Modules:
  0.0 246.4 jit_solution(17636714130490352928)
XLA Ops:
  0.0 3.3 %collective-permute-start.1 = (bf16[96,512]{1,0:T(8,128)(2,1)}, bf16[96,512]{1,0:T(8,128)(2,1)S(1)}, u32[]{:S(2)}, u32[]{:S(2)}) collective-permute-start(bf16[96,512]{1,0:T(8,128)(2,1)} %rest_0_), channel_id=1, source_target_pairs={{0,4},{1,5},{2,6},{3,7},{4,8},{5,9},{6,10},{7,11},{8,12},{9,13},{1... | collective-permute-start | bytes 294920 | tf_op jit(solution)/shard_map/ppermute | solution.py:28
  3.3 3.0 %collective-permute-start.4 = (bf16[96,512]{1,0:T(8,128)(2,1)}, bf16[96,512]{1,0:T(8,128)(2,1)S(1)}, u32[]{:S(2)}, u32[]{:S(2)}) collective-permute-start(bf16[96,512]{1,0:T(8,128)(2,1)} %rest_0_), channel_id=1, source_target_pairs={{0,12},{1,13},{2,14},{3,15},{4,0},{5,1},{6,2},{7,3},{8,4},{9,5},{1... | collective-permute-start | bytes 294920 | tf_op jit(solution)/shard_map/ppermute | solution.py:28
  7.3 5.0 %collective-permute-start.3 = (bf16[96,512]{1,0:T(8,128)(2,1)}, bf16[96,512]{1,0:T(8,128)(2,1)S(1)}, u32[]{:S(2)}, u32[]{:S(2)}) collective-permute-start(bf16[96,512]{1,0:T(8,128)(2,1)} %rest_0_), channel_id=1, source_target_pairs={{0,8},{1,9},{2,10},{3,11},{4,12},{5,13},{6,14},{7,15},{8,0},{9,1},... | collective-permute-start | bytes 294920 | tf_op jit(solution)/shard_map/ppermute | solution.py:28
  14.6 3.2 %collective-permute-start.5 = (bf16[96,512]{1,0:T(8,128)(2,1)S(1)}, bf16[96,512]{1,0:T(8,128)(2,1)S(1)}, u32[]{:S(2)}, u32[]{:S(2)}) collective-permute-start(bf16[96,512]{1,0:T(8,128)(2,1)S(1)} %collective-permute-done.4.rest_6_), channel_id=1, source_target_pairs={{0,14},{1,15},{2,0},{3,1},{4,2},{5,3},{6,4},{7,5},{8,6},{9,7},{10,... | collective-permute-start | bytes 294920 | tf_op jit(solution)/shard_map/ppermute | solution.py:28
  17.8 3.8 %slice_units.1 = (bf16[8,320,512]{2,1,0:T(8,128)(2,1)}, bf16[8,128,512]{2,1,0:T(8,128)(2,1)}) custom-call(bf16[512,1792]{1,0:T(8,128)(2,1)} %g_ref.1, bf16[512,1792]{1,0:T(8,128)(2,1)} %u_ref.1), custom_call_target="tpu_custom_call" | custom-call | bytes 114688 | tf_op jit(solution)/shard_map/slice_units/pallas_call | solution.py:91
  22.4 4.7 %all-to-all-start = ((bf16[8,320,512]{2,1,0:T(8,128)(2,1)}), bf16[8,320,512]{2,1,0:T(8,128)(2,1)}, u32[]{:S(2)}, u32[]{:S(2)}) async-start(bf16[8,320,512]{2,1,0:T(8,128)(2,1)} %get-tuple-element.41), calls=%async_computation | async-start | bytes 5242880 | tf_op jit(solution)/shard_map/all_to_all | solution.py:227
  30.5 3.0 %collective-permute-start.10 = (bf16[8,96,512]{2,1,0:T(8,128)(2,1)}, bf16[8,96,512]{2,1,0:T(8,128)(2,1)S(1)}, u32[]{:S(2)}, u32[]{:S(2)}) collective-permute-start(bf16[8,96,512]{2,1,0:T(8,128)(2,1)} %regroup.1.rest_0_), channel_id=1, source_target_pairs={{0,96},{1,97},{2,98},{3,99},{4,100},{5,101},{6,102},{7,103},{8,104... | collective-permute-start | bytes 2359304 | tf_op jit(solution)/shard_map/ppermute | solution.py:28
  33.5 15.2 %collective-permute-done.7.rest_1_ = bf16[8,96,512]{2,1,0:T(8,128)(2,1)S(1)} collective-permute-done((bf16[8,96,512]{2,1,0:T(8,128)(2,1)}, bf16[8,96,512]{2,1,0:T(8,128)(2,1)S(1)}, u32[]{:S(2)}, u32[]{:S(2)}) %collective-permute-start.7) | collective-permute-done | bytes 786464 | tf_op jit(solution)/shard_map/ppermute | solution.py:28
  52.0 2.9 %collective-permute-done.9.rest_6_ = bf16[8,96,512]{2,1,0:T(8,128)(2,1)S(1)} collective-permute-done((bf16[8,96,512]{2,1,0:T(8,128)(2,1)}, bf16[8,96,512]{2,1,0:T(8,128)(2,1)S(1)}, u32[]{:S(2)}, u32[]{:S(2)}) %collective-permute-start.9) | collective-permute-done | bytes 786464 | tf_op jit(solution)/shard_map/ppermute | solution.py:28
  54.9 14.9 %collective-permute-done.11.rest_7_ = bf16[8,96,512]{2,1,0:T(8,128)(2,1)S(1)} collective-permute-done((bf16[8,96,512]{2,1,0:T(8,128)(2,1)S(1)}, bf16[8,96,512]{2,1,0:T(8,128)(2,1)S(1)}, u32[]{:S(2)}, u32[]{:S(2)}) %collective-permute-start.11) | collective-permute-done | bytes 786464 | tf_op jit(solution)/shard_map/ppermute | solution.py:28
  69.8 19.6 %all-to-all-done.w_ref = bf16[8,320,512]{2,1,0:T(8,128)(2,1)} async-done(((bf16[8,320,512]{2,1,0:T(8,128)(2,1)}), bf16[8,320,512]{2,1,0:T(8,128)(2,1)}, u32[]{:S(2)}, u32[]{:S(2)}) %all-to-all-start) | async-done | bytes 2621472 | tf_op jit(solution)/shard_map/all_to_all | solution.py:227
  91.3 4.2 %all-to-all-start.1 = ((bf16[8,128,512]{2,1,0:T(8,128)(2,1)}), bf16[8,128,512]{2,1,0:T(8,128)(2,1)}, u32[]{:S(2)}, u32[]{:S(2)}) async-start(bf16[8,128,512]{2,1,0:T(8,128)(2,1)} %get-tuple-element.42), calls=%async_computation.1 | async-start | bytes 2097152 | tf_op jit(solution)/shard_map/all_to_all | solution.py:236
  98.9 17.0 %collective-permute-done.14.rest_4_ = bf16[8,96,512]{2,1,0:T(8,128)(2,1)S(1)} collective-permute-done((bf16[8,96,512]{2,1,0:T(8,128)(2,1)S(1)}, bf16[8,96,512]{2,1,0:T(8,128)(2,1)S(1)}, u32[]{:S(2)}, u32[]{:S(2)}) %collective-permute-start.14) | collective-permute-done | bytes 786464 | tf_op jit(solution)/shard_map/ppermute | solution.py:28
  116.9 7.2 %project.2.rest_8_ = f32[320,768]{1,0:T(8,128)} custom-call(s32[5]{0:T(128)} %stack.23.place_ref, bf16[8,320,512]{2,1,0:T(8,128)(2,1)} %all-to-all-done.w_ref, bf16[8,96,512]{2,1,0:T(8,128)(2,1)} %regroup.1.rest_0_, bf16[8,96,512]{2,1,0:T(8,128)(2,1)} %copy-done.1, bf16[8,96,512]{2,1,0:T(8,128)(2,1)} %copy-done.2, ...), custom_call_target="tpu_custom_call" | custom-call | flops 31457280 | bytes 139264 | tf_op jit(solution)/shard_map/project/pallas_call | solution.py:146
  124.2 8.3 %project_last.2 = (f32[320,768]{1,0:T(8,128)}, f32[320,768]{1,0:T(8,128)}) custom-call(s32[5]{0:T(128)} %stack.23.place_ref, bf16[8,320,512]{2,1,0:T(8,128)(2,1)} %collective-permute-done.13.w_ref, bf16[8,96,512]{2,1,0:T(8,128)(2,1)} %regroup.1.rest_0_, bf16[8,96,512]{2,1,0:T(8,128)(2,1)} %copy-done.1, bf16[8,96,512]{2,1,0:T(8,128)(2,1)} %copy-done.2, ...), custom_call_target="tpu_custom_call" | custom-call | flops 31457280 | bytes 154624 | tf_op jit(solution)/shard_map/project_last/pallas_call | solution.py:146
  137.3 7.0 %project.3.rest_8_ = f32[128,768]{1,0:T(8,128)} custom-call(s32[5]{0:T(128)} %stack.23.place_ref, bf16[8,128,512]{2,1,0:T(8,128)(2,1)} %all-to-all-done.1.w_ref, bf16[8,96,512]{2,1,0:T(8,128)(2,1)} %regroup.1.rest_0_, bf16[8,96,512]{2,1,0:T(8,128)(2,1)} %copy-done.1, bf16[8,96,512]{2,1,0:T(8,128)(2,1)} %copy-done.2, ...), custom_call_target="tpu_custom_call" | custom-call | flops 12582912 | bytes 114688 | tf_op jit(solution)/shard_map/project/pallas_call | solution.py:146
  145.3 6.9 %project_last.3 = (f32[128,768]{1,0:T(8,128)}, f32[128,768]{1,0:T(8,128)}) custom-call(s32[5]{0:T(128)} %stack.23.place_ref, bf16[8,128,512]{2,1,0:T(8,128)(2,1)} %copy-done.8, bf16[8,96,512]{2,1,0:T(8,128)(2,1)} %regroup.1.rest_0_, bf16[8,96,512]{2,1,0:T(8,128)(2,1)} %copy-done.1, bf16[8,96,512]{2,1,0:T(8,128)(2,1)} %copy-done.2, ...), custom_call_target="tpu_custom_call" | custom-call | flops 12582912 | bytes 120832 | tf_op jit(solution)/shard_map/project_last/pallas_call | solution.py:146
  152.4 6.8 %collective-permute-done.18.got_ref = f32[320,768]{1,0:T(8,128)} collective-permute-done((f32[320,768]{1,0:T(8,128)}, f32[320,768]{1,0:T(8,128)}, u32[]{:S(2)}, u32[]{:S(2)}) %collective-permute-start.18) | collective-permute-done | bytes 983072 | tf_op jit(solution)/shard_map/ppermute | solution.py:28
  167.1 3.5 %collective-permute-done.19.rest_1_ = bf16[160,768]{1,0:T(8,128)(2,1)S(1)} collective-permute-done((bf16[160,768]{1,0:T(8,128)(2,1)}, bf16[160,768]{1,0:T(8,128)(2,1)S(1)}, u32[]{:S(2)}, u32[]{:S(2)}) %collective-permute-start.19) | collective-permute-done | bytes 245792 | tf_op jit(solution)/shard_map/ppermute | solution.py:28
  173.8 4.5 %collective-permute-done.20.rest_2_ = bf16[160,768]{1,0:T(8,128)(2,1)S(1)} collective-permute-done((bf16[160,768]{1,0:T(8,128)(2,1)S(1)}, bf16[160,768]{1,0:T(8,128)(2,1)S(1)}, u32[]{:S(2)}, u32[]{:S(2)}) %collective-permute-start.20) | collective-permute-done | bytes 245792 | tf_op jit(solution)/shard_map/ppermute | solution.py:28
  178.3 3.2 %collective-permute-start.25 = (bf16[160,768]{1,0:T(8,128)(2,1)S(1)}, bf16[160,768]{1,0:T(8,128)(2,1)S(1)}, u32[]{:S(2)}, u32[]{:S(2)}) collective-permute-start(bf16[160,768]{1,0:T(8,128)(2,1)S(1)} %collective-permute-done.24.rest_7_), channel_id=1, source_target_pairs={{0,14},{1,15},{2,0},{3,1},{4,2},{5,3},{6,4},{7,5},{8,6},{9,7},{10,... | collective-permute-start | bytes 737288 | tf_op jit(solution)/shard_map/ppermute | solution.py:28
  183.4 3.2 %collective-permute-start.32 = (bf16[64,768]{1,0:T(8,128)(2,1)}, bf16[64,768]{1,0:T(8,128)(2,1)S(1)}, u32[]{:S(2)}, u32[]{:S(2)}) collective-permute-start(bf16[64,768]{1,0:T(8,128)(2,1)} %activate.3.rest_9_), channel_id=1, source_target_pairs={{0,14},{1,15},{2,0},{3,1},{4,2},{5,3},{6,4},{7,5},{8,6},{9,7},{10,... | collective-permute-start | bytes 294920 | tf_op jit(solution)/shard_map/ppermute | solution.py:28
  189.4 3.2 %collective-permute-start.33 = (bf16[64,768]{1,0:T(8,128)(2,1)S(1)}, bf16[64,768]{1,0:T(8,128)(2,1)S(1)}, u32[]{:S(2)}, u32[]{:S(2)}) collective-permute-start(bf16[64,768]{1,0:T(8,128)(2,1)S(1)} %collective-permute-done.32.rest_17_), channel_id=1, source_target_pairs={{0,14},{1,15},{2,0},{3,1},{4,2},{5,3},{6,4},{7,5},{8,6},{9,7},{10,... | collective-permute-start | bytes 294920 | tf_op jit(solution)/shard_map/ppermute | solution.py:28
  195.3 3.4 %collective-permute-start.34 = (bf16[64,768]{1,0:T(8,128)(2,1)S(1)}, bf16[64,768]{1,0:T(8,128)(2,1)S(1)}, u32[]{:S(2)}, u32[]{:S(2)}) collective-permute-start(bf16[64,768]{1,0:T(8,128)(2,1)S(1)} %collective-permute-done.33.rest_16_), channel_id=1, source_target_pairs={{0,14},{1,15},{2,0},{3,1},{4,2},{5,3},{6,4},{7,5},{8,6},{9,7},{10,... | collective-permute-start | bytes 294920 | tf_op jit(solution)/shard_map/ppermute | solution.py:28
  198.8 3.3 %collective-permute-start.26 = (bf16[80,768]{1,0:T(8,128)(2,1)S(1)}, bf16[80,768]{1,0:T(8,128)(2,1)}, u32[]{:S(2)}, u32[]{:S(2)}) collective-permute-start(bf16[80,768]{1,0:T(8,128)(2,1)S(1)} %slice.17), channel_id=1, source_target_pairs={{0,14},{1,15},{2,0},{3,1},{4,2},{5,3},{6,4},{7,5},{8,6},{9,7},{10,... | collective-permute-start | bytes 368648 | tf_op jit(solution)/shard_map/ppermute | solution.py:28
  202.2 3.3 %collective-permute-start.35 = (bf16[32,768]{1,0:T(8,128)(2,1)S(1)}, bf16[32,768]{1,0:T(8,128)(2,1)}, u32[]{:S(2)}, u32[]{:S(2)}) collective-permute-start(bf16[32,768]{1,0:T(8,128)(2,1)S(1)} %slice.19), channel_id=1, source_target_pairs={{0,14},{1,15},{2,0},{3,1},{4,2},{5,3},{6,4},{7,5},{8,6},{9,7},{10,... | collective-permute-start | bytes 147464 | tf_op jit(solution)/shard_map/ppermute | solution.py:28
  208.1 5.0 %mix.2 = bf16[2,384,512]{2,1,0:T(8,128)(2,1)} custom-call(s32[5]{0:T(128)} %stack.23.place_ref, bf16[1792,512]{1,0:T(8,128)(2,1)} %copy-done, bf16[1792,512]{1,0:T(8,128)(2,1)} %collective-permute-done.17.theirs_ref, bf16[160,768]{1,0:T(8,128)(2,1)} %activate.2.rest_0_, bf16[160,768]{1,0:T(8,128)(2,1)} %copy-done.9, bf16[160,768]{1,0:T(8,128)(2,1)} %copy-done.11, ...), custom_call_target="tpu_custom_call" | custom-call | flops 22020096 | bytes 100352 | tf_op jit(solution)/shard_map/mix/pallas_call | solution.py:201
  213.1 7.1 %all-to-all-start.2 = ((bf16[16,48,512]{2,1,0:T(8,128)(2,1)}), bf16[16,48,512]{2,1,0:T(8,128)(2,1)S(1)}, u32[]{:S(2)}, u32[]{:S(2)}) async-start(bf16[16,48,512]{2,1,0:T(8,128)(2,1)} %bitcast.8), calls=%async_computation.2 | async-start | bytes 1572864 | tf_op jit(solution)/shard_map/all_to_all | solution.py:275
  220.2 5.0 %mix.3 = bf16[2,384,512]{2,1,0:T(8,128)(2,1)} custom-call(s32[5]{0:T(128)} %stack.23.place_ref, bf16[1792,512]{1,0:T(8,128)(2,1)} %copy-done, bf16[1792,512]{1,0:T(8,128)(2,1)} %collective-permute-done.17.theirs_ref, bf16[160,768]{1,0:T(8,128)(2,1)} %activate.2.rest_0_, bf16[160,768]{1,0:T(8,128)(2,1)} %copy-done.9, bf16[160,768]{1,0:T(8,128)(2,1)} %copy-done.11, ...), custom_call_target="tpu_custom_call" | custom-call | flops 22020096 | bytes 100352 | tf_op jit(solution)/shard_map/mix/pallas_call | solution.py:201
  225.2 5.2 %all-to-all-done.2 = bf16[16,48,512]{2,1,0:T(8,128)(2,1)S(1)} async-done(((bf16[16,48,512]{2,1,0:T(8,128)(2,1)}), bf16[16,48,512]{2,1,0:T(8,128)(2,1)S(1)}, u32[]{:S(2)}, u32[]{:S(2)}) %all-to-all-start.2) | async-done | bytes 786464 | tf_op jit(solution)/shard_map/all_to_all | solution.py:275
  230.4 4.9 %all-to-all-start.3 = ((bf16[16,48,512]{2,1,0:T(8,128)(2,1)}), bf16[16,48,512]{2,1,0:T(8,128)(2,1)S(1)}, u32[]{:S(2)}, u32[]{:S(2)}) async-start(bf16[16,48,512]{2,1,0:T(8,128)(2,1)} %bitcast.7), calls=%async_computation.3 | async-start | bytes 1572864 | tf_op jit(solution)/shard_map/all_to_all | solution.py:275
  235.4 10.2 %all-to-all-done.3 = bf16[16,48,512]{2,1,0:T(8,128)(2,1)S(1)} async-done(((bf16[16,48,512]{2,1,0:T(8,128)(2,1)}), bf16[16,48,512]{2,1,0:T(8,128)(2,1)S(1)}, u32[]{:S(2)}, u32[]{:S(2)}) %all-to-all-start.3) | async-done | bytes 786464 | tf_op jit(solution)/shard_map/all_to_all | solution.py:275
  (121 shorter events, 45.0 us)
Async XLA Ops:
  0.0 14.6 %collective-permute-start.1 = (bf16[96,512]{1,0:T(8,128)(2,1)}, bf16[96,512]{1,0:T(8,128)(2,1)S(1)}, u32[]{:S(2)}, u32[]{:S(2)}) collective-permute-start(bf16[96,512]{1,0:T(8,128)(2,1)} %rest_0_), channel_id=1, source_target_pairs={{0,4},{1,5},{2,6},{3,7},{4,8},{5,9},{6,10},{7,11},{8,12},{9,13},{1... | collective-permute-start | bytes 294920 | tf_op jit(solution)/shard_map/ppermute | solution.py:28
  3.3 11.3 %collective-permute-start.4 = (bf16[96,512]{1,0:T(8,128)(2,1)}, bf16[96,512]{1,0:T(8,128)(2,1)S(1)}, u32[]{:S(2)}, u32[]{:S(2)}) collective-permute-start(bf16[96,512]{1,0:T(8,128)(2,1)} %rest_0_), channel_id=1, source_target_pairs={{0,12},{1,13},{2,14},{3,15},{4,0},{5,1},{6,2},{7,3},{8,4},{9,5},{1... | collective-permute-start | bytes 294920 | tf_op jit(solution)/shard_map/ppermute | solution.py:28
  6.3 15.3 %collective-permute-start = (bf16[96,512]{1,0:T(8,128)(2,1)}, bf16[96,512]{1,0:T(8,128)(2,1)S(1)}, u32[]{:S(2)}, u32[]{:S(2)}) collective-permute-start(bf16[96,512]{1,0:T(8,128)(2,1)} %rest_0_), channel_id=1, source_target_pairs={{0,2},{1,3},{2,4},{3,5},{4,6},{5,7},{6,8},{7,9},{8,10},{9,11},{10,... | collective-permute-start | bytes 294920 | tf_op jit(solution)/shard_map/ppermute | solution.py:28
  7.3 14.3 %collective-permute-start.3 = (bf16[96,512]{1,0:T(8,128)(2,1)}, bf16[96,512]{1,0:T(8,128)(2,1)S(1)}, u32[]{:S(2)}, u32[]{:S(2)}) collective-permute-start(bf16[96,512]{1,0:T(8,128)(2,1)} %rest_0_), channel_id=1, source_target_pairs={{0,8},{1,9},{2,10},{3,11},{4,12},{5,13},{6,14},{7,15},{8,0},{9,1},... | collective-permute-start | bytes 294920 | tf_op jit(solution)/shard_map/ppermute | solution.py:28
  12.3 9.3 %collective-permute-start.6 = (bf16[96,512]{1,0:T(8,128)(2,1)}, bf16[96,512]{1,0:T(8,128)(2,1)S(1)}, u32[]{:S(2)}, u32[]{:S(2)}) collective-permute-start(bf16[96,512]{1,0:T(8,128)(2,1)} %rest_0_), channel_id=1, source_target_pairs={{0,14},{1,15},{2,0},{3,1},{4,2},{5,3},{6,4},{7,5},{8,6},{9,7},{10,... | collective-permute-start | bytes 294920 | tf_op jit(solution)/shard_map/ppermute | solution.py:28
  14.6 7.1 %collective-permute-start.2 = (bf16[96,512]{1,0:T(8,128)(2,1)S(1)}, bf16[96,512]{1,0:T(8,128)(2,1)S(1)}, u32[]{:S(2)}, u32[]{:S(2)}) collective-permute-start(bf16[96,512]{1,0:T(8,128)(2,1)S(1)} %collective-permute-done.1.rest_2_), channel_id=1, source_target_pairs={{0,2},{1,3},{2,4},{3,5},{4,6},{5,7},{6,8},{7,9},{8,10},{9,11},{10,... | collective-permute-start | bytes 294920 | tf_op jit(solution)/shard_map/ppermute | solution.py:28
  14.6 7.1 %collective-permute-start.5 = (bf16[96,512]{1,0:T(8,128)(2,1)S(1)}, bf16[96,512]{1,0:T(8,128)(2,1)S(1)}, u32[]{:S(2)}, u32[]{:S(2)}) collective-permute-start(bf16[96,512]{1,0:T(8,128)(2,1)S(1)} %collective-permute-done.4.rest_6_), channel_id=1, source_target_pairs={{0,14},{1,15},{2,0},{3,1},{4,2},{5,3},{6,4},{7,5},{8,6},{9,7},{10,... | collective-permute-start | bytes 294920 | tf_op jit(solution)/shard_map/ppermute | solution.py:28
  22.4 66.9 %all-to-all-start = ((bf16[8,320,512]{2,1,0:T(8,128)(2,1)}), bf16[8,320,512]{2,1,0:T(8,128)(2,1)}, u32[]{:S(2)}, u32[]{:S(2)}) async-start(bf16[8,320,512]{2,1,0:T(8,128)(2,1)} %get-tuple-element.41), calls=%async_computation | async-start | bytes 5242880 | tf_op jit(solution)/shard_map/all_to_all | solution.py:227
  29.9 18.8 %collective-permute-start.7 = (bf16[8,96,512]{2,1,0:T(8,128)(2,1)}, bf16[8,96,512]{2,1,0:T(8,128)(2,1)S(1)}, u32[]{:S(2)}, u32[]{:S(2)}) collective-permute-start(bf16[8,96,512]{2,1,0:T(8,128)(2,1)} %regroup.1.rest_0_), channel_id=1, source_target_pairs={{0,128},{1,129},{2,130},{3,131},{4,132},{5,133},{6,134},{7,135},{8... | collective-permute-start | bytes 2359304 | tf_op jit(solution)/shard_map/ppermute | solution.py:28
  30.5 21.5 %collective-permute-start.10 = (bf16[8,96,512]{2,1,0:T(8,128)(2,1)}, bf16[8,96,512]{2,1,0:T(8,128)(2,1)S(1)}, u32[]{:S(2)}, u32[]{:S(2)}) collective-permute-start(bf16[8,96,512]{2,1,0:T(8,128)(2,1)} %regroup.1.rest_0_), channel_id=1, source_target_pairs={{0,96},{1,97},{2,98},{3,99},{4,100},{5,101},{6,102},{7,103},{8,104... | collective-permute-start | bytes 2359304 | tf_op jit(solution)/shard_map/ppermute | solution.py:28
  33.5 21.4 %collective-permute-start.9 = (bf16[8,96,512]{2,1,0:T(8,128)(2,1)}, bf16[8,96,512]{2,1,0:T(8,128)(2,1)S(1)}, u32[]{:S(2)}, u32[]{:S(2)}) collective-permute-start(bf16[8,96,512]{2,1,0:T(8,128)(2,1)} %regroup.1.rest_0_), channel_id=1, source_target_pairs={{0,32},{1,33},{2,34},{3,35},{4,36},{5,37},{6,38},{7,39},{8,40},{9,... | collective-permute-start | bytes 2359304 | tf_op jit(solution)/shard_map/ppermute | solution.py:28
  48.7 21.1 %collective-permute-start.11 = (bf16[8,96,512]{2,1,0:T(8,128)(2,1)S(1)}, bf16[8,96,512]{2,1,0:T(8,128)(2,1)S(1)}, u32[]{:S(2)}, u32[]{:S(2)}) collective-permute-start(bf16[8,96,512]{2,1,0:T(8,128)(2,1)S(1)} %collective-permute-done.7.rest_1_), channel_id=1, source_target_pairs={{0,32},{1,33},{2,34},{3,35},{4,36},{5,37},{6,38},{7,39},{8,40},{9,... | collective-permute-start | bytes 2359304 | tf_op jit(solution)/shard_map/ppermute | solution.py:28
  50.3 19.5 %collective-permute-start.12 = (bf16[8,96,512]{2,1,0:T(8,128)(2,1)S(1)}, bf16[8,96,512]{2,1,0:T(8,128)(2,1)}, u32[]{:S(2)}, u32[]{:S(2)}) collective-permute-start(bf16[8,96,512]{2,1,0:T(8,128)(2,1)S(1)} %collective-permute-done.7.rest_1_), channel_id=1, source_target_pairs={{0,96},{1,97},{2,98},{3,99},{4,100},{5,101},{6,102},{7,103},{8,104... | collective-permute-start | bytes 2359304 | tf_op jit(solution)/shard_map/ppermute | solution.py:28
  89.4 34.8 %collective-permute-start.13 = (bf16[8,320,512]{2,1,0:T(8,128)(2,1)}, bf16[8,320,512]{2,1,0:T(8,128)(2,1)}, u32[]{:S(2)}, u32[]{:S(2)}) collective-permute-start(bf16[8,320,512]{2,1,0:T(8,128)(2,1)} %all-to-all-done.w_ref), channel_id=1, source_target_pairs={{0,16},{1,17},{2,18},{3,19},{4,20},{5,21},{6,22},{7,23},{8,24},{9,... | collective-permute-start | bytes 7864328 | tf_op jit(solution)/shard_map/ppermute | solution.py:28
  89.4 43.1 %collective-permute-start.8 = (bf16[1792,512]{1,0:T(8,128)(2,1)}, bf16[1792,512]{1,0:T(8,128)(2,1)}, u32[]{:S(2)}, u32[]{:S(2)}) collective-permute-start(bf16[1792,512]{1,0:T(8,128)(2,1)} %param.7), channel_id=1, source_target_pairs={{1,16},{3,18},{5,20},{7,22},{9,24},{11,26},{13,28},{15,30},{16,1},... | collective-permute-start | bytes 5505032 | tf_op jit(solution)/shard_map/ppermute | solution.py:28
  91.3 41.2 %all-to-all-start.1 = ((bf16[8,128,512]{2,1,0:T(8,128)(2,1)}), bf16[8,128,512]{2,1,0:T(8,128)(2,1)}, u32[]{:S(2)}, u32[]{:S(2)}) async-start(bf16[8,128,512]{2,1,0:T(8,128)(2,1)} %get-tuple-element.42), calls=%async_computation.1 | async-start | bytes 2097152 | tf_op jit(solution)/shard_map/all_to_all | solution.py:236
  95.5 20.3 %collective-permute-start.14 = (bf16[8,96,512]{2,1,0:T(8,128)(2,1)S(1)}, bf16[8,96,512]{2,1,0:T(8,128)(2,1)S(1)}, u32[]{:S(2)}, u32[]{:S(2)}) collective-permute-start(bf16[8,96,512]{2,1,0:T(8,128)(2,1)S(1)} %collective-permute-done.9.rest_6_), channel_id=1, source_target_pairs={{0,32},{1,33},{2,34},{3,35},{4,36},{5,37},{6,38},{7,39},{8,40},{9,... | collective-permute-start | bytes 2359304 | tf_op jit(solution)/shard_map/ppermute | solution.py:28
  97.2 19.7 %collective-permute-start.15 = (bf16[8,96,512]{2,1,0:T(8,128)(2,1)}, bf16[8,96,512]{2,1,0:T(8,128)(2,1)}, u32[]{:S(2)}, u32[]{:S(2)}) collective-permute-start(bf16[8,96,512]{2,1,0:T(8,128)(2,1)} %collective-permute-done.12.rest_3_), channel_id=1, source_target_pairs={{0,96},{1,97},{2,98},{3,99},{4,100},{5,101},{6,102},{7,103},{8,104... | collective-permute-start | bytes 2359304 | tf_op jit(solution)/shard_map/ppermute | solution.py:28
  132.5 11.8 %collective-permute-start.16 = (bf16[8,128,512]{2,1,0:T(8,128)(2,1)}, bf16[8,128,512]{2,1,0:T(8,128)(2,1)S(1)}, u32[]{:S(2)}, u32[]{:S(2)}) collective-permute-start(bf16[8,128,512]{2,1,0:T(8,128)(2,1)} %all-to-all-done.1.w_ref), channel_id=1, source_target_pairs={{0,16},{1,17},{2,18},{3,19},{4,20},{5,21},{6,22},{7,23},{8,24},{9,... | collective-permute-start | bytes 3145736 | tf_op jit(solution)/shard_map/ppermute | solution.py:28
  133.6 25.6 %collective-permute-start.18 = (f32[320,768]{1,0:T(8,128)}, f32[320,768]{1,0:T(8,128)}, u32[]{:S(2)}, u32[]{:S(2)}) collective-permute-start(f32[320,768]{1,0:T(8,128)} %get-tuple-element.48), channel_id=1, source_target_pairs={{0,1},{1,0},{2,3},{3,2},{4,5},{5,4},{6,7},{7,6},{8,9},{9,8},{10,11... | collective-permute-start | bytes 2949128 | tf_op jit(solution)/shard_map/ppermute | solution.py:28
  152.1 55.3 %collective-permute-start.17 = (bf16[1792,512]{1,0:T(8,128)(2,1)S(1)}, bf16[1792,512]{1,0:T(8,128)(2,1)}, u32[]{:S(2)}, u32[]{:S(2)}) collective-permute-start(bf16[1792,512]{1,0:T(8,128)(2,1)S(1)} %broadcast_select_fusion.mine_ref), channel_id=1, source_target_pairs={{0,16},{1,17},{2,18},{3,19},{4,20},{5,21},{6,22},{7,23},{8,24},{9,... | collective-permute-start | bytes 5505032 | tf_op jit(solution)/shard_map/ppermute | solution.py:28
  161.5 9.1 %collective-permute-start.19 = (bf16[160,768]{1,0:T(8,128)(2,1)}, bf16[160,768]{1,0:T(8,128)(2,1)S(1)}, u32[]{:S(2)}, u32[]{:S(2)}) collective-permute-start(bf16[160,768]{1,0:T(8,128)(2,1)} %activate.2.rest_0_), channel_id=1, source_target_pairs={{0,2},{1,3},{2,4},{3,5},{4,6},{5,7},{6,8},{7,9},{8,10},{9,11},{10,... | collective-permute-start | bytes 737288 | tf_op jit(solution)/shard_map/ppermute | solution.py:28
  163.7 7.3 %collective-permute-start.23 = (bf16[160,768]{1,0:T(8,128)(2,1)}, bf16[160,768]{1,0:T(8,128)(2,1)S(1)}, u32[]{:S(2)}, u32[]{:S(2)}) collective-permute-start(bf16[160,768]{1,0:T(8,128)(2,1)} %activate.2.rest_0_), channel_id=1, source_target_pairs={{0,14},{1,15},{2,0},{3,1},{4,2},{5,3},{6,4},{7,5},{8,6},{9,7},{10,... | collective-permute-start | bytes 737288 | tf_op jit(solution)/shard_map/ppermute | solution.py:28
  165.0 16.6 %collective-permute-start.27 = (f32[128,768]{1,0:T(8,128)}, f32[128,768]{1,0:T(8,128)}, u32[]{:S(2)}, u32[]{:S(2)}) collective-permute-start(f32[128,768]{1,0:T(8,128)} %get-tuple-element.51), channel_id=1, source_target_pairs={{0,1},{1,0},{2,3},{3,2},{4,5},{5,4},{6,7},{7,6},{8,9},{9,8},{10,11... | collective-permute-start | bytes 1179656 | tf_op jit(solution)/shard_map/ppermute | solution.py:28
  170.6 7.7 %collective-permute-start.20 = (bf16[160,768]{1,0:T(8,128)(2,1)S(1)}, bf16[160,768]{1,0:T(8,128)(2,1)S(1)}, u32[]{:S(2)}, u32[]{:S(2)}) collective-permute-start(bf16[160,768]{1,0:T(8,128)(2,1)S(1)} %collective-permute-done.19.rest_1_), channel_id=1, source_target_pairs={{0,2},{1,3},{2,4},{3,5},{4,6},{5,7},{6,8},{7,9},{8,10},{9,11},{10,... | collective-permute-start | bytes 737288 | tf_op jit(solution)/shard_map/ppermute | solution.py:28
  171.1 7.2 %collective-permute-start.24 = (bf16[160,768]{1,0:T(8,128)(2,1)S(1)}, bf16[160,768]{1,0:T(8,128)(2,1)S(1)}, u32[]{:S(2)}, u32[]{:S(2)}) collective-permute-start(bf16[160,768]{1,0:T(8,128)(2,1)S(1)} %collective-permute-done.23.rest_8_), channel_id=1, source_target_pairs={{0,14},{1,15},{2,0},{3,1},{4,2},{5,3},{6,4},{7,5},{8,6},{9,7},{10,... | collective-permute-start | bytes 737288 | tf_op jit(solution)/shard_map/ppermute | solution.py:28
  178.3 20.3 %collective-permute-start.21 = (bf16[160,768]{1,0:T(8,128)(2,1)S(1)}, bf16[160,768]{1,0:T(8,128)(2,1)S(1)}, u32[]{:S(2)}, u32[]{:S(2)}) collective-permute-start(bf16[160,768]{1,0:T(8,128)(2,1)S(1)} %collective-permute-done.20.rest_2_), channel_id=1, source_target_pairs={{0,2},{1,3},{2,4},{3,5},{4,6},{5,7},{6,8},{7,9},{8,10},{9,11},{10,... | collective-permute-start | bytes 737288 | tf_op jit(solution)/shard_map/ppermute | solution.py:28
  178.3 20.4 %collective-permute-start.25 = (bf16[160,768]{1,0:T(8,128)(2,1)S(1)}, bf16[160,768]{1,0:T(8,128)(2,1)S(1)}, u32[]{:S(2)}, u32[]{:S(2)}) collective-permute-start(bf16[160,768]{1,0:T(8,128)(2,1)S(1)} %collective-permute-done.24.rest_7_), channel_id=1, source_target_pairs={{0,14},{1,15},{2,0},{3,1},{4,2},{5,3},{6,4},{7,5},{8,6},{9,7},{10,... | collective-permute-start | bytes 737288 | tf_op jit(solution)/shard_map/ppermute | solution.py:28
  198.6 8.8 %collective-permute-start.22 = (bf16[80,768]{1,0:T(8,128)(2,1)S(1)}, bf16[80,768]{1,0:T(8,128)(2,1)}, u32[]{:S(2)}, u32[]{:S(2)}) collective-permute-start(bf16[80,768]{1,0:T(8,128)(2,1)S(1)} %slice.16), channel_id=1, source_target_pairs={{0,2},{1,3},{2,4},{3,5},{4,6},{5,7},{6,8},{7,9},{8,10},{9,11},{10,... | collective-permute-start | bytes 368648 | tf_op jit(solution)/shard_map/ppermute | solution.py:28
  198.8 8.7 %collective-permute-start.26 = (bf16[80,768]{1,0:T(8,128)(2,1)S(1)}, bf16[80,768]{1,0:T(8,128)(2,1)}, u32[]{:S(2)}, u32[]{:S(2)}) collective-permute-start(bf16[80,768]{1,0:T(8,128)(2,1)S(1)} %slice.17), channel_id=1, source_target_pairs={{0,14},{1,15},{2,0},{3,1},{4,2},{5,3},{6,4},{7,5},{8,6},{9,7},{10,... | collective-permute-start | bytes 368648 | tf_op jit(solution)/shard_map/ppermute | solution.py:28
  213.1 17.4 %all-to-all-start.2 = ((bf16[16,48,512]{2,1,0:T(8,128)(2,1)}), bf16[16,48,512]{2,1,0:T(8,128)(2,1)S(1)}, u32[]{:S(2)}, u32[]{:S(2)}) async-start(bf16[16,48,512]{2,1,0:T(8,128)(2,1)} %bitcast.8), calls=%async_computation.2 | async-start | bytes 1572864 | tf_op jit(solution)/shard_map/all_to_all | solution.py:275
  230.4 15.2 %all-to-all-start.3 = ((bf16[16,48,512]{2,1,0:T(8,128)(2,1)}), bf16[16,48,512]{2,1,0:T(8,128)(2,1)S(1)}, u32[]{:S(2)}, u32[]{:S(2)}) async-start(bf16[16,48,512]{2,1,0:T(8,128)(2,1)} %bitcast.7), calls=%async_computation.3 | async-start | bytes 1572864 | tf_op jit(solution)/shard_map/all_to_all | solution.py:275
  (35 other events, 514.3 us)

commit v3 on v2

--- a/solution.py
+++ b/solution.py
@@ -52,6 +52,10 @@
     return lax.optimization_barrier(values)
 
 
+def room(mib):
+    return pltpu.CompilerParams(vmem_limit_bytes=mib << 20)
+
+
 def cost(flops, *arrays):
     size = sum(a.size * a.dtype.itemsize for a in arrays)
     return pl.CostEstimate(flops=flops // 64, bytes_accessed=size // 64, transcendentals=0)
@@ -72,6 +76,7 @@
         out_shape=jax.ShapeDtypeStruct((nz, *parts[0].shape), BF16),
         cost_estimate=cost(0, *parts, *parts),
         name="regroup",
+        compiler_params=room(4),
     )(place, *parts)
 
 
@@ -96,64 +101,71 @@
         out_shape=outs,
         cost_estimate=cost(0, gate, up, *outs),
         name="slice_units",
+        compiler_params=room(12),
     )(gate, up)
 
 
-def project(place, weight, pieces, here=None):
-    nz, units, depth = weight.shape
+def project(place, own, other, pieces):
+    nz, units, depth = own.shape
     rows = pieces[0].shape[1] // CHUNKS
     width = 8 * rows * CHUNKS
-    last = here is not None
-
-    def body(place_ref, w_ref, *rest):
-        piece_refs, rest = rest[:8], rest[8:]
-        here_ref = rest[0] if last else None
-        outs, (t_ref, acc_ref) = rest[last:-2], rest[-2:]
+    groups = nz // TOGETHER
+
+    def body(place_ref, own_ref, other_ref, *rest):
+        piece_refs, (keep_ref, give_ref, t_ref, w_ref, acc_ref, sems) = rest[:8], rest[8:]
         xl, y = place_ref[0], place_ref[1]
-        k = pl.program_id(0)
-        term = None
-        for j in range(TOGETHER):
+
+        def copies(g):
+            zs = pl.ds(g * TOGETHER, TOGETHER)
+            pairs = [(own_ref.at[zs], w_ref.at[0, zs]), (other_ref.at[zs], w_ref.at[1, zs])]
             for n, piece_ref in enumerate(piece_refs):
                 at = ((y + n // 2) % 4) * 2 + (xl + n % 2) % 2
                 for i in range(CHUNKS):
                     to = pl.multiple_of((8 * i + at) * rows, rows)
-                    t_ref[j, pl.ds(to, rows)] = piece_ref[j, i * rows : (i + 1) * rows]
-            product = lax.dot_general(
-                w_ref[j], t_ref[j], (((1,), (1,)), ((), ())), preferred_element_type=F32
-            )
-            term = product if term is None else term + product
-
-        @pl.when(k == 0)
-        def _():
-            acc_ref[...] = term
-
-        @pl.when(k > 0)
-        def _():
-            acc_ref[...] += term
-
-        @pl.when(k == nz // TOGETHER - 1)
-        def _():
-            if last:
-                same = place_ref[2] == place_ref[4]
-                outs[0][...] = jnp.where(same, here_ref[...], acc_ref[...])
-                outs[1][...] = jnp.where(same, acc_ref[...], here_ref[...])
-            else:
-                outs[0][...] = acc_ref[...]
-
-    full = pl.BlockSpec((units, width), lambda k: (0, 0))
+                    pairs.append((piece_ref.at[zs, i * rows : (i + 1) * rows], t_ref.at[zs, pl.ds(to, rows)]))
+            return [pltpu.make_async_copy(*pair, sems.at[g, n]) for n, pair in enumerate(pairs)]
+
+        @pl.loop(0, groups)
+        def _(g):
+            for copy in copies(g):
+                copy.start()
+
+        acc_ref[...] = jnp.zeros_like(acc_ref)
+
+        @pl.loop(0, groups)
+        def _(g):
+            for copy in copies(g):
+                copy.wait()
+            for side in range(2):
+                term = None
+                for j in range(TOGETHER):
+                    product = lax.dot_general(
+                        w_ref[side, g * TOGETHER + j], t_ref[g * TOGETHER + j],
+                        (((1,), (1,)), ((), ())), preferred_element_type=F32,
+                    )
+                    term = product if term is None else term + product
+                acc_ref[side] += term
+
+        kept = jnp.where(place_ref[2] == place_ref[4], 0, 1)
+        keep_ref[...] = acc_ref[kept]
+        give_ref[...] = acc_ref[1 - kept]
+
     out = jax.ShapeDtypeStruct((units, width), F32)
-    args = (weight, *pieces) + ((here,) if last else ())
-    return pl.pallas_call(
-        body,
-        grid=(nz // TOGETHER,),
-        in_specs=[SCALARS, pl.BlockSpec((TOGETHER, units, depth), lambda k: (k, 0, 0))]
-        + [pl.BlockSpec((TOGETHER, CHUNKS * rows, depth), lambda k: (k, 0, 0))] * 8
-        + [full] * last,
-        out_specs=[full] * (1 + last),
-        out_shape=[out] * (1 + last),
-        scratch_shapes=[pltpu.VMEM((TOGETHER, width, depth), BF16), pltpu.VMEM((units, width), F32)],
-        cost_estimate=cost(2 * nz * units * depth * width, *args),
-        name="project_last" if last else "project",
+    args = (own, other, *pieces)
+    return pl.pallas_call(
+        body,
+        in_specs=[SCALARS] + [pl.BlockSpec(memory_space=pl.ANY)] * 10,
+        out_specs=[WHOLE] * 2,
+        out_shape=[out] * 2,
+        scratch_shapes=[
+            pltpu.VMEM((nz, width, depth), BF16),
+            pltpu.VMEM((2, nz, units, depth), BF16),
+            pltpu.VMEM((2, units, width), F32),
+            pltpu.SemaphoreType.DMA((groups, 18)),
+        ],
+        cost_estimate=cost(4 * nz * units * depth * width, *args),
+        name="project",
+        compiler_params=room(22),
     )(place, *args)
 
 
@@ -172,6 +184,7 @@
         out_shape=jax.ShapeDtypeStruct((units, rows), BF16),
         cost_estimate=cost(0, keep, got),
         name="activate",
+        compiler_params=room(6),
     )(keep, got)
 
 
@@ -209,6 +222,7 @@
         scratch_shapes=[pltpu.VMEM((nz * units, rows), BF16)],
         cost_estimate=cost(4 * nz * units * rows * width, mine, theirs, *parts),
         name="mix",
+        compiler_params=room(16),
     )(place, mine, theirs, *parts)
 
 
@@ -230,17 +244,13 @@
     far = swap_xl(near)
     near_before, near_after = along_y(near, 1), along_y(near, -1)
     far_before, far_after = along_y(far, 1), along_y(far, -1)
-    ready, weights[0], near_before, near_after, far_before, far_after = together(
-        sliced[1], weights[0], near_before, near_after, far_before, far_after
-    )
+    near_across, far_across = along_y(near_before, 1), along_y(far_after, -1)
+    ready, weights[0], near_across, far_across = together(sliced[1], weights[0], near_across, far_across)
     weights.append(lax.all_to_all(ready, "z", 0, 0, tiled=True))
-    near_across, far_across = along_y(near_before, 1), along_y(far_after, -1)
     pieces = (near, far, near_after, far_after, near_across, far_across, near_before, far_before)
 
     def sums(weight):
-        other = swap_core(weight)
-        here = project(place, weight, pieces)[0]
-        return project(place, other, pieces, here)
+        return project(place, weight, swap_core(weight), pieces)
 
     keep, give = sums(weights[0])
     got = swap_xh(give)
@@ -251,7 +261,7 @@
         down_weight,
         lambda xl, y, c, z, xh: (xl, y, 1 - c, z, 1 - xh) if c != xh else None,
     )
-    moved, weights[1], _ = together(moved, weights[1], give)
+    moved, weights[1], _ = together(moved, weights[1], got)
     mine = jnp.where(c == xh, down_weight, moved)
     keep, give = sums(weights[1])
     hiddens.append(activate(keep, swap_xh(give)))

time: 249 us -> 275 us (1.10)
  local copies, waits for them, and re-layouts: 3.79 us -> 38.4 us
  Pallas kernels: 49.6 us -> 31.8 us
  waiting for transfers between devices: 107 us -> 114 us
    unnamed x54 -> x138, local copies, waits for them, and re-layouts: 3.09 us -> 38.3 us
    ppermute x36, waiting for transfers between devices: 72.4 us -> 103 us  [send(): return lax.ppermute(value, AXES, pairs)]
    all_to_all x1, waiting for transfers between devices: 19.6 us -> 2.43 us  [shards(): weights = [lax.all_to_all(ready, 'z', 0, 0, tiled=True)]]
    all_to_all x2, waiting for transfers between devices: 15.4 us -> 8.97 us  [shards(): got = lax.all_to_all(out, ('xh', 'y', 'xl'), 0, 0, tiled=True)]
    pallas_call x4 -> x2, Pallas kernels: 29.4 us -> 23.2 us  [project(): pl.pallas_call(body, in_specs=[SCALARS] + [pl.BlockSpec(memory_space=pl.A...]
    pallas_call x2, Pallas kernels: 4.21 us -> 0.25 us  [activate(): pl.pallas_call(body, in_specs=[WHOLE] * 2, out_specs=WHOLE, out_shape=jax...]
    pallas_call x2, Pallas kernels: 10 us -> 6.37 us  [mix(): pl.pallas_call(body, grid=(1,), in_specs=[SCALARS] + [pl.BlockSpec(mine.s...]
  transfers between devices with their start and end apart: 40 -> 40, of which waited for: 14 -> 14; matrix products, arithmetic and copies ran while one was open for 1% -> 1% of each run, Pallas kernels for 18% -> 7%
where the time goes in v3:
time: 275 us; the launch traced here: 271 us
  waiting for transfers between devices  114 us (41%)
  starting transfers between devices  82.1 us (30%)
  local copies, waits for them, and re-layouts  38.4 us (14%)
  Pallas kernels  31.8 us (12%)
  other arithmetic  3.91 us (1%)
    ppermute x36, waiting for transfers between devices, send(): return lax.ppermute(value, AXES, pairs)  103 us
    ppermute x36, starting transfers between devices, send(): return lax.ppermute(value, AXES, pairs)  61.1 us
    unnamed x138, local copies, waits for them, and re-layouts  38.3 us
    pallas_call x2, Pallas kernels, project(): pl.pallas_call(body, in_specs=[SCALARS] + [pl.BlockSpec(memory_space=pl.A...  23.2 us
    all_to_all x2, starting transfers between devices, shards(): got = lax.all_to_all(out, ('xh', 'y', 'xl'), 0, 0, tiled=True)  12 us
    all_to_all x2, waiting for transfers between devices, shards(): got = lax.all_to_all(out, ('xh', 'y', 'xl'), 0, 0, tiled=True)  8.97 us
    pallas_call x2, Pallas kernels, mix(): pl.pallas_call(body, grid=(1,), in_specs=[SCALARS] + [pl.BlockSpec(mine.s...  6.37 us
  transfers between devices with their start and end apart: 40, of which 14 were waited for; matrix products, arithmetic and copies ran while one was open for 1% of the time, Pallas kernels for 7%

profile of v3, /device:TPU:2, one launch (start us, length us, event | category | flops | bytes accessed | tf_op | source)
XLA Modules:
  0.0 271.2 jit_solution(14145873369513398813)
XLA Ops:
  0.0 3.3 %collective-permute-start.1 = (bf16[96,512]{1,0:T(8,128)(2,1)}, bf16[96,512]{1,0:T(8,128)(2,1)S(1)}, u32[]{:S(2)}, u32[]{:S(2)}) collective-permute-start(bf16[96,512]{1,0:T(8,128)(2,1)} %rest_0_), channel_id=1, source_target_pairs={{0,4},{1,5},{2,6},{3,7},{4,8},{5,9},{6,10},{7,11},{8,12},{9,13},{1... | collective-permute-start | bytes 294920 | tf_op jit(solution)/shard_map/ppermute | solution.py:28
  3.3 3.0 %collective-permute-start.4 = (bf16[96,512]{1,0:T(8,128)(2,1)}, bf16[96,512]{1,0:T(8,128)(2,1)S(1)}, u32[]{:S(2)}, u32[]{:S(2)}) collective-permute-start(bf16[96,512]{1,0:T(8,128)(2,1)} %rest_0_), channel_id=1, source_target_pairs={{0,12},{1,13},{2,14},{3,15},{4,0},{5,1},{6,2},{7,3},{8,4},{9,5},{1... | collective-permute-start | bytes 294920 | tf_op jit(solution)/shard_map/ppermute | solution.py:28
  7.3 5.0 %collective-permute-start.3 = (bf16[96,512]{1,0:T(8,128)(2,1)}, bf16[96,512]{1,0:T(8,128)(2,1)S(1)}, u32[]{:S(2)}, u32[]{:S(2)}) collective-permute-start(bf16[96,512]{1,0:T(8,128)(2,1)} %rest_0_), channel_id=1, source_target_pairs={{0,8},{1,9},{2,10},{3,11},{4,12},{5,13},{6,14},{7,15},{8,0},{9,1},... | collective-permute-start | bytes 294920 | tf_op jit(solution)/shard_map/ppermute | solution.py:28
  14.6 3.2 %collective-permute-start.5 = (bf16[96,512]{1,0:T(8,128)(2,1)S(1)}, bf16[96,512]{1,0:T(8,128)(2,1)S(1)}, u32[]{:S(2)}, u32[]{:S(2)}) collective-permute-start(bf16[96,512]{1,0:T(8,128)(2,1)S(1)} %collective-permute-done.4.rest_6_), channel_id=1, source_target_pairs={{0,14},{1,15},{2,0},{3,1},{4,2},{5,3},{6,4},{7,5},{8,6},{9,7},{10,... | collective-permute-start | bytes 294920 | tf_op jit(solution)/shard_map/ppermute | solution.py:28
  27.9 4.8 %all-to-all-start = ((bf16[8,320,512]{2,1,0:T(8,128)(2,1)}), bf16[8,320,512]{2,1,0:T(8,128)(2,1)S(1)}, u32[]{:S(2)}, u32[]{:S(2)}) async-start(bf16[8,320,512]{2,1,0:T(8,128)(2,1)} %copy-done.21), calls=%async_computation | async-start | bytes 5242880 | tf_op jit(solution)/shard_map/all_to_all | solution.py:241
  41.9 14.5 %collective-permute-done.7.rest_1_ = bf16[8,96,512]{2,1,0:T(8,128)(2,1)S(1)} collective-permute-done((bf16[8,96,512]{2,1,0:T(8,128)(2,1)S(1)}, bf16[8,96,512]{2,1,0:T(8,128)(2,1)S(1)}, u32[]{:S(2)}, u32[]{:S(2)}) %collective-permute-start.7) | collective-permute-done | bytes 786464 | tf_op jit(solution)/shard_map/ppermute | solution.py:28
  56.4 3.0 %collective-permute-start.11 = (bf16[8,96,512]{2,1,0:T(8,128)(2,1)S(1)}, bf16[8,96,512]{2,1,0:T(8,128)(2,1)S(1)}, u32[]{:S(2)}, u32[]{:S(2)}) collective-permute-start(bf16[8,96,512]{2,1,0:T(8,128)(2,1)S(1)} %collective-permute-done.7.rest_1_), channel_id=1, source_target_pairs={{0,96},{1,97},{2,98},{3,99},{4,100},{5,101},{6,102},{7,103},{8,104... | collective-permute-start | bytes 2359304 | tf_op jit(solution)/shard_map/ppermute | solution.py:28
  60.3 13.2 %collective-permute-done.11.rest_3_ = bf16[8,96,512]{2,1,0:T(8,128)(2,1)S(1)} collective-permute-done((bf16[8,96,512]{2,1,0:T(8,128)(2,1)S(1)}, bf16[8,96,512]{2,1,0:T(8,128)(2,1)S(1)}, u32[]{:S(2)}, u32[]{:S(2)}) %collective-permute-start.11) | collective-permute-done | bytes 786464 | tf_op jit(solution)/shard_map/ppermute | solution.py:28
  73.5 3.5 %collective-permute-start.12 = (bf16[8,96,512]{2,1,0:T(8,128)(2,1)S(1)}, bf16[8,96,512]{2,1,0:T(8,128)(2,1)S(1)}, u32[]{:S(2)}, u32[]{:S(2)}) collective-permute-start(bf16[8,96,512]{2,1,0:T(8,128)(2,1)S(1)} %collective-permute-done.11.rest_3_), channel_id=1, source_target_pairs={{0,96},{1,97},{2,98},{3,99},{4,100},{5,101},{6,102},{7,103},{8,104... | collective-permute-start | bytes 2359304 | tf_op jit(solution)/shard_map/ppermute | solution.py:28
  78.9 10.5 %collective-permute-done.12.rest_5_ = bf16[8,96,512]{2,1,0:T(8,128)(2,1)S(1)} collective-permute-done((bf16[8,96,512]{2,1,0:T(8,128)(2,1)S(1)}, bf16[8,96,512]{2,1,0:T(8,128)(2,1)S(1)}, u32[]{:S(2)}, u32[]{:S(2)}) %collective-permute-start.12) | collective-permute-done | bytes 786464 | tf_op jit(solution)/shard_map/ppermute | solution.py:28
  94.6 4.2 %all-to-all-start.1 = ((bf16[8,128,512]{2,1,0:T(8,128)(2,1)}), bf16[8,128,512]{2,1,0:T(8,128)(2,1)}, u32[]{:S(2)}, u32[]{:S(2)}) async-start(bf16[8,128,512]{2,1,0:T(8,128)(2,1)} %copy-done.24), calls=%async_computation.1 | async-start | bytes 2097152 | tf_op jit(solution)/shard_map/all_to_all | solution.py:249
  98.9 3.7 %collective-permute-start.14 = (bf16[8,96,512]{2,1,0:T(8,128)(2,1)S(1)}, bf16[8,96,512]{2,1,0:T(8,128)(2,1)S(1)}, u32[]{:S(2)}, u32[]{:S(2)}) collective-permute-start(bf16[8,96,512]{2,1,0:T(8,128)(2,1)S(1)} %regroup.1.rest_0_), channel_id=1, source_target_pairs={{0,96},{1,97},{2,98},{3,99},{4,100},{5,101},{6,102},{7,103},{8,104... | collective-permute-start | bytes 2359304 | tf_op jit(solution)/shard_map/ppermute | solution.py:28
  102.6 16.9 %collective-permute-done.14.rest_2_ = bf16[8,96,512]{2,1,0:T(8,128)(2,1)S(1)} collective-permute-done((bf16[8,96,512]{2,1,0:T(8,128)(2,1)S(1)}, bf16[8,96,512]{2,1,0:T(8,128)(2,1)S(1)}, u32[]{:S(2)}, u32[]{:S(2)}) %collective-permute-start.14) | collective-permute-done | bytes 786464 | tf_op jit(solution)/shard_map/ppermute | solution.py:28
  119.5 4.2 %collective-permute-done.15.rest_7_ = bf16[8,96,512]{2,1,0:T(8,128)(2,1)S(1)} collective-permute-done((bf16[8,96,512]{2,1,0:T(8,128)(2,1)}, bf16[8,96,512]{2,1,0:T(8,128)(2,1)S(1)}, u32[]{:S(2)}, u32[]{:S(2)}) %collective-permute-start.15) | collective-permute-done | bytes 786464 | tf_op jit(solution)/shard_map/ppermute | solution.py:28
  129.7 12.7 %project.2 = (f32[320,768]{1,0:T(8,128)S(1)}, f32[320,768]{1,0:T(8,128)}) custom-call(s32[5]{0:T(128)S(1)} %stack.23.place_ref, bf16[8,320,512]{2,1,0:T(8,128)(2,1)S(1)} %all-to-all-done.own_ref, bf16[8,320,512]{2,1,0:T(8,128)(2,1)} %collective-permute-done.13.other_ref, bf16[8,96,512]{2,1,0:T(8,128)(2,1)S(1)} %regroup.1.rest_0_, ...), custom_call_target="tpu_custom_call" | custom-call | flops 62914560 | bytes 180224 | tf_op jit(solution)/shard_map/project/pallas_call | solution.py:155
  145.2 24.5 %collective-permute-done.16.got_ref = f32[320,768]{1,0:T(8,128)S(1)} collective-permute-done((f32[320,768]{1,0:T(8,128)}, f32[320,768]{1,0:T(8,128)S(1)}, u32[]{:S(2)}, u32[]{:S(2)}) %collective-permute-start.16) | collective-permute-done | bytes 983072 | tf_op jit(solution)/shard_map/ppermute | solution.py:28
  173.8 10.5 %project.3 = (f32[128,768]{1,0:T(8,128)S(1)}, f32[128,768]{1,0:T(8,128)S(1)}) custom-call(s32[5]{0:T(128)S(1)} %stack.23.place_ref, bf16[8,128,512]{2,1,0:T(8,128)(2,1)} %all-to-all-done.1.own_ref, bf16[8,128,512]{2,1,0:T(8,128)(2,1)} %collective-permute-done.17.other_ref, bf16[8,96,512]{2,1,0:T(8,128)(2,1)S(1)} %regroup.1.rest_0_, ...), custom_call_target="tpu_custom_call" | custom-call | flops 25165824 | bytes 131072 | tf_op jit(solution)/shard_map/project/pallas_call | solution.py:155
  188.6 5.6 %collective-permute-done.19.rest_1_ = bf16[160,768]{1,0:T(8,128)(2,1)S(1)} collective-permute-done((bf16[160,768]{1,0:T(8,128)(2,1)S(1)}, bf16[160,768]{1,0:T(8,128)(2,1)S(1)}, u32[]{:S(2)}, u32[]{:S(2)}) %collective-permute-start.19) | collective-permute-done | bytes 245792 | tf_op jit(solution)/shard_map/ppermute | solution.py:28
  197.5 5.1 %collective-permute-done.20.rest_2_ = bf16[160,768]{1,0:T(8,128)(2,1)S(1)} collective-permute-done((bf16[160,768]{1,0:T(8,128)(2,1)S(1)}, bf16[160,768]{1,0:T(8,128)(2,1)S(1)}, u32[]{:S(2)}, u32[]{:S(2)}) %collective-permute-start.20) | collective-permute-done | bytes 245792 | tf_op jit(solution)/shard_map/ppermute | solution.py:28
  202.5 3.2 %collective-permute-start.25 = (bf16[160,768]{1,0:T(8,128)(2,1)S(1)}, bf16[160,768]{1,0:T(8,128)(2,1)S(1)}, u32[]{:S(2)}, u32[]{:S(2)}) collective-permute-start(bf16[160,768]{1,0:T(8,128)(2,1)S(1)} %collective-permute-done.24.rest_7_), channel_id=1, source_target_pairs={{0,14},{1,15},{2,0},{3,1},{4,2},{5,3},{6,4},{7,5},{8,6},{9,7},{10,... | collective-permute-start | bytes 737288 | tf_op jit(solution)/shard_map/ppermute | solution.py:28
  206.0 3.2 %collective-permute-start.32 = (bf16[64,768]{1,0:T(8,128)(2,1)S(1)}, bf16[64,768]{1,0:T(8,128)(2,1)S(1)}, u32[]{:S(2)}, u32[]{:S(2)}) collective-permute-start(bf16[64,768]{1,0:T(8,128)(2,1)S(1)} %activate.3.rest_9_), channel_id=1, source_target_pairs={{0,14},{1,15},{2,0},{3,1},{4,2},{5,3},{6,4},{7,5},{8,6},{9,7},{10,... | collective-permute-start | bytes 294920 | tf_op jit(solution)/shard_map/ppermute | solution.py:28
  209.2 2.9 %collective-permute-done.28.rest_10_ = bf16[64,768]{1,0:T(8,128)(2,1)S(1)} collective-permute-done((bf16[64,768]{1,0:T(8,128)(2,1)S(1)}, bf16[64,768]{1,0:T(8,128)(2,1)S(1)}, u32[]{:S(2)}, u32[]{:S(2)}) %collective-permute-start.28) | collective-permute-done | bytes 98336 | tf_op jit(solution)/shard_map/ppermute | solution.py:28
  212.1 3.2 %collective-permute-start.33 = (bf16[64,768]{1,0:T(8,128)(2,1)S(1)}, bf16[64,768]{1,0:T(8,128)(2,1)S(1)}, u32[]{:S(2)}, u32[]{:S(2)}) collective-permute-start(bf16[64,768]{1,0:T(8,128)(2,1)S(1)} %collective-permute-done.32.rest_17_), channel_id=1, source_target_pairs={{0,14},{1,15},{2,0},{3,1},{4,2},{5,3},{6,4},{7,5},{8,6},{9,7},{10,... | collective-permute-start | bytes 294920 | tf_op jit(solution)/shard_map/ppermute | solution.py:28
  215.3 2.6 collective-permute-done.29.rest_11_
  217.9 3.2 %collective-permute-start.34 = (bf16[64,768]{1,0:T(8,128)(2,1)S(1)}, bf16[64,768]{1,0:T(8,128)(2,1)S(1)}, u32[]{:S(2)}, u32[]{:S(2)}) collective-permute-start(bf16[64,768]{1,0:T(8,128)(2,1)S(1)} %collective-permute-done.33.rest_16_), channel_id=1, source_target_pairs={{0,14},{1,15},{2,0},{3,1},{4,2},{5,3},{6,4},{7,5},{8,6},{9,7},{10,... | collective-permute-start | bytes 294920 | tf_op jit(solution)/shard_map/ppermute | solution.py:28
  221.3 3.3 %collective-permute-start.26 = (bf16[80,768]{1,0:T(8,128)(2,1)S(1)}, bf16[80,768]{1,0:T(8,128)(2,1)S(1)}, u32[]{:S(2)}, u32[]{:S(2)}) collective-permute-start(bf16[80,768]{1,0:T(8,128)(2,1)S(1)} %slice.17), channel_id=1, source_target_pairs={{0,14},{1,15},{2,0},{3,1},{4,2},{5,3},{6,4},{7,5},{8,6},{9,7},{10,... | collective-permute-start | bytes 368648 | tf_op jit(solution)/shard_map/ppermute | solution.py:28
  224.7 3.3 %collective-permute-start.35 = (bf16[32,768]{1,0:T(8,128)(2,1)S(1)}, bf16[32,768]{1,0:T(8,128)(2,1)S(1)}, u32[]{:S(2)}, u32[]{:S(2)}) collective-permute-start(bf16[32,768]{1,0:T(8,128)(2,1)S(1)} %slice.19), channel_id=1, source_target_pairs={{0,14},{1,15},{2,0},{3,1},{4,2},{5,3},{6,4},{7,5},{8,6},{9,7},{10,... | collective-permute-start | bytes 147464 | tf_op jit(solution)/shard_map/ppermute | solution.py:28
  230.0 3.2 %mix.2 = bf16[2,384,512]{2,1,0:T(8,128)(2,1)} custom-call(s32[5]{0:T(128)S(1)} %copy-done.67, bf16[1792,512]{1,0:T(8,128)(2,1)S(1)} %broadcast_select_fusion.mine_ref, bf16[1792,512]{1,0:T(8,128)(2,1)S(1)} %collective-permute-done.18.theirs_ref, bf16[160,768]{1,0:T(8,128)(2,1)S(1)} %activate.2.rest_0_, bf16[160,768]{1,0:T(8,128)(2,1)S(1)} %collective-permute-done.19.rest_1_, ...), custom_call_target="tpu_custom_call" | custom-call | flops 22020096 | bytes 100352 | tf_op jit(solution)/shard_map/mix/pallas_call | solution.py:214
  233.3 4.7 %all-to-all-start.2 = ((bf16[16,48,512]{2,1,0:T(8,128)(2,1)}), bf16[16,48,512]{2,1,0:T(8,128)(2,1)}, u32[]{:S(2)}, u32[]{:S(2)}) async-start(bf16[16,48,512]{2,1,0:T(8,128)(2,1)} %bitcast.5), calls=%async_computation.2 | async-start | bytes 1572864 | tf_op jit(solution)/shard_map/all_to_all | solution.py:285
  249.7 3.2 %mix.3 = bf16[2,384,512]{2,1,0:T(8,128)(2,1)} custom-call(s32[5]{0:T(128)S(1)} %copy-done.68, bf16[1792,512]{1,0:T(8,128)(2,1)S(1)} %broadcast_select_fusion.mine_ref, bf16[1792,512]{1,0:T(8,128)(2,1)S(1)} %copy-done.1, bf16[160,768]{1,0:T(8,128)(2,1)S(1)} %activate.2.rest_0_, bf16[160,768]{1,0:T(8,128)(2,1)S(1)} %collective-permute-done.19.rest_1_, ...), custom_call_target="tpu_custom_call" | custom-call | flops 22020096 | bytes 100352 | tf_op jit(solution)/shard_map/mix/pallas_call | solution.py:214
  252.9 7.3 %all-to-all-start.3 = ((bf16[16,48,512]{2,1,0:T(8,128)(2,1)}), bf16[16,48,512]{2,1,0:T(8,128)(2,1)S(1)}, u32[]{:S(2)}, u32[]{:S(2)}) async-start(bf16[16,48,512]{2,1,0:T(8,128)(2,1)} %bitcast.6), calls=%async_computation.3 | async-start | bytes 1572864 | tf_op jit(solution)/shard_map/all_to_all | solution.py:285
  261.4 9.0 %all-to-all-done.3 = bf16[16,48,512]{2,1,0:T(8,128)(2,1)S(1)} async-done(((bf16[16,48,512]{2,1,0:T(8,128)(2,1)}), bf16[16,48,512]{2,1,0:T(8,128)(2,1)S(1)}, u32[]{:S(2)}, u32[]{:S(2)}) %all-to-all-start.3) | async-done | bytes 786464 | tf_op jit(solution)/shard_map/all_to_all | solution.py:285
  (203 shorter events, 66.9 us)
Async XLA Ops:
  0.0 14.6 %collective-permute-start.1 = (bf16[96,512]{1,0:T(8,128)(2,1)}, bf16[96,512]{1,0:T(8,128)(2,1)S(1)}, u32[]{:S(2)}, u32[]{:S(2)}) collective-permute-start(bf16[96,512]{1,0:T(8,128)(2,1)} %rest_0_), channel_id=1, source_target_pairs={{0,4},{1,5},{2,6},{3,7},{4,8},{5,9},{6,10},{7,11},{8,12},{9,13},{1... | collective-permute-start | bytes 294920 | tf_op jit(solution)/shard_map/ppermute | solution.py:28
  3.3 11.3 %collective-permute-start.4 = (bf16[96,512]{1,0:T(8,128)(2,1)}, bf16[96,512]{1,0:T(8,128)(2,1)S(1)}, u32[]{:S(2)}, u32[]{:S(2)}) collective-permute-start(bf16[96,512]{1,0:T(8,128)(2,1)} %rest_0_), channel_id=1, source_target_pairs={{0,12},{1,13},{2,14},{3,15},{4,0},{5,1},{6,2},{7,3},{8,4},{9,5},{1... | collective-permute-start | bytes 294920 | tf_op jit(solution)/shard_map/ppermute | solution.py:28
  6.3 18.4 %collective-permute-start = (bf16[96,512]{1,0:T(8,128)(2,1)}, bf16[96,512]{1,0:T(8,128)(2,1)S(1)}, u32[]{:S(2)}, u32[]{:S(2)}) collective-permute-start(bf16[96,512]{1,0:T(8,128)(2,1)} %rest_0_), channel_id=1, source_target_pairs={{0,2},{1,3},{2,4},{3,5},{4,6},{5,7},{6,8},{7,9},{8,10},{9,11},{10,... | collective-permute-start | bytes 294920 | tf_op jit(solution)/shard_map/ppermute | solution.py:28
  7.3 18.0 %collective-permute-start.3 = (bf16[96,512]{1,0:T(8,128)(2,1)}, bf16[96,512]{1,0:T(8,128)(2,1)S(1)}, u32[]{:S(2)}, u32[]{:S(2)}) collective-permute-start(bf16[96,512]{1,0:T(8,128)(2,1)} %rest_0_), channel_id=1, source_target_pairs={{0,8},{1,9},{2,10},{3,11},{4,12},{5,13},{6,14},{7,15},{8,0},{9,1},... | collective-permute-start | bytes 294920 | tf_op jit(solution)/shard_map/ppermute | solution.py:28
  12.3 13.6 %collective-permute-start.6 = (bf16[96,512]{1,0:T(8,128)(2,1)}, bf16[96,512]{1,0:T(8,128)(2,1)S(1)}, u32[]{:S(2)}, u32[]{:S(2)}) collective-permute-start(bf16[96,512]{1,0:T(8,128)(2,1)} %rest_0_), channel_id=1, source_target_pairs={{0,14},{1,15},{2,0},{3,1},{4,2},{5,3},{6,4},{7,5},{8,6},{9,7},{10,... | collective-permute-start | bytes 294920 | tf_op jit(solution)/shard_map/ppermute | solution.py:28
  14.6 12.0 %collective-permute-start.2 = (bf16[96,512]{1,0:T(8,128)(2,1)S(1)}, bf16[96,512]{1,0:T(8,128)(2,1)S(1)}, u32[]{:S(2)}, u32[]{:S(2)}) collective-permute-start(bf16[96,512]{1,0:T(8,128)(2,1)S(1)} %collective-permute-done.1.rest_2_), channel_id=1, source_target_pairs={{0,2},{1,3},{2,4},{3,5},{4,6},{5,7},{6,8},{7,9},{8,10},{9,11},{10,... | collective-permute-start | bytes 294920 | tf_op jit(solution)/shard_map/ppermute | solution.py:28
  14.6 12.6 %collective-permute-start.5 = (bf16[96,512]{1,0:T(8,128)(2,1)S(1)}, bf16[96,512]{1,0:T(8,128)(2,1)S(1)}, u32[]{:S(2)}, u32[]{:S(2)}) collective-permute-start(bf16[96,512]{1,0:T(8,128)(2,1)S(1)} %collective-permute-done.4.rest_6_), channel_id=1, source_target_pairs={{0,14},{1,15},{2,0},{3,1},{4,2},{5,3},{6,4},{7,5},{8,6},{9,7},{10,... | collective-permute-start | bytes 294920 | tf_op jit(solution)/shard_map/ppermute | solution.py:28
  27.9 64.9 %all-to-all-start = ((bf16[8,320,512]{2,1,0:T(8,128)(2,1)}), bf16[8,320,512]{2,1,0:T(8,128)(2,1)S(1)}, u32[]{:S(2)}, u32[]{:S(2)}) async-start(bf16[8,320,512]{2,1,0:T(8,128)(2,1)} %copy-done.21), calls=%async_computation | async-start | bytes 5242880 | tf_op jit(solution)/shard_map/all_to_all | solution.py:241
  39.7 16.7 %collective-permute-start.7 = (bf16[8,96,512]{2,1,0:T(8,128)(2,1)S(1)}, bf16[8,96,512]{2,1,0:T(8,128)(2,1)S(1)}, u32[]{:S(2)}, u32[]{:S(2)}) collective-permute-start(bf16[8,96,512]{2,1,0:T(8,128)(2,1)S(1)} %regroup.1.rest_0_), channel_id=1, source_target_pairs={{0,128},{1,129},{2,130},{3,131},{4,132},{5,133},{6,134},{7,135},{8... | collective-permute-start | bytes 2359304 | tf_op jit(solution)/shard_map/ppermute | solution.py:28
  40.3 19.1 %collective-permute-start.9 = (bf16[8,96,512]{2,1,0:T(8,128)(2,1)S(1)}, bf16[8,96,512]{2,1,0:T(8,128)(2,1)S(1)}, u32[]{:S(2)}, u32[]{:S(2)}) collective-permute-start(bf16[8,96,512]{2,1,0:T(8,128)(2,1)S(1)} %regroup.1.rest_0_), channel_id=1, source_target_pairs={{0,32},{1,33},{2,34},{3,35},{4,36},{5,37},{6,38},{7,39},{8,40},{9,... | collective-permute-start | bytes 2359304 | tf_op jit(solution)/shard_map/ppermute | solution.py:28
  56.4 17.2 %collective-permute-start.11 = (bf16[8,96,512]{2,1,0:T(8,128)(2,1)S(1)}, bf16[8,96,512]{2,1,0:T(8,128)(2,1)S(1)}, u32[]{:S(2)}, u32[]{:S(2)}) collective-permute-start(bf16[8,96,512]{2,1,0:T(8,128)(2,1)S(1)} %collective-permute-done.7.rest_1_), channel_id=1, source_target_pairs={{0,96},{1,97},{2,98},{3,99},{4,100},{5,101},{6,102},{7,103},{8,104... | collective-permute-start | bytes 2359304 | tf_op jit(solution)/shard_map/ppermute | solution.py:28
  59.4 18.6 %collective-permute-start.10 = (bf16[8,96,512]{2,1,0:T(8,128)(2,1)S(1)}, bf16[8,96,512]{2,1,0:T(8,128)(2,1)S(1)}, u32[]{:S(2)}, u32[]{:S(2)}) collective-permute-start(bf16[8,96,512]{2,1,0:T(8,128)(2,1)S(1)} %collective-permute-done.9.rest_6_), channel_id=1, source_target_pairs={{0,32},{1,33},{2,34},{3,35},{4,36},{5,37},{6,38},{7,39},{8,40},{9,... | collective-permute-start | bytes 2359304 | tf_op jit(solution)/shard_map/ppermute | solution.py:28
  73.5 15.9 %collective-permute-start.12 = (bf16[8,96,512]{2,1,0:T(8,128)(2,1)S(1)}, bf16[8,96,512]{2,1,0:T(8,128)(2,1)S(1)}, u32[]{:S(2)}, u32[]{:S(2)}) collective-permute-start(bf16[8,96,512]{2,1,0:T(8,128)(2,1)S(1)} %collective-permute-done.11.rest_3_), channel_id=1, source_target_pairs={{0,96},{1,97},{2,98},{3,99},{4,100},{5,101},{6,102},{7,103},{8,104... | collective-permute-start | bytes 2359304 | tf_op jit(solution)/shard_map/ppermute | solution.py:28
  92.7 31.0 %collective-permute-start.13 = (bf16[8,320,512]{2,1,0:T(8,128)(2,1)S(1)}, bf16[8,320,512]{2,1,0:T(8,128)(2,1)}, u32[]{:S(2)}, u32[]{:S(2)}) collective-permute-start(bf16[8,320,512]{2,1,0:T(8,128)(2,1)S(1)} %all-to-all-done.own_ref), channel_id=1, source_target_pairs={{0,16},{1,17},{2,18},{3,19},{4,20},{5,21},{6,22},{7,23},{8,24},{9,... | collective-permute-start | bytes 7864328 | tf_op jit(solution)/shard_map/ppermute | solution.py:28
  92.7 52.4 %collective-permute-start.8 = (bf16[1792,512]{1,0:T(8,128)(2,1)}, bf16[1792,512]{1,0:T(8,128)(2,1)}, u32[]{:S(2)}, u32[]{:S(2)}) collective-permute-start(bf16[1792,512]{1,0:T(8,128)(2,1)} %param.7), channel_id=1, source_target_pairs={{1,16},{3,18},{5,20},{7,22},{9,24},{11,26},{13,28},{15,30},{16,1},... | collective-permute-start | bytes 5505032 | tf_op jit(solution)/shard_map/ppermute | solution.py:28
  94.6 50.5 %all-to-all-start.1 = ((bf16[8,128,512]{2,1,0:T(8,128)(2,1)}), bf16[8,128,512]{2,1,0:T(8,128)(2,1)}, u32[]{:S(2)}, u32[]{:S(2)}) async-start(bf16[8,128,512]{2,1,0:T(8,128)(2,1)} %copy-done.24), calls=%async_computation.1 | async-start | bytes 2097152 | tf_op jit(solution)/shard_map/all_to_all | solution.py:249
  98.9 20.6 %collective-permute-start.14 = (bf16[8,96,512]{2,1,0:T(8,128)(2,1)S(1)}, bf16[8,96,512]{2,1,0:T(8,128)(2,1)S(1)}, u32[]{:S(2)}, u32[]{:S(2)}) collective-permute-start(bf16[8,96,512]{2,1,0:T(8,128)(2,1)S(1)} %regroup.1.rest_0_), channel_id=1, source_target_pairs={{0,96},{1,97},{2,98},{3,99},{4,100},{5,101},{6,102},{7,103},{8,104... | collective-permute-start | bytes 2359304 | tf_op jit(solution)/shard_map/ppermute | solution.py:28
  102.6 21.1 %collective-permute-start.15 = (bf16[8,96,512]{2,1,0:T(8,128)(2,1)}, bf16[8,96,512]{2,1,0:T(8,128)(2,1)S(1)}, u32[]{:S(2)}, u32[]{:S(2)}) collective-permute-start(bf16[8,96,512]{2,1,0:T(8,128)(2,1)} %copy-done.2), channel_id=1, source_target_pairs={{0,32},{1,33},{2,34},{3,35},{4,36},{5,37},{6,38},{7,39},{8,40},{9,... | collective-permute-start | bytes 2359304 | tf_op jit(solution)/shard_map/ppermute | solution.py:28
  143.4 26.3 %collective-permute-start.16 = (f32[320,768]{1,0:T(8,128)}, f32[320,768]{1,0:T(8,128)S(1)}, u32[]{:S(2)}, u32[]{:S(2)}) collective-permute-start(f32[320,768]{1,0:T(8,128)} %get-tuple-element.44), channel_id=1, source_target_pairs={{0,1},{1,0},{2,3},{3,2},{4,5},{5,4},{6,7},{7,6},{8,9},{9,8},{10,11... | collective-permute-start | bytes 2949128 | tf_op jit(solution)/shard_map/ppermute | solution.py:28
  184.3 45.6 %collective-permute-start.18 = (bf16[1792,512]{1,0:T(8,128)(2,1)S(1)}, bf16[1792,512]{1,0:T(8,128)(2,1)S(1)}, u32[]{:S(2)}, u32[]{:S(2)}) collective-permute-start(bf16[1792,512]{1,0:T(8,128)(2,1)S(1)} %broadcast_select_fusion.mine_ref), channel_id=1, source_target_pairs={{0,16},{1,17},{2,18},{3,19},{4,20},{5,21},{6,22},{7,23},{8,24},{9,... | collective-permute-start | bytes 5505032 | tf_op jit(solution)/shard_map/ppermute | solution.py:28
  185.0 9.2 %collective-permute-start.19 = (bf16[160,768]{1,0:T(8,128)(2,1)S(1)}, bf16[160,768]{1,0:T(8,128)(2,1)S(1)}, u32[]{:S(2)}, u32[]{:S(2)}) collective-permute-start(bf16[160,768]{1,0:T(8,128)(2,1)S(1)} %activate.2.rest_0_), channel_id=1, source_target_pairs={{0,2},{1,3},{2,4},{3,5},{4,6},{5,7},{6,8},{7,9},{8,10},{9,11},{10,... | collective-permute-start | bytes 737288 | tf_op jit(solution)/shard_map/ppermute | solution.py:28
  187.1 7.9 %collective-permute-start.23 = (bf16[160,768]{1,0:T(8,128)(2,1)S(1)}, bf16[160,768]{1,0:T(8,128)(2,1)S(1)}, u32[]{:S(2)}, u32[]{:S(2)}) collective-permute-start(bf16[160,768]{1,0:T(8,128)(2,1)S(1)} %activate.2.rest_0_), channel_id=1, source_target_pairs={{0,14},{1,15},{2,0},{3,1},{4,2},{5,3},{6,4},{7,5},{8,6},{9,7},{10,... | collective-permute-start | bytes 737288 | tf_op jit(solution)/shard_map/ppermute | solution.py:28
  188.3 17.5 %collective-permute-start.27 = (f32[128,768]{1,0:T(8,128)S(1)}, f32[128,768]{1,0:T(8,128)S(1)}, u32[]{:S(2)}, u32[]{:S(2)}) collective-permute-start(f32[128,768]{1,0:T(8,128)S(1)} %get-tuple-element.47), channel_id=1, source_target_pairs={{0,1},{1,0},{2,3},{3,2},{4,5},{5,4},{6,7},{7,6},{8,9},{9,8},{10,11... | collective-permute-start | bytes 1179656 | tf_op jit(solution)/shard_map/ppermute | solution.py:28
  194.2 8.3 %collective-permute-start.20 = (bf16[160,768]{1,0:T(8,128)(2,1)S(1)}, bf16[160,768]{1,0:T(8,128)(2,1)S(1)}, u32[]{:S(2)}, u32[]{:S(2)}) collective-permute-start(bf16[160,768]{1,0:T(8,128)(2,1)S(1)} %collective-permute-done.19.rest_1_), channel_id=1, source_target_pairs={{0,2},{1,3},{2,4},{3,5},{4,6},{5,7},{6,8},{7,9},{8,10},{9,11},{10,... | collective-permute-start | bytes 737288 | tf_op jit(solution)/shard_map/ppermute | solution.py:28
  195.0 7.5 %collective-permute-start.24 = (bf16[160,768]{1,0:T(8,128)(2,1)S(1)}, bf16[160,768]{1,0:T(8,128)(2,1)S(1)}, u32[]{:S(2)}, u32[]{:S(2)}) collective-permute-start(bf16[160,768]{1,0:T(8,128)(2,1)S(1)} %collective-permute-done.23.rest_8_), channel_id=1, source_target_pairs={{0,14},{1,15},{2,0},{3,1},{4,2},{5,3},{6,4},{7,5},{8,6},{9,7},{10,... | collective-permute-start | bytes 737288 | tf_op jit(solution)/shard_map/ppermute | solution.py:28
  202.5 18.6 %collective-permute-start.21 = (bf16[160,768]{1,0:T(8,128)(2,1)S(1)}, bf16[160,768]{1,0:T(8,128)(2,1)S(1)}, u32[]{:S(2)}, u32[]{:S(2)}) collective-permute-start(bf16[160,768]{1,0:T(8,128)(2,1)S(1)} %collective-permute-done.20.rest_2_), channel_id=1, source_target_pairs={{0,2},{1,3},{2,4},{3,5},{4,6},{5,7},{6,8},{7,9},{8,10},{9,11},{10,... | collective-permute-start | bytes 737288 | tf_op jit(solution)/shard_map/ppermute | solution.py:28
  202.5 18.7 %collective-permute-start.25 = (bf16[160,768]{1,0:T(8,128)(2,1)S(1)}, bf16[160,768]{1,0:T(8,128)(2,1)S(1)}, u32[]{:S(2)}, u32[]{:S(2)}) collective-permute-start(bf16[160,768]{1,0:T(8,128)(2,1)S(1)} %collective-permute-done.24.rest_7_), channel_id=1, source_target_pairs={{0,14},{1,15},{2,0},{3,1},{4,2},{5,3},{6,4},{7,5},{8,6},{9,7},{10,... | collective-permute-start | bytes 737288 | tf_op jit(solution)/shard_map/ppermute | solution.py:28
  217.9 6.8 %collective-permute-start.34 = (bf16[64,768]{1,0:T(8,128)(2,1)S(1)}, bf16[64,768]{1,0:T(8,128)(2,1)S(1)}, u32[]{:S(2)}, u32[]{:S(2)}) collective-permute-start(bf16[64,768]{1,0:T(8,128)(2,1)S(1)} %collective-permute-done.33.rest_16_), channel_id=1, source_target_pairs={{0,14},{1,15},{2,0},{3,1},{4,2},{5,3},{6,4},{7,5},{8,6},{9,7},{10,... | collective-permute-start | bytes 294920 | tf_op jit(solution)/shard_map/ppermute | solution.py:28
  221.1 6.8 %collective-permute-start.22 = (bf16[80,768]{1,0:T(8,128)(2,1)S(1)}, bf16[80,768]{1,0:T(8,128)(2,1)S(1)}, u32[]{:S(2)}, u32[]{:S(2)}) collective-permute-start(bf16[80,768]{1,0:T(8,128)(2,1)S(1)} %slice.16), channel_id=1, source_target_pairs={{0,2},{1,3},{2,4},{3,5},{4,6},{5,7},{6,8},{7,9},{8,10},{9,11},{10,... | collective-permute-start | bytes 368648 | tf_op jit(solution)/shard_map/ppermute | solution.py:28
  221.3 6.7 %collective-permute-start.26 = (bf16[80,768]{1,0:T(8,128)(2,1)S(1)}, bf16[80,768]{1,0:T(8,128)(2,1)S(1)}, u32[]{:S(2)}, u32[]{:S(2)}) collective-permute-start(bf16[80,768]{1,0:T(8,128)(2,1)S(1)} %slice.17), channel_id=1, source_target_pairs={{0,14},{1,15},{2,0},{3,1},{4,2},{5,3},{6,4},{7,5},{8,6},{9,7},{10,... | collective-permute-start | bytes 368648 | tf_op jit(solution)/shard_map/ppermute | solution.py:28
  233.3 19.6 %all-to-all-start.2 = ((bf16[16,48,512]{2,1,0:T(8,128)(2,1)}), bf16[16,48,512]{2,1,0:T(8,128)(2,1)}, u32[]{:S(2)}, u32[]{:S(2)}) async-start(bf16[16,48,512]{2,1,0:T(8,128)(2,1)} %bitcast.5), calls=%async_computation.2 | async-start | bytes 1572864 | tf_op jit(solution)/shard_map/all_to_all | solution.py:285
  252.9 17.5 %all-to-all-start.3 = ((bf16[16,48,512]{2,1,0:T(8,128)(2,1)}), bf16[16,48,512]{2,1,0:T(8,128)(2,1)S(1)}, u32[]{:S(2)}, u32[]{:S(2)}) async-start(bf16[16,48,512]{2,1,0:T(8,128)(2,1)} %bitcast.6), calls=%async_computation.3 | async-start | bytes 1572864 | tf_op jit(solution)/shard_map/all_to_all | solution.py:285
  (77 other events, 528.5 us)

commit v4 on v3

--- a/solution.py
+++ b/solution.py
@@ -10,7 +10,6 @@
 
 AXES = ("xl", "y", "c", "z", "xh")
 SIZES = (2, 4, 2, 8, 2)
-CHUNKS = 2
 FIRST = 160
 TOGETHER = 2
 F32, BF16 = jnp.float32, jnp.bfloat16
@@ -52,10 +51,6 @@
     return lax.optimization_barrier(values)
 
 
-def room(mib):
-    return pltpu.CompilerParams(vmem_limit_bytes=mib << 20)
-
-
 def cost(flops, *arrays):
     size = sum(a.size * a.dtype.itemsize for a in arrays)
     return pl.CostEstimate(flops=flops // 64, bytes_accessed=size // 64, transcendentals=0)
@@ -76,7 +71,6 @@
         out_shape=jax.ShapeDtypeStruct((nz, *parts[0].shape), BF16),
         cost_estimate=cost(0, *parts, *parts),
         name="regroup",
-        compiler_params=room(4),
     )(place, *parts)
 
 
@@ -101,28 +95,29 @@
         out_shape=outs,
         cost_estimate=cost(0, gate, up, *outs),
         name="slice_units",
-        compiler_params=room(12),
     )(gate, up)
 
 
-def project(place, own, other, pieces):
+def project(place, own, other, pieces, cuts):
     nz, units, depth = own.shape
-    rows = pieces[0].shape[1] // CHUNKS
-    width = 8 * rows * CHUNKS
+    rows = pieces[0].shape[1]
+    width = 8 * rows
     groups = nz // TOGETHER
 
     def body(place_ref, own_ref, other_ref, *rest):
-        piece_refs, (keep_ref, give_ref, t_ref, w_ref, acc_ref, sems) = rest[:8], rest[8:]
+        piece_refs, (keep_ref, *give_refs, t_ref, w_ref, acc_ref, sems) = rest[:8], rest[8:]
         xl, y = place_ref[0], place_ref[1]
 
         def copies(g):
             zs = pl.ds(g * TOGETHER, TOGETHER)
-            pairs = [(own_ref.at[zs], w_ref.at[0, zs]), (other_ref.at[zs], w_ref.at[1, zs])]
+            pairs = [
+                (own_ref.at[zs], w_ref.at[zs, pl.ds(0, units)]),
+                (other_ref.at[zs], w_ref.at[zs, pl.ds(units, units)]),
+            ]
             for n, piece_ref in enumerate(piece_refs):
                 at = ((y + n // 2) % 4) * 2 + (xl + n % 2) % 2
-                for i in range(CHUNKS):
-                    to = pl.multiple_of((8 * i + at) * rows, rows)
-                    pairs.append((piece_ref.at[zs, i * rows : (i + 1) * rows], t_ref.at[zs, pl.ds(to, rows)]))
+                to = pl.multiple_of(at * rows, rows)
+                pairs.append((piece_ref.at[zs], t_ref.at[zs, pl.ds(to, rows)]))
             return [pltpu.make_async_copy(*pair, sems.at[g, n]) for n, pair in enumerate(pairs)]
 
         @pl.loop(0, groups)
@@ -136,62 +131,66 @@
         def _(g):
             for copy in copies(g):
                 copy.wait()
-            for side in range(2):
-                term = None
-                for j in range(TOGETHER):
-                    product = lax.dot_general(
-                        w_ref[side, g * TOGETHER + j], t_ref[g * TOGETHER + j],
-                        (((1,), (1,)), ((), ())), preferred_element_type=F32,
-                    )
-                    term = product if term is None else term + product
-                acc_ref[side] += term
-
-        kept = jnp.where(place_ref[2] == place_ref[4], 0, 1)
-        keep_ref[...] = acc_ref[kept]
-        give_ref[...] = acc_ref[1 - kept]
-
-    out = jax.ShapeDtypeStruct((units, width), F32)
+            for j in range(TOGETHER):
+                acc_ref[...] += lax.dot_general(
+                    w_ref[g * TOGETHER + j], t_ref[g * TOGETHER + j],
+                    (((1,), (1,)), ((), ())), preferred_element_type=F32,
+                )
+
+        kept = pl.multiple_of(jnp.where(place_ref[2] == place_ref[4], 0, units), units)
+        keep_ref[...] = acc_ref[pl.ds(kept, units)]
+        for lo, hi, give_ref in zip((0, *cuts), (*cuts, units), give_refs):
+            give_ref[...] = acc_ref[pl.ds(pl.multiple_of(units - kept + lo, 8), hi - lo)]
+
+    outs = [
+        jax.ShapeDtypeStruct((hi - lo, width), F32)
+        for lo, hi in ((0, units), *zip((0, *cuts), (*cuts, units)))
+    ]
     args = (own, other, *pieces)
     return pl.pallas_call(
         body,
         in_specs=[SCALARS] + [pl.BlockSpec(memory_space=pl.ANY)] * 10,
-        out_specs=[WHOLE] * 2,
-        out_shape=[out] * 2,
+        out_specs=[WHOLE] * len(outs),
+        out_shape=outs,
         scratch_shapes=[
             pltpu.VMEM((nz, width, depth), BF16),
-            pltpu.VMEM((2, nz, units, depth), BF16),
-            pltpu.VMEM((2, units, width), F32),
-            pltpu.SemaphoreType.DMA((groups, 18)),
+            pltpu.VMEM((nz, 2 * units, depth), BF16),
+            pltpu.VMEM((2 * units, width), F32),
+            pltpu.SemaphoreType.DMA((groups, 10)),
         ],
         cost_estimate=cost(4 * nz * units * depth * width, *args),
         name="project",
-        compiler_params=room(22),
     )(place, *args)
 
 
-def activate(keep, got):
+def activate(keep, gots):
     units, rows = keep.shape[0] // 2, keep.shape[1]
 
-    def body(keep_ref, got_ref, o_ref):
-        gate = keep_ref[:units] + got_ref[:units]
-        up = keep_ref[units:] + got_ref[units:]
+    def body(keep_ref, *rest):
+        got_refs, (o_ref, sum_ref) = rest[:-2], rest[-2:]
+        at = 0
+        for got_ref in got_refs:
+            here = slice(at, at + got_ref.shape[0])
+            sum_ref[here] = keep_ref[here] + got_ref[...]
+            at += got_ref.shape[0]
+        gate, up = sum_ref[:units], sum_ref[units:]
         o_ref[...] = (gate / (1 + jnp.exp(-gate)) * up).astype(o_ref.dtype)
 
     return pl.pallas_call(
         body,
-        in_specs=[WHOLE] * 2,
+        in_specs=[WHOLE] * (1 + len(gots)),
         out_specs=WHOLE,
         out_shape=jax.ShapeDtypeStruct((units, rows), BF16),
-        cost_estimate=cost(0, keep, got),
+        scratch_shapes=[pltpu.VMEM(keep.shape, F32)],
+        cost_estimate=cost(0, keep, *gots),
         name="activate",
-        compiler_params=room(6),
-    )(keep, got)
-
-
-def mix(place, chunk, rings, mine, theirs):
+    )(keep, *gots)
+
+
+def mix(place, rings, mine, theirs):
     nz = SIZES[3]
     sizes = [ring[0].shape[0] for ring in rings]
-    units, rows = sum(sizes), rings[0][0].shape[1] // CHUNKS
+    units, rows = sum(sizes), rings[0][0].shape[1]
     width = mine.shape[1]
     order = (0, 1, 2, 3, 4, -4, -3, -2, -1)
     parts = [ring[s] for ring in rings for s in order]
@@ -213,16 +212,12 @@
 
     return pl.pallas_call(
         body,
-        grid=(1,),
-        in_specs=[SCALARS]
-        + [pl.BlockSpec(mine.shape, lambda k: (0, 0))] * 2
-        + [pl.BlockSpec((p.shape[0], rows), lambda k: (0, chunk)) for p in parts],
-        out_specs=pl.BlockSpec((2, rows, width), lambda k: (0, 0, 0)),
+        in_specs=[SCALARS] + [WHOLE] * (2 + len(parts)),
+        out_specs=WHOLE,
         out_shape=jax.ShapeDtypeStruct((2, rows, width), BF16),
         scratch_shapes=[pltpu.VMEM((nz * units, rows), BF16)],
         cost_estimate=cost(4 * nz * units * rows * width, mine, theirs, *parts),
         name="mix",
-        compiler_params=room(16),
     )(place, mine, theirs, *parts)
 
 
@@ -230,7 +225,6 @@
     xl, y, c, z, xh = (lax.axis_index(a) for a in AXES)
     place = jnp.stack([xl, y, c, z, xh]).astype(jnp.int32)
     nz = SIZES[3]
-    rows = tokens.shape[0] // CHUNKS
 
     around = {0: tokens}
     for s in (1, -1, 2, -2, 4):
@@ -245,26 +239,24 @@
     near_before, near_after = along_y(near, 1), along_y(near, -1)
     far_before, far_after = along_y(far, 1), along_y(far, -1)
     near_across, far_across = along_y(near_before, 1), along_y(far_after, -1)
-    ready, weights[0], near_across, far_across = together(sliced[1], weights[0], near_across, far_across)
+    pieces = (near, far, near_after, far_after, near_across, far_across, near_before, far_before)
+    ready, weights[0], pieces = together(sliced[1], weights[0], pieces)
     weights.append(lax.all_to_all(ready, "z", 0, 0, tiled=True))
-    pieces = (near, far, near_after, far_after, near_across, far_across, near_before, far_before)
-
-    def sums(weight):
-        return project(place, weight, swap_core(weight), pieces)
-
-    keep, give = sums(weights[0])
-    got = swap_xh(give)
-    hiddens = [activate(keep, got)]
+
+    keep, *gives = project(place, weights[0], swap_core(weights[0]), pieces, ())
+    gots = [swap_xh(give) for give in gives]
+    hiddens = [activate(keep, gots)]
 
     down_weight, _ = together(down_weight, far)
     moved = send(
         down_weight,
         lambda xl, y, c, z, xh: (xl, y, 1 - c, z, 1 - xh) if c != xh else None,
     )
-    moved, weights[1], _ = together(moved, weights[1], got)
+    moved, weights[1], _ = together(moved, weights[1], gives[0])
     mine = jnp.where(c == xh, down_weight, moved)
-    keep, give = sums(weights[1])
-    hiddens.append(activate(keep, swap_xh(give)))
+
+    keep, give = project(place, weights[1], swap_core(weights[1]), pieces, ())
+    hiddens.append(activate(keep, [swap_xh(give)]))
     mine, _ = together(mine, give)
     theirs = swap_core(mine)
 
@@ -279,12 +271,9 @@
             ring.update({at + 1: up, -at - 1: down})
         rings.append(ring)
 
-    outs = []
-    for i in range(CHUNKS):
-        out = mix(place, i, rings, mine, theirs).reshape(16, rows, -1)
-        got = lax.all_to_all(out, ("xh", "y", "xl"), 0, 0, tiled=True)
-        outs.append(jnp.sum(got.astype(F32), 0))
-    return jnp.concatenate(outs)
+    out = mix(place, rings, mine, theirs).reshape(16, tokens.shape[0], -1)
+    got = lax.all_to_all(out, ("xh", "y", "xl"), 0, 0, tiled=True)
+    return jnp.sum(got.astype(F32), 0)
 
 
 def solution(mesh):

time: 275 us -> 247 us (0.90); the launches traced: 271 us -> 247 us
  local copies, waits for them, and re-layouts: 38.4 us -> 5.68 us
  blocking collectives: 0 us -> 22.1 us
  starting transfers between devices: 82.1 us -> 71.2 us
    unnamed x138 -> x64, local copies, waits for them, and re-layouts: 38.3 us -> 5.04 us
    all_to_all x0 -> x1, blocking collectives: none -> 22.1 us  [shards(): got = lax.all_to_all(out, ('xh', 'y', 'xl'), 0, 0, tiled=True)]
    all_to_all x1, waiting for transfers between devices: 0.01 us -> 21 us  [shards(): weights.append(lax.all_to_all(ready, 'z', 0, 0, tiled=True))]
    ppermute x36, waiting for transfers between devices: 103 us -> 91 us  [send(): return lax.ppermute(value, AXES, pairs)]
    all_to_all x2 -> x0, starting transfers between devices: 12 us -> none  [shards(): got = lax.all_to_all(out, ('xh', 'y', 'xl'), 0, 0, tiled=True)]
    all_to_all x2 -> x0, waiting for transfers between devices: 8.97 us -> none  [shards(): got = lax.all_to_all(out, ('xh', 'y', 'xl'), 0, 0, tiled=True)]
    pallas_call x2, Pallas kernels: 23.2 us -> 15.1 us  [project(): pl.pallas_call(body, in_specs=[SCALARS] + [pl.BlockSpec(memory_space=pl.A...]
    pallas_call x4 -> x3, Pallas kernels: 6.62 us -> 11.5 us  [the longest x1 7.26 us: mix(): pl.pallas_call(body, in_specs=[SCALARS] + [WHOLE] * (2 + len(parts)), out...]
  transfers between devices with their start and end apart: 40 -> 38, of which waited for: 14 -> 12; matrix products, arithmetic and copies ran while one was open for 1% -> 1% of each run, Pallas kernels for 7% -> 10%
where the time goes in v4:
time: 247 us
  waiting for transfers between devices  112 us (45%)
  starting transfers between devices  71.2 us (29%)
  Pallas kernels  32.6 us (13%)
  blocking collectives  22.1 us (9%)
  local copies, waits for them, and re-layouts  5.68 us (2%)
  other arithmetic  2.59 us (1%)
    ppermute x36, waiting for transfers between devices, send(): return lax.ppermute(value, AXES, pairs)  91 us
    ppermute x36, starting transfers between devices, send(): return lax.ppermute(value, AXES, pairs)  59.9 us
    all_to_all x1, blocking collectives, shards(): got = lax.all_to_all(out, ('xh', 'y', 'xl'), 0, 0, tiled=True)  22.1 us
    all_to_all x1, waiting for transfers between devices, shards(): weights.append(lax.all_to_all(ready, 'z', 0, 0, tiled=True))  21 us
    pallas_call x2, Pallas kernels, project(): pl.pallas_call(body, in_specs=[SCALARS] + [pl.BlockSpec(memory_space=pl.A...  15.1 us
    pallas_call x1, Pallas kernels, mix(): pl.pallas_call(body, in_specs=[SCALARS] + [WHOLE] * (2 + len(parts)), out...  7.26 us
    all_to_all x1, starting transfers between devices, shards(): weights.append(lax.all_to_all(ready, 'z', 0, 0, tiled=True))  6.65 us
    unnamed x64, local copies, waits for them, and re-layouts  5.04 us
  transfers between devices with their start and end apart: 38, of which 12 were waited for; matrix products, arithmetic and copies ran while one was open for 1% of the time, Pallas kernels for 10%

profile of v4, /device:TPU:2, one launch (start us, length us, event | category | flops | bytes accessed | tf_op | source)
XLA Modules:
  0.0 246.7 jit_solution(11140341818017934621)
XLA Ops:
  0.0 3.3 %collective-permute-start.1 = (bf16[96,512]{1,0:T(8,128)(2,1)}, bf16[96,512]{1,0:T(8,128)(2,1)S(1)}, u32[]{:S(2)}, u32[]{:S(2)}) collective-permute-start(bf16[96,512]{1,0:T(8,128)(2,1)} %rest_0_), channel_id=1, source_target_pairs={{0,4},{1,5},{2,6},{3,7},{4,8},{5,9},{6,10},{7,11},{8,12},{9,13},{1... | collective-permute-start | bytes 294920 | tf_op jit(solution)/shard_map/ppermute | solution.py:27
  3.3 3.0 %collective-permute-start.4 = (bf16[96,512]{1,0:T(8,128)(2,1)}, bf16[96,512]{1,0:T(8,128)(2,1)S(1)}, u32[]{:S(2)}, u32[]{:S(2)}) collective-permute-start(bf16[96,512]{1,0:T(8,128)(2,1)} %rest_0_), channel_id=1, source_target_pairs={{0,12},{1,13},{2,14},{3,15},{4,0},{5,1},{6,2},{7,3},{8,4},{9,5},{1... | collective-permute-start | bytes 294920 | tf_op jit(solution)/shard_map/ppermute | solution.py:27
  7.3 5.0 %collective-permute-start.3 = (bf16[96,512]{1,0:T(8,128)(2,1)}, bf16[96,512]{1,0:T(8,128)(2,1)S(1)}, u32[]{:S(2)}, u32[]{:S(2)}) collective-permute-start(bf16[96,512]{1,0:T(8,128)(2,1)} %rest_0_), channel_id=1, source_target_pairs={{0,8},{1,9},{2,10},{3,11},{4,12},{5,13},{6,14},{7,15},{8,0},{9,1},... | collective-permute-start | bytes 294920 | tf_op jit(solution)/shard_map/ppermute | solution.py:27
  14.6 3.2 %collective-permute-start.5 = (bf16[96,512]{1,0:T(8,128)(2,1)S(1)}, bf16[96,512]{1,0:T(8,128)(2,1)S(1)}, u32[]{:S(2)}, u32[]{:S(2)}) collective-permute-start(bf16[96,512]{1,0:T(8,128)(2,1)S(1)} %collective-permute-done.4.rest_6_), channel_id=1, source_target_pairs={{0,14},{1,15},{2,0},{3,1},{4,2},{5,3},{6,4},{7,5},{8,6},{9,7},{10,... | collective-permute-start | bytes 294920 | tf_op jit(solution)/shard_map/ppermute | solution.py:27
  17.8 3.9 %slice_units.1 = (bf16[8,320,512]{2,1,0:T(8,128)(2,1)}, bf16[8,128,512]{2,1,0:T(8,128)(2,1)}) custom-call(bf16[512,1792]{1,0:T(8,128)(2,1)} %g_ref.1, bf16[512,1792]{1,0:T(8,128)(2,1)} %u_ref.1), custom_call_target="tpu_custom_call" | custom-call | bytes 114688 | tf_op jit(solution)/shard_map/slice_units/pallas_call | solution.py:90
  22.5 4.7 %all-to-all-start = ((bf16[8,320,512]{2,1,0:T(8,128)(2,1)}), bf16[8,320,512]{2,1,0:T(8,128)(2,1)S(1)}, u32[]{:S(2)}, u32[]{:S(2)}) async-start(bf16[8,320,512]{2,1,0:T(8,128)(2,1)} %get-tuple-element.45), calls=%async_computation | async-start | bytes 5242880 | tf_op jit(solution)/shard_map/all_to_all | solution.py:235
  32.1 16.6 %collective-permute-done.7.rest_1_ = bf16[8,96,512]{2,1,0:T(8,128)(2,1)S(1)} collective-permute-done((bf16[8,96,512]{2,1,0:T(8,128)(2,1)}, bf16[8,96,512]{2,1,0:T(8,128)(2,1)S(1)}, u32[]{:S(2)}, u32[]{:S(2)}) %collective-permute-start.7) | collective-permute-done | bytes 786464 | tf_op jit(solution)/shard_map/ppermute | solution.py:27
  48.7 3.0 %collective-permute-start.10 = (bf16[8,96,512]{2,1,0:T(8,128)(2,1)S(1)}, bf16[8,96,512]{2,1,0:T(8,128)(2,1)S(1)}, u32[]{:S(2)}, u32[]{:S(2)}) collective-permute-start(bf16[8,96,512]{2,1,0:T(8,128)(2,1)S(1)} %collective-permute-done.7.rest_1_), channel_id=1, source_target_pairs={{0,96},{1,97},{2,98},{3,99},{4,100},{5,101},{6,102},{7,103},{8,104... | collective-permute-start | bytes 2359304 | tf_op jit(solution)/shard_map/ppermute | solution.py:27
  53.8 15.9 %collective-permute-done.10.rest_3_ = bf16[8,96,512]{2,1,0:T(8,128)(2,1)S(1)} collective-permute-done((bf16[8,96,512]{2,1,0:T(8,128)(2,1)S(1)}, bf16[8,96,512]{2,1,0:T(8,128)(2,1)S(1)}, u32[]{:S(2)}, u32[]{:S(2)}) %collective-permute-start.10) | collective-permute-done | bytes 786464 | tf_op jit(solution)/shard_map/ppermute | solution.py:27
  69.7 3.7 %collective-permute-start.13 = (bf16[8,96,512]{2,1,0:T(8,128)(2,1)S(1)}, bf16[8,96,512]{2,1,0:T(8,128)(2,1)}, u32[]{:S(2)}, u32[]{:S(2)}) collective-permute-start(bf16[8,96,512]{2,1,0:T(8,128)(2,1)S(1)} %collective-permute-done.10.rest_3_), channel_id=1, source_target_pairs={{0,96},{1,97},{2,98},{3,99},{4,100},{5,101},{6,102},{7,103},{8,104... | collective-permute-start | bytes 2359304 | tf_op jit(solution)/shard_map/ppermute | solution.py:27
  73.4 13.3 %collective-permute-done.9.rest_2_ = bf16[8,96,512]{2,1,0:T(8,128)(2,1)S(1)} collective-permute-done((bf16[8,96,512]{2,1,0:T(8,128)(2,1)}, bf16[8,96,512]{2,1,0:T(8,128)(2,1)S(1)}, u32[]{:S(2)}, u32[]{:S(2)}) %collective-permute-start.9) | collective-permute-done | bytes 786464 | tf_op jit(solution)/shard_map/ppermute | solution.py:27
  88.8 11.8 %collective-permute-done.13.rest_5_ = bf16[8,96,512]{2,1,0:T(8,128)(2,1)} collective-permute-done((bf16[8,96,512]{2,1,0:T(8,128)(2,1)S(1)}, bf16[8,96,512]{2,1,0:T(8,128)(2,1)}, u32[]{:S(2)}, u32[]{:S(2)}) %collective-permute-start.13) | collective-permute-done | bytes 786464 | tf_op jit(solution)/shard_map/ppermute | solution.py:27
  102.6 6.6 %all-to-all-start.1 = ((bf16[8,128,512]{2,1,0:T(8,128)(2,1)}), bf16[8,128,512]{2,1,0:T(8,128)(2,1)}, u32[]{:S(2)}, u32[]{:S(2)}) async-start(bf16[8,128,512]{2,1,0:T(8,128)(2,1)} %get-tuple-element.46), calls=%async_computation.1 | async-start | bytes 2097152 | tf_op jit(solution)/shard_map/all_to_all | solution.py:244
  109.2 9.1 %project.2 = (f32[320,768]{1,0:T(8,128)}, f32[320,768]{1,0:T(8,128)}) custom-call(s32[5]{0:T(128)} %stack.23.place_ref, bf16[8,320,512]{2,1,0:T(8,128)(2,1)} %copy-done, bf16[8,320,512]{2,1,0:T(8,128)(2,1)} %collective-permute-done.15.other_ref, bf16[8,96,512]{2,1,0:T(8,128)(2,1)} %regroup.1.rest_0_, bf16[8,96,512]{2,1,0:T(8,128)(2,1)} %copy-done.2, ...), custom_call_target="tpu_custom_call" | custom-call | flops 62914560 | bytes 180224 | tf_op jit(solution)/shard_map/project/pallas_call | solution.py:150
  118.3 21.0 %all-to-all-done.1.own_ref = bf16[8,128,512]{2,1,0:T(8,128)(2,1)} async-done(((bf16[8,128,512]{2,1,0:T(8,128)(2,1)}), bf16[8,128,512]{2,1,0:T(8,128)(2,1)}, u32[]{:S(2)}, u32[]{:S(2)}) %all-to-all-start.1) | async-done | bytes 1048608 | tf_op jit(solution)/shard_map/all_to_all | solution.py:244
  143.5 6.0 %project.3 = (f32[128,768]{1,0:T(8,128)}, f32[128,768]{1,0:T(8,128)}) custom-call(s32[5]{0:T(128)} %stack.23.place_ref, bf16[8,128,512]{2,1,0:T(8,128)(2,1)} %all-to-all-done.1.own_ref, bf16[8,128,512]{2,1,0:T(8,128)(2,1)} %copy-done.8, bf16[8,96,512]{2,1,0:T(8,128)(2,1)} %regroup.1.rest_0_, bf16[8,96,512]{2,1,0:T(8,128)(2,1)} %copy-done.2, ...), custom_call_target="tpu_custom_call" | custom-call | flops 25165824 | bytes 131072 | tf_op jit(solution)/shard_map/project/pallas_call | solution.py:150
  149.8 15.6 %collective-permute-done.18.rest_0_ = f32[320,768]{1,0:T(8,128)} collective-permute-done((f32[320,768]{1,0:T(8,128)}, f32[320,768]{1,0:T(8,128)}, u32[]{:S(2)}, u32[]{:S(2)}) %collective-permute-start.18) | collective-permute-done | bytes 983072 | tf_op jit(solution)/shard_map/ppermute | solution.py:27
  165.4 2.4 activate.2.rest_0_
  167.7 3.2 %collective-permute-start.23 = (bf16[160,768]{1,0:T(8,128)(2,1)}, bf16[160,768]{1,0:T(8,128)(2,1)S(1)}, u32[]{:S(2)}, u32[]{:S(2)}) collective-permute-start(bf16[160,768]{1,0:T(8,128)(2,1)} %activate.2.rest_0_), channel_id=1, source_target_pairs={{0,14},{1,15},{2,0},{3,1},{4,2},{5,3},{6,4},{7,5},{8,6},{9,7},{10,... | collective-permute-start | bytes 737288 | tf_op jit(solution)/shard_map/ppermute | solution.py:27
  172.3 4.3 %collective-permute-done.19.rest_1_ = bf16[160,768]{1,0:T(8,128)(2,1)S(1)} collective-permute-done((bf16[160,768]{1,0:T(8,128)(2,1)}, bf16[160,768]{1,0:T(8,128)(2,1)S(1)}, u32[]{:S(2)}, u32[]{:S(2)}) %collective-permute-start.19) | collective-permute-done | bytes 245792 | tf_op jit(solution)/shard_map/ppermute | solution.py:27
  176.6 3.2 %collective-permute-start.24 = (bf16[160,768]{1,0:T(8,128)(2,1)S(1)}, bf16[160,768]{1,0:T(8,128)(2,1)}, u32[]{:S(2)}, u32[]{:S(2)}) collective-permute-start(bf16[160,768]{1,0:T(8,128)(2,1)S(1)} %collective-permute-done.23.rest_8_), channel_id=1, source_target_pairs={{0,14},{1,15},{2,0},{3,1},{4,2},{5,3},{6,4},{7,5},{8,6},{9,7},{10,... | collective-permute-start | bytes 737288 | tf_op jit(solution)/shard_map/ppermute | solution.py:27
  179.8 4.5 %collective-permute-done.20.rest_2_ = bf16[160,768]{1,0:T(8,128)(2,1)S(1)} collective-permute-done((bf16[160,768]{1,0:T(8,128)(2,1)S(1)}, bf16[160,768]{1,0:T(8,128)(2,1)S(1)}, u32[]{:S(2)}, u32[]{:S(2)}) %collective-permute-start.20) | collective-permute-done | bytes 245792 | tf_op jit(solution)/shard_map/ppermute | solution.py:27
  184.3 3.2 %collective-permute-start.25 = (bf16[160,768]{1,0:T(8,128)(2,1)}, bf16[160,768]{1,0:T(8,128)(2,1)S(1)}, u32[]{:S(2)}, u32[]{:S(2)}) collective-permute-start(bf16[160,768]{1,0:T(8,128)(2,1)} %collective-permute-done.24.rest_7_), channel_id=1, source_target_pairs={{0,14},{1,15},{2,0},{3,1},{4,2},{5,3},{6,4},{7,5},{8,6},{9,7},{10,... | collective-permute-start | bytes 737288 | tf_op jit(solution)/shard_map/ppermute | solution.py:27
  190.2 3.2 %collective-permute-start.32 = (bf16[64,768]{1,0:T(8,128)(2,1)}, bf16[64,768]{1,0:T(8,128)(2,1)S(1)}, u32[]{:S(2)}, u32[]{:S(2)}) collective-permute-start(bf16[64,768]{1,0:T(8,128)(2,1)} %activate.3.rest_9_), channel_id=1, source_target_pairs={{0,14},{1,15},{2,0},{3,1},{4,2},{5,3},{6,4},{7,5},{8,6},{9,7},{10,... | collective-permute-start | bytes 294920 | tf_op jit(solution)/shard_map/ppermute | solution.py:27
  193.4 2.8 %collective-permute-done.28.rest_10_ = bf16[64,768]{1,0:T(8,128)(2,1)S(1)} collective-permute-done((bf16[64,768]{1,0:T(8,128)(2,1)}, bf16[64,768]{1,0:T(8,128)(2,1)S(1)}, u32[]{:S(2)}, u32[]{:S(2)}) %collective-permute-start.28) | collective-permute-done | bytes 98336 | tf_op jit(solution)/shard_map/ppermute | solution.py:27
  196.2 3.2 %collective-permute-start.33 = (bf16[64,768]{1,0:T(8,128)(2,1)S(1)}, bf16[64,768]{1,0:T(8,128)(2,1)S(1)}, u32[]{:S(2)}, u32[]{:S(2)}) collective-permute-start(bf16[64,768]{1,0:T(8,128)(2,1)S(1)} %collective-permute-done.32.rest_17_), channel_id=1, source_target_pairs={{0,14},{1,15},{2,0},{3,1},{4,2},{5,3},{6,4},{7,5},{8,6},{9,7},{10,... | collective-permute-start | bytes 294920 | tf_op jit(solution)/shard_map/ppermute | solution.py:27
  199.4 3.5 %collective-permute-done.29.rest_11_ = bf16[64,768]{1,0:T(8,128)(2,1)S(1)} collective-permute-done((bf16[64,768]{1,0:T(8,128)(2,1)S(1)}, bf16[64,768]{1,0:T(8,128)(2,1)S(1)}, u32[]{:S(2)}, u32[]{:S(2)}) %collective-permute-start.29) | collective-permute-done | bytes 98336 | tf_op jit(solution)/shard_map/ppermute | solution.py:27
  203.0 3.3 %collective-permute-start.34 = (bf16[64,768]{1,0:T(8,128)(2,1)S(1)}, bf16[64,768]{1,0:T(8,128)(2,1)S(1)}, u32[]{:S(2)}, u32[]{:S(2)}) collective-permute-start(bf16[64,768]{1,0:T(8,128)(2,1)S(1)} %collective-permute-done.33.rest_16_), channel_id=1, source_target_pairs={{0,14},{1,15},{2,0},{3,1},{4,2},{5,3},{6,4},{7,5},{8,6},{9,7},{10,... | collective-permute-start | bytes 294920 | tf_op jit(solution)/shard_map/ppermute | solution.py:27
  206.4 3.3 %collective-permute-start.26 = (bf16[80,768]{1,0:T(8,128)(2,1)S(1)}, bf16[80,768]{1,0:T(8,128)(2,1)S(1)}, u32[]{:S(2)}, u32[]{:S(2)}) collective-permute-start(bf16[80,768]{1,0:T(8,128)(2,1)S(1)} %slice.17), channel_id=1, source_target_pairs={{0,14},{1,15},{2,0},{3,1},{4,2},{5,3},{6,4},{7,5},{8,6},{9,7},{10,... | collective-permute-start | bytes 368648 | tf_op jit(solution)/shard_map/ppermute | solution.py:27
  209.8 3.3 %collective-permute-start.35 = (bf16[32,768]{1,0:T(8,128)(2,1)S(1)}, bf16[32,768]{1,0:T(8,128)(2,1)S(1)}, u32[]{:S(2)}, u32[]{:S(2)}) collective-permute-start(bf16[32,768]{1,0:T(8,128)(2,1)S(1)} %slice.19), channel_id=1, source_target_pairs={{0,14},{1,15},{2,0},{3,1},{4,2},{5,3},{6,4},{7,5},{8,6},{9,7},{10,... | collective-permute-start | bytes 147464 | tf_op jit(solution)/shard_map/ppermute | solution.py:27
  216.5 7.3 %mix.1 = bf16[2,768,512]{2,1,0:T(8,128)(2,1)} custom-call(s32[5]{0:T(128)} %stack.23.place_ref, bf16[1792,512]{1,0:T(8,128)(2,1)} %copy-done.1, bf16[1792,512]{1,0:T(8,128)(2,1)} %collective-permute-done.17.theirs_ref, bf16[160,768]{1,0:T(8,128)(2,1)} %activate.2.rest_0_, bf16[160,768]{1,0:T(8,128)(2,1)} %copy-done.12, bf16[160,768]{1,0:T(8,128)(2,1)} %copy-done.14, ...), custom_call_target="tpu_custom_call" | custom-call | flops 44040192 | bytes 100352 | tf_op jit(solution)/shard_map/mix/pallas_call | solution.py:213
  223.8 22.1 %all_to_all.15 = bf16[16,96,512]{2,1,0:T(8,128)(2,1)S(1)} all-to-all(bf16[16,96,512]{2,1,0:T(8,128)(2,1)} %bitcast.6), channel_id=1, replica_groups=mesh['xl'=2,'y'=4,'c'=2,'z'=8,'xh'=2] {'xh','y','xl'}, dimensions={0} | all-to-all | bytes 3145728 | tf_op jit(solution)/shard_map/all_to_all | solution.py:275
  (123 shorter events, 27.9 us)
Async XLA Ops:
  0.0 14.6 %collective-permute-start.1 = (bf16[96,512]{1,0:T(8,128)(2,1)}, bf16[96,512]{1,0:T(8,128)(2,1)S(1)}, u32[]{:S(2)}, u32[]{:S(2)}) collective-permute-start(bf16[96,512]{1,0:T(8,128)(2,1)} %rest_0_), channel_id=1, source_target_pairs={{0,4},{1,5},{2,6},{3,7},{4,8},{5,9},{6,10},{7,11},{8,12},{9,13},{1... | collective-permute-start | bytes 294920 | tf_op jit(solution)/shard_map/ppermute | solution.py:27
  3.3 11.3 %collective-permute-start.4 = (bf16[96,512]{1,0:T(8,128)(2,1)}, bf16[96,512]{1,0:T(8,128)(2,1)S(1)}, u32[]{:S(2)}, u32[]{:S(2)}) collective-permute-start(bf16[96,512]{1,0:T(8,128)(2,1)} %rest_0_), channel_id=1, source_target_pairs={{0,12},{1,13},{2,14},{3,15},{4,0},{5,1},{6,2},{7,3},{8,4},{9,5},{1... | collective-permute-start | bytes 294920 | tf_op jit(solution)/shard_map/ppermute | solution.py:27
  6.3 15.4 %collective-permute-start = (bf16[96,512]{1,0:T(8,128)(2,1)}, bf16[96,512]{1,0:T(8,128)(2,1)S(1)}, u32[]{:S(2)}, u32[]{:S(2)}) collective-permute-start(bf16[96,512]{1,0:T(8,128)(2,1)} %rest_0_), channel_id=1, source_target_pairs={{0,2},{1,3},{2,4},{3,5},{4,6},{5,7},{6,8},{7,9},{8,10},{9,11},{10,... | collective-permute-start | bytes 294920 | tf_op jit(solution)/shard_map/ppermute | solution.py:27
  7.3 14.4 %collective-permute-start.3 = (bf16[96,512]{1,0:T(8,128)(2,1)}, bf16[96,512]{1,0:T(8,128)(2,1)S(1)}, u32[]{:S(2)}, u32[]{:S(2)}) collective-permute-start(bf16[96,512]{1,0:T(8,128)(2,1)} %rest_0_), channel_id=1, source_target_pairs={{0,8},{1,9},{2,10},{3,11},{4,12},{5,13},{6,14},{7,15},{8,0},{9,1},... | collective-permute-start | bytes 294920 | tf_op jit(solution)/shard_map/ppermute | solution.py:27
  12.3 9.4 %collective-permute-start.6 = (bf16[96,512]{1,0:T(8,128)(2,1)}, bf16[96,512]{1,0:T(8,128)(2,1)S(1)}, u32[]{:S(2)}, u32[]{:S(2)}) collective-permute-start(bf16[96,512]{1,0:T(8,128)(2,1)} %rest_0_), channel_id=1, source_target_pairs={{0,14},{1,15},{2,0},{3,1},{4,2},{5,3},{6,4},{7,5},{8,6},{9,7},{10,... | collective-permute-start | bytes 294920 | tf_op jit(solution)/shard_map/ppermute | solution.py:27
  14.6 7.2 %collective-permute-start.2 = (bf16[96,512]{1,0:T(8,128)(2,1)S(1)}, bf16[96,512]{1,0:T(8,128)(2,1)S(1)}, u32[]{:S(2)}, u32[]{:S(2)}) collective-permute-start(bf16[96,512]{1,0:T(8,128)(2,1)S(1)} %collective-permute-done.1.rest_2_), channel_id=1, source_target_pairs={{0,2},{1,3},{2,4},{3,5},{4,6},{5,7},{6,8},{7,9},{8,10},{9,11},{10,... | collective-permute-start | bytes 294920 | tf_op jit(solution)/shard_map/ppermute | solution.py:27
  14.6 7.2 %collective-permute-start.5 = (bf16[96,512]{1,0:T(8,128)(2,1)S(1)}, bf16[96,512]{1,0:T(8,128)(2,1)S(1)}, u32[]{:S(2)}, u32[]{:S(2)}) collective-permute-start(bf16[96,512]{1,0:T(8,128)(2,1)S(1)} %collective-permute-done.4.rest_6_), channel_id=1, source_target_pairs={{0,14},{1,15},{2,0},{3,1},{4,2},{5,3},{6,4},{7,5},{8,6},{9,7},{10,... | collective-permute-start | bytes 294920 | tf_op jit(solution)/shard_map/ppermute | solution.py:27
  22.5 78.1 %all-to-all-start = ((bf16[8,320,512]{2,1,0:T(8,128)(2,1)}), bf16[8,320,512]{2,1,0:T(8,128)(2,1)S(1)}, u32[]{:S(2)}, u32[]{:S(2)}) async-start(bf16[8,320,512]{2,1,0:T(8,128)(2,1)} %get-tuple-element.45), calls=%async_computation | async-start | bytes 5242880 | tf_op jit(solution)/shard_map/all_to_all | solution.py:235
  30.0 18.7 %collective-permute-start.7 = (bf16[8,96,512]{2,1,0:T(8,128)(2,1)}, bf16[8,96,512]{2,1,0:T(8,128)(2,1)S(1)}, u32[]{:S(2)}, u32[]{:S(2)}) collective-permute-start(bf16[8,96,512]{2,1,0:T(8,128)(2,1)} %regroup.1.rest_0_), channel_id=1, source_target_pairs={{0,128},{1,129},{2,130},{3,131},{4,132},{5,133},{6,134},{7,135},{8... | collective-permute-start | bytes 2359304 | tf_op jit(solution)/shard_map/ppermute | solution.py:27
  30.5 23.2 %collective-permute-start.11 = (bf16[8,96,512]{2,1,0:T(8,128)(2,1)}, bf16[8,96,512]{2,1,0:T(8,128)(2,1)S(1)}, u32[]{:S(2)}, u32[]{:S(2)}) collective-permute-start(bf16[8,96,512]{2,1,0:T(8,128)(2,1)} %regroup.1.rest_0_), channel_id=1, source_target_pairs={{0,32},{1,33},{2,34},{3,35},{4,36},{5,37},{6,38},{7,39},{8,40},{9,... | collective-permute-start | bytes 2359304 | tf_op jit(solution)/shard_map/ppermute | solution.py:27
  48.7 21.0 %collective-permute-start.10 = (bf16[8,96,512]{2,1,0:T(8,128)(2,1)S(1)}, bf16[8,96,512]{2,1,0:T(8,128)(2,1)S(1)}, u32[]{:S(2)}, u32[]{:S(2)}) collective-permute-start(bf16[8,96,512]{2,1,0:T(8,128)(2,1)S(1)} %collective-permute-done.7.rest_1_), channel_id=1, source_target_pairs={{0,96},{1,97},{2,98},{3,99},{4,100},{5,101},{6,102},{7,103},{8,104... | collective-permute-start | bytes 2359304 | tf_op jit(solution)/shard_map/ppermute | solution.py:27
  51.7 35.0 %collective-permute-start.9 = (bf16[8,96,512]{2,1,0:T(8,128)(2,1)}, bf16[8,96,512]{2,1,0:T(8,128)(2,1)S(1)}, u32[]{:S(2)}, u32[]{:S(2)}) collective-permute-start(bf16[8,96,512]{2,1,0:T(8,128)(2,1)} %regroup.1.rest_0_), channel_id=1, source_target_pairs={{0,96},{1,97},{2,98},{3,99},{4,100},{5,101},{6,102},{7,103},{8,104... | collective-permute-start | bytes 2359304 | tf_op jit(solution)/shard_map/ppermute | solution.py:27
  52.5 34.2 %collective-permute-start.14 = (bf16[8,96,512]{2,1,0:T(8,128)(2,1)S(1)}, bf16[8,96,512]{2,1,0:T(8,128)(2,1)S(1)}, u32[]{:S(2)}, u32[]{:S(2)}) collective-permute-start(bf16[8,96,512]{2,1,0:T(8,128)(2,1)S(1)} %collective-permute-done.7.rest_1_), channel_id=1, source_target_pairs={{0,32},{1,33},{2,34},{3,35},{4,36},{5,37},{6,38},{7,39},{8,40},{9,... | collective-permute-start | bytes 2359304 | tf_op jit(solution)/shard_map/ppermute | solution.py:27
  53.7 33.8 %collective-permute-start.12 = (bf16[8,96,512]{2,1,0:T(8,128)(2,1)S(1)}, bf16[8,96,512]{2,1,0:T(8,128)(2,1)S(1)}, u32[]{:S(2)}, u32[]{:S(2)}) collective-permute-start(bf16[8,96,512]{2,1,0:T(8,128)(2,1)S(1)} %collective-permute-done.11.rest_6_), channel_id=1, source_target_pairs={{0,32},{1,33},{2,34},{3,35},{4,36},{5,37},{6,38},{7,39},{8,40},{9,... | collective-permute-start | bytes 2359304 | tf_op jit(solution)/shard_map/ppermute | solution.py:27
  69.7 30.8 %collective-permute-start.13 = (bf16[8,96,512]{2,1,0:T(8,128)(2,1)S(1)}, bf16[8,96,512]{2,1,0:T(8,128)(2,1)}, u32[]{:S(2)}, u32[]{:S(2)}) collective-permute-start(bf16[8,96,512]{2,1,0:T(8,128)(2,1)S(1)} %collective-permute-done.10.rest_3_), channel_id=1, source_target_pairs={{0,96},{1,97},{2,98},{3,99},{4,100},{5,101},{6,102},{7,103},{8,104... | collective-permute-start | bytes 2359304 | tf_op jit(solution)/shard_map/ppermute | solution.py:27
  100.5 8.7 %collective-permute-start.15 = (bf16[8,320,512]{2,1,0:T(8,128)(2,1)S(1)}, bf16[8,320,512]{2,1,0:T(8,128)(2,1)}, u32[]{:S(2)}, u32[]{:S(2)}) collective-permute-start(bf16[8,320,512]{2,1,0:T(8,128)(2,1)S(1)} %all-to-all-done.own_ref), channel_id=1, source_target_pairs={{0,16},{1,17},{2,18},{3,19},{4,20},{5,21},{6,22},{7,23},{8,24},{9,... | collective-permute-start | bytes 7864328 | tf_op jit(solution)/shard_map/ppermute | solution.py:27
  100.5 17.8 %collective-permute-start.8 = (bf16[1792,512]{1,0:T(8,128)(2,1)}, bf16[1792,512]{1,0:T(8,128)(2,1)}, u32[]{:S(2)}, u32[]{:S(2)}) collective-permute-start(bf16[1792,512]{1,0:T(8,128)(2,1)} %param.7), channel_id=1, source_target_pairs={{1,16},{3,18},{5,20},{7,22},{9,24},{11,26},{13,28},{15,30},{16,1},... | collective-permute-start | bytes 5505032 | tf_op jit(solution)/shard_map/ppermute | solution.py:27
  102.6 36.8 %all-to-all-start.1 = ((bf16[8,128,512]{2,1,0:T(8,128)(2,1)}), bf16[8,128,512]{2,1,0:T(8,128)(2,1)}, u32[]{:S(2)}, u32[]{:S(2)}) async-start(bf16[8,128,512]{2,1,0:T(8,128)(2,1)} %get-tuple-element.46), calls=%async_computation.1 | async-start | bytes 2097152 | tf_op jit(solution)/shard_map/all_to_all | solution.py:244
  139.5 25.9 %collective-permute-start.18 = (f32[320,768]{1,0:T(8,128)}, f32[320,768]{1,0:T(8,128)}, u32[]{:S(2)}, u32[]{:S(2)}) collective-permute-start(f32[320,768]{1,0:T(8,128)} %get-tuple-element.56), channel_id=1, source_target_pairs={{0,1},{1,0},{2,3},{3,2},{4,5},{5,4},{6,7},{7,6},{8,9},{9,8},{10,11... | collective-permute-start | bytes 2949128 | tf_op jit(solution)/shard_map/ppermute | solution.py:27
  149.5 67.0 %collective-permute-start.17 = (bf16[1792,512]{1,0:T(8,128)(2,1)S(1)}, bf16[1792,512]{1,0:T(8,128)(2,1)}, u32[]{:S(2)}, u32[]{:S(2)}) collective-permute-start(bf16[1792,512]{1,0:T(8,128)(2,1)S(1)} %broadcast_select_fusion.mine_ref), channel_id=1, source_target_pairs={{0,16},{1,17},{2,18},{3,19},{4,20},{5,21},{6,22},{7,23},{8,24},{9,... | collective-permute-start | bytes 5505032 | tf_op jit(solution)/shard_map/ppermute | solution.py:27
  167.7 8.8 %collective-permute-start.19 = (bf16[160,768]{1,0:T(8,128)(2,1)}, bf16[160,768]{1,0:T(8,128)(2,1)S(1)}, u32[]{:S(2)}, u32[]{:S(2)}) collective-permute-start(bf16[160,768]{1,0:T(8,128)(2,1)} %activate.2.rest_0_), channel_id=1, source_target_pairs={{0,2},{1,3},{2,4},{3,5},{4,6},{5,7},{6,8},{7,9},{8,10},{9,11},{10,... | collective-permute-start | bytes 737288 | tf_op jit(solution)/shard_map/ppermute | solution.py:27
  167.7 8.8 %collective-permute-start.23 = (bf16[160,768]{1,0:T(8,128)(2,1)}, bf16[160,768]{1,0:T(8,128)(2,1)S(1)}, u32[]{:S(2)}, u32[]{:S(2)}) collective-permute-start(bf16[160,768]{1,0:T(8,128)(2,1)} %activate.2.rest_0_), channel_id=1, source_target_pairs={{0,14},{1,15},{2,0},{3,1},{4,2},{5,3},{6,4},{7,5},{8,6},{9,7},{10,... | collective-permute-start | bytes 737288 | tf_op jit(solution)/shard_map/ppermute | solution.py:27
  171.0 16.6 %collective-permute-start.27 = (f32[128,768]{1,0:T(8,128)}, f32[128,768]{1,0:T(8,128)S(1)}, u32[]{:S(2)}, u32[]{:S(2)}) collective-permute-start(f32[128,768]{1,0:T(8,128)} %get-tuple-element.59), channel_id=1, source_target_pairs={{0,1},{1,0},{2,3},{3,2},{4,5},{5,4},{6,7},{7,6},{8,9},{9,8},{10,11... | collective-permute-start | bytes 1179656 | tf_op jit(solution)/shard_map/ppermute | solution.py:27
  176.6 7.7 %collective-permute-start.20 = (bf16[160,768]{1,0:T(8,128)(2,1)S(1)}, bf16[160,768]{1,0:T(8,128)(2,1)S(1)}, u32[]{:S(2)}, u32[]{:S(2)}) collective-permute-start(bf16[160,768]{1,0:T(8,128)(2,1)S(1)} %collective-permute-done.19.rest_1_), channel_id=1, source_target_pairs={{0,2},{1,3},{2,4},{3,5},{4,6},{5,7},{6,8},{7,9},{8,10},{9,11},{10,... | collective-permute-start | bytes 737288 | tf_op jit(solution)/shard_map/ppermute | solution.py:27
  176.6 7.7 %collective-permute-start.24 = (bf16[160,768]{1,0:T(8,128)(2,1)S(1)}, bf16[160,768]{1,0:T(8,128)(2,1)}, u32[]{:S(2)}, u32[]{:S(2)}) collective-permute-start(bf16[160,768]{1,0:T(8,128)(2,1)S(1)} %collective-permute-done.23.rest_8_), channel_id=1, source_target_pairs={{0,14},{1,15},{2,0},{3,1},{4,2},{5,3},{6,4},{7,5},{8,6},{9,7},{10,... | collective-permute-start | bytes 737288 | tf_op jit(solution)/shard_map/ppermute | solution.py:27
  184.3 22.0 %collective-permute-start.21 = (bf16[160,768]{1,0:T(8,128)(2,1)S(1)}, bf16[160,768]{1,0:T(8,128)(2,1)S(1)}, u32[]{:S(2)}, u32[]{:S(2)}) collective-permute-start(bf16[160,768]{1,0:T(8,128)(2,1)S(1)} %collective-permute-done.20.rest_2_), channel_id=1, source_target_pairs={{0,2},{1,3},{2,4},{3,5},{4,6},{5,7},{6,8},{7,9},{8,10},{9,11},{10,... | collective-permute-start | bytes 737288 | tf_op jit(solution)/shard_map/ppermute | solution.py:27
  184.3 22.1 %collective-permute-start.25 = (bf16[160,768]{1,0:T(8,128)(2,1)}, bf16[160,768]{1,0:T(8,128)(2,1)S(1)}, u32[]{:S(2)}, u32[]{:S(2)}) collective-permute-start(bf16[160,768]{1,0:T(8,128)(2,1)} %collective-permute-done.24.rest_7_), channel_id=1, source_target_pairs={{0,14},{1,15},{2,0},{3,1},{4,2},{5,3},{6,4},{7,5},{8,6},{9,7},{10,... | collective-permute-start | bytes 737288 | tf_op jit(solution)/shard_map/ppermute | solution.py:27
  196.2 6.8 %collective-permute-start.29 = (bf16[64,768]{1,0:T(8,128)(2,1)S(1)}, bf16[64,768]{1,0:T(8,128)(2,1)S(1)}, u32[]{:S(2)}, u32[]{:S(2)}) collective-permute-start(bf16[64,768]{1,0:T(8,128)(2,1)S(1)} %collective-permute-done.28.rest_10_), channel_id=1, source_target_pairs={{0,2},{1,3},{2,4},{3,5},{4,6},{5,7},{6,8},{7,9},{8,10},{9,11},{10,... | collective-permute-start | bytes 294920 | tf_op jit(solution)/shard_map/ppermute | solution.py:27
  196.2 6.8 %collective-permute-start.33 = (bf16[64,768]{1,0:T(8,128)(2,1)S(1)}, bf16[64,768]{1,0:T(8,128)(2,1)S(1)}, u32[]{:S(2)}, u32[]{:S(2)}) collective-permute-start(bf16[64,768]{1,0:T(8,128)(2,1)S(1)} %collective-permute-done.32.rest_17_), channel_id=1, source_target_pairs={{0,14},{1,15},{2,0},{3,1},{4,2},{5,3},{6,4},{7,5},{8,6},{9,7},{10,... | collective-permute-start | bytes 294920 | tf_op jit(solution)/shard_map/ppermute | solution.py:27
  203.0 6.8 %collective-permute-start.34 = (bf16[64,768]{1,0:T(8,128)(2,1)S(1)}, bf16[64,768]{1,0:T(8,128)(2,1)S(1)}, u32[]{:S(2)}, u32[]{:S(2)}) collective-permute-start(bf16[64,768]{1,0:T(8,128)(2,1)S(1)} %collective-permute-done.33.rest_16_), channel_id=1, source_target_pairs={{0,14},{1,15},{2,0},{3,1},{4,2},{5,3},{6,4},{7,5},{8,6},{9,7},{10,... | collective-permute-start | bytes 294920 | tf_op jit(solution)/shard_map/ppermute | solution.py:27
  206.3 8.8 %collective-permute-start.22 = (bf16[80,768]{1,0:T(8,128)(2,1)S(1)}, bf16[80,768]{1,0:T(8,128)(2,1)S(1)}, u32[]{:S(2)}, u32[]{:S(2)}) collective-permute-start(bf16[80,768]{1,0:T(8,128)(2,1)S(1)} %slice.16), channel_id=1, source_target_pairs={{0,2},{1,3},{2,4},{3,5},{4,6},{5,7},{6,8},{7,9},{8,10},{9,11},{10,... | collective-permute-start | bytes 368648 | tf_op jit(solution)/shard_map/ppermute | solution.py:27
  206.4 8.7 %collective-permute-start.26 = (bf16[80,768]{1,0:T(8,128)(2,1)S(1)}, bf16[80,768]{1,0:T(8,128)(2,1)S(1)}, u32[]{:S(2)}, u32[]{:S(2)}) collective-permute-start(bf16[80,768]{1,0:T(8,128)(2,1)S(1)} %slice.17), channel_id=1, source_target_pairs={{0,14},{1,15},{2,0},{3,1},{4,2},{5,3},{6,4},{7,5},{8,6},{9,7},{10,... | collective-permute-start | bytes 368648 | tf_op jit(solution)/shard_map/ppermute | solution.py:27
  (38 other events, 383.3 us)

commit v5 on v4

--- a/solution.py
+++ b/solution.py
@@ -49,6 +49,10 @@
 
 def together(*values):
     return lax.optimization_barrier(values)
+
+
+def room(mib):
+    return pltpu.CompilerParams(vmem_limit_bytes=mib << 20)
 
 
 def cost(flops, *arrays):
@@ -184,6 +188,7 @@
         scratch_shapes=[pltpu.VMEM(keep.shape, F32)],
         cost_estimate=cost(0, keep, *gots),
         name="activate",
+        compiler_params=room(8),
     )(keep, *gots)
 
 
@@ -218,6 +223,7 @@
         scratch_shapes=[pltpu.VMEM((nz * units, rows), BF16)],
         cost_estimate=cost(4 * nz * units * rows * width, mine, theirs, *parts),
         name="mix",
+        compiler_params=room(24),
     )(place, mine, theirs, *parts)
 
 
@@ -237,6 +243,7 @@
     near = regroup(place, around)
     far = swap_xl(near)
     near_before, near_after = along_y(near, 1), along_y(near, -1)
+    far, near_before, near_after = together(far, near_before, near_after)
     far_before, far_after = along_y(far, 1), along_y(far, -1)
     near_across, far_across = along_y(near_before, 1), along_y(far_after, -1)
     pieces = (near, far, near_after, far_after, near_across, far_across, near_before, far_before)
@@ -252,10 +259,11 @@
         down_weight,
         lambda xl, y, c, z, xh: (xl, y, 1 - c, z, 1 - xh) if c != xh else None,
     )
-    moved, weights[1], _ = together(moved, weights[1], gives[0])
+    moved, weights[1], _ = together(moved, weights[1], gots[0])
     mine = jnp.where(c == xh, down_weight, moved)
 
-    keep, give = project(place, weights[1], swap_core(weights[1]), pieces, ())
+    both = together(weights[1], swap_core(weights[1]), hiddens[0])
+    keep, give = project(place, *both[:2], pieces, ())
     hiddens.append(activate(keep, [swap_xh(give)]))
     mine, _ = together(mine, give)
     theirs = swap_core(mine)

time: 247 us -> 224 us (0.907)
  waiting for transfers between devices: 112 us -> 90.9 us
  Pallas kernels: 32.6 us -> 25.2 us
  starting transfers between devices: 71.2 us -> 75.1 us
    ppermute x36, waiting for transfers between devices: 91 us -> 73.6 us  [send(): return lax.ppermute(value, AXES, pairs)]
    pallas_call x2, Pallas kernels: 4.21 us -> 0.24 us  [activate(): pl.pallas_call(body, in_specs=[WHOLE] * (1 + len(gots)), out_specs=WHOLE,...]
    ppermute x36, starting transfers between devices: 59.9 us -> 63.8 us  [send(): return lax.ppermute(value, AXES, pairs)]
    all_to_all x1, waiting for transfers between devices: 21 us -> 17.3 us  [shards(): weights.append(lax.all_to_all(ready, 'z', 0, 0, tiled=True))]
    pallas_call x1, Pallas kernels: 7.26 us -> 3.79 us  [mix(): pl.pallas_call(body, in_specs=[SCALARS] + [WHOLE] * (2 + len(parts)), out...]
    unnamed x64 -> x38, local copies, waits for them, and re-layouts: 5.04 us -> 7.01 us
  transfers between devices with their start and end apart: 38 -> 38, of which waited for: 12 -> 11; matrix products, arithmetic and copies ran while one was open for 1% -> 0% of each run, Pallas kernels for 10% -> 7%
where the time goes in v5:
time: 224 us; the launch traced here: 223 us
  waiting for transfers between devices  90.9 us (41%)
  starting transfers between devices  75.1 us (34%)
  Pallas kernels  25.2 us (11%)
  blocking collectives  22.8 us (10%)
  local copies, waits for them, and re-layouts  7.72 us (3%)
    ppermute x36, waiting for transfers between devices, send(): return lax.ppermute(value, AXES, pairs)  73.6 us
    ppermute x36, starting transfers between devices, send(): return lax.ppermute(value, AXES, pairs)  63.8 us
    all_to_all x1, blocking collectives, shards(): got = lax.all_to_all(out, ('xh', 'y', 'xl'), 0, 0, tiled=True)  22.8 us
    all_to_all x1, waiting for transfers between devices, shards(): weights.append(lax.all_to_all(ready, 'z', 0, 0, tiled=True))  17.3 us
    pallas_call x2, Pallas kernels, project(): pl.pallas_call(body, in_specs=[SCALARS] + [pl.BlockSpec(memory_space=pl.A...  15.1 us
    unnamed x38, local copies, waits for them, and re-layouts  7.01 us
    all_to_all x1, starting transfers between devices, shards(): weights.append(lax.all_to_all(ready, 'z', 0, 0, tiled=True))  6.65 us
    all_to_all x1, starting transfers between devices, shards(): weights = [lax.all_to_all(ready, 'z', 0, 0, tiled=True)]  4.68 us
  transfers between devices with their start and end apart: 38, of which 11 were waited for; matrix products, arithmetic and copies ran while one was open for 0% of the time, Pallas kernels for 7%

profile of v5, /device:TPU:2, one launch (start us, length us, event | category | flops | bytes accessed | tf_op | source)
XLA Modules:
  0.0 223.1 jit_solution(9360787502779316534)
XLA Ops:
  0.0 3.3 %collective-permute-start.1 = (bf16[96,512]{1,0:T(8,128)(2,1)}, bf16[96,512]{1,0:T(8,128)(2,1)S(1)}, u32[]{:S(2)}, u32[]{:S(2)}) collective-permute-start(bf16[96,512]{1,0:T(8,128)(2,1)} %rest_0_), channel_id=1, source_target_pairs={{0,4},{1,5},{2,6},{3,7},{4,8},{5,9},{6,10},{7,11},{8,12},{9,13},{1... | collective-permute-start | bytes 294920 | tf_op jit(solution)/shard_map/ppermute | solution.py:27
  3.3 3.0 %collective-permute-start.4 = (bf16[96,512]{1,0:T(8,128)(2,1)}, bf16[96,512]{1,0:T(8,128)(2,1)S(1)}, u32[]{:S(2)}, u32[]{:S(2)}) collective-permute-start(bf16[96,512]{1,0:T(8,128)(2,1)} %rest_0_), channel_id=1, source_target_pairs={{0,12},{1,13},{2,14},{3,15},{4,0},{5,1},{6,2},{7,3},{8,4},{9,5},{1... | collective-permute-start | bytes 294920 | tf_op jit(solution)/shard_map/ppermute | solution.py:27
  7.3 5.0 %collective-permute-start.3 = (bf16[96,512]{1,0:T(8,128)(2,1)}, bf16[96,512]{1,0:T(8,128)(2,1)S(1)}, u32[]{:S(2)}, u32[]{:S(2)}) collective-permute-start(bf16[96,512]{1,0:T(8,128)(2,1)} %rest_0_), channel_id=1, source_target_pairs={{0,8},{1,9},{2,10},{3,11},{4,12},{5,13},{6,14},{7,15},{8,0},{9,1},... | collective-permute-start | bytes 294920 | tf_op jit(solution)/shard_map/ppermute | solution.py:27
  12.3 2.2 collective-permute-start.6
  14.6 3.2 %collective-permute-start.5 = (bf16[96,512]{1,0:T(8,128)(2,1)S(1)}, bf16[96,512]{1,0:T(8,128)(2,1)S(1)}, u32[]{:S(2)}, u32[]{:S(2)}) collective-permute-start(bf16[96,512]{1,0:T(8,128)(2,1)S(1)} %collective-permute-done.4.rest_6_), channel_id=1, source_target_pairs={{0,14},{1,15},{2,0},{3,1},{4,2},{5,3},{6,4},{7,5},{8,6},{9,7},{10,... | collective-permute-start | bytes 294920 | tf_op jit(solution)/shard_map/ppermute | solution.py:27
  17.8 3.9 %slice_units.1 = (bf16[8,320,512]{2,1,0:T(8,128)(2,1)}, bf16[8,128,512]{2,1,0:T(8,128)(2,1)}) custom-call(bf16[512,1792]{1,0:T(8,128)(2,1)} %g_ref.1, bf16[512,1792]{1,0:T(8,128)(2,1)} %u_ref.1), custom_call_target="tpu_custom_call" | custom-call | bytes 114688 | tf_op jit(solution)/shard_map/slice_units/pallas_call | solution.py:94
  22.5 4.7 %all-to-all-start = ((bf16[8,320,512]{2,1,0:T(8,128)(2,1)}), bf16[8,320,512]{2,1,0:T(8,128)(2,1)S(1)}, u32[]{:S(2)}, u32[]{:S(2)}) async-start(bf16[8,320,512]{2,1,0:T(8,128)(2,1)} %get-tuple-element.51), calls=%async_computation | async-start | bytes 5242880 | tf_op jit(solution)/shard_map/all_to_all | solution.py:241
  27.8 2.2 regroup.1.rest_0_
  33.8 14.9 %collective-permute-done.7.rest_1_ = bf16[8,96,512]{2,1,0:T(8,128)(2,1)S(1)} collective-permute-done((bf16[8,96,512]{2,1,0:T(8,128)(2,1)}, bf16[8,96,512]{2,1,0:T(8,128)(2,1)S(1)}, u32[]{:S(2)}, u32[]{:S(2)}) %collective-permute-start.7) | collective-permute-done | bytes 786464 | tf_op jit(solution)/shard_map/ppermute | solution.py:27
  50.3 2.9 %collective-permute-start.11 = (bf16[8,96,512]{2,1,0:T(8,128)(2,1)S(1)}, bf16[8,96,512]{2,1,0:T(8,128)(2,1)S(1)}, u32[]{:S(2)}, u32[]{:S(2)}) collective-permute-start(bf16[8,96,512]{2,1,0:T(8,128)(2,1)S(1)} %collective-permute-done.7.rest_1_), channel_id=1, source_target_pairs={{0,96},{1,97},{2,98},{3,99},{4,100},{5,101},{6,102},{7,103},{8,104... | collective-permute-start | bytes 2359304 | tf_op jit(solution)/shard_map/ppermute | solution.py:27
  53.9 14.2 %collective-permute-done.11.rest_3_ = bf16[8,96,512]{2,1,0:T(8,128)(2,1)S(1)} collective-permute-done((bf16[8,96,512]{2,1,0:T(8,128)(2,1)S(1)}, bf16[8,96,512]{2,1,0:T(8,128)(2,1)S(1)}, u32[]{:S(2)}, u32[]{:S(2)}) %collective-permute-start.11) | collective-permute-done | bytes 786464 | tf_op jit(solution)/shard_map/ppermute | solution.py:27
  68.1 3.4 %collective-permute-start.13 = (bf16[8,96,512]{2,1,0:T(8,128)(2,1)S(1)}, bf16[8,96,512]{2,1,0:T(8,128)(2,1)}, u32[]{:S(2)}, u32[]{:S(2)}) collective-permute-start(bf16[8,96,512]{2,1,0:T(8,128)(2,1)S(1)} %collective-permute-done.11.rest_3_), channel_id=1, source_target_pairs={{0,96},{1,97},{2,98},{3,99},{4,100},{5,101},{6,102},{7,103},{8,104... | collective-permute-start | bytes 2359304 | tf_op jit(solution)/shard_map/ppermute | solution.py:27
  71.5 16.6 %collective-permute-done.12.rest_4_ = bf16[8,96,512]{2,1,0:T(8,128)(2,1)S(1)} collective-permute-done((bf16[8,96,512]{2,1,0:T(8,128)(2,1)S(1)}, bf16[8,96,512]{2,1,0:T(8,128)(2,1)S(1)}, u32[]{:S(2)}, u32[]{:S(2)}) %collective-permute-start.12) | collective-permute-done | bytes 786464 | tf_op jit(solution)/shard_map/ppermute | solution.py:27
  91.9 6.6 %all-to-all-start.1 = ((bf16[8,128,512]{2,1,0:T(8,128)(2,1)}), bf16[8,128,512]{2,1,0:T(8,128)(2,1)}, u32[]{:S(2)}, u32[]{:S(2)}) async-start(bf16[8,128,512]{2,1,0:T(8,128)(2,1)} %get-tuple-element.54), calls=%async_computation.1 | async-start | bytes 2097152 | tf_op jit(solution)/shard_map/all_to_all | solution.py:251
  98.6 9.1 %project.2 = (f32[320,768]{1,0:T(8,128)}, f32[320,768]{1,0:T(8,128)}) custom-call(s32[5]{0:T(128)} %stack.23.place_ref, bf16[8,320,512]{2,1,0:T(8,128)(2,1)} %copy-done.3, bf16[8,320,512]{2,1,0:T(8,128)(2,1)} %collective-permute-done.15.other_ref, bf16[8,96,512]{2,1,0:T(8,128)(2,1)} %regroup.1.rest_0_, bf16[8,96,512]{2,1,0:T(8,128)(2,1)} %copy-done.4, ...), custom_call_target="tpu_custom_call" | custom-call | flops 62914560 | bytes 180224 | tf_op jit(solution)/shard_map/project/pallas_call | solution.py:154
  107.7 3.7 %collective-permute-start.16 = (f32[320,768]{1,0:T(8,128)}, f32[320,768]{1,0:T(8,128)S(1)}, u32[]{:S(2)}, u32[]{:S(2)}) collective-permute-start(f32[320,768]{1,0:T(8,128)} %get-tuple-element.64), channel_id=1, source_target_pairs={{0,1},{1,0},{2,3},{3,2},{4,5},{5,4},{6,7},{7,6},{8,9},{9,8},{10,11... | collective-permute-start | bytes 2949128 | tf_op jit(solution)/shard_map/ppermute | solution.py:27
  111.4 17.3 %all-to-all-done.1.own_ref = bf16[8,128,512]{2,1,0:T(8,128)(2,1)} async-done(((bf16[8,128,512]{2,1,0:T(8,128)(2,1)}), bf16[8,128,512]{2,1,0:T(8,128)(2,1)}, u32[]{:S(2)}, u32[]{:S(2)}) %all-to-all-start.1) | async-done | bytes 1048608 | tf_op jit(solution)/shard_map/all_to_all | solution.py:251
  128.7 9.3 %collective-permute-done.16.rest_0_ = f32[320,768]{1,0:T(8,128)S(1)} collective-permute-done((f32[320,768]{1,0:T(8,128)}, f32[320,768]{1,0:T(8,128)S(1)}, u32[]{:S(2)}, u32[]{:S(2)}) %collective-permute-start.16) | collective-permute-done | bytes 983072 | tf_op jit(solution)/shard_map/ppermute | solution.py:27
  141.9 6.0 %project.3 = (f32[128,768]{1,0:T(8,128)}, f32[128,768]{1,0:T(8,128)}) custom-call(s32[5]{0:T(128)} %stack.23.place_ref, bf16[8,128,512]{2,1,0:T(8,128)(2,1)} %all-to-all-done.1.own_ref, bf16[8,128,512]{2,1,0:T(8,128)(2,1)} %copy-done.11, bf16[8,96,512]{2,1,0:T(8,128)(2,1)} %regroup.1.rest_0_, bf16[8,96,512]{2,1,0:T(8,128)(2,1)} %copy-done.4, ...), custom_call_target="tpu_custom_call" | custom-call | flops 25165824 | bytes 131072 | tf_op jit(solution)/shard_map/project/pallas_call | solution.py:154
  154.4 4.8 %collective-permute-done.19.rest_1_ = bf16[160,768]{1,0:T(8,128)(2,1)S(1)} collective-permute-done((bf16[160,768]{1,0:T(8,128)(2,1)S(1)}, bf16[160,768]{1,0:T(8,128)(2,1)S(1)}, u32[]{:S(2)}, u32[]{:S(2)}) %collective-permute-start.19) | collective-permute-done | bytes 245792 | tf_op jit(solution)/shard_map/ppermute | solution.py:27
  159.4 3.0 %collective-permute-start.24 = (bf16[160,768]{1,0:T(8,128)(2,1)S(1)}, bf16[160,768]{1,0:T(8,128)(2,1)S(1)}, u32[]{:S(2)}, u32[]{:S(2)}) collective-permute-start(bf16[160,768]{1,0:T(8,128)(2,1)S(1)} %collective-permute-done.23.rest_8_), channel_id=1, source_target_pairs={{0,14},{1,15},{2,0},{3,1},{4,2},{5,3},{6,4},{7,5},{8,6},{9,7},{10,... | collective-permute-start | bytes 737288 | tf_op jit(solution)/shard_map/ppermute | solution.py:27
  162.4 5.1 %collective-permute-done.20.rest_2_ = bf16[160,768]{1,0:T(8,128)(2,1)S(1)} collective-permute-done((bf16[160,768]{1,0:T(8,128)(2,1)S(1)}, bf16[160,768]{1,0:T(8,128)(2,1)S(1)}, u32[]{:S(2)}, u32[]{:S(2)}) %collective-permute-start.20) | collective-permute-done | bytes 245792 | tf_op jit(solution)/shard_map/ppermute | solution.py:27
  167.5 3.2 %collective-permute-start.25 = (bf16[160,768]{1,0:T(8,128)(2,1)S(1)}, bf16[160,768]{1,0:T(8,128)(2,1)S(1)}, u32[]{:S(2)}, u32[]{:S(2)}) collective-permute-start(bf16[160,768]{1,0:T(8,128)(2,1)S(1)} %collective-permute-done.24.rest_7_), channel_id=1, source_target_pairs={{0,14},{1,15},{2,0},{3,1},{4,2},{5,3},{6,4},{7,5},{8,6},{9,7},{10,... | collective-permute-start | bytes 737288 | tf_op jit(solution)/shard_map/ppermute | solution.py:27
  171.9 3.2 %collective-permute-start.32 = (bf16[64,768]{1,0:T(8,128)(2,1)S(1)}, bf16[64,768]{1,0:T(8,128)(2,1)S(1)}, u32[]{:S(2)}, u32[]{:S(2)}) collective-permute-start(bf16[64,768]{1,0:T(8,128)(2,1)S(1)} %activate.3.rest_9_), channel_id=1, source_target_pairs={{0,14},{1,15},{2,0},{3,1},{4,2},{5,3},{6,4},{7,5},{8,6},{9,7},{10,... | collective-permute-start | bytes 294920 | tf_op jit(solution)/shard_map/ppermute | solution.py:27
  175.1 2.6 %collective-permute-done.28.rest_10_ = bf16[64,768]{1,0:T(8,128)(2,1)S(1)} collective-permute-done((bf16[64,768]{1,0:T(8,128)(2,1)S(1)}, bf16[64,768]{1,0:T(8,128)(2,1)S(1)}, u32[]{:S(2)}, u32[]{:S(2)}) %collective-permute-start.28) | collective-permute-done | bytes 98336 | tf_op jit(solution)/shard_map/ppermute | solution.py:27
  177.7 3.2 %collective-permute-start.33 = (bf16[64,768]{1,0:T(8,128)(2,1)S(1)}, bf16[64,768]{1,0:T(8,128)(2,1)S(1)}, u32[]{:S(2)}, u32[]{:S(2)}) collective-permute-start(bf16[64,768]{1,0:T(8,128)(2,1)S(1)} %collective-permute-done.32.rest_17_), channel_id=1, source_target_pairs={{0,14},{1,15},{2,0},{3,1},{4,2},{5,3},{6,4},{7,5},{8,6},{9,7},{10,... | collective-permute-start | bytes 294920 | tf_op jit(solution)/shard_map/ppermute | solution.py:27
  181.0 2.6 %collective-permute-done.29.rest_11_ = bf16[64,768]{1,0:T(8,128)(2,1)S(1)} collective-permute-done((bf16[64,768]{1,0:T(8,128)(2,1)S(1)}, bf16[64,768]{1,0:T(8,128)(2,1)S(1)}, u32[]{:S(2)}, u32[]{:S(2)}) %collective-permute-start.29) | collective-permute-done | bytes 98336 | tf_op jit(solution)/shard_map/ppermute | solution.py:27
  183.6 3.2 %collective-permute-start.34 = (bf16[64,768]{1,0:T(8,128)(2,1)S(1)}, bf16[64,768]{1,0:T(8,128)(2,1)S(1)}, u32[]{:S(2)}, u32[]{:S(2)}) collective-permute-start(bf16[64,768]{1,0:T(8,128)(2,1)S(1)} %collective-permute-done.33.rest_16_), channel_id=1, source_target_pairs={{0,14},{1,15},{2,0},{3,1},{4,2},{5,3},{6,4},{7,5},{8,6},{9,7},{10,... | collective-permute-start | bytes 294920 | tf_op jit(solution)/shard_map/ppermute | solution.py:27
  186.9 3.3 %collective-permute-start.26 = (bf16[80,768]{1,0:T(8,128)(2,1)S(1)}, bf16[80,768]{1,0:T(8,128)(2,1)S(1)}, u32[]{:S(2)}, u32[]{:S(2)}) collective-permute-start(bf16[80,768]{1,0:T(8,128)(2,1)S(1)} %slice.17), channel_id=1, source_target_pairs={{0,14},{1,15},{2,0},{3,1},{4,2},{5,3},{6,4},{7,5},{8,6},{9,7},{10,... | collective-permute-start | bytes 368648 | tf_op jit(solution)/shard_map/ppermute | solution.py:27
  190.4 3.3 %collective-permute-start.35 = (bf16[32,768]{1,0:T(8,128)(2,1)S(1)}, bf16[32,768]{1,0:T(8,128)(2,1)S(1)}, u32[]{:S(2)}, u32[]{:S(2)}) collective-permute-start(bf16[32,768]{1,0:T(8,128)(2,1)S(1)} %slice.19), channel_id=1, source_target_pairs={{0,14},{1,15},{2,0},{3,1},{4,2},{5,3},{6,4},{7,5},{8,6},{9,7},{10,... | collective-permute-start | bytes 147464 | tf_op jit(solution)/shard_map/ppermute | solution.py:27
  195.6 3.8 %mix.1 = bf16[2,768,512]{2,1,0:T(8,128)(2,1)S(1)} custom-call(s32[5]{0:T(128)S(1)} %copy-done.2, bf16[1792,512]{1,0:T(8,128)(2,1)S(1)} %broadcast_select_fusion.mine_ref, bf16[1792,512]{1,0:T(8,128)(2,1)S(1)} %collective-permute-done.18.theirs_ref, bf16[160,768]{1,0:T(8,128)(2,1)S(1)} %activate.2.rest_0_, ...), custom_call_target="tpu_custom_call" | custom-call | flops 44040192 | bytes 100352 | tf_op jit(solution)/shard_map/mix/pallas_call | solution.py:218
  199.4 22.8 %all_to_all.15 = bf16[16,96,512]{2,1,0:T(8,128)(2,1)S(1)} all-to-all(bf16[16,96,512]{2,1,0:T(8,128)(2,1)S(1)} %bitcast.6), channel_id=1, replica_groups=mesh['xl'=2,'y'=4,'c'=2,'z'=8,'xh'=2] {'xh','y','xl'}, dimensions={0} | all-to-all | bytes 3145728 | tf_op jit(solution)/shard_map/all_to_all | solution.py:283
  (97 shorter events, 27.1 us)
Async XLA Ops:
  0.0 14.6 %collective-permute-start.1 = (bf16[96,512]{1,0:T(8,128)(2,1)}, bf16[96,512]{1,0:T(8,128)(2,1)S(1)}, u32[]{:S(2)}, u32[]{:S(2)}) collective-permute-start(bf16[96,512]{1,0:T(8,128)(2,1)} %rest_0_), channel_id=1, source_target_pairs={{0,4},{1,5},{2,6},{3,7},{4,8},{5,9},{6,10},{7,11},{8,12},{9,13},{1... | collective-permute-start | bytes 294920 | tf_op jit(solution)/shard_map/ppermute | solution.py:27
  3.3 11.3 %collective-permute-start.4 = (bf16[96,512]{1,0:T(8,128)(2,1)}, bf16[96,512]{1,0:T(8,128)(2,1)S(1)}, u32[]{:S(2)}, u32[]{:S(2)}) collective-permute-start(bf16[96,512]{1,0:T(8,128)(2,1)} %rest_0_), channel_id=1, source_target_pairs={{0,12},{1,13},{2,14},{3,15},{4,0},{5,1},{6,2},{7,3},{8,4},{9,5},{1... | collective-permute-start | bytes 294920 | tf_op jit(solution)/shard_map/ppermute | solution.py:27
  6.3 15.4 %collective-permute-start = (bf16[96,512]{1,0:T(8,128)(2,1)}, bf16[96,512]{1,0:T(8,128)(2,1)S(1)}, u32[]{:S(2)}, u32[]{:S(2)}) collective-permute-start(bf16[96,512]{1,0:T(8,128)(2,1)} %rest_0_), channel_id=1, source_target_pairs={{0,2},{1,3},{2,4},{3,5},{4,6},{5,7},{6,8},{7,9},{8,10},{9,11},{10,... | collective-permute-start | bytes 294920 | tf_op jit(solution)/shard_map/ppermute | solution.py:27
  7.3 14.4 %collective-permute-start.3 = (bf16[96,512]{1,0:T(8,128)(2,1)}, bf16[96,512]{1,0:T(8,128)(2,1)S(1)}, u32[]{:S(2)}, u32[]{:S(2)}) collective-permute-start(bf16[96,512]{1,0:T(8,128)(2,1)} %rest_0_), channel_id=1, source_target_pairs={{0,8},{1,9},{2,10},{3,11},{4,12},{5,13},{6,14},{7,15},{8,0},{9,1},... | collective-permute-start | bytes 294920 | tf_op jit(solution)/shard_map/ppermute | solution.py:27
  12.3 9.4 %collective-permute-start.6 = (bf16[96,512]{1,0:T(8,128)(2,1)}, bf16[96,512]{1,0:T(8,128)(2,1)S(1)}, u32[]{:S(2)}, u32[]{:S(2)}) collective-permute-start(bf16[96,512]{1,0:T(8,128)(2,1)} %rest_0_), channel_id=1, source_target_pairs={{0,14},{1,15},{2,0},{3,1},{4,2},{5,3},{6,4},{7,5},{8,6},{9,7},{10,... | collective-permute-start | bytes 294920 | tf_op jit(solution)/shard_map/ppermute | solution.py:27
  14.6 7.2 %collective-permute-start.2 = (bf16[96,512]{1,0:T(8,128)(2,1)S(1)}, bf16[96,512]{1,0:T(8,128)(2,1)S(1)}, u32[]{:S(2)}, u32[]{:S(2)}) collective-permute-start(bf16[96,512]{1,0:T(8,128)(2,1)S(1)} %collective-permute-done.1.rest_2_), channel_id=1, source_target_pairs={{0,2},{1,3},{2,4},{3,5},{4,6},{5,7},{6,8},{7,9},{8,10},{9,11},{10,... | collective-permute-start | bytes 294920 | tf_op jit(solution)/shard_map/ppermute | solution.py:27
  14.6 7.2 %collective-permute-start.5 = (bf16[96,512]{1,0:T(8,128)(2,1)S(1)}, bf16[96,512]{1,0:T(8,128)(2,1)S(1)}, u32[]{:S(2)}, u32[]{:S(2)}) collective-permute-start(bf16[96,512]{1,0:T(8,128)(2,1)S(1)} %collective-permute-done.4.rest_6_), channel_id=1, source_target_pairs={{0,14},{1,15},{2,0},{3,1},{4,2},{5,3},{6,4},{7,5},{8,6},{9,7},{10,... | collective-permute-start | bytes 294920 | tf_op jit(solution)/shard_map/ppermute | solution.py:27
  22.5 67.4 %all-to-all-start = ((bf16[8,320,512]{2,1,0:T(8,128)(2,1)}), bf16[8,320,512]{2,1,0:T(8,128)(2,1)S(1)}, u32[]{:S(2)}, u32[]{:S(2)}) async-start(bf16[8,320,512]{2,1,0:T(8,128)(2,1)} %get-tuple-element.51), calls=%async_computation | async-start | bytes 5242880 | tf_op jit(solution)/shard_map/all_to_all | solution.py:241
  30.0 18.7 %collective-permute-start.7 = (bf16[8,96,512]{2,1,0:T(8,128)(2,1)}, bf16[8,96,512]{2,1,0:T(8,128)(2,1)S(1)}, u32[]{:S(2)}, u32[]{:S(2)}) collective-permute-start(bf16[8,96,512]{2,1,0:T(8,128)(2,1)} %regroup.1.rest_0_), channel_id=1, source_target_pairs={{0,128},{1,129},{2,130},{3,131},{4,132},{5,133},{6,134},{7,135},{8... | collective-permute-start | bytes 2359304 | tf_op jit(solution)/shard_map/ppermute | solution.py:27
  30.6 19.7 %collective-permute-start.8 = (bf16[8,96,512]{2,1,0:T(8,128)(2,1)}, bf16[8,96,512]{2,1,0:T(8,128)(2,1)S(1)}, u32[]{:S(2)}, u32[]{:S(2)}) collective-permute-start(bf16[8,96,512]{2,1,0:T(8,128)(2,1)} %regroup.1.rest_0_), channel_id=1, source_target_pairs={{0,32},{1,33},{2,34},{3,35},{4,36},{5,37},{6,38},{7,39},{8,40},{9,... | collective-permute-start | bytes 2359304 | tf_op jit(solution)/shard_map/ppermute | solution.py:27
  32.1 18.2 %collective-permute-start.9 = (bf16[8,96,512]{2,1,0:T(8,128)(2,1)}, bf16[8,96,512]{2,1,0:T(8,128)(2,1)S(1)}, u32[]{:S(2)}, u32[]{:S(2)}) collective-permute-start(bf16[8,96,512]{2,1,0:T(8,128)(2,1)} %regroup.1.rest_0_), channel_id=1, source_target_pairs={{0,96},{1,97},{2,98},{3,99},{4,100},{5,101},{6,102},{7,103},{8,104... | collective-permute-start | bytes 2359304 | tf_op jit(solution)/shard_map/ppermute | solution.py:27
  50.3 17.8 %collective-permute-start.11 = (bf16[8,96,512]{2,1,0:T(8,128)(2,1)S(1)}, bf16[8,96,512]{2,1,0:T(8,128)(2,1)S(1)}, u32[]{:S(2)}, u32[]{:S(2)}) collective-permute-start(bf16[8,96,512]{2,1,0:T(8,128)(2,1)S(1)} %collective-permute-done.7.rest_1_), channel_id=1, source_target_pairs={{0,96},{1,97},{2,98},{3,99},{4,100},{5,101},{6,102},{7,103},{8,104... | collective-permute-start | bytes 2359304 | tf_op jit(solution)/shard_map/ppermute | solution.py:27
  53.2 34.9 %collective-permute-start.14 = (bf16[8,96,512]{2,1,0:T(8,128)(2,1)S(1)}, bf16[8,96,512]{2,1,0:T(8,128)(2,1)S(1)}, u32[]{:S(2)}, u32[]{:S(2)}) collective-permute-start(bf16[8,96,512]{2,1,0:T(8,128)(2,1)S(1)} %collective-permute-done.7.rest_1_), channel_id=1, source_target_pairs={{0,32},{1,33},{2,34},{3,35},{4,36},{5,37},{6,38},{7,39},{8,40},{9,... | collective-permute-start | bytes 2359304 | tf_op jit(solution)/shard_map/ppermute | solution.py:27
  53.2 34.9 %collective-permute-start.12 = (bf16[8,96,512]{2,1,0:T(8,128)(2,1)S(1)}, bf16[8,96,512]{2,1,0:T(8,128)(2,1)S(1)}, u32[]{:S(2)}, u32[]{:S(2)}) collective-permute-start(bf16[8,96,512]{2,1,0:T(8,128)(2,1)S(1)} %collective-permute-done.8.rest_6_), channel_id=1, source_target_pairs={{0,32},{1,33},{2,34},{3,35},{4,36},{5,37},{6,38},{7,39},{8,40},{9,... | collective-permute-start | bytes 2359304 | tf_op jit(solution)/shard_map/ppermute | solution.py:27
  68.1 21.8 %collective-permute-start.13 = (bf16[8,96,512]{2,1,0:T(8,128)(2,1)S(1)}, bf16[8,96,512]{2,1,0:T(8,128)(2,1)}, u32[]{:S(2)}, u32[]{:S(2)}) collective-permute-start(bf16[8,96,512]{2,1,0:T(8,128)(2,1)S(1)} %collective-permute-done.11.rest_3_), channel_id=1, source_target_pairs={{0,96},{1,97},{2,98},{3,99},{4,100},{5,101},{6,102},{7,103},{8,104... | collective-permute-start | bytes 2359304 | tf_op jit(solution)/shard_map/ppermute | solution.py:27
  89.9 8.7 %collective-permute-start.15 = (bf16[8,320,512]{2,1,0:T(8,128)(2,1)S(1)}, bf16[8,320,512]{2,1,0:T(8,128)(2,1)}, u32[]{:S(2)}, u32[]{:S(2)}) collective-permute-start(bf16[8,320,512]{2,1,0:T(8,128)(2,1)S(1)} %all-to-all-done.own_ref), channel_id=1, source_target_pairs={{0,16},{1,17},{2,18},{3,19},{4,20},{5,21},{6,22},{7,23},{8,24},{9,... | collective-permute-start | bytes 7864328 | tf_op jit(solution)/shard_map/ppermute | solution.py:27
  90.0 21.4 %collective-permute-start.10 = (bf16[1792,512]{1,0:T(8,128)(2,1)}, bf16[1792,512]{1,0:T(8,128)(2,1)}, u32[]{:S(2)}, u32[]{:S(2)}) collective-permute-start(bf16[1792,512]{1,0:T(8,128)(2,1)} %param.7), channel_id=1, source_target_pairs={{1,16},{3,18},{5,20},{7,22},{9,24},{11,26},{13,28},{15,30},{16,1},... | collective-permute-start | bytes 5505032 | tf_op jit(solution)/shard_map/ppermute | solution.py:27
  91.9 36.8 %all-to-all-start.1 = ((bf16[8,128,512]{2,1,0:T(8,128)(2,1)}), bf16[8,128,512]{2,1,0:T(8,128)(2,1)}, u32[]{:S(2)}, u32[]{:S(2)}) async-start(bf16[8,128,512]{2,1,0:T(8,128)(2,1)} %get-tuple-element.54), calls=%async_computation.1 | async-start | bytes 2097152 | tf_op jit(solution)/shard_map/all_to_all | solution.py:251
  107.7 30.3 %collective-permute-start.16 = (f32[320,768]{1,0:T(8,128)}, f32[320,768]{1,0:T(8,128)S(1)}, u32[]{:S(2)}, u32[]{:S(2)}) collective-permute-start(f32[320,768]{1,0:T(8,128)} %get-tuple-element.64), channel_id=1, source_target_pairs={{0,1},{1,0},{2,3},{3,2},{4,5},{5,4},{6,7},{7,6},{8,9},{9,8},{10,11... | collective-permute-start | bytes 2949128 | tf_op jit(solution)/shard_map/ppermute | solution.py:27
  147.9 47.7 %collective-permute-start.18 = (bf16[1792,512]{1,0:T(8,128)(2,1)S(1)}, bf16[1792,512]{1,0:T(8,128)(2,1)S(1)}, u32[]{:S(2)}, u32[]{:S(2)}) collective-permute-start(bf16[1792,512]{1,0:T(8,128)(2,1)S(1)} %broadcast_select_fusion.mine_ref), channel_id=1, source_target_pairs={{0,16},{1,17},{2,18},{3,19},{4,20},{5,21},{6,22},{7,23},{8,24},{9,... | collective-permute-start | bytes 5505032 | tf_op jit(solution)/shard_map/ppermute | solution.py:27
  150.0 9.2 %collective-permute-start.19 = (bf16[160,768]{1,0:T(8,128)(2,1)S(1)}, bf16[160,768]{1,0:T(8,128)(2,1)S(1)}, u32[]{:S(2)}, u32[]{:S(2)}) collective-permute-start(bf16[160,768]{1,0:T(8,128)(2,1)S(1)} %activate.2.rest_0_), channel_id=1, source_target_pairs={{0,2},{1,3},{2,4},{3,5},{4,6},{5,7},{6,8},{7,9},{8,10},{9,11},{10,... | collective-permute-start | bytes 737288 | tf_op jit(solution)/shard_map/ppermute | solution.py:27
  151.5 8.0 %collective-permute-start.23 = (bf16[160,768]{1,0:T(8,128)(2,1)S(1)}, bf16[160,768]{1,0:T(8,128)(2,1)S(1)}, u32[]{:S(2)}, u32[]{:S(2)}) collective-permute-start(bf16[160,768]{1,0:T(8,128)(2,1)S(1)} %activate.2.rest_0_), channel_id=1, source_target_pairs={{0,14},{1,15},{2,0},{3,1},{4,2},{5,3},{6,4},{7,5},{8,6},{9,7},{10,... | collective-permute-start | bytes 737288 | tf_op jit(solution)/shard_map/ppermute | solution.py:27
  153.3 17.5 %collective-permute-start.27 = (f32[128,768]{1,0:T(8,128)}, f32[128,768]{1,0:T(8,128)S(1)}, u32[]{:S(2)}, u32[]{:S(2)}) collective-permute-start(f32[128,768]{1,0:T(8,128)} %get-tuple-element.70), channel_id=1, source_target_pairs={{0,1},{1,0},{2,3},{3,2},{4,5},{5,4},{6,7},{7,6},{8,9},{9,8},{10,11... | collective-permute-start | bytes 1179656 | tf_op jit(solution)/shard_map/ppermute | solution.py:27
  159.2 8.3 %collective-permute-start.20 = (bf16[160,768]{1,0:T(8,128)(2,1)S(1)}, bf16[160,768]{1,0:T(8,128)(2,1)S(1)}, u32[]{:S(2)}, u32[]{:S(2)}) collective-permute-start(bf16[160,768]{1,0:T(8,128)(2,1)S(1)} %collective-permute-done.19.rest_1_), channel_id=1, source_target_pairs={{0,2},{1,3},{2,4},{3,5},{4,6},{5,7},{6,8},{7,9},{8,10},{9,11},{10,... | collective-permute-start | bytes 737288 | tf_op jit(solution)/shard_map/ppermute | solution.py:27
  159.4 8.1 %collective-permute-start.24 = (bf16[160,768]{1,0:T(8,128)(2,1)S(1)}, bf16[160,768]{1,0:T(8,128)(2,1)S(1)}, u32[]{:S(2)}, u32[]{:S(2)}) collective-permute-start(bf16[160,768]{1,0:T(8,128)(2,1)S(1)} %collective-permute-done.23.rest_8_), channel_id=1, source_target_pairs={{0,14},{1,15},{2,0},{3,1},{4,2},{5,3},{6,4},{7,5},{8,6},{9,7},{10,... | collective-permute-start | bytes 737288 | tf_op jit(solution)/shard_map/ppermute | solution.py:27
  167.5 19.3 %collective-permute-start.21 = (bf16[160,768]{1,0:T(8,128)(2,1)S(1)}, bf16[160,768]{1,0:T(8,128)(2,1)S(1)}, u32[]{:S(2)}, u32[]{:S(2)}) collective-permute-start(bf16[160,768]{1,0:T(8,128)(2,1)S(1)} %collective-permute-done.20.rest_2_), channel_id=1, source_target_pairs={{0,2},{1,3},{2,4},{3,5},{4,6},{5,7},{6,8},{7,9},{8,10},{9,11},{10,... | collective-permute-start | bytes 737288 | tf_op jit(solution)/shard_map/ppermute | solution.py:27
  167.5 19.4 %collective-permute-start.25 = (bf16[160,768]{1,0:T(8,128)(2,1)S(1)}, bf16[160,768]{1,0:T(8,128)(2,1)S(1)}, u32[]{:S(2)}, u32[]{:S(2)}) collective-permute-start(bf16[160,768]{1,0:T(8,128)(2,1)S(1)} %collective-permute-done.24.rest_7_), channel_id=1, source_target_pairs={{0,14},{1,15},{2,0},{3,1},{4,2},{5,3},{6,4},{7,5},{8,6},{9,7},{10,... | collective-permute-start | bytes 737288 | tf_op jit(solution)/shard_map/ppermute | solution.py:27
  171.8 5.9 %collective-permute-start.28 = (bf16[64,768]{1,0:T(8,128)(2,1)S(1)}, bf16[64,768]{1,0:T(8,128)(2,1)S(1)}, u32[]{:S(2)}, u32[]{:S(2)}) collective-permute-start(bf16[64,768]{1,0:T(8,128)(2,1)S(1)} %activate.3.rest_9_), channel_id=1, source_target_pairs={{0,2},{1,3},{2,4},{3,5},{4,6},{5,7},{6,8},{7,9},{8,10},{9,11},{10,... | collective-permute-start | bytes 294920 | tf_op jit(solution)/shard_map/ppermute | solution.py:27
  183.6 6.7 %collective-permute-start.30 = (bf16[64,768]{1,0:T(8,128)(2,1)S(1)}, bf16[64,768]{1,0:T(8,128)(2,1)S(1)}, u32[]{:S(2)}, u32[]{:S(2)}) collective-permute-start(bf16[64,768]{1,0:T(8,128)(2,1)S(1)} %collective-permute-done.29.rest_11_), channel_id=1, source_target_pairs={{0,2},{1,3},{2,4},{3,5},{4,6},{5,7},{6,8},{7,9},{8,10},{9,11},{10,... | collective-permute-start | bytes 294920 | tf_op jit(solution)/shard_map/ppermute | solution.py:27
  183.6 6.8 %collective-permute-start.34 = (bf16[64,768]{1,0:T(8,128)(2,1)S(1)}, bf16[64,768]{1,0:T(8,128)(2,1)S(1)}, u32[]{:S(2)}, u32[]{:S(2)}) collective-permute-start(bf16[64,768]{1,0:T(8,128)(2,1)S(1)} %collective-permute-done.33.rest_16_), channel_id=1, source_target_pairs={{0,14},{1,15},{2,0},{3,1},{4,2},{5,3},{6,4},{7,5},{8,6},{9,7},{10,... | collective-permute-start | bytes 294920 | tf_op jit(solution)/shard_map/ppermute | solution.py:27
  186.8 6.8 %collective-permute-start.22 = (bf16[80,768]{1,0:T(8,128)(2,1)S(1)}, bf16[80,768]{1,0:T(8,128)(2,1)S(1)}, u32[]{:S(2)}, u32[]{:S(2)}) collective-permute-start(bf16[80,768]{1,0:T(8,128)(2,1)S(1)} %slice.16), channel_id=1, source_target_pairs={{0,2},{1,3},{2,4},{3,5},{4,6},{5,7},{6,8},{7,9},{8,10},{9,11},{10,... | collective-permute-start | bytes 368648 | tf_op jit(solution)/shard_map/ppermute | solution.py:27
  186.9 6.7 %collective-permute-start.26 = (bf16[80,768]{1,0:T(8,128)(2,1)S(1)}, bf16[80,768]{1,0:T(8,128)(2,1)S(1)}, u32[]{:S(2)}, u32[]{:S(2)}) collective-permute-start(bf16[80,768]{1,0:T(8,128)(2,1)S(1)} %slice.17), channel_id=1, source_target_pairs={{0,14},{1,15},{2,0},{3,1},{4,2},{5,3},{6,4},{7,5},{8,6},{9,7},{10,... | collective-permute-start | bytes 368648 | tf_op jit(solution)/shard_map/ppermute | solution.py:27
  (25 other events, 263.9 us)

commit v6 on v5

--- a/solution.py
+++ b/solution.py
@@ -10,7 +10,7 @@
 
 AXES = ("xl", "y", "c", "z", "xh")
 SIZES = (2, 4, 2, 8, 2)
-FIRST = 160
+FIRST = 128
 TOGETHER = 2
 F32, BF16 = jnp.float32, jnp.bfloat16
 SCALARS = pl.BlockSpec(memory_space=pltpu.SMEM)
@@ -227,6 +227,20 @@
     )(place, mine, theirs, *parts)
 
 
+def round_z(hidden, other):
+    nz = SIZES[3]
+    ring, up, down = {0: hidden}, hidden, hidden
+    for at in range(nz // 2):
+        if at == nz // 2 - 1:
+            half = up.shape[0] // 2
+            up, down = up[:half], down[half:]
+        up, down = along_z(up, 1), along_z(down, -1)
+        if at == 1:
+            up, down, other = together(up, down, other)
+        ring.update({at + 1: up, -at - 1: down})
+    return ring, other
+
+
 def shards(tokens, gate_weight, up_weight, down_weight):
     xl, y, c, z, xh = (lax.axis_index(a) for a in AXES)
     place = jnp.stack([xl, y, c, z, xh]).astype(jnp.int32)
@@ -247,7 +261,7 @@
     far_before, far_after = along_y(far, 1), along_y(far, -1)
     near_across, far_across = along_y(near_before, 1), along_y(far_after, -1)
     pieces = (near, far, near_after, far_after, near_across, far_across, near_before, far_before)
-    ready, weights[0], pieces = together(sliced[1], weights[0], pieces)
+    ready, weights[0], *_ = together(sliced[1], weights[0], far_before, far_after, near_across)
     weights.append(lax.all_to_all(ready, "z", 0, 0, tiled=True))
 
     keep, *gives = project(place, weights[0], swap_core(weights[0]), pieces, ())
@@ -264,22 +278,12 @@
 
     both = together(weights[1], swap_core(weights[1]), hiddens[0])
     keep, give = project(place, *both[:2], pieces, ())
-    hiddens.append(activate(keep, [swap_xh(give)]))
-    mine, _ = together(mine, give)
+    got = swap_xh(give)
+    first, (got, mine) = round_z(hiddens[0], (got, mine))
     theirs = swap_core(mine)
-
-    rings = []
-    for hidden in hiddens:
-        ring, up, down = {0: hidden}, hidden, hidden
-        for at in range(nz // 2):
-            if at == nz // 2 - 1:
-                half = up.shape[0] // 2
-                up, down = up[:half], down[half:]
-            up, down = along_z(up, 1), along_z(down, -1)
-            ring.update({at + 1: up, -at - 1: down})
-        rings.append(ring)
-
-    out = mix(place, rings, mine, theirs).reshape(16, tokens.shape[0], -1)
+    second, _ = round_z(activate(keep, [got]), (first[3], first[-3]))
+
+    out = mix(place, (first, second), mine, theirs).reshape(16, tokens.shape[0], -1)
     got = lax.all_to_all(out, ("xh", "y", "xl"), 0, 0, tiled=True)
     return jnp.sum(got.astype(F32), 0)
 

time: 224 us -> 240 us (1.071)
  waiting for transfers between devices: 90.9 us -> 109 us
  blocking collectives: 22.8 us -> 26.4 us
  local copies, waits for them, and re-layouts: 7.72 us -> 4.26 us
  starting transfers between devices: 75.1 us -> 72.3 us
    ppermute x36, waiting for transfers between devices: 73.6 us -> 101 us  [send(): return lax.ppermute(value, AXES, pairs)]
    all_to_all x1, waiting for transfers between devices: 17.3 us -> 8.23 us  [shards(): weights.append(lax.all_to_all(ready, 'z', 0, 0, tiled=True))]
    all_to_all x1, blocking collectives: 22.8 us -> 26.4 us  [shards(): got = lax.all_to_all(out, ('xh', 'y', 'xl'), 0, 0, tiled=True)]
    unnamed x38 -> x34, local copies, waits for them, and re-layouts: 7.01 us -> 3.62 us
    ppermute x36, starting transfers between devices: 63.8 us -> 61 us  [send(): return lax.ppermute(value, AXES, pairs)]
  transfers between devices with their start and end apart: 38 -> 38, of which waited for: 11 -> 16; matrix products, arithmetic and copies ran while one was open for 0% -> 0% of each run, Pallas kernels for 7% -> 9%
where the time goes in v6:
time: 240 us; the launch traced here: 238 us
  waiting for transfers between devices  109 us (45%)
  starting transfers between devices  72.3 us (30%)
  blocking collectives  26.4 us (11%)
  Pallas kernels  25.1 us (10%)
  local copies, waits for them, and re-layouts  4.26 us (2%)
    ppermute x36, waiting for transfers between devices, send(): return lax.ppermute(value, AXES, pairs)  101 us
    ppermute x36, starting transfers between devices, send(): return lax.ppermute(value, AXES, pairs)  61 us
    all_to_all x1, blocking collectives, shards(): got = lax.all_to_all(out, ('xh', 'y', 'xl'), 0, 0, tiled=True)  26.4 us
    pallas_call x2, Pallas kernels, project(): pl.pallas_call(body, in_specs=[SCALARS] + [pl.BlockSpec(memory_space=pl.A...  15.1 us
    all_to_all x1, waiting for transfers between devices, shards(): weights.append(lax.all_to_all(ready, 'z', 0, 0, tiled=True))  8.23 us
    all_to_all x1, starting transfers between devices, shards(): weights.append(lax.all_to_all(ready, 'z', 0, 0, tiled=True))  6.65 us
  transfers between devices with their start and end apart: 38, of which 16 were waited for; matrix products, arithmetic and copies ran while one was open for 0% of the time, Pallas kernels for 9%

profile of v6, /device:TPU:2, one launch (start us, length us, event | category | flops | bytes accessed | tf_op | source)
XLA Modules:
  0.0 238.3 jit_solution(15501234630862809762)
XLA Ops:
  0.0 3.3 %collective-permute-start.1 = (bf16[96,512]{1,0:T(8,128)(2,1)}, bf16[96,512]{1,0:T(8,128)(2,1)S(1)}, u32[]{:S(2)}, u32[]{:S(2)}) collective-permute-start(bf16[96,512]{1,0:T(8,128)(2,1)} %rest_0_), channel_id=1, source_target_pairs={{0,4},{1,5},{2,6},{3,7},{4,8},{5,9},{6,10},{7,11},{8,12},{9,13},{1... | collective-permute-start | bytes 294920 | tf_op jit(solution)/shard_map/ppermute | solution.py:27
  3.3 3.0 %collective-permute-start.4 = (bf16[96,512]{1,0:T(8,128)(2,1)}, bf16[96,512]{1,0:T(8,128)(2,1)S(1)}, u32[]{:S(2)}, u32[]{:S(2)}) collective-permute-start(bf16[96,512]{1,0:T(8,128)(2,1)} %rest_0_), channel_id=1, source_target_pairs={{0,12},{1,13},{2,14},{3,15},{4,0},{5,1},{6,2},{7,3},{8,4},{9,5},{1... | collective-permute-start | bytes 294920 | tf_op jit(solution)/shard_map/ppermute | solution.py:27
  7.3 5.0 %collective-permute-start.3 = (bf16[96,512]{1,0:T(8,128)(2,1)}, bf16[96,512]{1,0:T(8,128)(2,1)S(1)}, u32[]{:S(2)}, u32[]{:S(2)}) collective-permute-start(bf16[96,512]{1,0:T(8,128)(2,1)} %rest_0_), channel_id=1, source_target_pairs={{0,8},{1,9},{2,10},{3,11},{4,12},{5,13},{6,14},{7,15},{8,0},{9,1},... | collective-permute-start | bytes 294920 | tf_op jit(solution)/shard_map/ppermute | solution.py:27
  12.3 2.2 collective-permute-start.6
  14.6 3.2 %collective-permute-start.5 = (bf16[96,512]{1,0:T(8,128)(2,1)S(1)}, bf16[96,512]{1,0:T(8,128)(2,1)S(1)}, u32[]{:S(2)}, u32[]{:S(2)}) collective-permute-start(bf16[96,512]{1,0:T(8,128)(2,1)S(1)} %collective-permute-done.4.rest_6_), channel_id=1, source_target_pairs={{0,14},{1,15},{2,0},{3,1},{4,2},{5,3},{6,4},{7,5},{8,6},{9,7},{10,... | collective-permute-start | bytes 294920 | tf_op jit(solution)/shard_map/ppermute | solution.py:27
  17.8 3.8 %slice_units.1 = (bf16[8,256,512]{2,1,0:T(8,128)(2,1)}, bf16[8,192,512]{2,1,0:T(8,128)(2,1)}) custom-call(bf16[512,1792]{1,0:T(8,128)(2,1)} %g_ref.1, bf16[512,1792]{1,0:T(8,128)(2,1)} %u_ref.1), custom_call_target="tpu_custom_call" | custom-call | bytes 114688 | tf_op jit(solution)/shard_map/slice_units/pallas_call | solution.py:94
  22.4 4.7 %all-to-all-start = ((bf16[8,256,512]{2,1,0:T(8,128)(2,1)}), bf16[8,256,512]{2,1,0:T(8,128)(2,1)S(1)}, u32[]{:S(2)}, u32[]{:S(2)}) async-start(bf16[8,256,512]{2,1,0:T(8,128)(2,1)} %get-tuple-element.38), calls=%async_computation | async-start | bytes 4194304 | tf_op jit(solution)/shard_map/all_to_all | solution.py:255
  27.7 2.2 regroup.1.rest_0_
  33.7 15.0 %collective-permute-done.7.rest_1_ = bf16[8,96,512]{2,1,0:T(8,128)(2,1)S(1)} collective-permute-done((bf16[8,96,512]{2,1,0:T(8,128)(2,1)}, bf16[8,96,512]{2,1,0:T(8,128)(2,1)S(1)}, u32[]{:S(2)}, u32[]{:S(2)}) %collective-permute-start.7) | collective-permute-done | bytes 786464 | tf_op jit(solution)/shard_map/ppermute | solution.py:27
  53.8 18.2 %collective-permute-done.10.rest_7_ = bf16[8,96,512]{2,1,0:T(8,128)(2,1)S(1)} collective-permute-done((bf16[8,96,512]{2,1,0:T(8,128)(2,1)S(1)}, bf16[8,96,512]{2,1,0:T(8,128)(2,1)S(1)}, u32[]{:S(2)}, u32[]{:S(2)}) %collective-permute-start.10) | collective-permute-done | bytes 786464 | tf_op jit(solution)/shard_map/ppermute | solution.py:27
  73.8 12.1 %collective-permute-done.12.rest_4_ = bf16[8,96,512]{2,1,0:T(8,128)(2,1)} collective-permute-done((bf16[8,96,512]{2,1,0:T(8,128)(2,1)S(1)}, bf16[8,96,512]{2,1,0:T(8,128)(2,1)}, u32[]{:S(2)}, u32[]{:S(2)}) %collective-permute-start.12) | collective-permute-done | bytes 786464 | tf_op jit(solution)/shard_map/ppermute | solution.py:27
  85.9 6.7 %all-to-all-start.1 = ((bf16[8,192,512]{2,1,0:T(8,128)(2,1)}), bf16[8,192,512]{2,1,0:T(8,128)(2,1)}, u32[]{:S(2)}, u32[]{:S(2)}) async-start(bf16[8,192,512]{2,1,0:T(8,128)(2,1)} %get-tuple-element.54), calls=%async_computation.1 | async-start | bytes 3145728 | tf_op jit(solution)/shard_map/all_to_all | solution.py:265
  95.8 17.6 %collective-permute-done.14.rest_5_ = bf16[8,96,512]{2,1,0:T(8,128)(2,1)} collective-permute-done((bf16[8,96,512]{2,1,0:T(8,128)(2,1)}, bf16[8,96,512]{2,1,0:T(8,128)(2,1)}, u32[]{:S(2)}, u32[]{:S(2)}) %collective-permute-start.14) | collective-permute-done | bytes 786464 | tf_op jit(solution)/shard_map/ppermute | solution.py:27
  113.4 8.0 %project.2 = (f32[256,768]{1,0:T(8,128)}, f32[256,768]{1,0:T(8,128)}) custom-call(s32[5]{0:T(128)} %stack.23.place_ref, bf16[8,256,512]{2,1,0:T(8,128)(2,1)} %copy-done.3, bf16[8,256,512]{2,1,0:T(8,128)(2,1)} %collective-permute-done.13.other_ref, bf16[8,96,512]{2,1,0:T(8,128)(2,1)} %regroup.1.rest_0_, bf16[8,96,512]{2,1,0:T(8,128)(2,1)} %copy-done.4, ...), custom_call_target="tpu_custom_call" | custom-call | flops 50331648 | bytes 163840 | tf_op jit(solution)/shard_map/project/pallas_call | solution.py:154
  121.5 3.6 %collective-permute-start.15 = (f32[256,768]{1,0:T(8,128)}, f32[256,768]{1,0:T(8,128)S(1)}, u32[]{:S(2)}, u32[]{:S(2)}) collective-permute-start(f32[256,768]{1,0:T(8,128)} %get-tuple-element.52), channel_id=1, source_target_pairs={{0,1},{1,0},{2,3},{3,2},{4,5},{5,4},{6,7},{7,6},{8,9},{9,8},{10,11... | collective-permute-start | bytes 2359304 | tf_op jit(solution)/shard_map/ppermute | solution.py:27
  125.1 8.2 %all-to-all-done.1.own_ref = bf16[8,192,512]{2,1,0:T(8,128)(2,1)} async-done(((bf16[8,192,512]{2,1,0:T(8,128)(2,1)}), bf16[8,192,512]{2,1,0:T(8,128)(2,1)}, u32[]{:S(2)}, u32[]{:S(2)}) %all-to-all-start.1) | async-done | bytes 1572896 | tf_op jit(solution)/shard_map/all_to_all | solution.py:265
  133.3 9.4 %collective-permute-done.15.rest_0_ = f32[256,768]{1,0:T(8,128)S(1)} collective-permute-done((f32[256,768]{1,0:T(8,128)}, f32[256,768]{1,0:T(8,128)S(1)}, u32[]{:S(2)}, u32[]{:S(2)}) %collective-permute-start.15) | collective-permute-done | bytes 786464 | tf_op jit(solution)/shard_map/ppermute | solution.py:27
  144.8 2.1 collective-permute-start.16
  148.2 5.0 %collective-permute-done.16.rest_1_ = bf16[128,768]{1,0:T(8,128)(2,1)S(1)} collective-permute-done((bf16[128,768]{1,0:T(8,128)(2,1)S(1)}, bf16[128,768]{1,0:T(8,128)(2,1)S(1)}, u32[]{:S(2)}, u32[]{:S(2)}) %collective-permute-start.16) | collective-permute-done | bytes 196640 | tf_op jit(solution)/shard_map/ppermute | solution.py:27
  153.7 2.7 %collective-permute-start.19 = (bf16[128,768]{1,0:T(8,128)(2,1)S(1)}, bf16[128,768]{1,0:T(8,128)(2,1)S(1)}, u32[]{:S(2)}, u32[]{:S(2)}) collective-permute-start(bf16[128,768]{1,0:T(8,128)(2,1)S(1)} %collective-permute-done.18.rest_8_), channel_id=1, source_target_pairs={{0,14},{1,15},{2,0},{3,1},{4,2},{5,3},{6,4},{7,5},{8,6},{9,7},{10,... | collective-permute-start | bytes 589832 | tf_op jit(solution)/shard_map/ppermute | solution.py:27
  156.4 7.0 %project.3 = (f32[192,768]{1,0:T(8,128)}, f32[192,768]{1,0:T(8,128)}) custom-call(s32[5]{0:T(128)} %stack.23.place_ref, bf16[8,192,512]{2,1,0:T(8,128)(2,1)} %all-to-all-done.1.own_ref, bf16[8,192,512]{2,1,0:T(8,128)(2,1)} %collective-permute-done.21.other_ref, bf16[8,96,512]{2,1,0:T(8,128)(2,1)} %regroup.1.rest_0_, bf16[8,96,512]{2,1,0:T(8,128)(2,1)} %copy-done.4, ...), custom_call_target="tpu_custom_call" | custom-call | flops 37748736 | bytes 147456 | tf_op jit(solution)/shard_map/project/pallas_call | solution.py:154
  165.7 13.7 %collective-permute-done.22.rest_0_ = f32[192,768]{1,0:T(8,128)S(1)} collective-permute-done((f32[192,768]{1,0:T(8,128)}, f32[192,768]{1,0:T(8,128)S(1)}, u32[]{:S(2)}, u32[]{:S(2)}) %collective-permute-start.22) | collective-permute-done | bytes 589856 | tf_op jit(solution)/shard_map/ppermute | solution.py:27
  179.6 3.2 %collective-permute-start.30 = (bf16[96,768]{1,0:T(8,128)(2,1)S(1)}, bf16[96,768]{1,0:T(8,128)(2,1)S(1)}, u32[]{:S(2)}, u32[]{:S(2)}) collective-permute-start(bf16[96,768]{1,0:T(8,128)(2,1)S(1)} %activate.3.rest_9_), channel_id=1, source_target_pairs={{0,14},{1,15},{2,0},{3,1},{4,2},{5,3},{6,4},{7,5},{8,6},{9,7},{10,... | collective-permute-start | bytes 442376 | tf_op jit(solution)/shard_map/ppermute | solution.py:27
  182.8 3.2 %collective-permute-start.26 = (bf16[128,768]{1,0:T(8,128)(2,1)S(1)}, bf16[128,768]{1,0:T(8,128)(2,1)S(1)}, u32[]{:S(2)}, u32[]{:S(2)}) collective-permute-start(bf16[128,768]{1,0:T(8,128)(2,1)S(1)} %collective-permute-done.19.rest_7_), channel_id=1, source_target_pairs={{0,14},{1,15},{2,0},{3,1},{4,2},{5,3},{6,4},{7,5},{8,6},{9,7},{10,... | collective-permute-start | bytes 589832 | tf_op jit(solution)/shard_map/ppermute | solution.py:27
  187.5 3.2 %collective-permute-start.31 = (bf16[96,768]{1,0:T(8,128)(2,1)S(1)}, bf16[96,768]{1,0:T(8,128)(2,1)S(1)}, u32[]{:S(2)}, u32[]{:S(2)}) collective-permute-start(bf16[96,768]{1,0:T(8,128)(2,1)S(1)} %collective-permute-done.30.rest_17_), channel_id=1, source_target_pairs={{0,14},{1,15},{2,0},{3,1},{4,2},{5,3},{6,4},{7,5},{8,6},{9,7},{10,... | collective-permute-start | bytes 442376 | tf_op jit(solution)/shard_map/ppermute | solution.py:27
  191.9 2.6 %collective-permute-done.29.rest_11_ = bf16[96,768]{1,0:T(8,128)(2,1)S(1)} collective-permute-done((bf16[96,768]{1,0:T(8,128)(2,1)S(1)}, bf16[96,768]{1,0:T(8,128)(2,1)S(1)}, u32[]{:S(2)}, u32[]{:S(2)}) %collective-permute-start.29) | collective-permute-done | bytes 147488 | tf_op jit(solution)/shard_map/ppermute | solution.py:27
  195.3 2.4 %collective-permute-start.34 = (bf16[96,768]{1,0:T(8,128)(2,1)S(1)}, bf16[96,768]{1,0:T(8,128)(2,1)S(1)}, u32[]{:S(2)}, u32[]{:S(2)}) collective-permute-start(bf16[96,768]{1,0:T(8,128)(2,1)S(1)} %collective-permute-done.31.rest_16_), channel_id=1, source_target_pairs={{0,14},{1,15},{2,0},{3,1},{4,2},{5,3},{6,4},{7,5},{8,6},{9,7},{10,... | collective-permute-start | bytes 442376 | tf_op jit(solution)/shard_map/ppermute | solution.py:27
  198.3 2.7 %collective-permute-start.27 = (bf16[64,768]{1,0:T(8,128)(2,1)S(1)}, bf16[64,768]{1,0:T(8,128)(2,1)S(1)}, u32[]{:S(2)}, u32[]{:S(2)}) collective-permute-start(bf16[64,768]{1,0:T(8,128)(2,1)S(1)} %slice.17), channel_id=1, source_target_pairs={{0,14},{1,15},{2,0},{3,1},{4,2},{5,3},{6,4},{7,5},{8,6},{9,7},{10,... | collective-permute-start | bytes 294920 | tf_op jit(solution)/shard_map/ppermute | solution.py:27
  202.3 2.7 %collective-permute-start.35 = (bf16[48,768]{1,0:T(8,128)(2,1)S(1)}, bf16[48,768]{1,0:T(8,128)(2,1)S(1)}, u32[]{:S(2)}, u32[]{:S(2)}) collective-permute-start(bf16[48,768]{1,0:T(8,128)(2,1)S(1)} %slice.19), channel_id=1, source_target_pairs={{0,14},{1,15},{2,0},{3,1},{4,2},{5,3},{6,4},{7,5},{8,6},{9,7},{10,... | collective-permute-start | bytes 221192 | tf_op jit(solution)/shard_map/ppermute | solution.py:27
  205.0 2.1 collective-permute-done.33.rest_13_
  207.2 3.8 %mix.1 = bf16[2,768,512]{2,1,0:T(8,128)(2,1)S(1)} custom-call(s32[5]{0:T(128)S(1)} %copy-done.2, bf16[1792,512]{1,0:T(8,128)(2,1)S(1)} %broadcast_select_fusion.mine_ref, bf16[1792,512]{1,0:T(8,128)(2,1)S(1)} %collective-permute-done.23.theirs_ref, bf16[128,768]{1,0:T(8,128)(2,1)S(1)} %activate.2.rest_0_, ...), custom_call_target="tpu_custom_call" | custom-call | flops 44040192 | bytes 100352 | tf_op jit(solution)/shard_map/mix/pallas_call | solution.py:218
  211.0 26.4 %all_to_all.15 = bf16[16,96,512]{2,1,0:T(8,128)(2,1)S(1)} all-to-all(bf16[16,96,512]{2,1,0:T(8,128)(2,1)S(1)} %bitcast.6), channel_id=1, replica_groups=mesh['xl'=2,'y'=4,'c'=2,'z'=8,'xh'=2] {'xh','y','xl'}, dimensions={0} | all-to-all | bytes 3145728 | tf_op jit(solution)/shard_map/all_to_all | solution.py:287
  (93 shorter events, 29.0 us)
Async XLA Ops:
  0.0 14.6 %collective-permute-start.1 = (bf16[96,512]{1,0:T(8,128)(2,1)}, bf16[96,512]{1,0:T(8,128)(2,1)S(1)}, u32[]{:S(2)}, u32[]{:S(2)}) collective-permute-start(bf16[96,512]{1,0:T(8,128)(2,1)} %rest_0_), channel_id=1, source_target_pairs={{0,4},{1,5},{2,6},{3,7},{4,8},{5,9},{6,10},{7,11},{8,12},{9,13},{1... | collective-permute-start | bytes 294920 | tf_op jit(solution)/shard_map/ppermute | solution.py:27
  3.3 11.3 %collective-permute-start.4 = (bf16[96,512]{1,0:T(8,128)(2,1)}, bf16[96,512]{1,0:T(8,128)(2,1)S(1)}, u32[]{:S(2)}, u32[]{:S(2)}) collective-permute-start(bf16[96,512]{1,0:T(8,128)(2,1)} %rest_0_), channel_id=1, source_target_pairs={{0,12},{1,13},{2,14},{3,15},{4,0},{5,1},{6,2},{7,3},{8,4},{9,5},{1... | collective-permute-start | bytes 294920 | tf_op jit(solution)/shard_map/ppermute | solution.py:27
  6.3 15.4 %collective-permute-start = (bf16[96,512]{1,0:T(8,128)(2,1)}, bf16[96,512]{1,0:T(8,128)(2,1)S(1)}, u32[]{:S(2)}, u32[]{:S(2)}) collective-permute-start(bf16[96,512]{1,0:T(8,128)(2,1)} %rest_0_), channel_id=1, source_target_pairs={{0,2},{1,3},{2,4},{3,5},{4,6},{5,7},{6,8},{7,9},{8,10},{9,11},{10,... | collective-permute-start | bytes 294920 | tf_op jit(solution)/shard_map/ppermute | solution.py:27
  7.3 14.4 %collective-permute-start.3 = (bf16[96,512]{1,0:T(8,128)(2,1)}, bf16[96,512]{1,0:T(8,128)(2,1)S(1)}, u32[]{:S(2)}, u32[]{:S(2)}) collective-permute-start(bf16[96,512]{1,0:T(8,128)(2,1)} %rest_0_), channel_id=1, source_target_pairs={{0,8},{1,9},{2,10},{3,11},{4,12},{5,13},{6,14},{7,15},{8,0},{9,1},... | collective-permute-start | bytes 294920 | tf_op jit(solution)/shard_map/ppermute | solution.py:27
  12.3 9.4 %collective-permute-start.6 = (bf16[96,512]{1,0:T(8,128)(2,1)}, bf16[96,512]{1,0:T(8,128)(2,1)S(1)}, u32[]{:S(2)}, u32[]{:S(2)}) collective-permute-start(bf16[96,512]{1,0:T(8,128)(2,1)} %rest_0_), channel_id=1, source_target_pairs={{0,14},{1,15},{2,0},{3,1},{4,2},{5,3},{6,4},{7,5},{8,6},{9,7},{10,... | collective-permute-start | bytes 294920 | tf_op jit(solution)/shard_map/ppermute | solution.py:27
  14.6 7.2 %collective-permute-start.2 = (bf16[96,512]{1,0:T(8,128)(2,1)S(1)}, bf16[96,512]{1,0:T(8,128)(2,1)S(1)}, u32[]{:S(2)}, u32[]{:S(2)}) collective-permute-start(bf16[96,512]{1,0:T(8,128)(2,1)S(1)} %collective-permute-done.1.rest_2_), channel_id=1, source_target_pairs={{0,2},{1,3},{2,4},{3,5},{4,6},{5,7},{6,8},{7,9},{8,10},{9,11},{10,... | collective-permute-start | bytes 294920 | tf_op jit(solution)/shard_map/ppermute | solution.py:27
  14.6 7.2 %collective-permute-start.5 = (bf16[96,512]{1,0:T(8,128)(2,1)S(1)}, bf16[96,512]{1,0:T(8,128)(2,1)S(1)}, u32[]{:S(2)}, u32[]{:S(2)}) collective-permute-start(bf16[96,512]{1,0:T(8,128)(2,1)S(1)} %collective-permute-done.4.rest_6_), channel_id=1, source_target_pairs={{0,14},{1,15},{2,0},{3,1},{4,2},{5,3},{6,4},{7,5},{8,6},{9,7},{10,... | collective-permute-start | bytes 294920 | tf_op jit(solution)/shard_map/ppermute | solution.py:27
  22.4 63.5 %all-to-all-start = ((bf16[8,256,512]{2,1,0:T(8,128)(2,1)}), bf16[8,256,512]{2,1,0:T(8,128)(2,1)S(1)}, u32[]{:S(2)}, u32[]{:S(2)}) async-start(bf16[8,256,512]{2,1,0:T(8,128)(2,1)} %get-tuple-element.38), calls=%async_computation | async-start | bytes 4194304 | tf_op jit(solution)/shard_map/all_to_all | solution.py:255
  29.9 18.7 %collective-permute-start.7 = (bf16[8,96,512]{2,1,0:T(8,128)(2,1)}, bf16[8,96,512]{2,1,0:T(8,128)(2,1)S(1)}, u32[]{:S(2)}, u32[]{:S(2)}) collective-permute-start(bf16[8,96,512]{2,1,0:T(8,128)(2,1)} %regroup.1.rest_0_), channel_id=1, source_target_pairs={{0,128},{1,129},{2,130},{3,131},{4,132},{5,133},{6,134},{7,135},{8... | collective-permute-start | bytes 2359304 | tf_op jit(solution)/shard_map/ppermute | solution.py:27
  30.5 19.8 %collective-permute-start.8 = (bf16[8,96,512]{2,1,0:T(8,128)(2,1)}, bf16[8,96,512]{2,1,0:T(8,128)(2,1)S(1)}, u32[]{:S(2)}, u32[]{:S(2)}) collective-permute-start(bf16[8,96,512]{2,1,0:T(8,128)(2,1)} %regroup.1.rest_0_), channel_id=1, source_target_pairs={{0,32},{1,33},{2,34},{3,35},{4,36},{5,37},{6,38},{7,39},{8,40},{9,... | collective-permute-start | bytes 2359304 | tf_op jit(solution)/shard_map/ppermute | solution.py:27
  32.0 18.2 %collective-permute-start.9 = (bf16[8,96,512]{2,1,0:T(8,128)(2,1)}, bf16[8,96,512]{2,1,0:T(8,128)(2,1)S(1)}, u32[]{:S(2)}, u32[]{:S(2)}) collective-permute-start(bf16[8,96,512]{2,1,0:T(8,128)(2,1)} %regroup.1.rest_0_), channel_id=1, source_target_pairs={{0,96},{1,97},{2,98},{3,99},{4,100},{5,101},{6,102},{7,103},{8,104... | collective-permute-start | bytes 2359304 | tf_op jit(solution)/shard_map/ppermute | solution.py:27
  50.2 21.8 %collective-permute-start.10 = (bf16[8,96,512]{2,1,0:T(8,128)(2,1)S(1)}, bf16[8,96,512]{2,1,0:T(8,128)(2,1)S(1)}, u32[]{:S(2)}, u32[]{:S(2)}) collective-permute-start(bf16[8,96,512]{2,1,0:T(8,128)(2,1)S(1)} %collective-permute-done.7.rest_1_), channel_id=1, source_target_pairs={{0,32},{1,33},{2,34},{3,35},{4,36},{5,37},{6,38},{7,39},{8,40},{9,... | collective-permute-start | bytes 2359304 | tf_op jit(solution)/shard_map/ppermute | solution.py:27
  51.8 20.2 %collective-permute-start.11 = (bf16[8,96,512]{2,1,0:T(8,128)(2,1)S(1)}, bf16[8,96,512]{2,1,0:T(8,128)(2,1)S(1)}, u32[]{:S(2)}, u32[]{:S(2)}) collective-permute-start(bf16[8,96,512]{2,1,0:T(8,128)(2,1)S(1)} %collective-permute-done.7.rest_1_), channel_id=1, source_target_pairs={{0,96},{1,97},{2,98},{3,99},{4,100},{5,101},{6,102},{7,103},{8,104... | collective-permute-start | bytes 2359304 | tf_op jit(solution)/shard_map/ppermute | solution.py:27
  53.5 32.4 %collective-permute-start.12 = (bf16[8,96,512]{2,1,0:T(8,128)(2,1)S(1)}, bf16[8,96,512]{2,1,0:T(8,128)(2,1)}, u32[]{:S(2)}, u32[]{:S(2)}) collective-permute-start(bf16[8,96,512]{2,1,0:T(8,128)(2,1)S(1)} %collective-permute-done.8.rest_6_), channel_id=1, source_target_pairs={{0,32},{1,33},{2,34},{3,35},{4,36},{5,37},{6,38},{7,39},{8,40},{9,... | collective-permute-start | bytes 2359304 | tf_op jit(solution)/shard_map/ppermute | solution.py:27
  85.9 27.5 %collective-permute-start.13 = (bf16[8,256,512]{2,1,0:T(8,128)(2,1)S(1)}, bf16[8,256,512]{2,1,0:T(8,128)(2,1)}, u32[]{:S(2)}, u32[]{:S(2)}) collective-permute-start(bf16[8,256,512]{2,1,0:T(8,128)(2,1)S(1)} %all-to-all-done.own_ref), channel_id=1, source_target_pairs={{0,16},{1,17},{2,18},{3,19},{4,20},{5,21},{6,22},{7,23},{8,24},{9,... | collective-permute-start | bytes 6291464 | tf_op jit(solution)/shard_map/ppermute | solution.py:27
  85.9 47.4 %all-to-all-start.1 = ((bf16[8,192,512]{2,1,0:T(8,128)(2,1)}), bf16[8,192,512]{2,1,0:T(8,128)(2,1)}, u32[]{:S(2)}, u32[]{:S(2)}) async-start(bf16[8,192,512]{2,1,0:T(8,128)(2,1)} %get-tuple-element.54), calls=%async_computation.1 | async-start | bytes 3145728 | tf_op jit(solution)/shard_map/all_to_all | solution.py:265
  92.6 32.5 %collective-permute-start.20 = (bf16[1792,512]{1,0:T(8,128)(2,1)}, bf16[1792,512]{1,0:T(8,128)(2,1)}, u32[]{:S(2)}, u32[]{:S(2)}) collective-permute-start(bf16[1792,512]{1,0:T(8,128)(2,1)} %param.7), channel_id=1, source_target_pairs={{1,16},{3,18},{5,20},{7,22},{9,24},{11,26},{13,28},{15,30},{16,1},... | collective-permute-start | bytes 5505032 | tf_op jit(solution)/shard_map/ppermute | solution.py:27
  94.5 18.9 %collective-permute-start.14 = (bf16[8,96,512]{2,1,0:T(8,128)(2,1)}, bf16[8,96,512]{2,1,0:T(8,128)(2,1)}, u32[]{:S(2)}, u32[]{:S(2)}) collective-permute-start(bf16[8,96,512]{2,1,0:T(8,128)(2,1)} %copy-done.8), channel_id=1, source_target_pairs={{0,96},{1,97},{2,98},{3,99},{4,100},{5,101},{6,102},{7,103},{8,104... | collective-permute-start | bytes 2359304 | tf_op jit(solution)/shard_map/ppermute | solution.py:27
  121.5 21.2 %collective-permute-start.15 = (f32[256,768]{1,0:T(8,128)}, f32[256,768]{1,0:T(8,128)S(1)}, u32[]{:S(2)}, u32[]{:S(2)}) collective-permute-start(f32[256,768]{1,0:T(8,128)} %get-tuple-element.52), channel_id=1, source_target_pairs={{0,1},{1,0},{2,3},{3,2},{4,5},{5,4},{6,7},{7,6},{8,9},{9,8},{10,11... | collective-permute-start | bytes 2359304 | tf_op jit(solution)/shard_map/ppermute | solution.py:27
  142.7 13.7 %collective-permute-start.21 = (bf16[8,192,512]{2,1,0:T(8,128)(2,1)}, bf16[8,192,512]{2,1,0:T(8,128)(2,1)}, u32[]{:S(2)}, u32[]{:S(2)}) collective-permute-start(bf16[8,192,512]{2,1,0:T(8,128)(2,1)} %all-to-all-done.1.own_ref), channel_id=1, source_target_pairs={{0,16},{1,17},{2,18},{3,19},{4,20},{5,21},{6,22},{7,23},{8,24},{9,... | collective-permute-start | bytes 4718600 | tf_op jit(solution)/shard_map/ppermute | solution.py:27
  144.8 8.4 %collective-permute-start.16 = (bf16[128,768]{1,0:T(8,128)(2,1)S(1)}, bf16[128,768]{1,0:T(8,128)(2,1)S(1)}, u32[]{:S(2)}, u32[]{:S(2)}) collective-permute-start(bf16[128,768]{1,0:T(8,128)(2,1)S(1)} %activate.2.rest_0_), channel_id=1, source_target_pairs={{0,2},{1,3},{2,4},{3,5},{4,6},{5,7},{6,8},{7,9},{8,10},{9,11},{10,... | collective-permute-start | bytes 589832 | tf_op jit(solution)/shard_map/ppermute | solution.py:27
  153.2 12.6 %collective-permute-start.17 = (bf16[128,768]{1,0:T(8,128)(2,1)S(1)}, bf16[128,768]{1,0:T(8,128)(2,1)S(1)}, u32[]{:S(2)}, u32[]{:S(2)}) collective-permute-start(bf16[128,768]{1,0:T(8,128)(2,1)S(1)} %collective-permute-done.16.rest_1_), channel_id=1, source_target_pairs={{0,2},{1,3},{2,4},{3,5},{4,6},{5,7},{6,8},{7,9},{8,10},{9,11},{10,... | collective-permute-start | bytes 589832 | tf_op jit(solution)/shard_map/ppermute | solution.py:27
  153.7 12.0 %collective-permute-start.19 = (bf16[128,768]{1,0:T(8,128)(2,1)S(1)}, bf16[128,768]{1,0:T(8,128)(2,1)S(1)}, u32[]{:S(2)}, u32[]{:S(2)}) collective-permute-start(bf16[128,768]{1,0:T(8,128)(2,1)S(1)} %collective-permute-done.18.rest_8_), channel_id=1, source_target_pairs={{0,14},{1,15},{2,0},{3,1},{4,2},{5,3},{6,4},{7,5},{8,6},{9,7},{10,... | collective-permute-start | bytes 589832 | tf_op jit(solution)/shard_map/ppermute | solution.py:27
  163.5 15.9 %collective-permute-start.22 = (f32[192,768]{1,0:T(8,128)}, f32[192,768]{1,0:T(8,128)S(1)}, u32[]{:S(2)}, u32[]{:S(2)}) collective-permute-start(f32[192,768]{1,0:T(8,128)} %get-tuple-element.58), channel_id=1, source_target_pairs={{0,1},{1,0},{2,3},{3,2},{4,5},{5,4},{6,7},{7,6},{8,9},{9,8},{10,11... | collective-permute-start | bytes 1769480 | tf_op jit(solution)/shard_map/ppermute | solution.py:27
  179.4 27.8 %collective-permute-start.23 = (bf16[1792,512]{1,0:T(8,128)(2,1)S(1)}, bf16[1792,512]{1,0:T(8,128)(2,1)S(1)}, u32[]{:S(2)}, u32[]{:S(2)}) collective-permute-start(bf16[1792,512]{1,0:T(8,128)(2,1)S(1)} %broadcast_select_fusion.mine_ref), channel_id=1, source_target_pairs={{0,16},{1,17},{2,18},{3,19},{4,20},{5,21},{6,22},{7,23},{8,24},{9,... | collective-permute-start | bytes 5505032 | tf_op jit(solution)/shard_map/ppermute | solution.py:27
  179.5 7.9 %collective-permute-start.28 = (bf16[96,768]{1,0:T(8,128)(2,1)S(1)}, bf16[96,768]{1,0:T(8,128)(2,1)S(1)}, u32[]{:S(2)}, u32[]{:S(2)}) collective-permute-start(bf16[96,768]{1,0:T(8,128)(2,1)S(1)} %activate.3.rest_9_), channel_id=1, source_target_pairs={{0,2},{1,3},{2,4},{3,5},{4,6},{5,7},{6,8},{7,9},{8,10},{9,11},{10,... | collective-permute-start | bytes 442376 | tf_op jit(solution)/shard_map/ppermute | solution.py:27
  179.6 7.8 %collective-permute-start.30 = (bf16[96,768]{1,0:T(8,128)(2,1)S(1)}, bf16[96,768]{1,0:T(8,128)(2,1)S(1)}, u32[]{:S(2)}, u32[]{:S(2)}) collective-permute-start(bf16[96,768]{1,0:T(8,128)(2,1)S(1)} %activate.3.rest_9_), channel_id=1, source_target_pairs={{0,14},{1,15},{2,0},{3,1},{4,2},{5,3},{6,4},{7,5},{8,6},{9,7},{10,... | collective-permute-start | bytes 442376 | tf_op jit(solution)/shard_map/ppermute | solution.py:27
  182.8 9.0 %collective-permute-start.24 = (bf16[128,768]{1,0:T(8,128)(2,1)S(1)}, bf16[128,768]{1,0:T(8,128)(2,1)S(1)}, u32[]{:S(2)}, u32[]{:S(2)}) collective-permute-start(bf16[128,768]{1,0:T(8,128)(2,1)S(1)} %collective-permute-done.17.rest_2_), channel_id=1, source_target_pairs={{0,2},{1,3},{2,4},{3,5},{4,6},{5,7},{6,8},{7,9},{8,10},{9,11},{10,... | collective-permute-start | bytes 589832 | tf_op jit(solution)/shard_map/ppermute | solution.py:27
  182.8 9.0 %collective-permute-start.26 = (bf16[128,768]{1,0:T(8,128)(2,1)S(1)}, bf16[128,768]{1,0:T(8,128)(2,1)S(1)}, u32[]{:S(2)}, u32[]{:S(2)}) collective-permute-start(bf16[128,768]{1,0:T(8,128)(2,1)S(1)} %collective-permute-done.19.rest_7_), channel_id=1, source_target_pairs={{0,14},{1,15},{2,0},{3,1},{4,2},{5,3},{6,4},{7,5},{8,6},{9,7},{10,... | collective-permute-start | bytes 589832 | tf_op jit(solution)/shard_map/ppermute | solution.py:27
  194.4 7.1 %collective-permute-start.32 = (bf16[96,768]{1,0:T(8,128)(2,1)S(1)}, bf16[96,768]{1,0:T(8,128)(2,1)S(1)}, u32[]{:S(2)}, u32[]{:S(2)}) collective-permute-start(bf16[96,768]{1,0:T(8,128)(2,1)S(1)} %collective-permute-done.29.rest_11_), channel_id=1, source_target_pairs={{0,2},{1,3},{2,4},{3,5},{4,6},{5,7},{6,8},{7,9},{8,10},{9,11},{10,... | collective-permute-start | bytes 442376 | tf_op jit(solution)/shard_map/ppermute | solution.py:27
  195.3 7.0 %collective-permute-start.34 = (bf16[96,768]{1,0:T(8,128)(2,1)S(1)}, bf16[96,768]{1,0:T(8,128)(2,1)S(1)}, u32[]{:S(2)}, u32[]{:S(2)}) collective-permute-start(bf16[96,768]{1,0:T(8,128)(2,1)S(1)} %collective-permute-done.31.rest_16_), channel_id=1, source_target_pairs={{0,14},{1,15},{2,0},{3,1},{4,2},{5,3},{6,4},{7,5},{8,6},{9,7},{10,... | collective-permute-start | bytes 442376 | tf_op jit(solution)/shard_map/ppermute | solution.py:27
  197.7 7.3 %collective-permute-start.25 = (bf16[64,768]{1,0:T(8,128)(2,1)S(1)}, bf16[64,768]{1,0:T(8,128)(2,1)S(1)}, u32[]{:S(2)}, u32[]{:S(2)}) collective-permute-start(bf16[64,768]{1,0:T(8,128)(2,1)S(1)} %slice.16), channel_id=1, source_target_pairs={{0,2},{1,3},{2,4},{3,5},{4,6},{5,7},{6,8},{7,9},{8,10},{9,11},{10,... | collective-permute-start | bytes 294920 | tf_op jit(solution)/shard_map/ppermute | solution.py:27
  (23 other events, 268.9 us)

commit v7 on v6

--- a/solution.py
+++ b/solution.py
@@ -10,7 +10,7 @@
 
 AXES = ("xl", "y", "c", "z", "xh")
 SIZES = (2, 4, 2, 8, 2)
-FIRST = 128
+FIRST = 144
 TOGETHER = 2
 F32, BF16 = jnp.float32, jnp.bfloat16
 SCALARS = pl.BlockSpec(memory_space=pltpu.SMEM)
@@ -206,9 +206,10 @@
         first = 0
         for size in sizes:
             for s in order:
-                length = size // 2 if abs(s) == nz // 2 else size
-                at = ((z - s + nz) % nz) * units + first + (length if s == -nz // 2 else 0)
-                h_ref[pl.ds(pl.multiple_of(at, 16), length)] = part_refs.pop(0)[...]
+                part_ref = part_refs.pop(0)
+                length = part_ref.shape[0]
+                at = ((z - s + nz) % nz) * units + first + (size - length if s == -nz // 2 else 0)
+                h_ref[pl.ds(pl.multiple_of(at, 16), length)] = part_ref[...]
             first += size
         for side, w_ref in ((c, mine_ref), (1 - c, theirs_ref)):
             o_ref[side] = lax.dot_general(
@@ -232,7 +233,7 @@
     ring, up, down = {0: hidden}, hidden, hidden
     for at in range(nz // 2):
         if at == nz // 2 - 1:
-            half = up.shape[0] // 2
+            half = up.shape[0] // 32 * 16
             up, down = up[:half], down[half:]
         up, down = along_z(up, 1), along_z(down, -1)
         if at == 1:
@@ -251,17 +252,17 @@
         around[s] = along_z(tokens, s)
     around[3], around[-3] = along_z(around[2], 1), along_z(around[-2], -1)
     sliced = slice_units(gate_weight, up_weight, nz)
-    ready, *around = together(sliced[0], *(around[s] for s in (0, 1, 2, 3, 4, -3, -2, -1)))
+    near = regroup(place, [around[s] for s in (0, 1, 2, 3, 4, -3, -2, -1)])
+    ready, near = together(sliced[0], near)
     weights = [lax.all_to_all(ready, "z", 0, 0, tiled=True)]
 
-    near = regroup(place, around)
     far = swap_xl(near)
     near_before, near_after = along_y(near, 1), along_y(near, -1)
     far, near_before, near_after = together(far, near_before, near_after)
     far_before, far_after = along_y(far, 1), along_y(far, -1)
     near_across, far_across = along_y(near_before, 1), along_y(far_after, -1)
     pieces = (near, far, near_after, far_after, near_across, far_across, near_before, far_before)
-    ready, weights[0], *_ = together(sliced[1], weights[0], far_before, far_after, near_across)
+    ready, weights[0], pieces = together(sliced[1], weights[0], pieces)
     weights.append(lax.all_to_all(ready, "z", 0, 0, tiled=True))
 
     keep, *gives = project(place, weights[0], swap_core(weights[0]), pieces, ())
@@ -279,7 +280,8 @@
     both = together(weights[1], swap_core(weights[1]), hiddens[0])
     keep, give = project(place, *both[:2], pieces, ())
     got = swap_xh(give)
-    first, (got, mine) = round_z(hiddens[0], (got, mine))
+    hidden, _ = together(hiddens[0], give)
+    first, (got, mine) = round_z(hidden, (got, mine))
     theirs = swap_core(mine)
     second, _ = round_z(activate(keep, [got]), (first[3], first[-3]))
 

time: 240 us -> 227 us (0.946)
  waiting for transfers between devices: 109 us -> 99.3 us
  blocking collectives: 26.4 us -> 23.6 us
    ppermute x36, waiting for transfers between devices: 101 us -> 78.3 us  [send(): return lax.ppermute(value, AXES, pairs)]
    all_to_all x1, waiting for transfers between devices: 8.23 us -> 21 us  [shards(): weights.append(lax.all_to_all(ready, 'z', 0, 0, tiled=True))]
    all_to_all x1, blocking collectives: 26.4 us -> 23.6 us  [shards(): got = lax.all_to_all(out, ('xh', 'y', 'xl'), 0, 0, tiled=True)]
  transfers between devices with their start and end apart: 38 -> 38, of which waited for: 16 -> 19; matrix products, arithmetic and copies ran while one was open for 0% -> 0% of each run, Pallas kernels for 9% -> 6%
where the time goes in v7:
time: 227 us; the launch traced here: 226 us
  waiting for transfers between devices  99.3 us (44%)
  starting transfers between devices  72.8 us (32%)
  Pallas kernels  25.2 us (11%)
  blocking collectives  23.6 us (10%)
  local copies, waits for them, and re-layouts  4.1 us (2%)
    ppermute x36, waiting for transfers between devices, send(): return lax.ppermute(value, AXES, pairs)  78.3 us
    ppermute x36, starting transfers between devices, send(): return lax.ppermute(value, AXES, pairs)  61.4 us
    all_to_all x1, blocking collectives, shards(): got = lax.all_to_all(out, ('xh', 'y', 'xl'), 0, 0, tiled=True)  23.6 us
    all_to_all x1, waiting for transfers between devices, shards(): weights.append(lax.all_to_all(ready, 'z', 0, 0, tiled=True))  21 us
    pallas_call x2, Pallas kernels, project(): pl.pallas_call(body, in_specs=[SCALARS] + [pl.BlockSpec(memory_space=pl.A...  15.1 us
    all_to_all x1, starting transfers between devices, shards(): weights.append(lax.all_to_all(ready, 'z', 0, 0, tiled=True))  6.57 us
    all_to_all x1, starting transfers between devices, shards(): weights = [lax.all_to_all(ready, 'z', 0, 0, tiled=True)]  4.81 us
  transfers between devices with their start and end apart: 38, of which 19 were waited for; matrix products, arithmetic and copies ran while one was open for 0% of the time, Pallas kernels for 6%

profile of v7, /device:TPU:2, one launch (start us, length us, event | category | flops | bytes accessed | tf_op | source)
XLA Modules:
  0.0 226.3 jit_solution(10975733697030091518)
XLA Ops:
  0.0 3.3 %collective-permute-start.1 = (bf16[96,512]{1,0:T(8,128)(2,1)}, bf16[96,512]{1,0:T(8,128)(2,1)S(1)}, u32[]{:S(2)}, u32[]{:S(2)}) collective-permute-start(bf16[96,512]{1,0:T(8,128)(2,1)} %rest_0_.1), channel_id=1, source_target_pairs={{0,4},{1,5},{2,6},{3,7},{4,8},{5,9},{6,10},{7,11},{8,12},{9,13},{1... | collective-permute-start | bytes 294920 | tf_op jit(solution)/shard_map/ppermute | solution.py:27
  3.3 3.0 %collective-permute-start.4 = (bf16[96,512]{1,0:T(8,128)(2,1)}, bf16[96,512]{1,0:T(8,128)(2,1)S(1)}, u32[]{:S(2)}, u32[]{:S(2)}) collective-permute-start(bf16[96,512]{1,0:T(8,128)(2,1)} %rest_0_.1), channel_id=1, source_target_pairs={{0,12},{1,13},{2,14},{3,15},{4,0},{5,1},{6,2},{7,3},{8,4},{9,5},{1... | collective-permute-start | bytes 294920 | tf_op jit(solution)/shard_map/ppermute | solution.py:27
  7.3 5.0 %collective-permute-start.3 = (bf16[96,512]{1,0:T(8,128)(2,1)}, bf16[96,512]{1,0:T(8,128)(2,1)S(1)}, u32[]{:S(2)}, u32[]{:S(2)}) collective-permute-start(bf16[96,512]{1,0:T(8,128)(2,1)} %rest_0_.1), channel_id=1, source_target_pairs={{0,8},{1,9},{2,10},{3,11},{4,12},{5,13},{6,14},{7,15},{8,0},{9,1},... | collective-permute-start | bytes 294920 | tf_op jit(solution)/shard_map/ppermute | solution.py:27
  14.6 3.2 %collective-permute-start.5 = (bf16[96,512]{1,0:T(8,128)(2,1)S(1)}, bf16[96,512]{1,0:T(8,128)(2,1)S(1)}, u32[]{:S(2)}, u32[]{:S(2)}) collective-permute-start(bf16[96,512]{1,0:T(8,128)(2,1)S(1)} %collective-permute-done.4.rest_6_), channel_id=1, source_target_pairs={{0,14},{1,15},{2,0},{3,1},{4,2},{5,3},{6,4},{7,5},{8,6},{9,7},{10,... | collective-permute-start | bytes 294920 | tf_op jit(solution)/shard_map/ppermute | solution.py:27
  17.8 3.9 %slice_units.1 = (bf16[8,288,512]{2,1,0:T(8,128)(2,1)}, bf16[8,160,512]{2,1,0:T(8,128)(2,1)}) custom-call(bf16[512,1792]{1,0:T(8,128)(2,1)} %g_ref.1, bf16[512,1792]{1,0:T(8,128)(2,1)} %u_ref.1), custom_call_target="tpu_custom_call" | custom-call | bytes 114688 | tf_op jit(solution)/shard_map/slice_units/pallas_call | solution.py:94
  25.9 4.8 %all-to-all-start = ((bf16[8,288,512]{2,1,0:T(8,128)(2,1)}), bf16[8,288,512]{2,1,0:T(8,128)(2,1)S(1)}, u32[]{:S(2)}, u32[]{:S(2)}) async-start(bf16[8,288,512]{2,1,0:T(8,128)(2,1)} %get-tuple-element.40), calls=%async_computation | async-start | bytes 4718592 | tf_op jit(solution)/shard_map/all_to_all | solution.py:257
  34.6 14.1 %collective-permute-done.7.rest_1_ = bf16[8,96,512]{2,1,0:T(8,128)(2,1)S(1)} collective-permute-done((bf16[8,96,512]{2,1,0:T(8,128)(2,1)S(1)}, bf16[8,96,512]{2,1,0:T(8,128)(2,1)S(1)}, u32[]{:S(2)}, u32[]{:S(2)}) %collective-permute-start.7) | collective-permute-done | bytes 786464 | tf_op jit(solution)/shard_map/ppermute | solution.py:27
  50.3 2.9 %collective-permute-start.10 = (bf16[8,96,512]{2,1,0:T(8,128)(2,1)S(1)}, bf16[8,96,512]{2,1,0:T(8,128)(2,1)S(1)}, u32[]{:S(2)}, u32[]{:S(2)}) collective-permute-start(bf16[8,96,512]{2,1,0:T(8,128)(2,1)S(1)} %collective-permute-done.7.rest_1_), channel_id=1, source_target_pairs={{0,96},{1,97},{2,98},{3,99},{4,100},{5,101},{6,102},{7,103},{8,104... | collective-permute-start | bytes 2359304 | tf_op jit(solution)/shard_map/ppermute | solution.py:27
  54.3 13.7 %collective-permute-done.10.rest_3_ = bf16[8,96,512]{2,1,0:T(8,128)(2,1)S(1)} collective-permute-done((bf16[8,96,512]{2,1,0:T(8,128)(2,1)S(1)}, bf16[8,96,512]{2,1,0:T(8,128)(2,1)S(1)}, u32[]{:S(2)}, u32[]{:S(2)}) %collective-permute-start.10) | collective-permute-done | bytes 786464 | tf_op jit(solution)/shard_map/ppermute | solution.py:27
  68.0 2.9 %collective-permute-start.12 = (bf16[8,96,512]{2,1,0:T(8,128)(2,1)S(1)}, bf16[8,96,512]{2,1,0:T(8,128)(2,1)}, u32[]{:S(2)}, u32[]{:S(2)}) collective-permute-start(bf16[8,96,512]{2,1,0:T(8,128)(2,1)S(1)} %collective-permute-done.10.rest_3_), channel_id=1, source_target_pairs={{0,96},{1,97},{2,98},{3,99},{4,100},{5,101},{6,102},{7,103},{8,104... | collective-permute-start | bytes 2359304 | tf_op jit(solution)/shard_map/ppermute | solution.py:27
  70.9 4.0 %collective-permute-done.13.rest_7_ = bf16[8,96,512]{2,1,0:T(8,128)(2,1)S(1)} collective-permute-done((bf16[8,96,512]{2,1,0:T(8,128)(2,1)S(1)}, bf16[8,96,512]{2,1,0:T(8,128)(2,1)S(1)}, u32[]{:S(2)}, u32[]{:S(2)}) %collective-permute-start.13) | collective-permute-done | bytes 786464 | tf_op jit(solution)/shard_map/ppermute | solution.py:27
  74.9 12.5 %collective-permute-done.11.rest_4_ = bf16[8,96,512]{2,1,0:T(8,128)(2,1)S(1)} collective-permute-done((bf16[8,96,512]{2,1,0:T(8,128)(2,1)S(1)}, bf16[8,96,512]{2,1,0:T(8,128)(2,1)S(1)}, u32[]{:S(2)}, u32[]{:S(2)}) %collective-permute-start.11) | collective-permute-done | bytes 786464 | tf_op jit(solution)/shard_map/ppermute | solution.py:27
  88.4 6.6 %all-to-all-start.1 = ((bf16[8,160,512]{2,1,0:T(8,128)(2,1)}), bf16[8,160,512]{2,1,0:T(8,128)(2,1)}, u32[]{:S(2)}, u32[]{:S(2)}) async-start(bf16[8,160,512]{2,1,0:T(8,128)(2,1)} %get-tuple-element.57), calls=%async_computation.1 | async-start | bytes 2621440 | tf_op jit(solution)/shard_map/all_to_all | solution.py:266
  96.9 8.6 %project.2 = (f32[288,768]{1,0:T(8,128)}, f32[288,768]{1,0:T(8,128)}) custom-call(s32[5]{0:T(128)} %stack.23.place_ref, bf16[8,288,512]{2,1,0:T(8,128)(2,1)} %copy-done.3, bf16[8,288,512]{2,1,0:T(8,128)(2,1)} %collective-permute-done.14.other_ref, bf16[8,96,512]{2,1,0:T(8,128)(2,1)} %regroup.1.rest_0_, bf16[8,96,512]{2,1,0:T(8,128)(2,1)} %copy-done.5, ...), custom_call_target="tpu_custom_call" | custom-call | flops 56623104 | bytes 172032 | tf_op jit(solution)/shard_map/project/pallas_call | solution.py:154
  105.5 3.6 %collective-permute-start.15 = (f32[288,768]{1,0:T(8,128)}, f32[288,768]{1,0:T(8,128)S(1)}, u32[]{:S(2)}, u32[]{:S(2)}) collective-permute-start(f32[288,768]{1,0:T(8,128)} %get-tuple-element.55), channel_id=1, source_target_pairs={{0,1},{1,0},{2,3},{3,2},{4,5},{5,4},{6,7},{7,6},{8,9},{9,8},{10,11... | collective-permute-start | bytes 2654216 | tf_op jit(solution)/shard_map/ppermute | solution.py:27
  109.1 21.0 %all-to-all-done.1.own_ref = bf16[8,160,512]{2,1,0:T(8,128)(2,1)} async-done(((bf16[8,160,512]{2,1,0:T(8,128)(2,1)}), bf16[8,160,512]{2,1,0:T(8,128)(2,1)}, u32[]{:S(2)}, u32[]{:S(2)}) %all-to-all-start.1) | async-done | bytes 1310752 | tf_op jit(solution)/shard_map/all_to_all | solution.py:266
  130.1 10.5 %collective-permute-done.15.rest_0_ = f32[288,768]{1,0:T(8,128)S(1)} collective-permute-done((f32[288,768]{1,0:T(8,128)}, f32[288,768]{1,0:T(8,128)S(1)}, u32[]{:S(2)}, u32[]{:S(2)}) %collective-permute-start.15) | collective-permute-done | bytes 884768 | tf_op jit(solution)/shard_map/ppermute | solution.py:27
  143.9 6.5 %project.3 = (f32[160,768]{1,0:T(8,128)}, f32[160,768]{1,0:T(8,128)}) custom-call(s32[5]{0:T(128)} %stack.23.place_ref, bf16[8,160,512]{2,1,0:T(8,128)(2,1)} %all-to-all-done.1.own_ref, bf16[8,160,512]{2,1,0:T(8,128)(2,1)} %collective-permute-done.17.other_ref, bf16[8,96,512]{2,1,0:T(8,128)(2,1)} %regroup.1.rest_0_, bf16[8,96,512]{2,1,0:T(8,128)(2,1)} %copy-done.5, ...), custom_call_target="tpu_custom_call" | custom-call | flops 31457280 | bytes 139264 | tf_op jit(solution)/shard_map/project/pallas_call | solution.py:154
  155.3 3.9 %collective-permute-done.18.rest_1_ = bf16[144,768]{1,0:T(8,128)(2,1)S(1)} collective-permute-done((bf16[144,768]{1,0:T(8,128)(2,1)S(1)}, bf16[144,768]{1,0:T(8,128)(2,1)S(1)}, u32[]{:S(2)}, u32[]{:S(2)}) %collective-permute-start.18) | collective-permute-done | bytes 221216 | tf_op jit(solution)/shard_map/ppermute | solution.py:27
  159.7 2.7 %collective-permute-start.21 = (bf16[144,768]{1,0:T(8,128)(2,1)S(1)}, bf16[144,768]{1,0:T(8,128)(2,1)S(1)}, u32[]{:S(2)}, u32[]{:S(2)}) collective-permute-start(bf16[144,768]{1,0:T(8,128)(2,1)S(1)} %collective-permute-done.20.rest_8_), channel_id=1, source_target_pairs={{0,14},{1,15},{2,0},{3,1},{4,2},{5,3},{6,4},{7,5},{8,6},{9,7},{10,... | collective-permute-start | bytes 663560 | tf_op jit(solution)/shard_map/ppermute | solution.py:27
  162.7 4.4 %collective-permute-done.19.rest_2_ = bf16[144,768]{1,0:T(8,128)(2,1)S(1)} collective-permute-done((bf16[144,768]{1,0:T(8,128)(2,1)S(1)}, bf16[144,768]{1,0:T(8,128)(2,1)S(1)}, u32[]{:S(2)}, u32[]{:S(2)}) %collective-permute-start.19) | collective-permute-done | bytes 221216 | tf_op jit(solution)/shard_map/ppermute | solution.py:27
  168.9 2.8 %collective-permute-start.30 = (bf16[80,768]{1,0:T(8,128)(2,1)S(1)}, bf16[80,768]{1,0:T(8,128)(2,1)S(1)}, u32[]{:S(2)}, u32[]{:S(2)}) collective-permute-start(bf16[80,768]{1,0:T(8,128)(2,1)S(1)} %activate.3.rest_9_), channel_id=1, source_target_pairs={{0,14},{1,15},{2,0},{3,1},{4,2},{5,3},{6,4},{7,5},{8,6},{9,7},{10,... | collective-permute-start | bytes 368648 | tf_op jit(solution)/shard_map/ppermute | solution.py:27
  171.7 3.2 %collective-permute-start.26 = (bf16[144,768]{1,0:T(8,128)(2,1)S(1)}, bf16[144,768]{1,0:T(8,128)(2,1)S(1)}, u32[]{:S(2)}, u32[]{:S(2)}) collective-permute-start(bf16[144,768]{1,0:T(8,128)(2,1)S(1)} %collective-permute-done.21.rest_7_), channel_id=1, source_target_pairs={{0,14},{1,15},{2,0},{3,1},{4,2},{5,3},{6,4},{7,5},{8,6},{9,7},{10,... | collective-permute-start | bytes 663560 | tf_op jit(solution)/shard_map/ppermute | solution.py:27
  175.4 3.2 %collective-permute-start.31 = (bf16[80,768]{1,0:T(8,128)(2,1)S(1)}, bf16[80,768]{1,0:T(8,128)(2,1)S(1)}, u32[]{:S(2)}, u32[]{:S(2)}) collective-permute-start(bf16[80,768]{1,0:T(8,128)(2,1)S(1)} %collective-permute-done.30.rest_17_), channel_id=1, source_target_pairs={{0,14},{1,15},{2,0},{3,1},{4,2},{5,3},{6,4},{7,5},{8,6},{9,7},{10,... | collective-permute-start | bytes 368648 | tf_op jit(solution)/shard_map/ppermute | solution.py:27
  178.6 2.6 %collective-permute-done.24.rest_3_ = bf16[144,768]{1,0:T(8,128)(2,1)S(1)} collective-permute-done((bf16[144,768]{1,0:T(8,128)(2,1)S(1)}, bf16[144,768]{1,0:T(8,128)(2,1)S(1)}, u32[]{:S(2)}, u32[]{:S(2)}) %collective-permute-start.24) | collective-permute-done | bytes 221216 | tf_op jit(solution)/shard_map/ppermute | solution.py:27
  182.8 3.0 %collective-permute-start.34 = (bf16[80,768]{1,0:T(8,128)(2,1)S(1)}, bf16[80,768]{1,0:T(8,128)(2,1)S(1)}, u32[]{:S(2)}, u32[]{:S(2)}) collective-permute-start(bf16[80,768]{1,0:T(8,128)(2,1)S(1)} %collective-permute-done.31.rest_16_), channel_id=1, source_target_pairs={{0,14},{1,15},{2,0},{3,1},{4,2},{5,3},{6,4},{7,5},{8,6},{9,7},{10,... | collective-permute-start | bytes 368648 | tf_op jit(solution)/shard_map/ppermute | solution.py:27
  185.8 3.3 %collective-permute-start.27 = (bf16[80,768]{1,0:T(8,128)(2,1)S(1)}, bf16[80,768]{1,0:T(8,128)(2,1)S(1)}, u32[]{:S(2)}, u32[]{:S(2)}) collective-permute-start(bf16[80,768]{1,0:T(8,128)(2,1)S(1)} %slice.17), channel_id=1, source_target_pairs={{0,14},{1,15},{2,0},{3,1},{4,2},{5,3},{6,4},{7,5},{8,6},{9,7},{10,... | collective-permute-start | bytes 368648 | tf_op jit(solution)/shard_map/ppermute | solution.py:27
  189.6 3.0 %collective-permute-start.35 = (bf16[48,768]{1,0:T(8,128)(2,1)S(1)}, bf16[48,768]{1,0:T(8,128)(2,1)S(1)}, u32[]{:S(2)}, u32[]{:S(2)}) collective-permute-start(bf16[48,768]{1,0:T(8,128)(2,1)S(1)} %slice.19), channel_id=1, source_target_pairs={{0,14},{1,15},{2,0},{3,1},{4,2},{5,3},{6,4},{7,5},{8,6},{9,7},{10,... | collective-permute-start | bytes 221192 | tf_op jit(solution)/shard_map/ppermute | solution.py:27
  192.7 2.8 %collective-permute-done.25.rest_4_ = bf16[64,768]{1,0:T(8,128)(2,1)S(1)} collective-permute-done((bf16[64,768]{1,0:T(8,128)(2,1)S(1)}, bf16[64,768]{1,0:T(8,128)(2,1)S(1)}, u32[]{:S(2)}, u32[]{:S(2)}) %collective-permute-start.25) | collective-permute-done | bytes 98336 | tf_op jit(solution)/shard_map/ppermute | solution.py:27
  195.5 2.5 %collective-permute-done.33.rest_13_ = bf16[32,768]{1,0:T(8,128)(2,1)S(1)} collective-permute-done((bf16[32,768]{1,0:T(8,128)(2,1)S(1)}, bf16[32,768]{1,0:T(8,128)(2,1)S(1)}, u32[]{:S(2)}, u32[]{:S(2)}) %collective-permute-start.33) | collective-permute-done | bytes 49184 | tf_op jit(solution)/shard_map/ppermute | solution.py:27
  198.0 3.8 %mix.1 = bf16[2,768,512]{2,1,0:T(8,128)(2,1)S(1)} custom-call(s32[5]{0:T(128)S(1)} %copy-done.2, bf16[1792,512]{1,0:T(8,128)(2,1)S(1)} %broadcast_select_fusion.mine_ref, bf16[1792,512]{1,0:T(8,128)(2,1)S(1)} %collective-permute-done.23.theirs_ref, bf16[144,768]{1,0:T(8,128)(2,1)S(1)} %activate.2.rest_0_, ...), custom_call_target="tpu_custom_call" | custom-call | flops 44040192 | bytes 100352 | tf_op jit(solution)/shard_map/mix/pallas_call | solution.py:219
  201.8 23.6 %all_to_all.15 = bf16[16,96,512]{2,1,0:T(8,128)(2,1)S(1)} all-to-all(bf16[16,96,512]{2,1,0:T(8,128)(2,1)S(1)} %bitcast.6), channel_id=1, replica_groups=mesh['xl'=2,'y'=4,'c'=2,'z'=8,'xh'=2] {'xh','y','xl'}, dimensions={0} | all-to-all | bytes 3145728 | tf_op jit(solution)/shard_map/all_to_all | solution.py:289
  (97 shorter events, 31.4 us)
Async XLA Ops:
  0.0 14.6 %collective-permute-start.1 = (bf16[96,512]{1,0:T(8,128)(2,1)}, bf16[96,512]{1,0:T(8,128)(2,1)S(1)}, u32[]{:S(2)}, u32[]{:S(2)}) collective-permute-start(bf16[96,512]{1,0:T(8,128)(2,1)} %rest_0_.1), channel_id=1, source_target_pairs={{0,4},{1,5},{2,6},{3,7},{4,8},{5,9},{6,10},{7,11},{8,12},{9,13},{1... | collective-permute-start | bytes 294920 | tf_op jit(solution)/shard_map/ppermute | solution.py:27
  3.3 11.3 %collective-permute-start.4 = (bf16[96,512]{1,0:T(8,128)(2,1)}, bf16[96,512]{1,0:T(8,128)(2,1)S(1)}, u32[]{:S(2)}, u32[]{:S(2)}) collective-permute-start(bf16[96,512]{1,0:T(8,128)(2,1)} %rest_0_.1), channel_id=1, source_target_pairs={{0,12},{1,13},{2,14},{3,15},{4,0},{5,1},{6,2},{7,3},{8,4},{9,5},{1... | collective-permute-start | bytes 294920 | tf_op jit(solution)/shard_map/ppermute | solution.py:27
  6.3 16.1 %collective-permute-start = (bf16[96,512]{1,0:T(8,128)(2,1)}, bf16[96,512]{1,0:T(8,128)(2,1)S(1)}, u32[]{:S(2)}, u32[]{:S(2)}) collective-permute-start(bf16[96,512]{1,0:T(8,128)(2,1)} %rest_0_.1), channel_id=1, source_target_pairs={{0,2},{1,3},{2,4},{3,5},{4,6},{5,7},{6,8},{7,9},{8,10},{9,11},{10,... | collective-permute-start | bytes 294920 | tf_op jit(solution)/shard_map/ppermute | solution.py:27
  7.3 15.1 %collective-permute-start.3 = (bf16[96,512]{1,0:T(8,128)(2,1)}, bf16[96,512]{1,0:T(8,128)(2,1)S(1)}, u32[]{:S(2)}, u32[]{:S(2)}) collective-permute-start(bf16[96,512]{1,0:T(8,128)(2,1)} %rest_0_.1), channel_id=1, source_target_pairs={{0,8},{1,9},{2,10},{3,11},{4,12},{5,13},{6,14},{7,15},{8,0},{9,1},... | collective-permute-start | bytes 294920 | tf_op jit(solution)/shard_map/ppermute | solution.py:27
  12.3 10.0 %collective-permute-start.6 = (bf16[96,512]{1,0:T(8,128)(2,1)}, bf16[96,512]{1,0:T(8,128)(2,1)S(1)}, u32[]{:S(2)}, u32[]{:S(2)}) collective-permute-start(bf16[96,512]{1,0:T(8,128)(2,1)} %rest_0_.1), channel_id=1, source_target_pairs={{0,14},{1,15},{2,0},{3,1},{4,2},{5,3},{6,4},{7,5},{8,6},{9,7},{10,... | collective-permute-start | bytes 294920 | tf_op jit(solution)/shard_map/ppermute | solution.py:27
  14.6 7.8 %collective-permute-start.2 = (bf16[96,512]{1,0:T(8,128)(2,1)S(1)}, bf16[96,512]{1,0:T(8,128)(2,1)S(1)}, u32[]{:S(2)}, u32[]{:S(2)}) collective-permute-start(bf16[96,512]{1,0:T(8,128)(2,1)S(1)} %collective-permute-done.1.rest_2_), channel_id=1, source_target_pairs={{0,2},{1,3},{2,4},{3,5},{4,6},{5,7},{6,8},{7,9},{8,10},{9,11},{10,... | collective-permute-start | bytes 294920 | tf_op jit(solution)/shard_map/ppermute | solution.py:27
  14.6 7.8 %collective-permute-start.5 = (bf16[96,512]{1,0:T(8,128)(2,1)S(1)}, bf16[96,512]{1,0:T(8,128)(2,1)S(1)}, u32[]{:S(2)}, u32[]{:S(2)}) collective-permute-start(bf16[96,512]{1,0:T(8,128)(2,1)S(1)} %collective-permute-done.4.rest_6_), channel_id=1, source_target_pairs={{0,14},{1,15},{2,0},{3,1},{4,2},{5,3},{6,4},{7,5},{8,6},{9,7},{10,... | collective-permute-start | bytes 294920 | tf_op jit(solution)/shard_map/ppermute | solution.py:27
  25.9 62.3 %all-to-all-start = ((bf16[8,288,512]{2,1,0:T(8,128)(2,1)}), bf16[8,288,512]{2,1,0:T(8,128)(2,1)S(1)}, u32[]{:S(2)}, u32[]{:S(2)}) async-start(bf16[8,288,512]{2,1,0:T(8,128)(2,1)} %get-tuple-element.40), calls=%async_computation | async-start | bytes 4718592 | tf_op jit(solution)/shard_map/all_to_all | solution.py:257
  30.8 17.9 %collective-permute-start.7 = (bf16[8,96,512]{2,1,0:T(8,128)(2,1)S(1)}, bf16[8,96,512]{2,1,0:T(8,128)(2,1)S(1)}, u32[]{:S(2)}, u32[]{:S(2)}) collective-permute-start(bf16[8,96,512]{2,1,0:T(8,128)(2,1)S(1)} %copy-done.4), channel_id=1, source_target_pairs={{0,128},{1,129},{2,130},{3,131},{4,132},{5,133},{6,134},{7,135},{8... | collective-permute-start | bytes 2359304 | tf_op jit(solution)/shard_map/ppermute | solution.py:27
  31.4 18.8 %collective-permute-start.8 = (bf16[8,96,512]{2,1,0:T(8,128)(2,1)S(1)}, bf16[8,96,512]{2,1,0:T(8,128)(2,1)S(1)}, u32[]{:S(2)}, u32[]{:S(2)}) collective-permute-start(bf16[8,96,512]{2,1,0:T(8,128)(2,1)S(1)} %copy-done.4), channel_id=1, source_target_pairs={{0,32},{1,33},{2,34},{3,35},{4,36},{5,37},{6,38},{7,39},{8,40},{9,... | collective-permute-start | bytes 2359304 | tf_op jit(solution)/shard_map/ppermute | solution.py:27
  33.0 17.3 %collective-permute-start.9 = (bf16[8,96,512]{2,1,0:T(8,128)(2,1)S(1)}, bf16[8,96,512]{2,1,0:T(8,128)(2,1)S(1)}, u32[]{:S(2)}, u32[]{:S(2)}) collective-permute-start(bf16[8,96,512]{2,1,0:T(8,128)(2,1)S(1)} %copy-done.4), channel_id=1, source_target_pairs={{0,96},{1,97},{2,98},{3,99},{4,100},{5,101},{6,102},{7,103},{8,104... | collective-permute-start | bytes 2359304 | tf_op jit(solution)/shard_map/ppermute | solution.py:27
  50.3 17.7 %collective-permute-start.10 = (bf16[8,96,512]{2,1,0:T(8,128)(2,1)S(1)}, bf16[8,96,512]{2,1,0:T(8,128)(2,1)S(1)}, u32[]{:S(2)}, u32[]{:S(2)}) collective-permute-start(bf16[8,96,512]{2,1,0:T(8,128)(2,1)S(1)} %collective-permute-done.7.rest_1_), channel_id=1, source_target_pairs={{0,96},{1,97},{2,98},{3,99},{4,100},{5,101},{6,102},{7,103},{8,104... | collective-permute-start | bytes 2359304 | tf_op jit(solution)/shard_map/ppermute | solution.py:27
  53.2 21.7 %collective-permute-start.13 = (bf16[8,96,512]{2,1,0:T(8,128)(2,1)S(1)}, bf16[8,96,512]{2,1,0:T(8,128)(2,1)S(1)}, u32[]{:S(2)}, u32[]{:S(2)}) collective-permute-start(bf16[8,96,512]{2,1,0:T(8,128)(2,1)S(1)} %collective-permute-done.7.rest_1_), channel_id=1, source_target_pairs={{0,32},{1,33},{2,34},{3,35},{4,36},{5,37},{6,38},{7,39},{8,40},{9,... | collective-permute-start | bytes 2359304 | tf_op jit(solution)/shard_map/ppermute | solution.py:27
  53.2 34.2 %collective-permute-start.11 = (bf16[8,96,512]{2,1,0:T(8,128)(2,1)S(1)}, bf16[8,96,512]{2,1,0:T(8,128)(2,1)S(1)}, u32[]{:S(2)}, u32[]{:S(2)}) collective-permute-start(bf16[8,96,512]{2,1,0:T(8,128)(2,1)S(1)} %collective-permute-done.8.rest_6_), channel_id=1, source_target_pairs={{0,32},{1,33},{2,34},{3,35},{4,36},{5,37},{6,38},{7,39},{8,40},{9,... | collective-permute-start | bytes 2359304 | tf_op jit(solution)/shard_map/ppermute | solution.py:27
  68.0 20.3 %collective-permute-start.12 = (bf16[8,96,512]{2,1,0:T(8,128)(2,1)S(1)}, bf16[8,96,512]{2,1,0:T(8,128)(2,1)}, u32[]{:S(2)}, u32[]{:S(2)}) collective-permute-start(bf16[8,96,512]{2,1,0:T(8,128)(2,1)S(1)} %collective-permute-done.10.rest_3_), channel_id=1, source_target_pairs={{0,96},{1,97},{2,98},{3,99},{4,100},{5,101},{6,102},{7,103},{8,104... | collective-permute-start | bytes 2359304 | tf_op jit(solution)/shard_map/ppermute | solution.py:27
  88.3 8.6 %collective-permute-start.14 = (bf16[8,288,512]{2,1,0:T(8,128)(2,1)S(1)}, bf16[8,288,512]{2,1,0:T(8,128)(2,1)}, u32[]{:S(2)}, u32[]{:S(2)}) collective-permute-start(bf16[8,288,512]{2,1,0:T(8,128)(2,1)S(1)} %all-to-all-done.own_ref), channel_id=1, source_target_pairs={{0,16},{1,17},{2,18},{3,19},{4,20},{5,21},{6,22},{7,23},{8,24},{9,... | collective-permute-start | bytes 7077896 | tf_op jit(solution)/shard_map/ppermute | solution.py:27
  88.4 41.7 %all-to-all-start.1 = ((bf16[8,160,512]{2,1,0:T(8,128)(2,1)}), bf16[8,160,512]{2,1,0:T(8,128)(2,1)}, u32[]{:S(2)}, u32[]{:S(2)}) async-start(bf16[8,160,512]{2,1,0:T(8,128)(2,1)} %get-tuple-element.57), calls=%async_computation.1 | async-start | bytes 2621440 | tf_op jit(solution)/shard_map/all_to_all | solution.py:266
  95.0 14.1 %collective-permute-start.16 = (bf16[1792,512]{1,0:T(8,128)(2,1)}, bf16[1792,512]{1,0:T(8,128)(2,1)}, u32[]{:S(2)}, u32[]{:S(2)}) collective-permute-start(bf16[1792,512]{1,0:T(8,128)(2,1)} %param.7), channel_id=1, source_target_pairs={{1,16},{3,18},{5,20},{7,22},{9,24},{11,26},{13,28},{15,30},{16,1},... | collective-permute-start | bytes 5505032 | tf_op jit(solution)/shard_map/ppermute | solution.py:27
  105.5 35.1 %collective-permute-start.15 = (f32[288,768]{1,0:T(8,128)}, f32[288,768]{1,0:T(8,128)S(1)}, u32[]{:S(2)}, u32[]{:S(2)}) collective-permute-start(f32[288,768]{1,0:T(8,128)} %get-tuple-element.55), channel_id=1, source_target_pairs={{0,1},{1,0},{2,3},{3,2},{4,5},{5,4},{6,7},{7,6},{8,9},{9,8},{10,11... | collective-permute-start | bytes 2654216 | tf_op jit(solution)/shard_map/ppermute | solution.py:27
  150.4 8.8 %collective-permute-start.18 = (bf16[144,768]{1,0:T(8,128)(2,1)S(1)}, bf16[144,768]{1,0:T(8,128)(2,1)S(1)}, u32[]{:S(2)}, u32[]{:S(2)}) collective-permute-start(bf16[144,768]{1,0:T(8,128)(2,1)S(1)} %activate.2.rest_0_), channel_id=1, source_target_pairs={{0,2},{1,3},{2,4},{3,5},{4,6},{5,7},{6,8},{7,9},{8,10},{9,11},{10,... | collective-permute-start | bytes 663560 | tf_op jit(solution)/shard_map/ppermute | solution.py:27
  152.3 7.5 %collective-permute-start.20 = (bf16[144,768]{1,0:T(8,128)(2,1)S(1)}, bf16[144,768]{1,0:T(8,128)(2,1)S(1)}, u32[]{:S(2)}, u32[]{:S(2)}) collective-permute-start(bf16[144,768]{1,0:T(8,128)(2,1)S(1)} %activate.2.rest_0_), channel_id=1, source_target_pairs={{0,14},{1,15},{2,0},{3,1},{4,2},{5,3},{6,4},{7,5},{8,6},{9,7},{10,... | collective-permute-start | bytes 663560 | tf_op jit(solution)/shard_map/ppermute | solution.py:27
  153.8 14.5 %collective-permute-start.22 = (f32[160,768]{1,0:T(8,128)}, f32[160,768]{1,0:T(8,128)S(1)}, u32[]{:S(2)}, u32[]{:S(2)}) collective-permute-start(f32[160,768]{1,0:T(8,128)} %get-tuple-element.61), channel_id=1, source_target_pairs={{0,1},{1,0},{2,3},{3,2},{4,5},{5,4},{6,7},{7,6},{8,9},{9,8},{10,11... | collective-permute-start | bytes 1474568 | tf_op jit(solution)/shard_map/ppermute | solution.py:27
  159.2 7.9 %collective-permute-start.19 = (bf16[144,768]{1,0:T(8,128)(2,1)S(1)}, bf16[144,768]{1,0:T(8,128)(2,1)S(1)}, u32[]{:S(2)}, u32[]{:S(2)}) collective-permute-start(bf16[144,768]{1,0:T(8,128)(2,1)S(1)} %collective-permute-done.18.rest_1_), channel_id=1, source_target_pairs={{0,2},{1,3},{2,4},{3,5},{4,6},{5,7},{6,8},{7,9},{8,10},{9,11},{10,... | collective-permute-start | bytes 663560 | tf_op jit(solution)/shard_map/ppermute | solution.py:27
  159.7 7.3 %collective-permute-start.21 = (bf16[144,768]{1,0:T(8,128)(2,1)S(1)}, bf16[144,768]{1,0:T(8,128)(2,1)S(1)}, u32[]{:S(2)}, u32[]{:S(2)}) collective-permute-start(bf16[144,768]{1,0:T(8,128)(2,1)S(1)} %collective-permute-done.20.rest_8_), channel_id=1, source_target_pairs={{0,14},{1,15},{2,0},{3,1},{4,2},{5,3},{6,4},{7,5},{8,6},{9,7},{10,... | collective-permute-start | bytes 663560 | tf_op jit(solution)/shard_map/ppermute | solution.py:27
  168.3 29.8 %collective-permute-start.23 = (bf16[1792,512]{1,0:T(8,128)(2,1)S(1)}, bf16[1792,512]{1,0:T(8,128)(2,1)S(1)}, u32[]{:S(2)}, u32[]{:S(2)}) collective-permute-start(bf16[1792,512]{1,0:T(8,128)(2,1)S(1)} %broadcast_select_fusion.mine_ref), channel_id=1, source_target_pairs={{0,16},{1,17},{2,18},{3,19},{4,20},{5,21},{6,22},{7,23},{8,24},{9,... | collective-permute-start | bytes 5505032 | tf_op jit(solution)/shard_map/ppermute | solution.py:27
  168.4 7.0 %collective-permute-start.28 = (bf16[80,768]{1,0:T(8,128)(2,1)S(1)}, bf16[80,768]{1,0:T(8,128)(2,1)S(1)}, u32[]{:S(2)}, u32[]{:S(2)}) collective-permute-start(bf16[80,768]{1,0:T(8,128)(2,1)S(1)} %activate.3.rest_9_), channel_id=1, source_target_pairs={{0,2},{1,3},{2,4},{3,5},{4,6},{5,7},{6,8},{7,9},{8,10},{9,11},{10,... | collective-permute-start | bytes 368648 | tf_op jit(solution)/shard_map/ppermute | solution.py:27
  171.7 9.5 %collective-permute-start.24 = (bf16[144,768]{1,0:T(8,128)(2,1)S(1)}, bf16[144,768]{1,0:T(8,128)(2,1)S(1)}, u32[]{:S(2)}, u32[]{:S(2)}) collective-permute-start(bf16[144,768]{1,0:T(8,128)(2,1)S(1)} %collective-permute-done.19.rest_2_), channel_id=1, source_target_pairs={{0,2},{1,3},{2,4},{3,5},{4,6},{5,7},{6,8},{7,9},{8,10},{9,11},{10,... | collective-permute-start | bytes 663560 | tf_op jit(solution)/shard_map/ppermute | solution.py:27
  171.7 9.5 %collective-permute-start.26 = (bf16[144,768]{1,0:T(8,128)(2,1)S(1)}, bf16[144,768]{1,0:T(8,128)(2,1)S(1)}, u32[]{:S(2)}, u32[]{:S(2)}) collective-permute-start(bf16[144,768]{1,0:T(8,128)(2,1)S(1)} %collective-permute-done.21.rest_7_), channel_id=1, source_target_pairs={{0,14},{1,15},{2,0},{3,1},{4,2},{5,3},{6,4},{7,5},{8,6},{9,7},{10,... | collective-permute-start | bytes 663560 | tf_op jit(solution)/shard_map/ppermute | solution.py:27
  175.4 7.4 %collective-permute-start.29 = (bf16[80,768]{1,0:T(8,128)(2,1)S(1)}, bf16[80,768]{1,0:T(8,128)(2,1)S(1)}, u32[]{:S(2)}, u32[]{:S(2)}) collective-permute-start(bf16[80,768]{1,0:T(8,128)(2,1)S(1)} %collective-permute-done.28.rest_10_), channel_id=1, source_target_pairs={{0,2},{1,3},{2,4},{3,5},{4,6},{5,7},{6,8},{7,9},{8,10},{9,11},{10,... | collective-permute-start | bytes 368648 | tf_op jit(solution)/shard_map/ppermute | solution.py:27
  175.4 7.4 %collective-permute-start.31 = (bf16[80,768]{1,0:T(8,128)(2,1)S(1)}, bf16[80,768]{1,0:T(8,128)(2,1)S(1)}, u32[]{:S(2)}, u32[]{:S(2)}) collective-permute-start(bf16[80,768]{1,0:T(8,128)(2,1)S(1)} %collective-permute-done.30.rest_17_), channel_id=1, source_target_pairs={{0,14},{1,15},{2,0},{3,1},{4,2},{5,3},{6,4},{7,5},{8,6},{9,7},{10,... | collective-permute-start | bytes 368648 | tf_op jit(solution)/shard_map/ppermute | solution.py:27
  185.8 9.7 %collective-permute-start.27 = (bf16[80,768]{1,0:T(8,128)(2,1)S(1)}, bf16[80,768]{1,0:T(8,128)(2,1)S(1)}, u32[]{:S(2)}, u32[]{:S(2)}) collective-permute-start(bf16[80,768]{1,0:T(8,128)(2,1)S(1)} %slice.17), channel_id=1, source_target_pairs={{0,14},{1,15},{2,0},{3,1},{4,2},{5,3},{6,4},{7,5},{8,6},{9,7},{10,... | collective-permute-start | bytes 368648 | tf_op jit(solution)/shard_map/ppermute | solution.py:27
  189.6 8.5 %collective-permute-start.35 = (bf16[48,768]{1,0:T(8,128)(2,1)S(1)}, bf16[48,768]{1,0:T(8,128)(2,1)S(1)}, u32[]{:S(2)}, u32[]{:S(2)}) collective-permute-start(bf16[48,768]{1,0:T(8,128)(2,1)S(1)} %slice.19), channel_id=1, source_target_pairs={{0,14},{1,15},{2,0},{3,1},{4,2},{5,3},{6,4},{7,5},{8,6},{9,7},{10,... | collective-permute-start | bytes 221192 | tf_op jit(solution)/shard_map/ppermute | solution.py:27
  (25 other events, 302.0 us)

commit v8 on v7

--- a/solution.py
+++ b/solution.py
@@ -262,19 +262,19 @@
     far_before, far_after = along_y(far, 1), along_y(far, -1)
     near_across, far_across = along_y(near_before, 1), along_y(far_after, -1)
     pieces = (near, far, near_after, far_after, near_across, far_across, near_before, far_before)
-    ready, weights[0], pieces = together(sliced[1], weights[0], pieces)
-    weights.append(lax.all_to_all(ready, "z", 0, 0, tiled=True))
-
-    keep, *gives = project(place, weights[0], swap_core(weights[0]), pieces, ())
-    gots = [swap_xh(give) for give in gives]
-    hiddens = [activate(keep, gots)]
-
     down_weight, _ = together(down_weight, far)
     moved = send(
         down_weight,
         lambda xl, y, c, z, xh: (xl, y, 1 - c, z, 1 - xh) if c != xh else None,
     )
-    moved, weights[1], _ = together(moved, weights[1], gots[0])
+    ready, weights[0], pieces, moved = together(sliced[1], weights[0], pieces, moved)
+    weights.append(lax.all_to_all(ready, "z", 0, 0, tiled=True))
+
+    keep, *gives = project(place, weights[0], swap_core(weights[0]), pieces, ())
+    gots = [swap_xh(give) for give in gives]
+    hiddens = [activate(keep, gots)]
+
+    weights[1], _ = together(weights[1], gots[0])
     mine = jnp.where(c == xh, down_weight, moved)
 
     both = together(weights[1], swap_core(weights[1]), hiddens[0])

time: 227 us -> 221 us (0.974)
  starting transfers between devices: 72.8 us -> 56.2 us
  waiting for transfers between devices: 99.3 us -> 110 us
    ppermute x36, starting transfers between devices: 61.4 us -> 45.7 us  [send(): return lax.ppermute(value, AXES, pairs)]
    ppermute x36, waiting for transfers between devices: 78.3 us -> 84 us  [send(): return lax.ppermute(value, AXES, pairs)]
    all_to_all x1, waiting for transfers between devices: 21 us -> 25.9 us  [shards(): weights.append(lax.all_to_all(ready, 'z', 0, 0, tiled=True))]
where the time goes in v8:
time: 221 us
  waiting for transfers between devices  110 us (50%)
  starting transfers between devices  56.2 us (25%)
  Pallas kernels  25.2 us (11%)
  blocking collectives  23.2 us (10%)
  local copies, waits for them, and re-layouts  4.94 us (2%)
    ppermute x36, waiting for transfers between devices, send(): return lax.ppermute(value, AXES, pairs)  84 us
    ppermute x36, starting transfers between devices, send(): return lax.ppermute(value, AXES, pairs)  45.7 us
    all_to_all x1, waiting for transfers between devices, shards(): weights.append(lax.all_to_all(ready, 'z', 0, 0, tiled=True))  25.9 us
    all_to_all x1, blocking collectives, shards(): got = lax.all_to_all(out, ('xh', 'y', 'xl'), 0, 0, tiled=True)  23.2 us
    pallas_call x2, Pallas kernels, project(): pl.pallas_call(body, in_specs=[SCALARS] + [pl.BlockSpec(memory_space=pl.A...  15 us
    all_to_all x1, starting transfers between devices, shards(): weights.append(lax.all_to_all(ready, 'z', 0, 0, tiled=True))  6.76 us
  transfers between devices with their start and end apart: 38, of which 19 were waited for; matrix products, arithmetic and copies ran while one was open for 0% of the time, Pallas kernels for 6%

profile of v8, /device:TPU:2, one launch (start us, length us, event | category | flops | bytes accessed | tf_op | source)
XLA Modules:
  0.0 220.8 jit_solution(5436956385870319934)
XLA Ops:
  0.0 6.3 %collective-permute-start.4 = (bf16[96,512]{1,0:T(8,128)(2,1)}, bf16[96,512]{1,0:T(8,128)(2,1)S(1)}, u32[]{:S(2)}, u32[]{:S(2)}) collective-permute-start(bf16[96,512]{1,0:T(8,128)(2,1)} %rest_0_.1), channel_id=1, source_target_pairs={{0,12},{1,13},{2,14},{3,15},{4,0},{5,1},{6,2},{7,3},{8,4},{9,5},{1... | collective-permute-start | bytes 294920 | tf_op jit(solution)/shard_map/ppermute | solution.py:27
  6.3 3.8 %collective-permute-start.3 = (bf16[96,512]{1,0:T(8,128)(2,1)}, bf16[96,512]{1,0:T(8,128)(2,1)S(1)}, u32[]{:S(2)}, u32[]{:S(2)}) collective-permute-start(bf16[96,512]{1,0:T(8,128)(2,1)} %rest_0_.1), channel_id=1, source_target_pairs={{0,8},{1,9},{2,10},{3,11},{4,12},{5,13},{6,14},{7,15},{8,0},{9,1},... | collective-permute-start | bytes 294920 | tf_op jit(solution)/shard_map/ppermute | solution.py:27
  11.1 2.2 %collective-permute-start.6 = (bf16[96,512]{1,0:T(8,128)(2,1)}, bf16[96,512]{1,0:T(8,128)(2,1)S(1)}, u32[]{:S(2)}, u32[]{:S(2)}) collective-permute-start(bf16[96,512]{1,0:T(8,128)(2,1)} %rest_0_.1), channel_id=1, source_target_pairs={{0,14},{1,15},{2,0},{3,1},{4,2},{5,3},{6,4},{7,5},{8,6},{9,7},{10,... | collective-permute-start | bytes 294920 | tf_op jit(solution)/shard_map/ppermute | solution.py:27
  13.5 4.0 %collective-permute-done.1.rest_2_ = bf16[96,512]{1,0:T(8,128)(2,1)S(1)} collective-permute-done((bf16[96,512]{1,0:T(8,128)(2,1)}, bf16[96,512]{1,0:T(8,128)(2,1)S(1)}, u32[]{:S(2)}, u32[]{:S(2)}) %collective-permute-start.1) | collective-permute-done | bytes 98336 | tf_op jit(solution)/shard_map/ppermute | solution.py:27
  17.5 2.9 %collective-permute-start.2 = (bf16[96,512]{1,0:T(8,128)(2,1)S(1)}, bf16[96,512]{1,0:T(8,128)(2,1)S(1)}, u32[]{:S(2)}, u32[]{:S(2)}) collective-permute-start(bf16[96,512]{1,0:T(8,128)(2,1)S(1)} %collective-permute-done.1.rest_2_), channel_id=1, source_target_pairs={{0,2},{1,3},{2,4},{3,5},{4,6},{5,7},{6,8},{7,9},{8,10},{9,11},{10,... | collective-permute-start | bytes 294920 | tf_op jit(solution)/shard_map/ppermute | solution.py:27
  20.5 3.9 %slice_units.1 = (bf16[8,288,512]{2,1,0:T(8,128)(2,1)}, bf16[8,160,512]{2,1,0:T(8,128)(2,1)}) custom-call(bf16[512,1792]{1,0:T(8,128)(2,1)} %g_ref.1, bf16[512,1792]{1,0:T(8,128)(2,1)} %u_ref.1), custom_call_target="tpu_custom_call" | custom-call | bytes 114688 | tf_op jit(solution)/shard_map/slice_units/pallas_call | solution.py:94
  26.4 2.2 regroup.1.rest_0_
  28.6 3.7 %all-to-all-start = ((bf16[8,288,512]{2,1,0:T(8,128)(2,1)}), bf16[8,288,512]{2,1,0:T(8,128)(2,1)S(1)}, u32[]{:S(2)}, u32[]{:S(2)}) async-start(bf16[8,288,512]{2,1,0:T(8,128)(2,1)} %get-tuple-element.40), calls=%async_computation | async-start | bytes 4718592 | tf_op jit(solution)/shard_map/all_to_all | solution.py:257
  32.3 3.1 %collective-permute-start.9 = (bf16[8,96,512]{2,1,0:T(8,128)(2,1)S(1)}, bf16[8,96,512]{2,1,0:T(8,128)(2,1)S(1)}, u32[]{:S(2)}, u32[]{:S(2)}) collective-permute-start(bf16[8,96,512]{2,1,0:T(8,128)(2,1)S(1)} %copy-done.4), channel_id=1, source_target_pairs={{0,96},{1,97},{2,98},{3,99},{4,100},{5,101},{6,102},{7,103},{8,104... | collective-permute-start | bytes 2359304 | tf_op jit(solution)/shard_map/ppermute | solution.py:27
  36.0 12.4 %collective-permute-done.9.rest_2_ = bf16[8,96,512]{2,1,0:T(8,128)(2,1)S(1)} collective-permute-done((bf16[8,96,512]{2,1,0:T(8,128)(2,1)S(1)}, bf16[8,96,512]{2,1,0:T(8,128)(2,1)S(1)}, u32[]{:S(2)}, u32[]{:S(2)}) %collective-permute-start.9) | collective-permute-done | bytes 786464 | tf_op jit(solution)/shard_map/ppermute | solution.py:27
  48.4 3.4 %collective-permute-done.8.rest_6_ = bf16[8,96,512]{2,1,0:T(8,128)(2,1)S(1)} collective-permute-done((bf16[8,96,512]{2,1,0:T(8,128)(2,1)S(1)}, bf16[8,96,512]{2,1,0:T(8,128)(2,1)S(1)}, u32[]{:S(2)}, u32[]{:S(2)}) %collective-permute-start.8) | collective-permute-done | bytes 786464 | tf_op jit(solution)/shard_map/ppermute | solution.py:27
  55.8 17.0 %collective-permute-done.10.rest_3_ = bf16[8,96,512]{2,1,0:T(8,128)(2,1)S(1)} collective-permute-done((bf16[8,96,512]{2,1,0:T(8,128)(2,1)S(1)}, bf16[8,96,512]{2,1,0:T(8,128)(2,1)S(1)}, u32[]{:S(2)}, u32[]{:S(2)}) %collective-permute-start.10) | collective-permute-done | bytes 786464 | tf_op jit(solution)/shard_map/ppermute | solution.py:27
  72.8 2.9 %collective-permute-start.12 = (bf16[8,96,512]{2,1,0:T(8,128)(2,1)S(1)}, bf16[8,96,512]{2,1,0:T(8,128)(2,1)S(1)}, u32[]{:S(2)}, u32[]{:S(2)}) collective-permute-start(bf16[8,96,512]{2,1,0:T(8,128)(2,1)S(1)} %collective-permute-done.10.rest_3_), channel_id=1, source_target_pairs={{0,96},{1,97},{2,98},{3,99},{4,100},{5,101},{6,102},{7,103},{8,104... | collective-permute-start | bytes 2359304 | tf_op jit(solution)/shard_map/ppermute | solution.py:27
  75.7 17.2 %collective-permute-done.11.rest_4_ = bf16[8,96,512]{2,1,0:T(8,128)(2,1)S(1)} collective-permute-done((bf16[8,96,512]{2,1,0:T(8,128)(2,1)S(1)}, bf16[8,96,512]{2,1,0:T(8,128)(2,1)S(1)}, u32[]{:S(2)}, u32[]{:S(2)}) %collective-permute-start.11) | collective-permute-done | bytes 786464 | tf_op jit(solution)/shard_map/ppermute | solution.py:27
  95.9 6.8 %all-to-all-start.1 = ((bf16[8,160,512]{2,1,0:T(8,128)(2,1)}), bf16[8,160,512]{2,1,0:T(8,128)(2,1)}, u32[]{:S(2)}, u32[]{:S(2)}) async-start(bf16[8,160,512]{2,1,0:T(8,128)(2,1)} %get-tuple-element.57), calls=%async_computation.1 | async-start | bytes 2621440 | tf_op jit(solution)/shard_map/all_to_all | solution.py:271
  102.7 8.6 %project.2 = (f32[288,768]{1,0:T(8,128)}, f32[288,768]{1,0:T(8,128)}) custom-call(s32[5]{0:T(128)} %stack.23.place_ref, bf16[8,288,512]{2,1,0:T(8,128)(2,1)} %copy-done.3, bf16[8,288,512]{2,1,0:T(8,128)(2,1)} %collective-permute-done.15.other_ref, bf16[8,96,512]{2,1,0:T(8,128)(2,1)} %regroup.1.rest_0_, bf16[8,96,512]{2,1,0:T(8,128)(2,1)} %copy-done.7, ...), custom_call_target="tpu_custom_call" | custom-call | flops 56623104 | bytes 172032 | tf_op jit(solution)/shard_map/project/pallas_call | solution.py:154
  111.4 25.9 %all-to-all-done.1.own_ref = bf16[8,160,512]{2,1,0:T(8,128)(2,1)} async-done(((bf16[8,160,512]{2,1,0:T(8,128)(2,1)}), bf16[8,160,512]{2,1,0:T(8,128)(2,1)}, u32[]{:S(2)}, u32[]{:S(2)}) %all-to-all-start.1) | async-done | bytes 1310752 | tf_op jit(solution)/shard_map/all_to_all | solution.py:271
  138.7 2.0 collective-permute-done.17.other_ref
  140.7 6.5 %project.3 = (f32[160,768]{1,0:T(8,128)}, f32[160,768]{1,0:T(8,128)}) custom-call(s32[5]{0:T(128)} %stack.23.place_ref, bf16[8,160,512]{2,1,0:T(8,128)(2,1)} %all-to-all-done.1.own_ref, bf16[8,160,512]{2,1,0:T(8,128)(2,1)} %collective-permute-done.17.other_ref, bf16[8,96,512]{2,1,0:T(8,128)(2,1)} %regroup.1.rest_0_, bf16[8,96,512]{2,1,0:T(8,128)(2,1)} %copy-done.7, ...), custom_call_target="tpu_custom_call" | custom-call | flops 31457280 | bytes 139264 | tf_op jit(solution)/shard_map/project/pallas_call | solution.py:154
  147.3 2.0 collective-permute-start.18
  149.3 5.4 %collective-permute-done.20.rest_8_ = bf16[144,768]{1,0:T(8,128)(2,1)S(1)} collective-permute-done((bf16[144,768]{1,0:T(8,128)(2,1)S(1)}, bf16[144,768]{1,0:T(8,128)(2,1)S(1)}, u32[]{:S(2)}, u32[]{:S(2)}) %collective-permute-start.20) | collective-permute-done | bytes 221216 | tf_op jit(solution)/shard_map/ppermute | solution.py:27
  157.0 4.4 %collective-permute-done.21.rest_7_ = bf16[144,768]{1,0:T(8,128)(2,1)S(1)} collective-permute-done((bf16[144,768]{1,0:T(8,128)(2,1)S(1)}, bf16[144,768]{1,0:T(8,128)(2,1)S(1)}, u32[]{:S(2)}, u32[]{:S(2)}) %collective-permute-start.21) | collective-permute-done | bytes 221216 | tf_op jit(solution)/shard_map/ppermute | solution.py:27
  161.4 2.7 %collective-permute-done.19.rest_2_ = bf16[144,768]{1,0:T(8,128)(2,1)S(1)} collective-permute-done((bf16[144,768]{1,0:T(8,128)(2,1)S(1)}, bf16[144,768]{1,0:T(8,128)(2,1)S(1)}, u32[]{:S(2)}, u32[]{:S(2)}) %collective-permute-start.19) | collective-permute-done | bytes 221216 | tf_op jit(solution)/shard_map/ppermute | solution.py:27
  166.5 3.1 %collective-permute-start.26 = (bf16[144,768]{1,0:T(8,128)(2,1)S(1)}, bf16[144,768]{1,0:T(8,128)(2,1)S(1)}, u32[]{:S(2)}, u32[]{:S(2)}) collective-permute-start(bf16[144,768]{1,0:T(8,128)(2,1)S(1)} %collective-permute-done.21.rest_7_), channel_id=1, source_target_pairs={{0,14},{1,15},{2,0},{3,1},{4,2},{5,3},{6,4},{7,5},{8,6},{9,7},{10,... | collective-permute-start | bytes 663560 | tf_op jit(solution)/shard_map/ppermute | solution.py:27
  170.5 2.0 collective-permute-start.31
  172.9 4.7 %collective-permute-done.24.rest_3_ = bf16[144,768]{1,0:T(8,128)(2,1)S(1)} collective-permute-done((bf16[144,768]{1,0:T(8,128)(2,1)S(1)}, bf16[144,768]{1,0:T(8,128)(2,1)S(1)}, u32[]{:S(2)}, u32[]{:S(2)}) %collective-permute-start.24) | collective-permute-done | bytes 221216 | tf_op jit(solution)/shard_map/ppermute | solution.py:27
  177.6 1.9 collective-permute-done.29.rest_11_
  181.6 2.2 collective-permute-start.27
  187.8 2.2 collective-permute-done.25.rest_4_
  190.0 2.9 %collective-permute-done.33.rest_13_ = bf16[32,768]{1,0:T(8,128)(2,1)S(1)} collective-permute-done((bf16[32,768]{1,0:T(8,128)(2,1)S(1)}, bf16[32,768]{1,0:T(8,128)(2,1)S(1)}, u32[]{:S(2)}, u32[]{:S(2)}) %collective-permute-start.33) | collective-permute-done | bytes 49184 | tf_op jit(solution)/shard_map/ppermute | solution.py:27
  192.9 3.8 %mix.1 = bf16[2,768,512]{2,1,0:T(8,128)(2,1)S(1)} custom-call(s32[5]{0:T(128)S(1)} %copy-done.2, bf16[1792,512]{1,0:T(8,128)(2,1)S(1)} %broadcast_select_fusion.mine_ref, bf16[1792,512]{1,0:T(8,128)(2,1)S(1)} %collective-permute-done.23.theirs_ref, bf16[144,768]{1,0:T(8,128)(2,1)S(1)} %activate.2.rest_0_, ...), custom_call_target="tpu_custom_call" | custom-call | flops 44040192 | bytes 100352 | tf_op jit(solution)/shard_map/mix/pallas_call | solution.py:219
  196.7 23.2 %all_to_all.15 = bf16[16,96,512]{2,1,0:T(8,128)(2,1)S(1)} all-to-all(bf16[16,96,512]{2,1,0:T(8,128)(2,1)S(1)} %bitcast.6), channel_id=1, replica_groups=mesh['xl'=2,'y'=4,'c'=2,'z'=8,'xh'=2] {'xh','y','xl'}, dimensions={0} | all-to-all | bytes 3145728 | tf_op jit(solution)/shard_map/all_to_all | solution.py:289
  (99 shorter events, 25.1 us)
Async XLA Ops:
  0.0 13.4 %collective-permute-start.4 = (bf16[96,512]{1,0:T(8,128)(2,1)}, bf16[96,512]{1,0:T(8,128)(2,1)S(1)}, u32[]{:S(2)}, u32[]{:S(2)}) collective-permute-start(bf16[96,512]{1,0:T(8,128)(2,1)} %rest_0_.1), channel_id=1, source_target_pairs={{0,12},{1,13},{2,14},{3,15},{4,0},{5,1},{6,2},{7,3},{8,4},{9,5},{1... | collective-permute-start | bytes 294920 | tf_op jit(solution)/shard_map/ppermute | solution.py:27
  6.3 11.2 %collective-permute-start.1 = (bf16[96,512]{1,0:T(8,128)(2,1)}, bf16[96,512]{1,0:T(8,128)(2,1)S(1)}, u32[]{:S(2)}, u32[]{:S(2)}) collective-permute-start(bf16[96,512]{1,0:T(8,128)(2,1)} %rest_0_.1), channel_id=1, source_target_pairs={{0,4},{1,5},{2,6},{3,7},{4,8},{5,9},{6,10},{7,11},{8,12},{9,13},{1... | collective-permute-start | bytes 294920 | tf_op jit(solution)/shard_map/ppermute | solution.py:27
  6.3 18.7 %collective-permute-start.3 = (bf16[96,512]{1,0:T(8,128)(2,1)}, bf16[96,512]{1,0:T(8,128)(2,1)S(1)}, u32[]{:S(2)}, u32[]{:S(2)}) collective-permute-start(bf16[96,512]{1,0:T(8,128)(2,1)} %rest_0_.1), channel_id=1, source_target_pairs={{0,8},{1,9},{2,10},{3,11},{4,12},{5,13},{6,14},{7,15},{8,0},{9,1},... | collective-permute-start | bytes 294920 | tf_op jit(solution)/shard_map/ppermute | solution.py:27
  10.1 14.9 %collective-permute-start = (bf16[96,512]{1,0:T(8,128)(2,1)}, bf16[96,512]{1,0:T(8,128)(2,1)S(1)}, u32[]{:S(2)}, u32[]{:S(2)}) collective-permute-start(bf16[96,512]{1,0:T(8,128)(2,1)} %rest_0_.1), channel_id=1, source_target_pairs={{0,2},{1,3},{2,4},{3,5},{4,6},{5,7},{6,8},{7,9},{8,10},{9,11},{10,... | collective-permute-start | bytes 294920 | tf_op jit(solution)/shard_map/ppermute | solution.py:27
  11.1 13.9 %collective-permute-start.6 = (bf16[96,512]{1,0:T(8,128)(2,1)}, bf16[96,512]{1,0:T(8,128)(2,1)S(1)}, u32[]{:S(2)}, u32[]{:S(2)}) collective-permute-start(bf16[96,512]{1,0:T(8,128)(2,1)} %rest_0_.1), channel_id=1, source_target_pairs={{0,14},{1,15},{2,0},{3,1},{4,2},{5,3},{6,4},{7,5},{8,6},{9,7},{10,... | collective-permute-start | bytes 294920 | tf_op jit(solution)/shard_map/ppermute | solution.py:27
  13.4 11.7 %collective-permute-start.5 = (bf16[96,512]{1,0:T(8,128)(2,1)S(1)}, bf16[96,512]{1,0:T(8,128)(2,1)S(1)}, u32[]{:S(2)}, u32[]{:S(2)}) collective-permute-start(bf16[96,512]{1,0:T(8,128)(2,1)S(1)} %collective-permute-done.4.rest_6_), channel_id=1, source_target_pairs={{0,14},{1,15},{2,0},{3,1},{4,2},{5,3},{6,4},{7,5},{8,6},{9,7},{10,... | collective-permute-start | bytes 294920 | tf_op jit(solution)/shard_map/ppermute | solution.py:27
  17.5 7.5 %collective-permute-start.2 = (bf16[96,512]{1,0:T(8,128)(2,1)S(1)}, bf16[96,512]{1,0:T(8,128)(2,1)S(1)}, u32[]{:S(2)}, u32[]{:S(2)}) collective-permute-start(bf16[96,512]{1,0:T(8,128)(2,1)S(1)} %collective-permute-done.1.rest_2_), channel_id=1, source_target_pairs={{0,2},{1,3},{2,4},{3,5},{4,6},{5,7},{6,8},{7,9},{8,10},{9,11},{10,... | collective-permute-start | bytes 294920 | tf_op jit(solution)/shard_map/ppermute | solution.py:27
  28.6 66.3 %all-to-all-start = ((bf16[8,288,512]{2,1,0:T(8,128)(2,1)}), bf16[8,288,512]{2,1,0:T(8,128)(2,1)S(1)}, u32[]{:S(2)}, u32[]{:S(2)}) async-start(bf16[8,288,512]{2,1,0:T(8,128)(2,1)} %get-tuple-element.40), calls=%async_computation | async-start | bytes 4718592 | tf_op jit(solution)/shard_map/all_to_all | solution.py:257
  32.3 16.1 %collective-permute-start.9 = (bf16[8,96,512]{2,1,0:T(8,128)(2,1)S(1)}, bf16[8,96,512]{2,1,0:T(8,128)(2,1)S(1)}, u32[]{:S(2)}, u32[]{:S(2)}) collective-permute-start(bf16[8,96,512]{2,1,0:T(8,128)(2,1)S(1)} %copy-done.4), channel_id=1, source_target_pairs={{0,96},{1,97},{2,98},{3,99},{4,100},{5,101},{6,102},{7,103},{8,104... | collective-permute-start | bytes 2359304 | tf_op jit(solution)/shard_map/ppermute | solution.py:27
  35.4 16.4 %collective-permute-start.8 = (bf16[8,96,512]{2,1,0:T(8,128)(2,1)S(1)}, bf16[8,96,512]{2,1,0:T(8,128)(2,1)S(1)}, u32[]{:S(2)}, u32[]{:S(2)}) collective-permute-start(bf16[8,96,512]{2,1,0:T(8,128)(2,1)S(1)} %copy-done.4), channel_id=1, source_target_pairs={{0,32},{1,33},{2,34},{3,35},{4,36},{5,37},{6,38},{7,39},{8,40},{9,... | collective-permute-start | bytes 2359304 | tf_op jit(solution)/shard_map/ppermute | solution.py:27
  35.4 16.4 %collective-permute-start.7 = (bf16[8,96,512]{2,1,0:T(8,128)(2,1)S(1)}, bf16[8,96,512]{2,1,0:T(8,128)(2,1)S(1)}, u32[]{:S(2)}, u32[]{:S(2)}) collective-permute-start(bf16[8,96,512]{2,1,0:T(8,128)(2,1)S(1)} %copy-done.4), channel_id=1, source_target_pairs={{0,128},{1,129},{2,130},{3,131},{4,132},{5,133},{6,134},{7,135},{8... | collective-permute-start | bytes 2359304 | tf_op jit(solution)/shard_map/ppermute | solution.py:27
  51.8 43.1 %collective-permute-start.14 = (bf16[1792,512]{1,0:T(8,128)(2,1)}, bf16[1792,512]{1,0:T(8,128)(2,1)}, u32[]{:S(2)}, u32[]{:S(2)}) collective-permute-start(bf16[1792,512]{1,0:T(8,128)(2,1)} %param.7), channel_id=1, source_target_pairs={{1,16},{3,18},{5,20},{7,22},{9,24},{11,26},{13,28},{15,30},{16,1},... | collective-permute-start | bytes 5505032 | tf_op jit(solution)/shard_map/ppermute | solution.py:27
  53.7 19.0 %collective-permute-start.10 = (bf16[8,96,512]{2,1,0:T(8,128)(2,1)S(1)}, bf16[8,96,512]{2,1,0:T(8,128)(2,1)S(1)}, u32[]{:S(2)}, u32[]{:S(2)}) collective-permute-start(bf16[8,96,512]{2,1,0:T(8,128)(2,1)S(1)} %collective-permute-done.7.rest_1_), channel_id=1, source_target_pairs={{0,96},{1,97},{2,98},{3,99},{4,100},{5,101},{6,102},{7,103},{8,104... | collective-permute-start | bytes 2359304 | tf_op jit(solution)/shard_map/ppermute | solution.py:27
  55.5 37.4 %collective-permute-start.13 = (bf16[8,96,512]{2,1,0:T(8,128)(2,1)S(1)}, bf16[8,96,512]{2,1,0:T(8,128)(2,1)S(1)}, u32[]{:S(2)}, u32[]{:S(2)}) collective-permute-start(bf16[8,96,512]{2,1,0:T(8,128)(2,1)S(1)} %collective-permute-done.7.rest_1_), channel_id=1, source_target_pairs={{0,32},{1,33},{2,34},{3,35},{4,36},{5,37},{6,38},{7,39},{8,40},{9,... | collective-permute-start | bytes 2359304 | tf_op jit(solution)/shard_map/ppermute | solution.py:27
  55.8 37.1 %collective-permute-start.11 = (bf16[8,96,512]{2,1,0:T(8,128)(2,1)S(1)}, bf16[8,96,512]{2,1,0:T(8,128)(2,1)S(1)}, u32[]{:S(2)}, u32[]{:S(2)}) collective-permute-start(bf16[8,96,512]{2,1,0:T(8,128)(2,1)S(1)} %collective-permute-done.8.rest_6_), channel_id=1, source_target_pairs={{0,32},{1,33},{2,34},{3,35},{4,36},{5,37},{6,38},{7,39},{8,40},{9,... | collective-permute-start | bytes 2359304 | tf_op jit(solution)/shard_map/ppermute | solution.py:27
  72.8 20.4 %collective-permute-start.12 = (bf16[8,96,512]{2,1,0:T(8,128)(2,1)S(1)}, bf16[8,96,512]{2,1,0:T(8,128)(2,1)S(1)}, u32[]{:S(2)}, u32[]{:S(2)}) collective-permute-start(bf16[8,96,512]{2,1,0:T(8,128)(2,1)S(1)} %collective-permute-done.10.rest_3_), channel_id=1, source_target_pairs={{0,96},{1,97},{2,98},{3,99},{4,100},{5,101},{6,102},{7,103},{8,104... | collective-permute-start | bytes 2359304 | tf_op jit(solution)/shard_map/ppermute | solution.py:27
  94.9 7.8 %collective-permute-start.15 = (bf16[8,288,512]{2,1,0:T(8,128)(2,1)S(1)}, bf16[8,288,512]{2,1,0:T(8,128)(2,1)}, u32[]{:S(2)}, u32[]{:S(2)}) collective-permute-start(bf16[8,288,512]{2,1,0:T(8,128)(2,1)S(1)} %all-to-all-done.own_ref), channel_id=1, source_target_pairs={{0,16},{1,17},{2,18},{3,19},{4,20},{5,21},{6,22},{7,23},{8,24},{9,... | collective-permute-start | bytes 7077896 | tf_op jit(solution)/shard_map/ppermute | solution.py:27
  95.9 41.4 %all-to-all-start.1 = ((bf16[8,160,512]{2,1,0:T(8,128)(2,1)}), bf16[8,160,512]{2,1,0:T(8,128)(2,1)}, u32[]{:S(2)}, u32[]{:S(2)}) async-start(bf16[8,160,512]{2,1,0:T(8,128)(2,1)} %get-tuple-element.57), calls=%async_computation.1 | async-start | bytes 2621440 | tf_op jit(solution)/shard_map/all_to_all | solution.py:271
  111.3 26.1 %collective-permute-start.16 = (f32[288,768]{1,0:T(8,128)}, f32[288,768]{1,0:T(8,128)S(1)}, u32[]{:S(2)}, u32[]{:S(2)}) collective-permute-start(f32[288,768]{1,0:T(8,128)} %get-tuple-element.56), channel_id=1, source_target_pairs={{0,1},{1,0},{2,3},{3,2},{4,5},{5,4},{6,7},{7,6},{8,9},{9,8},{10,11... | collective-permute-start | bytes 2654216 | tf_op jit(solution)/shard_map/ppermute | solution.py:27
  147.2 7.6 %collective-permute-start.20 = (bf16[144,768]{1,0:T(8,128)(2,1)S(1)}, bf16[144,768]{1,0:T(8,128)(2,1)S(1)}, u32[]{:S(2)}, u32[]{:S(2)}) collective-permute-start(bf16[144,768]{1,0:T(8,128)(2,1)S(1)} %activate.2.rest_0_), channel_id=1, source_target_pairs={{0,14},{1,15},{2,0},{3,1},{4,2},{5,3},{6,4},{7,5},{8,6},{9,7},{10,... | collective-permute-start | bytes 663560 | tf_op jit(solution)/shard_map/ppermute | solution.py:27
  147.3 9.0 %collective-permute-start.18 = (bf16[144,768]{1,0:T(8,128)(2,1)S(1)}, bf16[144,768]{1,0:T(8,128)(2,1)S(1)}, u32[]{:S(2)}, u32[]{:S(2)}) collective-permute-start(bf16[144,768]{1,0:T(8,128)(2,1)S(1)} %activate.2.rest_0_), channel_id=1, source_target_pairs={{0,2},{1,3},{2,4},{3,5},{4,6},{5,7},{6,8},{7,9},{8,10},{9,11},{10,... | collective-permute-start | bytes 663560 | tf_op jit(solution)/shard_map/ppermute | solution.py:27
  149.3 14.8 %collective-permute-start.22 = (f32[160,768]{1,0:T(8,128)}, f32[160,768]{1,0:T(8,128)S(1)}, u32[]{:S(2)}, u32[]{:S(2)}) collective-permute-start(f32[160,768]{1,0:T(8,128)} %get-tuple-element.61), channel_id=1, source_target_pairs={{0,1},{1,0},{2,3},{3,2},{4,5},{5,4},{6,7},{7,6},{8,9},{9,8},{10,11... | collective-permute-start | bytes 1474568 | tf_op jit(solution)/shard_map/ppermute | solution.py:27
  156.3 7.9 %collective-permute-start.19 = (bf16[144,768]{1,0:T(8,128)(2,1)S(1)}, bf16[144,768]{1,0:T(8,128)(2,1)S(1)}, u32[]{:S(2)}, u32[]{:S(2)}) collective-permute-start(bf16[144,768]{1,0:T(8,128)(2,1)S(1)} %collective-permute-done.18.rest_1_), channel_id=1, source_target_pairs={{0,2},{1,3},{2,4},{3,5},{4,6},{5,7},{6,8},{7,9},{8,10},{9,11},{10,... | collective-permute-start | bytes 663560 | tf_op jit(solution)/shard_map/ppermute | solution.py:27
  164.1 28.7 %collective-permute-start.23 = (bf16[1792,512]{1,0:T(8,128)(2,1)S(1)}, bf16[1792,512]{1,0:T(8,128)(2,1)S(1)}, u32[]{:S(2)}, u32[]{:S(2)}) collective-permute-start(bf16[1792,512]{1,0:T(8,128)(2,1)S(1)} %broadcast_select_fusion.mine_ref), channel_id=1, source_target_pairs={{0,16},{1,17},{2,18},{3,19},{4,20},{5,21},{6,22},{7,23},{8,24},{9,... | collective-permute-start | bytes 5505032 | tf_op jit(solution)/shard_map/ppermute | solution.py:27
  165.5 7.4 %collective-permute-start.28 = (bf16[80,768]{1,0:T(8,128)(2,1)S(1)}, bf16[80,768]{1,0:T(8,128)(2,1)S(1)}, u32[]{:S(2)}, u32[]{:S(2)}) collective-permute-start(bf16[80,768]{1,0:T(8,128)(2,1)S(1)} %activate.3.rest_9_), channel_id=1, source_target_pairs={{0,2},{1,3},{2,4},{3,5},{4,6},{5,7},{6,8},{7,9},{8,10},{9,11},{10,... | collective-permute-start | bytes 368648 | tf_op jit(solution)/shard_map/ppermute | solution.py:27
  166.4 11.2 %collective-permute-start.24 = (bf16[144,768]{1,0:T(8,128)(2,1)S(1)}, bf16[144,768]{1,0:T(8,128)(2,1)S(1)}, u32[]{:S(2)}, u32[]{:S(2)}) collective-permute-start(bf16[144,768]{1,0:T(8,128)(2,1)S(1)} %collective-permute-done.19.rest_2_), channel_id=1, source_target_pairs={{0,2},{1,3},{2,4},{3,5},{4,6},{5,7},{6,8},{7,9},{8,10},{9,11},{10,... | collective-permute-start | bytes 663560 | tf_op jit(solution)/shard_map/ppermute | solution.py:27
  166.5 11.1 %collective-permute-start.26 = (bf16[144,768]{1,0:T(8,128)(2,1)S(1)}, bf16[144,768]{1,0:T(8,128)(2,1)S(1)}, u32[]{:S(2)}, u32[]{:S(2)}) collective-permute-start(bf16[144,768]{1,0:T(8,128)(2,1)S(1)} %collective-permute-done.21.rest_7_), channel_id=1, source_target_pairs={{0,14},{1,15},{2,0},{3,1},{4,2},{5,3},{6,4},{7,5},{8,6},{9,7},{10,... | collective-permute-start | bytes 663560 | tf_op jit(solution)/shard_map/ppermute | solution.py:27
  170.5 7.2 %collective-permute-start.31 = (bf16[80,768]{1,0:T(8,128)(2,1)S(1)}, bf16[80,768]{1,0:T(8,128)(2,1)S(1)}, u32[]{:S(2)}, u32[]{:S(2)}) collective-permute-start(bf16[80,768]{1,0:T(8,128)(2,1)S(1)} %collective-permute-done.30.rest_17_), channel_id=1, source_target_pairs={{0,14},{1,15},{2,0},{3,1},{4,2},{5,3},{6,4},{7,5},{8,6},{9,7},{10,... | collective-permute-start | bytes 368648 | tf_op jit(solution)/shard_map/ppermute | solution.py:27
  172.9 6.7 %collective-permute-start.29 = (bf16[80,768]{1,0:T(8,128)(2,1)S(1)}, bf16[80,768]{1,0:T(8,128)(2,1)S(1)}, u32[]{:S(2)}, u32[]{:S(2)}) collective-permute-start(bf16[80,768]{1,0:T(8,128)(2,1)S(1)} %collective-permute-done.28.rest_10_), channel_id=1, source_target_pairs={{0,2},{1,3},{2,4},{3,5},{4,6},{5,7},{6,8},{7,9},{8,10},{9,11},{10,... | collective-permute-start | bytes 368648 | tf_op jit(solution)/shard_map/ppermute | solution.py:27
  180.4 7.1 %collective-permute-start.32 = (bf16[80,768]{1,0:T(8,128)(2,1)S(1)}, bf16[80,768]{1,0:T(8,128)(2,1)S(1)}, u32[]{:S(2)}, u32[]{:S(2)}) collective-permute-start(bf16[80,768]{1,0:T(8,128)(2,1)S(1)} %collective-permute-done.29.rest_11_), channel_id=1, source_target_pairs={{0,2},{1,3},{2,4},{3,5},{4,6},{5,7},{6,8},{7,9},{8,10},{9,11},{10,... | collective-permute-start | bytes 368648 | tf_op jit(solution)/shard_map/ppermute | solution.py:27
  181.6 8.4 %collective-permute-start.27 = (bf16[80,768]{1,0:T(8,128)(2,1)S(1)}, bf16[80,768]{1,0:T(8,128)(2,1)S(1)}, u32[]{:S(2)}, u32[]{:S(2)}) collective-permute-start(bf16[80,768]{1,0:T(8,128)(2,1)S(1)} %slice.17), channel_id=1, source_target_pairs={{0,14},{1,15},{2,0},{3,1},{4,2},{5,3},{6,4},{7,5},{8,6},{9,7},{10,... | collective-permute-start | bytes 368648 | tf_op jit(solution)/shard_map/ppermute | solution.py:27
  185.7 7.2 %collective-permute-start.35 = (bf16[48,768]{1,0:T(8,128)(2,1)S(1)}, bf16[48,768]{1,0:T(8,128)(2,1)S(1)}, u32[]{:S(2)}, u32[]{:S(2)}) collective-permute-start(bf16[48,768]{1,0:T(8,128)(2,1)S(1)} %slice.19), channel_id=1, source_target_pairs={{0,14},{1,15},{2,0},{3,1},{4,2},{5,3},{6,4},{7,5},{8,6},{9,7},{10,... | collective-permute-start | bytes 221192 | tf_op jit(solution)/shard_map/ppermute | solution.py:27
  (26 other events, 304.6 us)

commit v9 on v8

--- a/solution.py
+++ b/solution.py
@@ -197,7 +197,7 @@
     sizes = [ring[0].shape[0] for ring in rings]
     units, rows = sum(sizes), rings[0][0].shape[1]
     width = mine.shape[1]
-    order = (0, 1, 2, 3, 4, -4, -3, -2, -1)
+    order = (0, 1, 2, 3, 4, -3, -2, -1)
     parts = [ring[s] for ring in rings for s in order]
 
     def body(place_ref, mine_ref, theirs_ref, *rest):
@@ -206,10 +206,8 @@
         first = 0
         for size in sizes:
             for s in order:
-                part_ref = part_refs.pop(0)
-                length = part_ref.shape[0]
-                at = ((z - s + nz) % nz) * units + first + (size - length if s == -nz // 2 else 0)
-                h_ref[pl.ds(pl.multiple_of(at, 16), length)] = part_ref[...]
+                at = ((z - s + nz) % nz) * units + first
+                h_ref[pl.ds(pl.multiple_of(at, 16), size)] = part_refs.pop(0)[...]
             first += size
         for side, w_ref in ((c, mine_ref), (1 - c, theirs_ref)):
             o_ref[side] = lax.dot_general(
@@ -228,17 +226,15 @@
     )(place, mine, theirs, *parts)
 
 
-def round_z(hidden, other):
-    nz = SIZES[3]
-    ring, up, down = {0: hidden}, hidden, hidden
-    for at in range(nz // 2):
-        if at == nz // 2 - 1:
-            half = up.shape[0] // 32 * 16
-            up, down = up[:half], down[half:]
+def round_z(hidden, other, way):
+    ring = {0: hidden}
+    up = down = hidden
+    for at in (1, 2, 3):
         up, down = along_z(up, 1), along_z(down, -1)
-        if at == 1:
+        if at == 2:
             up, down, other = together(up, down, other)
-        ring.update({at + 1: up, -at - 1: down})
+        ring.update({at: up, -at: down})
+    ring[4] = along_z(up if way > 0 else down, way)
     return ring, other
 
 
@@ -281,9 +277,9 @@
     keep, give = project(place, *both[:2], pieces, ())
     got = swap_xh(give)
     hidden, _ = together(hiddens[0], give)
-    first, (got, mine) = round_z(hidden, (got, mine))
+    first, (got, mine) = round_z(hidden, (got, mine), 1)
     theirs = swap_core(mine)
-    second, _ = round_z(activate(keep, [got]), (first[3], first[-3]))
+    second, _ = round_z(activate(keep, [got]), (first[3], first[-3]), -1)
 
     out = mix(place, (first, second), mine, theirs).reshape(16, tokens.shape[0], -1)
     got = lax.all_to_all(out, ("xh", "y", "xl"), 0, 0, tiled=True)

time: 221 us -> 220 us (level)
    ppermute x36 -> x34, starting transfers between devices: 45.7 us -> 43.7 us  [send(): return lax.ppermute(value, AXES, pairs)]
    ppermute x36 -> x34, waiting for transfers between devices: 84 us -> 83.2 us  [send(): return lax.ppermute(value, AXES, pairs)]
  transfers between devices with their start and end apart: 38 -> 36, of which waited for: 19 -> 17; matrix products, arithmetic and copies ran while one was open for 0% -> 0% of each run, Pallas kernels for 6% -> 6%
where the time goes in v9:
time: 220 us; the launch traced here: 219 us
  waiting for transfers between devices  109 us (50%)
  starting transfers between devices  54.2 us (25%)
  Pallas kernels  25.2 us (11%)
  blocking collectives  24.3 us (11%)
  local copies, waits for them, and re-layouts  4.88 us (2%)
    ppermute x34, waiting for transfers between devices, send(): return lax.ppermute(value, AXES, pairs)  83.2 us
    ppermute x34, starting transfers between devices, send(): return lax.ppermute(value, AXES, pairs)  43.7 us
    all_to_all x1, waiting for transfers between devices, shards(): weights.append(lax.all_to_all(ready, 'z', 0, 0, tiled=True))  26 us
    all_to_all x1, blocking collectives, shards(): got = lax.all_to_all(out, ('xh', 'y', 'xl'), 0, 0, tiled=True)  24.3 us
    pallas_call x2, Pallas kernels, project(): pl.pallas_call(body, in_specs=[SCALARS] + [pl.BlockSpec(memory_space=pl.A...  15.1 us
    all_to_all x1, starting transfers between devices, shards(): weights.append(lax.all_to_all(ready, 'z', 0, 0, tiled=True))  6.76 us
  transfers between devices with their start and end apart: 36, of which 17 were waited for; matrix products, arithmetic and copies ran while one was open for 0% of the time, Pallas kernels for 6%

profile of v9, /device:TPU:2, one launch (start us, length us, event | category | flops | bytes accessed | tf_op | source)
XLA Modules:
  0.0 219.1 jit_solution(5019446560275007338)
XLA Ops:
  0.0 6.3 %collective-permute-start.4 = (bf16[96,512]{1,0:T(8,128)(2,1)}, bf16[96,512]{1,0:T(8,128)(2,1)S(1)}, u32[]{:S(2)}, u32[]{:S(2)}) collective-permute-start(bf16[96,512]{1,0:T(8,128)(2,1)} %rest_0_.1), channel_id=1, source_target_pairs={{0,12},{1,13},{2,14},{3,15},{4,0},{5,1},{6,2},{7,3},{8,4},{9,5},{1... | collective-permute-start | bytes 294920 | tf_op jit(solution)/shard_map/ppermute | solution.py:27
  6.3 3.8 %collective-permute-start.3 = (bf16[96,512]{1,0:T(8,128)(2,1)}, bf16[96,512]{1,0:T(8,128)(2,1)S(1)}, u32[]{:S(2)}, u32[]{:S(2)}) collective-permute-start(bf16[96,512]{1,0:T(8,128)(2,1)} %rest_0_.1), channel_id=1, source_target_pairs={{0,8},{1,9},{2,10},{3,11},{4,12},{5,13},{6,14},{7,15},{8,0},{9,1},... | collective-permute-start | bytes 294920 | tf_op jit(solution)/shard_map/ppermute | solution.py:27
  11.1 2.2 %collective-permute-start.6 = (bf16[96,512]{1,0:T(8,128)(2,1)}, bf16[96,512]{1,0:T(8,128)(2,1)S(1)}, u32[]{:S(2)}, u32[]{:S(2)}) collective-permute-start(bf16[96,512]{1,0:T(8,128)(2,1)} %rest_0_.1), channel_id=1, source_target_pairs={{0,14},{1,15},{2,0},{3,1},{4,2},{5,3},{6,4},{7,5},{8,6},{9,7},{10,... | collective-permute-start | bytes 294920 | tf_op jit(solution)/shard_map/ppermute | solution.py:27
  13.5 4.0 %collective-permute-done.1.rest_2_ = bf16[96,512]{1,0:T(8,128)(2,1)S(1)} collective-permute-done((bf16[96,512]{1,0:T(8,128)(2,1)}, bf16[96,512]{1,0:T(8,128)(2,1)S(1)}, u32[]{:S(2)}, u32[]{:S(2)}) %collective-permute-start.1) | collective-permute-done | bytes 98336 | tf_op jit(solution)/shard_map/ppermute | solution.py:27
  17.5 2.9 %collective-permute-start.2 = (bf16[96,512]{1,0:T(8,128)(2,1)S(1)}, bf16[96,512]{1,0:T(8,128)(2,1)S(1)}, u32[]{:S(2)}, u32[]{:S(2)}) collective-permute-start(bf16[96,512]{1,0:T(8,128)(2,1)S(1)} %collective-permute-done.1.rest_2_), channel_id=1, source_target_pairs={{0,2},{1,3},{2,4},{3,5},{4,6},{5,7},{6,8},{7,9},{8,10},{9,11},{10,... | collective-permute-start | bytes 294920 | tf_op jit(solution)/shard_map/ppermute | solution.py:27
  20.5 3.9 %slice_units.1 = (bf16[8,288,512]{2,1,0:T(8,128)(2,1)}, bf16[8,160,512]{2,1,0:T(8,128)(2,1)}) custom-call(bf16[512,1792]{1,0:T(8,128)(2,1)} %g_ref.1, bf16[512,1792]{1,0:T(8,128)(2,1)} %u_ref.1), custom_call_target="tpu_custom_call" | custom-call | bytes 114688 | tf_op jit(solution)/shard_map/slice_units/pallas_call | solution.py:94
  26.4 2.2 %regroup.1.rest_0_ = bf16[8,96,512]{2,1,0:T(8,128)(2,1)} custom-call(s32[5]{0:T(128)} %stack.23.place_ref, bf16[96,512]{1,0:T(8,128)(2,1)} %rest_0_.1, bf16[96,512]{1,0:T(8,128)(2,1)} %copy-done.16, bf16[96,512]{1,0:T(8,128)(2,1)} %copy-done.14, bf16[96,512]{1,0:T(8,128)(2,1)} %copy-done.19, bf16[96,512]{1,0:T(8,128)(2,1)} %copy-done.15, ...), custom_call_target="tpu_custom_call" | custom-call | bytes 24576 | tf_op jit(solution)/shard_map/regroup/pallas_call | solution.py:71
  28.6 3.7 %all-to-all-start = ((bf16[8,288,512]{2,1,0:T(8,128)(2,1)}), bf16[8,288,512]{2,1,0:T(8,128)(2,1)S(1)}, u32[]{:S(2)}, u32[]{:S(2)}) async-start(bf16[8,288,512]{2,1,0:T(8,128)(2,1)} %get-tuple-element.40), calls=%async_computation | async-start | bytes 4718592 | tf_op jit(solution)/shard_map/all_to_all | solution.py:253
  32.4 3.1 %collective-permute-start.9 = (bf16[8,96,512]{2,1,0:T(8,128)(2,1)S(1)}, bf16[8,96,512]{2,1,0:T(8,128)(2,1)S(1)}, u32[]{:S(2)}, u32[]{:S(2)}) collective-permute-start(bf16[8,96,512]{2,1,0:T(8,128)(2,1)S(1)} %copy-done.4), channel_id=1, source_target_pairs={{0,96},{1,97},{2,98},{3,99},{4,100},{5,101},{6,102},{7,103},{8,104... | collective-permute-start | bytes 2359304 | tf_op jit(solution)/shard_map/ppermute | solution.py:27
  36.0 12.4 %collective-permute-done.9.rest_2_ = bf16[8,96,512]{2,1,0:T(8,128)(2,1)S(1)} collective-permute-done((bf16[8,96,512]{2,1,0:T(8,128)(2,1)S(1)}, bf16[8,96,512]{2,1,0:T(8,128)(2,1)S(1)}, u32[]{:S(2)}, u32[]{:S(2)}) %collective-permute-start.9) | collective-permute-done | bytes 786464 | tf_op jit(solution)/shard_map/ppermute | solution.py:27
  48.4 3.4 %collective-permute-done.8.rest_6_ = bf16[8,96,512]{2,1,0:T(8,128)(2,1)S(1)} collective-permute-done((bf16[8,96,512]{2,1,0:T(8,128)(2,1)S(1)}, bf16[8,96,512]{2,1,0:T(8,128)(2,1)S(1)}, u32[]{:S(2)}, u32[]{:S(2)}) %collective-permute-start.8) | collective-permute-done | bytes 786464 | tf_op jit(solution)/shard_map/ppermute | solution.py:27
  55.8 17.0 %collective-permute-done.10.rest_3_ = bf16[8,96,512]{2,1,0:T(8,128)(2,1)S(1)} collective-permute-done((bf16[8,96,512]{2,1,0:T(8,128)(2,1)S(1)}, bf16[8,96,512]{2,1,0:T(8,128)(2,1)S(1)}, u32[]{:S(2)}, u32[]{:S(2)}) %collective-permute-start.10) | collective-permute-done | bytes 786464 | tf_op jit(solution)/shard_map/ppermute | solution.py:27
  72.8 2.9 %collective-permute-start.12 = (bf16[8,96,512]{2,1,0:T(8,128)(2,1)S(1)}, bf16[8,96,512]{2,1,0:T(8,128)(2,1)S(1)}, u32[]{:S(2)}, u32[]{:S(2)}) collective-permute-start(bf16[8,96,512]{2,1,0:T(8,128)(2,1)S(1)} %collective-permute-done.10.rest_3_), channel_id=1, source_target_pairs={{0,96},{1,97},{2,98},{3,99},{4,100},{5,101},{6,102},{7,103},{8,104... | collective-permute-start | bytes 2359304 | tf_op jit(solution)/shard_map/ppermute | solution.py:27
  75.7 17.2 %collective-permute-done.11.rest_4_ = bf16[8,96,512]{2,1,0:T(8,128)(2,1)S(1)} collective-permute-done((bf16[8,96,512]{2,1,0:T(8,128)(2,1)S(1)}, bf16[8,96,512]{2,1,0:T(8,128)(2,1)S(1)}, u32[]{:S(2)}, u32[]{:S(2)}) %collective-permute-start.11) | collective-permute-done | bytes 786464 | tf_op jit(solution)/shard_map/ppermute | solution.py:27
  95.9 6.8 %all-to-all-start.1 = ((bf16[8,160,512]{2,1,0:T(8,128)(2,1)}), bf16[8,160,512]{2,1,0:T(8,128)(2,1)}, u32[]{:S(2)}, u32[]{:S(2)}) async-start(bf16[8,160,512]{2,1,0:T(8,128)(2,1)} %get-tuple-element.57), calls=%async_computation.1 | async-start | bytes 2621440 | tf_op jit(solution)/shard_map/all_to_all | solution.py:267
  102.7 8.6 %project.2 = (f32[288,768]{1,0:T(8,128)}, f32[288,768]{1,0:T(8,128)}) custom-call(s32[5]{0:T(128)} %stack.23.place_ref, bf16[8,288,512]{2,1,0:T(8,128)(2,1)} %copy-done.3, bf16[8,288,512]{2,1,0:T(8,128)(2,1)} %collective-permute-done.15.other_ref, bf16[8,96,512]{2,1,0:T(8,128)(2,1)} %regroup.1.rest_0_, bf16[8,96,512]{2,1,0:T(8,128)(2,1)} %copy-done.7, ...), custom_call_target="tpu_custom_call" | custom-call | flops 56623104 | bytes 172032 | tf_op jit(solution)/shard_map/project/pallas_call | solution.py:154
  111.4 26.0 %all-to-all-done.1.own_ref = bf16[8,160,512]{2,1,0:T(8,128)(2,1)} async-done(((bf16[8,160,512]{2,1,0:T(8,128)(2,1)}), bf16[8,160,512]{2,1,0:T(8,128)(2,1)}, u32[]{:S(2)}, u32[]{:S(2)}) %all-to-all-start.1) | async-done | bytes 1310752 | tf_op jit(solution)/shard_map/all_to_all | solution.py:267
  138.7 2.0 collective-permute-done.17.other_ref
  140.7 6.5 %project.3 = (f32[160,768]{1,0:T(8,128)}, f32[160,768]{1,0:T(8,128)}) custom-call(s32[5]{0:T(128)} %stack.23.place_ref, bf16[8,160,512]{2,1,0:T(8,128)(2,1)} %all-to-all-done.1.own_ref, bf16[8,160,512]{2,1,0:T(8,128)(2,1)} %collective-permute-done.17.other_ref, bf16[8,96,512]{2,1,0:T(8,128)(2,1)} %regroup.1.rest_0_, bf16[8,96,512]{2,1,0:T(8,128)(2,1)} %copy-done.7, ...), custom_call_target="tpu_custom_call" | custom-call | flops 31457280 | bytes 139264 | tf_op jit(solution)/shard_map/project/pallas_call | solution.py:154
  147.3 2.0 collective-permute-start.18
  149.3 5.4 %collective-permute-done.20.rest_7_ = bf16[144,768]{1,0:T(8,128)(2,1)S(1)} collective-permute-done((bf16[144,768]{1,0:T(8,128)(2,1)S(1)}, bf16[144,768]{1,0:T(8,128)(2,1)S(1)}, u32[]{:S(2)}, u32[]{:S(2)}) %collective-permute-start.20) | collective-permute-done | bytes 221216 | tf_op jit(solution)/shard_map/ppermute | solution.py:27
  157.0 4.3 %collective-permute-done.21.rest_6_ = bf16[144,768]{1,0:T(8,128)(2,1)S(1)} collective-permute-done((bf16[144,768]{1,0:T(8,128)(2,1)S(1)}, bf16[144,768]{1,0:T(8,128)(2,1)S(1)}, u32[]{:S(2)}, u32[]{:S(2)}) %collective-permute-start.21) | collective-permute-done | bytes 221216 | tf_op jit(solution)/shard_map/ppermute | solution.py:27
  161.4 2.8 %collective-permute-done.19.rest_2_ = bf16[144,768]{1,0:T(8,128)(2,1)S(1)} collective-permute-done((bf16[144,768]{1,0:T(8,128)(2,1)S(1)}, bf16[144,768]{1,0:T(8,128)(2,1)S(1)}, u32[]{:S(2)}, u32[]{:S(2)}) %collective-permute-start.19) | collective-permute-done | bytes 221216 | tf_op jit(solution)/shard_map/ppermute | solution.py:27
  166.5 3.1 %collective-permute-start.26 = (bf16[144,768]{1,0:T(8,128)(2,1)S(1)}, bf16[144,768]{1,0:T(8,128)(2,1)S(1)}, u32[]{:S(2)}, u32[]{:S(2)}) collective-permute-start(bf16[144,768]{1,0:T(8,128)(2,1)S(1)} %collective-permute-done.21.rest_6_), channel_id=1, source_target_pairs={{0,14},{1,15},{2,0},{3,1},{4,2},{5,3},{6,4},{7,5},{8,6},{9,7},{10,... | collective-permute-start | bytes 663560 | tf_op jit(solution)/shard_map/ppermute | solution.py:27
  170.4 2.0 collective-permute-start.30
  172.9 4.7 %collective-permute-done.24.rest_3_ = bf16[144,768]{1,0:T(8,128)(2,1)S(1)} collective-permute-done((bf16[144,768]{1,0:T(8,128)(2,1)S(1)}, bf16[144,768]{1,0:T(8,128)(2,1)S(1)}, u32[]{:S(2)}, u32[]{:S(2)}) %collective-permute-start.24) | collective-permute-done | bytes 221216 | tf_op jit(solution)/shard_map/ppermute | solution.py:27
  177.6 1.9 collective-permute-done.28.rest_10_
  181.6 2.8 %collective-permute-done.32.rest_13_ = bf16[80,768]{1,0:T(8,128)(2,1)S(1)} collective-permute-done((bf16[80,768]{1,0:T(8,128)(2,1)S(1)}, bf16[80,768]{1,0:T(8,128)(2,1)S(1)}, u32[]{:S(2)}, u32[]{:S(2)}) %collective-permute-start.32) | collective-permute-done | bytes 122912 | tf_op jit(solution)/shard_map/ppermute | solution.py:27
  184.4 2.1 collective-permute-start.33
  186.5 3.6 %collective-permute-done.31.rest_11_ = bf16[80,768]{1,0:T(8,128)(2,1)S(1)} collective-permute-done((bf16[80,768]{1,0:T(8,128)(2,1)S(1)}, bf16[80,768]{1,0:T(8,128)(2,1)S(1)}, u32[]{:S(2)}, u32[]{:S(2)}) %collective-permute-start.31) | collective-permute-done | bytes 122912 | tf_op jit(solution)/shard_map/ppermute | solution.py:27
  190.1 3.8 %mix.1 = bf16[2,768,512]{2,1,0:T(8,128)(2,1)S(1)} custom-call(s32[5]{0:T(128)S(1)} %copy-done.2, bf16[1792,512]{1,0:T(8,128)(2,1)S(1)} %broadcast_select_fusion.mine_ref, bf16[1792,512]{1,0:T(8,128)(2,1)S(1)} %collective-permute-done.23.theirs_ref, bf16[144,768]{1,0:T(8,128)(2,1)S(1)} %activate.2.rest_0_, ...), custom_call_target="tpu_custom_call" | custom-call | flops 44040192 | bytes 100352 | tf_op jit(solution)/shard_map/mix/pallas_call | solution.py:217
  193.9 24.3 %all_to_all.15 = bf16[16,96,512]{2,1,0:T(8,128)(2,1)S(1)} all-to-all(bf16[16,96,512]{2,1,0:T(8,128)(2,1)S(1)} %bitcast.6), channel_id=1, replica_groups=mesh['xl'=2,'y'=4,'c'=2,'z'=8,'xh'=2] {'xh','y','xl'}, dimensions={0} | all-to-all | bytes 3145728 | tf_op jit(solution)/shard_map/all_to_all | solution.py:285
  (91 shorter events, 21.1 us)
Async XLA Ops:
  0.0 13.4 %collective-permute-start.4 = (bf16[96,512]{1,0:T(8,128)(2,1)}, bf16[96,512]{1,0:T(8,128)(2,1)S(1)}, u32[]{:S(2)}, u32[]{:S(2)}) collective-permute-start(bf16[96,512]{1,0:T(8,128)(2,1)} %rest_0_.1), channel_id=1, source_target_pairs={{0,12},{1,13},{2,14},{3,15},{4,0},{5,1},{6,2},{7,3},{8,4},{9,5},{1... | collective-permute-start | bytes 294920 | tf_op jit(solution)/shard_map/ppermute | solution.py:27
  6.3 11.2 %collective-permute-start.1 = (bf16[96,512]{1,0:T(8,128)(2,1)}, bf16[96,512]{1,0:T(8,128)(2,1)S(1)}, u32[]{:S(2)}, u32[]{:S(2)}) collective-permute-start(bf16[96,512]{1,0:T(8,128)(2,1)} %rest_0_.1), channel_id=1, source_target_pairs={{0,4},{1,5},{2,6},{3,7},{4,8},{5,9},{6,10},{7,11},{8,12},{9,13},{1... | collective-permute-start | bytes 294920 | tf_op jit(solution)/shard_map/ppermute | solution.py:27
  6.3 18.7 %collective-permute-start.3 = (bf16[96,512]{1,0:T(8,128)(2,1)}, bf16[96,512]{1,0:T(8,128)(2,1)S(1)}, u32[]{:S(2)}, u32[]{:S(2)}) collective-permute-start(bf16[96,512]{1,0:T(8,128)(2,1)} %rest_0_.1), channel_id=1, source_target_pairs={{0,8},{1,9},{2,10},{3,11},{4,12},{5,13},{6,14},{7,15},{8,0},{9,1},... | collective-permute-start | bytes 294920 | tf_op jit(solution)/shard_map/ppermute | solution.py:27
  10.1 14.9 %collective-permute-start = (bf16[96,512]{1,0:T(8,128)(2,1)}, bf16[96,512]{1,0:T(8,128)(2,1)S(1)}, u32[]{:S(2)}, u32[]{:S(2)}) collective-permute-start(bf16[96,512]{1,0:T(8,128)(2,1)} %rest_0_.1), channel_id=1, source_target_pairs={{0,2},{1,3},{2,4},{3,5},{4,6},{5,7},{6,8},{7,9},{8,10},{9,11},{10,... | collective-permute-start | bytes 294920 | tf_op jit(solution)/shard_map/ppermute | solution.py:27
  11.1 13.9 %collective-permute-start.6 = (bf16[96,512]{1,0:T(8,128)(2,1)}, bf16[96,512]{1,0:T(8,128)(2,1)S(1)}, u32[]{:S(2)}, u32[]{:S(2)}) collective-permute-start(bf16[96,512]{1,0:T(8,128)(2,1)} %rest_0_.1), channel_id=1, source_target_pairs={{0,14},{1,15},{2,0},{3,1},{4,2},{5,3},{6,4},{7,5},{8,6},{9,7},{10,... | collective-permute-start | bytes 294920 | tf_op jit(solution)/shard_map/ppermute | solution.py:27
  13.4 11.7 %collective-permute-start.5 = (bf16[96,512]{1,0:T(8,128)(2,1)S(1)}, bf16[96,512]{1,0:T(8,128)(2,1)S(1)}, u32[]{:S(2)}, u32[]{:S(2)}) collective-permute-start(bf16[96,512]{1,0:T(8,128)(2,1)S(1)} %collective-permute-done.4.rest_6_), channel_id=1, source_target_pairs={{0,14},{1,15},{2,0},{3,1},{4,2},{5,3},{6,4},{7,5},{8,6},{9,7},{10,... | collective-permute-start | bytes 294920 | tf_op jit(solution)/shard_map/ppermute | solution.py:27
  17.5 7.5 %collective-permute-start.2 = (bf16[96,512]{1,0:T(8,128)(2,1)S(1)}, bf16[96,512]{1,0:T(8,128)(2,1)S(1)}, u32[]{:S(2)}, u32[]{:S(2)}) collective-permute-start(bf16[96,512]{1,0:T(8,128)(2,1)S(1)} %collective-permute-done.1.rest_2_), channel_id=1, source_target_pairs={{0,2},{1,3},{2,4},{3,5},{4,6},{5,7},{6,8},{7,9},{8,10},{9,11},{10,... | collective-permute-start | bytes 294920 | tf_op jit(solution)/shard_map/ppermute | solution.py:27
  28.6 66.3 %all-to-all-start = ((bf16[8,288,512]{2,1,0:T(8,128)(2,1)}), bf16[8,288,512]{2,1,0:T(8,128)(2,1)S(1)}, u32[]{:S(2)}, u32[]{:S(2)}) async-start(bf16[8,288,512]{2,1,0:T(8,128)(2,1)} %get-tuple-element.40), calls=%async_computation | async-start | bytes 4718592 | tf_op jit(solution)/shard_map/all_to_all | solution.py:253
  32.4 16.1 %collective-permute-start.9 = (bf16[8,96,512]{2,1,0:T(8,128)(2,1)S(1)}, bf16[8,96,512]{2,1,0:T(8,128)(2,1)S(1)}, u32[]{:S(2)}, u32[]{:S(2)}) collective-permute-start(bf16[8,96,512]{2,1,0:T(8,128)(2,1)S(1)} %copy-done.4), channel_id=1, source_target_pairs={{0,96},{1,97},{2,98},{3,99},{4,100},{5,101},{6,102},{7,103},{8,104... | collective-permute-start | bytes 2359304 | tf_op jit(solution)/shard_map/ppermute | solution.py:27
  35.5 16.4 %collective-permute-start.8 = (bf16[8,96,512]{2,1,0:T(8,128)(2,1)S(1)}, bf16[8,96,512]{2,1,0:T(8,128)(2,1)S(1)}, u32[]{:S(2)}, u32[]{:S(2)}) collective-permute-start(bf16[8,96,512]{2,1,0:T(8,128)(2,1)S(1)} %copy-done.4), channel_id=1, source_target_pairs={{0,32},{1,33},{2,34},{3,35},{4,36},{5,37},{6,38},{7,39},{8,40},{9,... | collective-permute-start | bytes 2359304 | tf_op jit(solution)/shard_map/ppermute | solution.py:27
  35.5 16.4 %collective-permute-start.7 = (bf16[8,96,512]{2,1,0:T(8,128)(2,1)S(1)}, bf16[8,96,512]{2,1,0:T(8,128)(2,1)S(1)}, u32[]{:S(2)}, u32[]{:S(2)}) collective-permute-start(bf16[8,96,512]{2,1,0:T(8,128)(2,1)S(1)} %copy-done.4), channel_id=1, source_target_pairs={{0,128},{1,129},{2,130},{3,131},{4,132},{5,133},{6,134},{7,135},{8... | collective-permute-start | bytes 2359304 | tf_op jit(solution)/shard_map/ppermute | solution.py:27
  51.9 43.1 %collective-permute-start.14 = (bf16[1792,512]{1,0:T(8,128)(2,1)}, bf16[1792,512]{1,0:T(8,128)(2,1)}, u32[]{:S(2)}, u32[]{:S(2)}) collective-permute-start(bf16[1792,512]{1,0:T(8,128)(2,1)} %param.7), channel_id=1, source_target_pairs={{1,16},{3,18},{5,20},{7,22},{9,24},{11,26},{13,28},{15,30},{16,1},... | collective-permute-start | bytes 5505032 | tf_op jit(solution)/shard_map/ppermute | solution.py:27
  53.8 19.0 %collective-permute-start.10 = (bf16[8,96,512]{2,1,0:T(8,128)(2,1)S(1)}, bf16[8,96,512]{2,1,0:T(8,128)(2,1)S(1)}, u32[]{:S(2)}, u32[]{:S(2)}) collective-permute-start(bf16[8,96,512]{2,1,0:T(8,128)(2,1)S(1)} %collective-permute-done.7.rest_1_), channel_id=1, source_target_pairs={{0,96},{1,97},{2,98},{3,99},{4,100},{5,101},{6,102},{7,103},{8,104... | collective-permute-start | bytes 2359304 | tf_op jit(solution)/shard_map/ppermute | solution.py:27
  55.5 37.4 %collective-permute-start.13 = (bf16[8,96,512]{2,1,0:T(8,128)(2,1)S(1)}, bf16[8,96,512]{2,1,0:T(8,128)(2,1)S(1)}, u32[]{:S(2)}, u32[]{:S(2)}) collective-permute-start(bf16[8,96,512]{2,1,0:T(8,128)(2,1)S(1)} %collective-permute-done.7.rest_1_), channel_id=1, source_target_pairs={{0,32},{1,33},{2,34},{3,35},{4,36},{5,37},{6,38},{7,39},{8,40},{9,... | collective-permute-start | bytes 2359304 | tf_op jit(solution)/shard_map/ppermute | solution.py:27
  55.8 37.1 %collective-permute-start.11 = (bf16[8,96,512]{2,1,0:T(8,128)(2,1)S(1)}, bf16[8,96,512]{2,1,0:T(8,128)(2,1)S(1)}, u32[]{:S(2)}, u32[]{:S(2)}) collective-permute-start(bf16[8,96,512]{2,1,0:T(8,128)(2,1)S(1)} %collective-permute-done.8.rest_6_), channel_id=1, source_target_pairs={{0,32},{1,33},{2,34},{3,35},{4,36},{5,37},{6,38},{7,39},{8,40},{9,... | collective-permute-start | bytes 2359304 | tf_op jit(solution)/shard_map/ppermute | solution.py:27
  72.8 20.4 %collective-permute-start.12 = (bf16[8,96,512]{2,1,0:T(8,128)(2,1)S(1)}, bf16[8,96,512]{2,1,0:T(8,128)(2,1)S(1)}, u32[]{:S(2)}, u32[]{:S(2)}) collective-permute-start(bf16[8,96,512]{2,1,0:T(8,128)(2,1)S(1)} %collective-permute-done.10.rest_3_), channel_id=1, source_target_pairs={{0,96},{1,97},{2,98},{3,99},{4,100},{5,101},{6,102},{7,103},{8,104... | collective-permute-start | bytes 2359304 | tf_op jit(solution)/shard_map/ppermute | solution.py:27
  94.9 7.7 %collective-permute-start.15 = (bf16[8,288,512]{2,1,0:T(8,128)(2,1)S(1)}, bf16[8,288,512]{2,1,0:T(8,128)(2,1)}, u32[]{:S(2)}, u32[]{:S(2)}) collective-permute-start(bf16[8,288,512]{2,1,0:T(8,128)(2,1)S(1)} %all-to-all-done.own_ref), channel_id=1, source_target_pairs={{0,16},{1,17},{2,18},{3,19},{4,20},{5,21},{6,22},{7,23},{8,24},{9,... | collective-permute-start | bytes 7077896 | tf_op jit(solution)/shard_map/ppermute | solution.py:27
  95.9 41.4 %all-to-all-start.1 = ((bf16[8,160,512]{2,1,0:T(8,128)(2,1)}), bf16[8,160,512]{2,1,0:T(8,128)(2,1)}, u32[]{:S(2)}, u32[]{:S(2)}) async-start(bf16[8,160,512]{2,1,0:T(8,128)(2,1)} %get-tuple-element.57), calls=%async_computation.1 | async-start | bytes 2621440 | tf_op jit(solution)/shard_map/all_to_all | solution.py:267
  111.3 26.1 %collective-permute-start.16 = (f32[288,768]{1,0:T(8,128)}, f32[288,768]{1,0:T(8,128)S(1)}, u32[]{:S(2)}, u32[]{:S(2)}) collective-permute-start(f32[288,768]{1,0:T(8,128)} %get-tuple-element.56), channel_id=1, source_target_pairs={{0,1},{1,0},{2,3},{3,2},{4,5},{5,4},{6,7},{7,6},{8,9},{9,8},{10,11... | collective-permute-start | bytes 2654216 | tf_op jit(solution)/shard_map/ppermute | solution.py:27
  147.2 7.5 %collective-permute-start.20 = (bf16[144,768]{1,0:T(8,128)(2,1)S(1)}, bf16[144,768]{1,0:T(8,128)(2,1)S(1)}, u32[]{:S(2)}, u32[]{:S(2)}) collective-permute-start(bf16[144,768]{1,0:T(8,128)(2,1)S(1)} %activate.2.rest_0_), channel_id=1, source_target_pairs={{0,14},{1,15},{2,0},{3,1},{4,2},{5,3},{6,4},{7,5},{8,6},{9,7},{10,... | collective-permute-start | bytes 663560 | tf_op jit(solution)/shard_map/ppermute | solution.py:27
  147.3 8.9 %collective-permute-start.18 = (bf16[144,768]{1,0:T(8,128)(2,1)S(1)}, bf16[144,768]{1,0:T(8,128)(2,1)S(1)}, u32[]{:S(2)}, u32[]{:S(2)}) collective-permute-start(bf16[144,768]{1,0:T(8,128)(2,1)S(1)} %activate.2.rest_0_), channel_id=1, source_target_pairs={{0,2},{1,3},{2,4},{3,5},{4,6},{5,7},{6,8},{7,9},{8,10},{9,11},{10,... | collective-permute-start | bytes 663560 | tf_op jit(solution)/shard_map/ppermute | solution.py:27
  149.3 14.8 %collective-permute-start.22 = (f32[160,768]{1,0:T(8,128)}, f32[160,768]{1,0:T(8,128)S(1)}, u32[]{:S(2)}, u32[]{:S(2)}) collective-permute-start(f32[160,768]{1,0:T(8,128)} %get-tuple-element.61), channel_id=1, source_target_pairs={{0,1},{1,0},{2,3},{3,2},{4,5},{5,4},{6,7},{7,6},{8,9},{9,8},{10,11... | collective-permute-start | bytes 1474568 | tf_op jit(solution)/shard_map/ppermute | solution.py:27
  154.7 6.6 %collective-permute-start.21 = (bf16[144,768]{1,0:T(8,128)(2,1)S(1)}, bf16[144,768]{1,0:T(8,128)(2,1)S(1)}, u32[]{:S(2)}, u32[]{:S(2)}) collective-permute-start(bf16[144,768]{1,0:T(8,128)(2,1)S(1)} %collective-permute-done.20.rest_7_), channel_id=1, source_target_pairs={{0,14},{1,15},{2,0},{3,1},{4,2},{5,3},{6,4},{7,5},{8,6},{9,7},{10,... | collective-permute-start | bytes 663560 | tf_op jit(solution)/shard_map/ppermute | solution.py:27
  156.2 7.9 %collective-permute-start.19 = (bf16[144,768]{1,0:T(8,128)(2,1)S(1)}, bf16[144,768]{1,0:T(8,128)(2,1)S(1)}, u32[]{:S(2)}, u32[]{:S(2)}) collective-permute-start(bf16[144,768]{1,0:T(8,128)(2,1)S(1)} %collective-permute-done.18.rest_1_), channel_id=1, source_target_pairs={{0,2},{1,3},{2,4},{3,5},{4,6},{5,7},{6,8},{7,9},{8,10},{9,11},{10,... | collective-permute-start | bytes 663560 | tf_op jit(solution)/shard_map/ppermute | solution.py:27
  164.1 26.0 %collective-permute-start.23 = (bf16[1792,512]{1,0:T(8,128)(2,1)S(1)}, bf16[1792,512]{1,0:T(8,128)(2,1)S(1)}, u32[]{:S(2)}, u32[]{:S(2)}) collective-permute-start(bf16[1792,512]{1,0:T(8,128)(2,1)S(1)} %broadcast_select_fusion.mine_ref), channel_id=1, source_target_pairs={{0,16},{1,17},{2,18},{3,19},{4,20},{5,21},{6,22},{7,23},{8,24},{9,... | collective-permute-start | bytes 5505032 | tf_op jit(solution)/shard_map/ppermute | solution.py:27
  165.5 7.4 %collective-permute-start.27 = (bf16[80,768]{1,0:T(8,128)(2,1)S(1)}, bf16[80,768]{1,0:T(8,128)(2,1)S(1)}, u32[]{:S(2)}, u32[]{:S(2)}) collective-permute-start(bf16[80,768]{1,0:T(8,128)(2,1)S(1)} %activate.3.rest_8_), channel_id=1, source_target_pairs={{0,2},{1,3},{2,4},{3,5},{4,6},{5,7},{6,8},{7,9},{8,10},{9,11},{10,... | collective-permute-start | bytes 368648 | tf_op jit(solution)/shard_map/ppermute | solution.py:27
  166.3 11.2 %collective-permute-start.24 = (bf16[144,768]{1,0:T(8,128)(2,1)S(1)}, bf16[144,768]{1,0:T(8,128)(2,1)S(1)}, u32[]{:S(2)}, u32[]{:S(2)}) collective-permute-start(bf16[144,768]{1,0:T(8,128)(2,1)S(1)} %collective-permute-done.19.rest_2_), channel_id=1, source_target_pairs={{0,2},{1,3},{2,4},{3,5},{4,6},{5,7},{6,8},{7,9},{8,10},{9,11},{10,... | collective-permute-start | bytes 663560 | tf_op jit(solution)/shard_map/ppermute | solution.py:27
  166.5 11.1 %collective-permute-start.26 = (bf16[144,768]{1,0:T(8,128)(2,1)S(1)}, bf16[144,768]{1,0:T(8,128)(2,1)S(1)}, u32[]{:S(2)}, u32[]{:S(2)}) collective-permute-start(bf16[144,768]{1,0:T(8,128)(2,1)S(1)} %collective-permute-done.21.rest_6_), channel_id=1, source_target_pairs={{0,14},{1,15},{2,0},{3,1},{4,2},{5,3},{6,4},{7,5},{8,6},{9,7},{10,... | collective-permute-start | bytes 663560 | tf_op jit(solution)/shard_map/ppermute | solution.py:27
  170.4 7.2 %collective-permute-start.30 = (bf16[80,768]{1,0:T(8,128)(2,1)S(1)}, bf16[80,768]{1,0:T(8,128)(2,1)S(1)}, u32[]{:S(2)}, u32[]{:S(2)}) collective-permute-start(bf16[80,768]{1,0:T(8,128)(2,1)S(1)} %collective-permute-done.29.rest_15_), channel_id=1, source_target_pairs={{0,14},{1,15},{2,0},{3,1},{4,2},{5,3},{6,4},{7,5},{8,6},{9,7},{10,... | collective-permute-start | bytes 368648 | tf_op jit(solution)/shard_map/ppermute | solution.py:27
  172.8 6.7 %collective-permute-start.28 = (bf16[80,768]{1,0:T(8,128)(2,1)S(1)}, bf16[80,768]{1,0:T(8,128)(2,1)S(1)}, u32[]{:S(2)}, u32[]{:S(2)}) collective-permute-start(bf16[80,768]{1,0:T(8,128)(2,1)S(1)} %collective-permute-done.27.rest_9_), channel_id=1, source_target_pairs={{0,2},{1,3},{2,4},{3,5},{4,6},{5,7},{6,8},{7,9},{8,10},{9,11},{10,... | collective-permute-start | bytes 368648 | tf_op jit(solution)/shard_map/ppermute | solution.py:27
  180.4 9.7 %collective-permute-start.25 = (bf16[144,768]{1,0:T(8,128)(2,1)S(1)}, bf16[144,768]{1,0:T(8,128)(2,1)S(1)}, u32[]{:S(2)}, u32[]{:S(2)}) collective-permute-start(bf16[144,768]{1,0:T(8,128)(2,1)S(1)} %collective-permute-done.24.rest_3_), channel_id=1, source_target_pairs={{0,2},{1,3},{2,4},{3,5},{4,6},{5,7},{6,8},{7,9},{8,10},{9,11},{10,... | collective-permute-start | bytes 663560 | tf_op jit(solution)/shard_map/ppermute | solution.py:27
  181.5 8.5 %collective-permute-start.31 = (bf16[80,768]{1,0:T(8,128)(2,1)S(1)}, bf16[80,768]{1,0:T(8,128)(2,1)S(1)}, u32[]{:S(2)}, u32[]{:S(2)}) collective-permute-start(bf16[80,768]{1,0:T(8,128)(2,1)S(1)} %collective-permute-done.28.rest_10_), channel_id=1, source_target_pairs={{0,2},{1,3},{2,4},{3,5},{4,6},{5,7},{6,8},{7,9},{8,10},{9,11},{10,... | collective-permute-start | bytes 368648 | tf_op jit(solution)/shard_map/ppermute | solution.py:27
  (24 other events, 288.0 us)

commit v10 on v9

--- a/solution.py
+++ b/solution.py
@@ -10,7 +10,7 @@
 
 AXES = ("xl", "y", "c", "z", "xh")
 SIZES = (2, 4, 2, 8, 2)
-FIRST = 144
+FIRST = 160
 TOGETHER = 2
 F32, BF16 = jnp.float32, jnp.bfloat16
 SCALARS = pl.BlockSpec(memory_space=pltpu.SMEM)

time: 220 us -> 225 us (1.023)
  waiting for transfers between devices: 109 us -> 114 us
  starting transfers between devices: 54.2 us -> 57.5 us
  blocking collectives: 24.3 us -> 22 us
    ppermute x34, waiting for transfers between devices: 83.2 us -> 93.8 us  [send(): return lax.ppermute(value, AXES, pairs)]
    all_to_all x1, waiting for transfers between devices: 26 us -> 19.8 us  [shards(): weights.append(lax.all_to_all(ready, 'z', 0, 0, tiled=True))]
    ppermute x34, starting transfers between devices: 43.7 us -> 47 us  [send(): return lax.ppermute(value, AXES, pairs)]
    all_to_all x1, blocking collectives: 24.3 us -> 22 us  [shards(): got = lax.all_to_all(out, ('xh', 'y', 'xl'), 0, 0, tiled=True)]
  transfers between devices with their start and end apart: 36 -> 36, of which waited for: 17 -> 18; matrix products, arithmetic and copies ran while one was open for 0% -> 0% of each run, Pallas kernels for 6% -> 6%
where the time goes in v10:
time: 225 us
  waiting for transfers between devices  114 us (51%)
  starting transfers between devices  57.5 us (26%)
  Pallas kernels  25.2 us (11%)
  blocking collectives  22 us (10%)
  local copies, waits for them, and re-layouts  4.95 us (2%)
    ppermute x34, waiting for transfers between devices, send(): return lax.ppermute(value, AXES, pairs)  93.8 us
    ppermute x34, starting transfers between devices, send(): return lax.ppermute(value, AXES, pairs)  47 us
    all_to_all x1, blocking collectives, shards(): got = lax.all_to_all(out, ('xh', 'y', 'xl'), 0, 0, tiled=True)  22 us
    all_to_all x1, waiting for transfers between devices, shards(): weights.append(lax.all_to_all(ready, 'z', 0, 0, tiled=True))  19.8 us
    pallas_call x2, Pallas kernels, project(): pl.pallas_call(body, in_specs=[SCALARS] + [pl.BlockSpec(memory_space=pl.A...  15.1 us
    all_to_all x1, starting transfers between devices, shards(): weights.append(lax.all_to_all(ready, 'z', 0, 0, tiled=True))  6.76 us
  transfers between devices with their start and end apart: 36, of which 18 were waited for; matrix products, arithmetic and copies ran while one was open for 0% of the time, Pallas kernels for 6%

profile of v10, /device:TPU:2, one launch (start us, length us, event | category | flops | bytes accessed | tf_op | source)
XLA Modules:
  0.0 224.6 jit_solution(3268629039066006230)
XLA Ops:
  0.0 6.3 %collective-permute-start.4 = (bf16[96,512]{1,0:T(8,128)(2,1)}, bf16[96,512]{1,0:T(8,128)(2,1)S(1)}, u32[]{:S(2)}, u32[]{:S(2)}) collective-permute-start(bf16[96,512]{1,0:T(8,128)(2,1)} %rest_0_.1), channel_id=1, source_target_pairs={{0,12},{1,13},{2,14},{3,15},{4,0},{5,1},{6,2},{7,3},{8,4},{9,5},{1... | collective-permute-start | bytes 294920 | tf_op jit(solution)/shard_map/ppermute | solution.py:27
  6.3 3.8 %collective-permute-start.3 = (bf16[96,512]{1,0:T(8,128)(2,1)}, bf16[96,512]{1,0:T(8,128)(2,1)S(1)}, u32[]{:S(2)}, u32[]{:S(2)}) collective-permute-start(bf16[96,512]{1,0:T(8,128)(2,1)} %rest_0_.1), channel_id=1, source_target_pairs={{0,8},{1,9},{2,10},{3,11},{4,12},{5,13},{6,14},{7,15},{8,0},{9,1},... | collective-permute-start | bytes 294920 | tf_op jit(solution)/shard_map/ppermute | solution.py:27
  11.1 2.2 collective-permute-start.6
  13.5 4.0 %collective-permute-done.1.rest_2_ = bf16[96,512]{1,0:T(8,128)(2,1)S(1)} collective-permute-done((bf16[96,512]{1,0:T(8,128)(2,1)}, bf16[96,512]{1,0:T(8,128)(2,1)S(1)}, u32[]{:S(2)}, u32[]{:S(2)}) %collective-permute-start.1) | collective-permute-done | bytes 98336 | tf_op jit(solution)/shard_map/ppermute | solution.py:27
  17.5 2.9 %collective-permute-start.2 = (bf16[96,512]{1,0:T(8,128)(2,1)S(1)}, bf16[96,512]{1,0:T(8,128)(2,1)S(1)}, u32[]{:S(2)}, u32[]{:S(2)}) collective-permute-start(bf16[96,512]{1,0:T(8,128)(2,1)S(1)} %collective-permute-done.1.rest_2_), channel_id=1, source_target_pairs={{0,2},{1,3},{2,4},{3,5},{4,6},{5,7},{6,8},{7,9},{8,10},{9,11},{10,... | collective-permute-start | bytes 294920 | tf_op jit(solution)/shard_map/ppermute | solution.py:27
  20.5 3.9 %slice_units.1 = (bf16[8,320,512]{2,1,0:T(8,128)(2,1)}, bf16[8,128,512]{2,1,0:T(8,128)(2,1)}) custom-call(bf16[512,1792]{1,0:T(8,128)(2,1)} %g_ref.1, bf16[512,1792]{1,0:T(8,128)(2,1)} %u_ref.1), custom_call_target="tpu_custom_call" | custom-call | bytes 114688 | tf_op jit(solution)/shard_map/slice_units/pallas_call | solution.py:94
  26.3 2.2 regroup.1.rest_0_
  28.5 3.8 %all-to-all-start = ((bf16[8,320,512]{2,1,0:T(8,128)(2,1)}), bf16[8,320,512]{2,1,0:T(8,128)(2,1)S(1)}, u32[]{:S(2)}, u32[]{:S(2)}) async-start(bf16[8,320,512]{2,1,0:T(8,128)(2,1)} %get-tuple-element.40), calls=%async_computation | async-start | bytes 5242880 | tf_op jit(solution)/shard_map/all_to_all | solution.py:253
  32.3 3.1 %collective-permute-start.9 = (bf16[8,96,512]{2,1,0:T(8,128)(2,1)S(1)}, bf16[8,96,512]{2,1,0:T(8,128)(2,1)S(1)}, u32[]{:S(2)}, u32[]{:S(2)}) collective-permute-start(bf16[8,96,512]{2,1,0:T(8,128)(2,1)S(1)} %copy-done.4), channel_id=1, source_target_pairs={{0,96},{1,97},{2,98},{3,99},{4,100},{5,101},{6,102},{7,103},{8,104... | collective-permute-start | bytes 2359304 | tf_op jit(solution)/shard_map/ppermute | solution.py:27
  35.9 12.5 %collective-permute-done.9.rest_2_ = bf16[8,96,512]{2,1,0:T(8,128)(2,1)S(1)} collective-permute-done((bf16[8,96,512]{2,1,0:T(8,128)(2,1)S(1)}, bf16[8,96,512]{2,1,0:T(8,128)(2,1)S(1)}, u32[]{:S(2)}, u32[]{:S(2)}) %collective-permute-start.9) | collective-permute-done | bytes 786464 | tf_op jit(solution)/shard_map/ppermute | solution.py:27
  48.4 3.4 %collective-permute-done.8.rest_6_ = bf16[8,96,512]{2,1,0:T(8,128)(2,1)S(1)} collective-permute-done((bf16[8,96,512]{2,1,0:T(8,128)(2,1)S(1)}, bf16[8,96,512]{2,1,0:T(8,128)(2,1)S(1)}, u32[]{:S(2)}, u32[]{:S(2)}) %collective-permute-start.8) | collective-permute-done | bytes 786464 | tf_op jit(solution)/shard_map/ppermute | solution.py:27
  55.8 16.9 %collective-permute-done.10.rest_3_ = bf16[8,96,512]{2,1,0:T(8,128)(2,1)S(1)} collective-permute-done((bf16[8,96,512]{2,1,0:T(8,128)(2,1)S(1)}, bf16[8,96,512]{2,1,0:T(8,128)(2,1)S(1)}, u32[]{:S(2)}, u32[]{:S(2)}) %collective-permute-start.10) | collective-permute-done | bytes 786464 | tf_op jit(solution)/shard_map/ppermute | solution.py:27
  72.8 2.9 %collective-permute-start.12 = (bf16[8,96,512]{2,1,0:T(8,128)(2,1)S(1)}, bf16[8,96,512]{2,1,0:T(8,128)(2,1)S(1)}, u32[]{:S(2)}, u32[]{:S(2)}) collective-permute-start(bf16[8,96,512]{2,1,0:T(8,128)(2,1)S(1)} %collective-permute-done.10.rest_3_), channel_id=1, source_target_pairs={{0,96},{1,97},{2,98},{3,99},{4,100},{5,101},{6,102},{7,103},{8,104... | collective-permute-start | bytes 2359304 | tf_op jit(solution)/shard_map/ppermute | solution.py:27
  75.7 17.2 %collective-permute-done.11.rest_4_ = bf16[8,96,512]{2,1,0:T(8,128)(2,1)S(1)} collective-permute-done((bf16[8,96,512]{2,1,0:T(8,128)(2,1)S(1)}, bf16[8,96,512]{2,1,0:T(8,128)(2,1)S(1)}, u32[]{:S(2)}, u32[]{:S(2)}) %collective-permute-start.11) | collective-permute-done | bytes 786464 | tf_op jit(solution)/shard_map/ppermute | solution.py:27
  96.0 6.8 %all-to-all-start.1 = ((bf16[8,128,512]{2,1,0:T(8,128)(2,1)}), bf16[8,128,512]{2,1,0:T(8,128)(2,1)}, u32[]{:S(2)}, u32[]{:S(2)}) async-start(bf16[8,128,512]{2,1,0:T(8,128)(2,1)} %get-tuple-element.57), calls=%async_computation.1 | async-start | bytes 2097152 | tf_op jit(solution)/shard_map/all_to_all | solution.py:267
  102.7 9.1 %project.2 = (f32[320,768]{1,0:T(8,128)}, f32[320,768]{1,0:T(8,128)}) custom-call(s32[5]{0:T(128)} %stack.23.place_ref, bf16[8,320,512]{2,1,0:T(8,128)(2,1)} %copy-done.3, bf16[8,320,512]{2,1,0:T(8,128)(2,1)} %collective-permute-done.15.other_ref, bf16[8,96,512]{2,1,0:T(8,128)(2,1)} %regroup.1.rest_0_, bf16[8,96,512]{2,1,0:T(8,128)(2,1)} %copy-done.7, ...), custom_call_target="tpu_custom_call" | custom-call | flops 62914560 | bytes 180224 | tf_op jit(solution)/shard_map/project/pallas_call | solution.py:154
  112.0 19.8 %all-to-all-done.1.own_ref = bf16[8,128,512]{2,1,0:T(8,128)(2,1)} async-done(((bf16[8,128,512]{2,1,0:T(8,128)(2,1)}), bf16[8,128,512]{2,1,0:T(8,128)(2,1)}, u32[]{:S(2)}, u32[]{:S(2)}) %all-to-all-start.1) | async-done | bytes 1048608 | tf_op jit(solution)/shard_map/all_to_all | solution.py:267
  131.8 5.3 %collective-permute-done.16.rest_0_ = f32[320,768]{1,0:T(8,128)S(1)} collective-permute-done((f32[320,768]{1,0:T(8,128)}, f32[320,768]{1,0:T(8,128)S(1)}, u32[]{:S(2)}, u32[]{:S(2)}) %collective-permute-start.16) | collective-permute-done | bytes 983072 | tf_op jit(solution)/shard_map/ppermute | solution.py:27
  140.1 6.0 %project.3 = (f32[128,768]{1,0:T(8,128)}, f32[128,768]{1,0:T(8,128)}) custom-call(s32[5]{0:T(128)} %stack.23.place_ref, bf16[8,128,512]{2,1,0:T(8,128)(2,1)} %all-to-all-done.1.own_ref, bf16[8,128,512]{2,1,0:T(8,128)(2,1)} %collective-permute-done.17.other_ref, bf16[8,96,512]{2,1,0:T(8,128)(2,1)} %regroup.1.rest_0_, bf16[8,96,512]{2,1,0:T(8,128)(2,1)} %copy-done.7, ...), custom_call_target="tpu_custom_call" | custom-call | flops 25165824 | bytes 131072 | tf_op jit(solution)/shard_map/project/pallas_call | solution.py:154
  146.1 3.0 %collective-permute-start.20 = (bf16[160,768]{1,0:T(8,128)(2,1)S(1)}, bf16[160,768]{1,0:T(8,128)(2,1)S(1)}, u32[]{:S(2)}, u32[]{:S(2)}) collective-permute-start(bf16[160,768]{1,0:T(8,128)(2,1)S(1)} %activate.2.rest_0_), channel_id=1, source_target_pairs={{0,14},{1,15},{2,0},{3,1},{4,2},{5,3},{6,4},{7,5},{8,6},{9,7},{10,... | collective-permute-start | bytes 737288 | tf_op jit(solution)/shard_map/ppermute | solution.py:27
  149.4 5.2 %collective-permute-done.20.rest_7_ = bf16[160,768]{1,0:T(8,128)(2,1)S(1)} collective-permute-done((bf16[160,768]{1,0:T(8,128)(2,1)S(1)}, bf16[160,768]{1,0:T(8,128)(2,1)S(1)}, u32[]{:S(2)}, u32[]{:S(2)}) %collective-permute-start.20) | collective-permute-done | bytes 245792 | tf_op jit(solution)/shard_map/ppermute | solution.py:27
  154.6 3.7 %collective-permute-start.21 = (bf16[160,768]{1,0:T(8,128)(2,1)S(1)}, bf16[160,768]{1,0:T(8,128)(2,1)S(1)}, u32[]{:S(2)}, u32[]{:S(2)}) collective-permute-start(bf16[160,768]{1,0:T(8,128)(2,1)S(1)} %collective-permute-done.20.rest_7_), channel_id=1, source_target_pairs={{0,14},{1,15},{2,0},{3,1},{4,2},{5,3},{6,4},{7,5},{8,6},{9,7},{10,... | collective-permute-start | bytes 737288 | tf_op jit(solution)/shard_map/ppermute | solution.py:27
  158.5 3.2 %collective-permute-done.22.rest_0_ = f32[128,768]{1,0:T(8,128)S(1)} collective-permute-done((f32[128,768]{1,0:T(8,128)}, f32[128,768]{1,0:T(8,128)S(1)}, u32[]{:S(2)}, u32[]{:S(2)}) %collective-permute-start.22) | collective-permute-done | bytes 393248 | tf_op jit(solution)/shard_map/ppermute | solution.py:27
  163.0 3.4 %collective-permute-done.19.rest_2_ = bf16[160,768]{1,0:T(8,128)(2,1)S(1)} collective-permute-done((bf16[160,768]{1,0:T(8,128)(2,1)S(1)}, bf16[160,768]{1,0:T(8,128)(2,1)S(1)}, u32[]{:S(2)}, u32[]{:S(2)}) %collective-permute-start.19) | collective-permute-done | bytes 245792 | tf_op jit(solution)/shard_map/ppermute | solution.py:27
  166.4 3.3 %collective-permute-start.26 = (bf16[160,768]{1,0:T(8,128)(2,1)S(1)}, bf16[160,768]{1,0:T(8,128)(2,1)S(1)}, u32[]{:S(2)}, u32[]{:S(2)}) collective-permute-start(bf16[160,768]{1,0:T(8,128)(2,1)S(1)} %collective-permute-done.21.rest_6_), channel_id=1, source_target_pairs={{0,14},{1,15},{2,0},{3,1},{4,2},{5,3},{6,4},{7,5},{8,6},{9,7},{10,... | collective-permute-start | bytes 737288 | tf_op jit(solution)/shard_map/ppermute | solution.py:27
  171.9 5.5 %collective-permute-done.29.rest_15_ = bf16[64,768]{1,0:T(8,128)(2,1)S(1)} collective-permute-done((bf16[64,768]{1,0:T(8,128)(2,1)S(1)}, bf16[64,768]{1,0:T(8,128)(2,1)S(1)}, u32[]{:S(2)}, u32[]{:S(2)}) %collective-permute-start.29) | collective-permute-done | bytes 98336 | tf_op jit(solution)/shard_map/ppermute | solution.py:27
  177.4 3.7 %collective-permute-start.30 = (bf16[64,768]{1,0:T(8,128)(2,1)S(1)}, bf16[64,768]{1,0:T(8,128)(2,1)S(1)}, u32[]{:S(2)}, u32[]{:S(2)}) collective-permute-start(bf16[64,768]{1,0:T(8,128)(2,1)S(1)} %collective-permute-done.29.rest_15_), channel_id=1, source_target_pairs={{0,14},{1,15},{2,0},{3,1},{4,2},{5,3},{6,4},{7,5},{8,6},{9,7},{10,... | collective-permute-start | bytes 294920 | tf_op jit(solution)/shard_map/ppermute | solution.py:27
  183.3 4.7 %collective-permute-done.28.rest_10_ = bf16[64,768]{1,0:T(8,128)(2,1)S(1)} collective-permute-done((bf16[64,768]{1,0:T(8,128)(2,1)S(1)}, bf16[64,768]{1,0:T(8,128)(2,1)S(1)}, u32[]{:S(2)}, u32[]{:S(2)}) %collective-permute-start.28) | collective-permute-done | bytes 98336 | tf_op jit(solution)/shard_map/ppermute | solution.py:27
  190.0 3.3 %collective-permute-done.32.rest_13_ = bf16[64,768]{1,0:T(8,128)(2,1)S(1)} collective-permute-done((bf16[64,768]{1,0:T(8,128)(2,1)S(1)}, bf16[64,768]{1,0:T(8,128)(2,1)S(1)}, u32[]{:S(2)}, u32[]{:S(2)}) %collective-permute-start.32) | collective-permute-done | bytes 98336 | tf_op jit(solution)/shard_map/ppermute | solution.py:27
  194.1 3.8 %collective-permute-done.33.rest_12_ = bf16[64,768]{1,0:T(8,128)(2,1)S(1)} collective-permute-done((bf16[64,768]{1,0:T(8,128)(2,1)S(1)}, bf16[64,768]{1,0:T(8,128)(2,1)S(1)}, u32[]{:S(2)}, u32[]{:S(2)}) %collective-permute-start.33) | collective-permute-done | bytes 98336 | tf_op jit(solution)/shard_map/ppermute | solution.py:27
  197.9 3.8 %mix.1 = bf16[2,768,512]{2,1,0:T(8,128)(2,1)S(1)} custom-call(s32[5]{0:T(128)S(1)} %copy-done.2, bf16[1792,512]{1,0:T(8,128)(2,1)S(1)} %broadcast_select_fusion.mine_ref, bf16[1792,512]{1,0:T(8,128)(2,1)S(1)} %collective-permute-done.23.theirs_ref, bf16[160,768]{1,0:T(8,128)(2,1)S(1)} %activate.2.rest_0_, ...), custom_call_target="tpu_custom_call" | custom-call | flops 44040192 | bytes 100352 | tf_op jit(solution)/shard_map/mix/pallas_call | solution.py:217
  201.7 22.0 %all_to_all.15 = bf16[16,96,512]{2,1,0:T(8,128)(2,1)S(1)} all-to-all(bf16[16,96,512]{2,1,0:T(8,128)(2,1)S(1)} %bitcast.6), channel_id=1, replica_groups=mesh['xl'=2,'y'=4,'c'=2,'z'=8,'xh'=2] {'xh','y','xl'}, dimensions={0} | all-to-all | bytes 3145728 | tf_op jit(solution)/shard_map/all_to_all | solution.py:285
  (91 shorter events, 23.6 us)
Async XLA Ops:
  0.0 13.4 %collective-permute-start.4 = (bf16[96,512]{1,0:T(8,128)(2,1)}, bf16[96,512]{1,0:T(8,128)(2,1)S(1)}, u32[]{:S(2)}, u32[]{:S(2)}) collective-permute-start(bf16[96,512]{1,0:T(8,128)(2,1)} %rest_0_.1), channel_id=1, source_target_pairs={{0,12},{1,13},{2,14},{3,15},{4,0},{5,1},{6,2},{7,3},{8,4},{9,5},{1... | collective-permute-start | bytes 294920 | tf_op jit(solution)/shard_map/ppermute | solution.py:27
  6.3 11.2 %collective-permute-start.1 = (bf16[96,512]{1,0:T(8,128)(2,1)}, bf16[96,512]{1,0:T(8,128)(2,1)S(1)}, u32[]{:S(2)}, u32[]{:S(2)}) collective-permute-start(bf16[96,512]{1,0:T(8,128)(2,1)} %rest_0_.1), channel_id=1, source_target_pairs={{0,4},{1,5},{2,6},{3,7},{4,8},{5,9},{6,10},{7,11},{8,12},{9,13},{1... | collective-permute-start | bytes 294920 | tf_op jit(solution)/shard_map/ppermute | solution.py:27
  6.3 18.6 %collective-permute-start.3 = (bf16[96,512]{1,0:T(8,128)(2,1)}, bf16[96,512]{1,0:T(8,128)(2,1)S(1)}, u32[]{:S(2)}, u32[]{:S(2)}) collective-permute-start(bf16[96,512]{1,0:T(8,128)(2,1)} %rest_0_.1), channel_id=1, source_target_pairs={{0,8},{1,9},{2,10},{3,11},{4,12},{5,13},{6,14},{7,15},{8,0},{9,1},... | collective-permute-start | bytes 294920 | tf_op jit(solution)/shard_map/ppermute | solution.py:27
  10.1 14.8 %collective-permute-start = (bf16[96,512]{1,0:T(8,128)(2,1)}, bf16[96,512]{1,0:T(8,128)(2,1)S(1)}, u32[]{:S(2)}, u32[]{:S(2)}) collective-permute-start(bf16[96,512]{1,0:T(8,128)(2,1)} %rest_0_.1), channel_id=1, source_target_pairs={{0,2},{1,3},{2,4},{3,5},{4,6},{5,7},{6,8},{7,9},{8,10},{9,11},{10,... | collective-permute-start | bytes 294920 | tf_op jit(solution)/shard_map/ppermute | solution.py:27
  11.1 13.8 %collective-permute-start.6 = (bf16[96,512]{1,0:T(8,128)(2,1)}, bf16[96,512]{1,0:T(8,128)(2,1)S(1)}, u32[]{:S(2)}, u32[]{:S(2)}) collective-permute-start(bf16[96,512]{1,0:T(8,128)(2,1)} %rest_0_.1), channel_id=1, source_target_pairs={{0,14},{1,15},{2,0},{3,1},{4,2},{5,3},{6,4},{7,5},{8,6},{9,7},{10,... | collective-permute-start | bytes 294920 | tf_op jit(solution)/shard_map/ppermute | solution.py:27
  13.4 11.6 %collective-permute-start.5 = (bf16[96,512]{1,0:T(8,128)(2,1)S(1)}, bf16[96,512]{1,0:T(8,128)(2,1)S(1)}, u32[]{:S(2)}, u32[]{:S(2)}) collective-permute-start(bf16[96,512]{1,0:T(8,128)(2,1)S(1)} %collective-permute-done.4.rest_6_), channel_id=1, source_target_pairs={{0,14},{1,15},{2,0},{3,1},{4,2},{5,3},{6,4},{7,5},{8,6},{9,7},{10,... | collective-permute-start | bytes 294920 | tf_op jit(solution)/shard_map/ppermute | solution.py:27
  17.5 7.5 %collective-permute-start.2 = (bf16[96,512]{1,0:T(8,128)(2,1)S(1)}, bf16[96,512]{1,0:T(8,128)(2,1)S(1)}, u32[]{:S(2)}, u32[]{:S(2)}) collective-permute-start(bf16[96,512]{1,0:T(8,128)(2,1)S(1)} %collective-permute-done.1.rest_2_), channel_id=1, source_target_pairs={{0,2},{1,3},{2,4},{3,5},{4,6},{5,7},{6,8},{7,9},{8,10},{9,11},{10,... | collective-permute-start | bytes 294920 | tf_op jit(solution)/shard_map/ppermute | solution.py:27
  28.5 66.4 %all-to-all-start = ((bf16[8,320,512]{2,1,0:T(8,128)(2,1)}), bf16[8,320,512]{2,1,0:T(8,128)(2,1)S(1)}, u32[]{:S(2)}, u32[]{:S(2)}) async-start(bf16[8,320,512]{2,1,0:T(8,128)(2,1)} %get-tuple-element.40), calls=%async_computation | async-start | bytes 5242880 | tf_op jit(solution)/shard_map/all_to_all | solution.py:253
  32.3 16.1 %collective-permute-start.9 = (bf16[8,96,512]{2,1,0:T(8,128)(2,1)S(1)}, bf16[8,96,512]{2,1,0:T(8,128)(2,1)S(1)}, u32[]{:S(2)}, u32[]{:S(2)}) collective-permute-start(bf16[8,96,512]{2,1,0:T(8,128)(2,1)S(1)} %copy-done.4), channel_id=1, source_target_pairs={{0,96},{1,97},{2,98},{3,99},{4,100},{5,101},{6,102},{7,103},{8,104... | collective-permute-start | bytes 2359304 | tf_op jit(solution)/shard_map/ppermute | solution.py:27
  35.4 16.5 %collective-permute-start.8 = (bf16[8,96,512]{2,1,0:T(8,128)(2,1)S(1)}, bf16[8,96,512]{2,1,0:T(8,128)(2,1)S(1)}, u32[]{:S(2)}, u32[]{:S(2)}) collective-permute-start(bf16[8,96,512]{2,1,0:T(8,128)(2,1)S(1)} %copy-done.4), channel_id=1, source_target_pairs={{0,32},{1,33},{2,34},{3,35},{4,36},{5,37},{6,38},{7,39},{8,40},{9,... | collective-permute-start | bytes 2359304 | tf_op jit(solution)/shard_map/ppermute | solution.py:27
  35.4 16.5 %collective-permute-start.7 = (bf16[8,96,512]{2,1,0:T(8,128)(2,1)S(1)}, bf16[8,96,512]{2,1,0:T(8,128)(2,1)S(1)}, u32[]{:S(2)}, u32[]{:S(2)}) collective-permute-start(bf16[8,96,512]{2,1,0:T(8,128)(2,1)S(1)} %copy-done.4), channel_id=1, source_target_pairs={{0,128},{1,129},{2,130},{3,131},{4,132},{5,133},{6,134},{7,135},{8... | collective-permute-start | bytes 2359304 | tf_op jit(solution)/shard_map/ppermute | solution.py:27
  51.8 43.1 %collective-permute-start.14 = (bf16[1792,512]{1,0:T(8,128)(2,1)}, bf16[1792,512]{1,0:T(8,128)(2,1)}, u32[]{:S(2)}, u32[]{:S(2)}) collective-permute-start(bf16[1792,512]{1,0:T(8,128)(2,1)} %param.7), channel_id=1, source_target_pairs={{1,16},{3,18},{5,20},{7,22},{9,24},{11,26},{13,28},{15,30},{16,1},... | collective-permute-start | bytes 5505032 | tf_op jit(solution)/shard_map/ppermute | solution.py:27
  53.7 19.0 %collective-permute-start.10 = (bf16[8,96,512]{2,1,0:T(8,128)(2,1)S(1)}, bf16[8,96,512]{2,1,0:T(8,128)(2,1)S(1)}, u32[]{:S(2)}, u32[]{:S(2)}) collective-permute-start(bf16[8,96,512]{2,1,0:T(8,128)(2,1)S(1)} %collective-permute-done.7.rest_1_), channel_id=1, source_target_pairs={{0,96},{1,97},{2,98},{3,99},{4,100},{5,101},{6,102},{7,103},{8,104... | collective-permute-start | bytes 2359304 | tf_op jit(solution)/shard_map/ppermute | solution.py:27
  55.5 37.4 %collective-permute-start.13 = (bf16[8,96,512]{2,1,0:T(8,128)(2,1)S(1)}, bf16[8,96,512]{2,1,0:T(8,128)(2,1)S(1)}, u32[]{:S(2)}, u32[]{:S(2)}) collective-permute-start(bf16[8,96,512]{2,1,0:T(8,128)(2,1)S(1)} %collective-permute-done.7.rest_1_), channel_id=1, source_target_pairs={{0,32},{1,33},{2,34},{3,35},{4,36},{5,37},{6,38},{7,39},{8,40},{9,... | collective-permute-start | bytes 2359304 | tf_op jit(solution)/shard_map/ppermute | solution.py:27
  55.8 37.1 %collective-permute-start.11 = (bf16[8,96,512]{2,1,0:T(8,128)(2,1)S(1)}, bf16[8,96,512]{2,1,0:T(8,128)(2,1)S(1)}, u32[]{:S(2)}, u32[]{:S(2)}) collective-permute-start(bf16[8,96,512]{2,1,0:T(8,128)(2,1)S(1)} %collective-permute-done.8.rest_6_), channel_id=1, source_target_pairs={{0,32},{1,33},{2,34},{3,35},{4,36},{5,37},{6,38},{7,39},{8,40},{9,... | collective-permute-start | bytes 2359304 | tf_op jit(solution)/shard_map/ppermute | solution.py:27
  72.8 20.4 %collective-permute-start.12 = (bf16[8,96,512]{2,1,0:T(8,128)(2,1)S(1)}, bf16[8,96,512]{2,1,0:T(8,128)(2,1)S(1)}, u32[]{:S(2)}, u32[]{:S(2)}) collective-permute-start(bf16[8,96,512]{2,1,0:T(8,128)(2,1)S(1)} %collective-permute-done.10.rest_3_), channel_id=1, source_target_pairs={{0,96},{1,97},{2,98},{3,99},{4,100},{5,101},{6,102},{7,103},{8,104... | collective-permute-start | bytes 2359304 | tf_op jit(solution)/shard_map/ppermute | solution.py:27
  95.0 7.8 %collective-permute-start.15 = (bf16[8,320,512]{2,1,0:T(8,128)(2,1)S(1)}, bf16[8,320,512]{2,1,0:T(8,128)(2,1)}, u32[]{:S(2)}, u32[]{:S(2)}) collective-permute-start(bf16[8,320,512]{2,1,0:T(8,128)(2,1)S(1)} %all-to-all-done.own_ref), channel_id=1, source_target_pairs={{0,16},{1,17},{2,18},{3,19},{4,20},{5,21},{6,22},{7,23},{8,24},{9,... | collective-permute-start | bytes 7864328 | tf_op jit(solution)/shard_map/ppermute | solution.py:27
  96.0 35.8 %all-to-all-start.1 = ((bf16[8,128,512]{2,1,0:T(8,128)(2,1)}), bf16[8,128,512]{2,1,0:T(8,128)(2,1)}, u32[]{:S(2)}, u32[]{:S(2)}) async-start(bf16[8,128,512]{2,1,0:T(8,128)(2,1)} %get-tuple-element.57), calls=%async_computation.1 | async-start | bytes 2097152 | tf_op jit(solution)/shard_map/all_to_all | solution.py:267
  111.8 25.2 %collective-permute-start.16 = (f32[320,768]{1,0:T(8,128)}, f32[320,768]{1,0:T(8,128)S(1)}, u32[]{:S(2)}, u32[]{:S(2)}) collective-permute-start(f32[320,768]{1,0:T(8,128)} %get-tuple-element.56), channel_id=1, source_target_pairs={{0,1},{1,0},{2,3},{3,2},{4,5},{5,4},{6,7},{7,6},{8,9},{9,8},{10,11... | collective-permute-start | bytes 2949128 | tf_op jit(solution)/shard_map/ppermute | solution.py:27
  146.1 8.5 %collective-permute-start.20 = (bf16[160,768]{1,0:T(8,128)(2,1)S(1)}, bf16[160,768]{1,0:T(8,128)(2,1)S(1)}, u32[]{:S(2)}, u32[]{:S(2)}) collective-permute-start(bf16[160,768]{1,0:T(8,128)(2,1)S(1)} %activate.2.rest_0_), channel_id=1, source_target_pairs={{0,14},{1,15},{2,0},{3,1},{4,2},{5,3},{6,4},{7,5},{8,6},{9,7},{10,... | collective-permute-start | bytes 737288 | tf_op jit(solution)/shard_map/ppermute | solution.py:27
  149.1 9.2 %collective-permute-start.18 = (bf16[160,768]{1,0:T(8,128)(2,1)S(1)}, bf16[160,768]{1,0:T(8,128)(2,1)S(1)}, u32[]{:S(2)}, u32[]{:S(2)}) collective-permute-start(bf16[160,768]{1,0:T(8,128)(2,1)S(1)} %activate.2.rest_0_), channel_id=1, source_target_pairs={{0,2},{1,3},{2,4},{3,5},{4,6},{5,7},{6,8},{7,9},{8,10},{9,11},{10,... | collective-permute-start | bytes 737288 | tf_op jit(solution)/shard_map/ppermute | solution.py:27
  149.1 12.6 %collective-permute-start.22 = (f32[128,768]{1,0:T(8,128)}, f32[128,768]{1,0:T(8,128)S(1)}, u32[]{:S(2)}, u32[]{:S(2)}) collective-permute-start(f32[128,768]{1,0:T(8,128)} %get-tuple-element.61), channel_id=1, source_target_pairs={{0,1},{1,0},{2,3},{3,2},{4,5},{5,4},{6,7},{7,6},{8,9},{9,8},{10,11... | collective-permute-start | bytes 1179656 | tf_op jit(solution)/shard_map/ppermute | solution.py:27
  154.6 8.4 %collective-permute-start.21 = (bf16[160,768]{1,0:T(8,128)(2,1)S(1)}, bf16[160,768]{1,0:T(8,128)(2,1)S(1)}, u32[]{:S(2)}, u32[]{:S(2)}) collective-permute-start(bf16[160,768]{1,0:T(8,128)(2,1)S(1)} %collective-permute-done.20.rest_7_), channel_id=1, source_target_pairs={{0,14},{1,15},{2,0},{3,1},{4,2},{5,3},{6,4},{7,5},{8,6},{9,7},{10,... | collective-permute-start | bytes 737288 | tf_op jit(solution)/shard_map/ppermute | solution.py:27
  158.3 8.1 %collective-permute-start.19 = (bf16[160,768]{1,0:T(8,128)(2,1)S(1)}, bf16[160,768]{1,0:T(8,128)(2,1)S(1)}, u32[]{:S(2)}, u32[]{:S(2)}) collective-permute-start(bf16[160,768]{1,0:T(8,128)(2,1)S(1)} %collective-permute-done.18.rest_1_), channel_id=1, source_target_pairs={{0,2},{1,3},{2,4},{3,5},{4,6},{5,7},{6,8},{7,9},{8,10},{9,11},{10,... | collective-permute-start | bytes 737288 | tf_op jit(solution)/shard_map/ppermute | solution.py:27
  166.4 31.5 %collective-permute-start.23 = (bf16[1792,512]{1,0:T(8,128)(2,1)S(1)}, bf16[1792,512]{1,0:T(8,128)(2,1)S(1)}, u32[]{:S(2)}, u32[]{:S(2)}) collective-permute-start(bf16[1792,512]{1,0:T(8,128)(2,1)S(1)} %broadcast_select_fusion.mine_ref), channel_id=1, source_target_pairs={{0,16},{1,17},{2,18},{3,19},{4,20},{5,21},{6,22},{7,23},{8,24},{9,... | collective-permute-start | bytes 5505032 | tf_op jit(solution)/shard_map/ppermute | solution.py:27
  166.4 14.7 %collective-permute-start.24 = (bf16[160,768]{1,0:T(8,128)(2,1)S(1)}, bf16[160,768]{1,0:T(8,128)(2,1)S(1)}, u32[]{:S(2)}, u32[]{:S(2)}) collective-permute-start(bf16[160,768]{1,0:T(8,128)(2,1)S(1)} %collective-permute-done.19.rest_2_), channel_id=1, source_target_pairs={{0,2},{1,3},{2,4},{3,5},{4,6},{5,7},{6,8},{7,9},{8,10},{9,11},{10,... | collective-permute-start | bytes 737288 | tf_op jit(solution)/shard_map/ppermute | solution.py:27
  166.4 21.6 %collective-permute-start.26 = (bf16[160,768]{1,0:T(8,128)(2,1)S(1)}, bf16[160,768]{1,0:T(8,128)(2,1)S(1)}, u32[]{:S(2)}, u32[]{:S(2)}) collective-permute-start(bf16[160,768]{1,0:T(8,128)(2,1)S(1)} %collective-permute-done.21.rest_6_), channel_id=1, source_target_pairs={{0,14},{1,15},{2,0},{3,1},{4,2},{5,3},{6,4},{7,5},{8,6},{9,7},{10,... | collective-permute-start | bytes 737288 | tf_op jit(solution)/shard_map/ppermute | solution.py:27
  169.8 7.6 %collective-permute-start.29 = (bf16[64,768]{1,0:T(8,128)(2,1)S(1)}, bf16[64,768]{1,0:T(8,128)(2,1)S(1)}, u32[]{:S(2)}, u32[]{:S(2)}) collective-permute-start(bf16[64,768]{1,0:T(8,128)(2,1)S(1)} %activate.3.rest_8_), channel_id=1, source_target_pairs={{0,14},{1,15},{2,0},{3,1},{4,2},{5,3},{6,4},{7,5},{8,6},{9,7},{10,... | collective-permute-start | bytes 294920 | tf_op jit(solution)/shard_map/ppermute | solution.py:27
  169.8 11.2 %collective-permute-start.27 = (bf16[64,768]{1,0:T(8,128)(2,1)S(1)}, bf16[64,768]{1,0:T(8,128)(2,1)S(1)}, u32[]{:S(2)}, u32[]{:S(2)}) collective-permute-start(bf16[64,768]{1,0:T(8,128)(2,1)S(1)} %activate.3.rest_8_), channel_id=1, source_target_pairs={{0,2},{1,3},{2,4},{3,5},{4,6},{5,7},{6,8},{7,9},{8,10},{9,11},{10,... | collective-permute-start | bytes 294920 | tf_op jit(solution)/shard_map/ppermute | solution.py:27
  181.1 6.9 %collective-permute-start.28 = (bf16[64,768]{1,0:T(8,128)(2,1)S(1)}, bf16[64,768]{1,0:T(8,128)(2,1)S(1)}, u32[]{:S(2)}, u32[]{:S(2)}) collective-permute-start(bf16[64,768]{1,0:T(8,128)(2,1)S(1)} %collective-permute-done.27.rest_9_), channel_id=1, source_target_pairs={{0,2},{1,3},{2,4},{3,5},{4,6},{5,7},{6,8},{7,9},{8,10},{9,11},{10,... | collective-permute-start | bytes 294920 | tf_op jit(solution)/shard_map/ppermute | solution.py:27
  181.1 16.9 %collective-permute-start.25 = (bf16[160,768]{1,0:T(8,128)(2,1)S(1)}, bf16[160,768]{1,0:T(8,128)(2,1)S(1)}, u32[]{:S(2)}, u32[]{:S(2)}) collective-permute-start(bf16[160,768]{1,0:T(8,128)(2,1)S(1)} %collective-permute-done.24.rest_3_), channel_id=1, source_target_pairs={{0,2},{1,3},{2,4},{3,5},{4,6},{5,7},{6,8},{7,9},{8,10},{9,11},{10,... | collective-permute-start | bytes 737288 | tf_op jit(solution)/shard_map/ppermute | solution.py:27
  188.0 6.1 %collective-permute-start.31 = (bf16[64,768]{1,0:T(8,128)(2,1)S(1)}, bf16[64,768]{1,0:T(8,128)(2,1)S(1)}, u32[]{:S(2)}, u32[]{:S(2)}) collective-permute-start(bf16[64,768]{1,0:T(8,128)(2,1)S(1)} %collective-permute-done.28.rest_10_), channel_id=1, source_target_pairs={{0,2},{1,3},{2,4},{3,5},{4,6},{5,7},{6,8},{7,9},{8,10},{9,11},{10,... | collective-permute-start | bytes 294920 | tf_op jit(solution)/shard_map/ppermute | solution.py:27
  (24 other events, 302.3 us)

commit v11 on v9

--- a/solution.py
+++ b/solution.py
@@ -244,9 +244,8 @@
     nz = SIZES[3]
 
     around = {0: tokens}
-    for s in (1, -1, 2, -2, 4):
+    for s in (4, 3, -3, 2, -2, 1, -1):
         around[s] = along_z(tokens, s)
-    around[3], around[-3] = along_z(around[2], 1), along_z(around[-2], -1)
     sliced = slice_units(gate_weight, up_weight, nz)
     near = regroup(place, [around[s] for s in (0, 1, 2, 3, 4, -3, -2, -1)])
     ready, near = together(sliced[0], near)

time: 220 us -> 228 us (1.036)
  waiting for transfers between devices: 109 us -> 118 us
    ppermute x34, waiting for transfers between devices: 83.2 us -> 92.5 us  [send(): return lax.ppermute(value, AXES, pairs)]
  transfers between devices with their start and end apart: 36 -> 36, of which waited for: 17 -> 20; matrix products, arithmetic and copies ran while one was open for 0% -> 0% of each run, Pallas kernels for 6% -> 6%
where the time goes in v11:
time: 228 us
  waiting for transfers between devices  118 us (52%)
  starting transfers between devices  53.9 us (24%)
  Pallas kernels  25.2 us (11%)
  blocking collectives  24.3 us (11%)
  local copies, waits for them, and re-layouts  4.83 us (2%)
    ppermute x34, waiting for transfers between devices, send(): return lax.ppermute(value, AXES, pairs)  92.5 us
    ppermute x34, starting transfers between devices, send(): return lax.ppermute(value, AXES, pairs)  42.4 us
    all_to_all x1, waiting for transfers between devices, shards(): weights.append(lax.all_to_all(ready, 'z', 0, 0, tiled=True))  26 us
    all_to_all x1, blocking collectives, shards(): got = lax.all_to_all(out, ('xh', 'y', 'xl'), 0, 0, tiled=True)  24.3 us
    pallas_call x2, Pallas kernels, project(): pl.pallas_call(body, in_specs=[SCALARS] + [pl.BlockSpec(memory_space=pl.A...  15 us
    all_to_all x1, starting transfers between devices, shards(): weights.append(lax.all_to_all(ready, 'z', 0, 0, tiled=True))  6.85 us
    all_to_all x1, starting transfers between devices, shards(): weights = [lax.all_to_all(ready, 'z', 0, 0, tiled=True)]  4.59 us
  transfers between devices with their start and end apart: 36, of which 20 were waited for; matrix products, arithmetic and copies ran while one was open for 0% of the time, Pallas kernels for 6%

profile of v11, /device:TPU:2, one launch (start us, length us, event | category | flops | bytes accessed | tf_op | source)
XLA Modules:
  0.0 228.0 jit_solution(16152493705508235481)
XLA Ops:
  0.0 6.3 %collective-permute-start.5 = (bf16[96,512]{1,0:T(8,128)(2,1)}, bf16[96,512]{1,0:T(8,128)(2,1)S(1)}, u32[]{:S(2)}, u32[]{:S(2)}) collective-permute-start(bf16[96,512]{1,0:T(8,128)(2,1)} %rest_0_.1), channel_id=1, source_target_pairs={{0,12},{1,13},{2,14},{3,15},{4,0},{5,1},{6,2},{7,3},{8,4},{9,5},{1... | collective-permute-start | bytes 294920 | tf_op jit(solution)/shard_map/ppermute | solution.py:27
  7.3 4.5 %collective-permute-start.3 = (bf16[96,512]{1,0:T(8,128)(2,1)}, bf16[96,512]{1,0:T(8,128)(2,1)S(1)}, u32[]{:S(2)}, u32[]{:S(2)}) collective-permute-start(bf16[96,512]{1,0:T(8,128)(2,1)} %rest_0_.1), channel_id=1, source_target_pairs={{0,8},{1,9},{2,10},{3,11},{4,12},{5,13},{6,14},{7,15},{8,0},{9,1},... | collective-permute-start | bytes 294920 | tf_op jit(solution)/shard_map/ppermute | solution.py:27
  11.8 3.4 %collective-permute-start.1 = (bf16[96,512]{1,0:T(8,128)(2,1)}, bf16[96,512]{1,0:T(8,128)(2,1)S(1)}, u32[]{:S(2)}, u32[]{:S(2)}) collective-permute-start(bf16[96,512]{1,0:T(8,128)(2,1)} %rest_0_.1), channel_id=1, source_target_pairs={{0,4},{1,5},{2,6},{3,7},{4,8},{5,9},{6,10},{7,11},{8,12},{9,13},{1... | collective-permute-start | bytes 294920 | tf_op jit(solution)/shard_map/ppermute | solution.py:27
  16.4 5.9 %collective-permute-done.4.rest_5_ = bf16[96,512]{1,0:T(8,128)(2,1)S(1)} collective-permute-done((bf16[96,512]{1,0:T(8,128)(2,1)}, bf16[96,512]{1,0:T(8,128)(2,1)S(1)}, u32[]{:S(2)}, u32[]{:S(2)}) %collective-permute-start.4) | collective-permute-done | bytes 98336 | tf_op jit(solution)/shard_map/ppermute | solution.py:27
  22.3 3.9 %slice_units.1 = (bf16[8,288,512]{2,1,0:T(8,128)(2,1)}, bf16[8,160,512]{2,1,0:T(8,128)(2,1)}) custom-call(bf16[512,1792]{1,0:T(8,128)(2,1)} %g_ref.1, bf16[512,1792]{1,0:T(8,128)(2,1)} %u_ref.1), custom_call_target="tpu_custom_call" | custom-call | bytes 114688 | tf_op jit(solution)/shard_map/slice_units/pallas_call | solution.py:94
  26.9 2.2 collective-permute-done.1.rest_2_
  31.0 2.2 regroup.1.rest_0_
  33.3 4.6 %all-to-all-start = ((bf16[8,288,512]{2,1,0:T(8,128)(2,1)}), bf16[8,288,512]{2,1,0:T(8,128)(2,1)S(1)}, u32[]{:S(2)}, u32[]{:S(2)}) async-start(bf16[8,288,512]{2,1,0:T(8,128)(2,1)} %get-tuple-element.40), calls=%async_computation | async-start | bytes 4718592 | tf_op jit(solution)/shard_map/all_to_all | solution.py:252
  37.8 3.1 %collective-permute-start.9 = (bf16[8,96,512]{2,1,0:T(8,128)(2,1)S(1)}, bf16[8,96,512]{2,1,0:T(8,128)(2,1)S(1)}, u32[]{:S(2)}, u32[]{:S(2)}) collective-permute-start(bf16[8,96,512]{2,1,0:T(8,128)(2,1)S(1)} %copy-done.4), channel_id=1, source_target_pairs={{0,96},{1,97},{2,98},{3,99},{4,100},{5,101},{6,102},{7,103},{8,104... | collective-permute-start | bytes 2359304 | tf_op jit(solution)/shard_map/ppermute | solution.py:27
  41.5 15.8 %collective-permute-done.9.rest_2_ = bf16[8,96,512]{2,1,0:T(8,128)(2,1)S(1)} collective-permute-done((bf16[8,96,512]{2,1,0:T(8,128)(2,1)S(1)}, bf16[8,96,512]{2,1,0:T(8,128)(2,1)S(1)}, u32[]{:S(2)}, u32[]{:S(2)}) %collective-permute-start.9) | collective-permute-done | bytes 786464 | tf_op jit(solution)/shard_map/ppermute | solution.py:27
  57.3 3.4 %collective-permute-done.8.rest_6_ = bf16[8,96,512]{2,1,0:T(8,128)(2,1)S(1)} collective-permute-done((bf16[8,96,512]{2,1,0:T(8,128)(2,1)S(1)}, bf16[8,96,512]{2,1,0:T(8,128)(2,1)S(1)}, u32[]{:S(2)}, u32[]{:S(2)}) %collective-permute-start.8) | collective-permute-done | bytes 786464 | tf_op jit(solution)/shard_map/ppermute | solution.py:27
  64.6 17.0 %collective-permute-done.10.rest_3_ = bf16[8,96,512]{2,1,0:T(8,128)(2,1)S(1)} collective-permute-done((bf16[8,96,512]{2,1,0:T(8,128)(2,1)S(1)}, bf16[8,96,512]{2,1,0:T(8,128)(2,1)S(1)}, u32[]{:S(2)}, u32[]{:S(2)}) %collective-permute-start.10) | collective-permute-done | bytes 786464 | tf_op jit(solution)/shard_map/ppermute | solution.py:27
  81.6 2.9 %collective-permute-start.12 = (bf16[8,96,512]{2,1,0:T(8,128)(2,1)S(1)}, bf16[8,96,512]{2,1,0:T(8,128)(2,1)S(1)}, u32[]{:S(2)}, u32[]{:S(2)}) collective-permute-start(bf16[8,96,512]{2,1,0:T(8,128)(2,1)S(1)} %collective-permute-done.10.rest_3_), channel_id=1, source_target_pairs={{0,96},{1,97},{2,98},{3,99},{4,100},{5,101},{6,102},{7,103},{8,104... | collective-permute-start | bytes 2359304 | tf_op jit(solution)/shard_map/ppermute | solution.py:27
  84.6 17.2 %collective-permute-done.11.rest_4_ = bf16[8,96,512]{2,1,0:T(8,128)(2,1)S(1)} collective-permute-done((bf16[8,96,512]{2,1,0:T(8,128)(2,1)S(1)}, bf16[8,96,512]{2,1,0:T(8,128)(2,1)S(1)}, u32[]{:S(2)}, u32[]{:S(2)}) %collective-permute-start.11) | collective-permute-done | bytes 786464 | tf_op jit(solution)/shard_map/ppermute | solution.py:27
  104.7 6.8 %all-to-all-start.1 = ((bf16[8,160,512]{2,1,0:T(8,128)(2,1)}), bf16[8,160,512]{2,1,0:T(8,128)(2,1)}, u32[]{:S(2)}, u32[]{:S(2)}) async-start(bf16[8,160,512]{2,1,0:T(8,128)(2,1)} %get-tuple-element.57), calls=%async_computation.1 | async-start | bytes 2621440 | tf_op jit(solution)/shard_map/all_to_all | solution.py:266
  111.6 8.6 %project.2 = (f32[288,768]{1,0:T(8,128)}, f32[288,768]{1,0:T(8,128)}) custom-call(s32[5]{0:T(128)} %stack.23.place_ref, bf16[8,288,512]{2,1,0:T(8,128)(2,1)} %copy-done.3, bf16[8,288,512]{2,1,0:T(8,128)(2,1)} %collective-permute-done.15.other_ref, bf16[8,96,512]{2,1,0:T(8,128)(2,1)} %regroup.1.rest_0_, bf16[8,96,512]{2,1,0:T(8,128)(2,1)} %copy-done.7, ...), custom_call_target="tpu_custom_call" | custom-call | flops 56623104 | bytes 172032 | tf_op jit(solution)/shard_map/project/pallas_call | solution.py:154
  120.3 26.0 %all-to-all-done.1.own_ref = bf16[8,160,512]{2,1,0:T(8,128)(2,1)} async-done(((bf16[8,160,512]{2,1,0:T(8,128)(2,1)}), bf16[8,160,512]{2,1,0:T(8,128)(2,1)}, u32[]{:S(2)}, u32[]{:S(2)}) %all-to-all-start.1) | async-done | bytes 1310752 | tf_op jit(solution)/shard_map/all_to_all | solution.py:266
  147.6 2.0 collective-permute-done.17.other_ref
  149.6 6.5 %project.3 = (f32[160,768]{1,0:T(8,128)}, f32[160,768]{1,0:T(8,128)}) custom-call(s32[5]{0:T(128)} %stack.23.place_ref, bf16[8,160,512]{2,1,0:T(8,128)(2,1)} %all-to-all-done.1.own_ref, bf16[8,160,512]{2,1,0:T(8,128)(2,1)} %collective-permute-done.17.other_ref, bf16[8,96,512]{2,1,0:T(8,128)(2,1)} %regroup.1.rest_0_, bf16[8,96,512]{2,1,0:T(8,128)(2,1)} %copy-done.7, ...), custom_call_target="tpu_custom_call" | custom-call | flops 31457280 | bytes 139264 | tf_op jit(solution)/shard_map/project/pallas_call | solution.py:154
  156.2 2.0 collective-permute-start.18
  158.2 5.4 %collective-permute-done.20.rest_7_ = bf16[144,768]{1,0:T(8,128)(2,1)S(1)} collective-permute-done((bf16[144,768]{1,0:T(8,128)(2,1)S(1)}, bf16[144,768]{1,0:T(8,128)(2,1)S(1)}, u32[]{:S(2)}, u32[]{:S(2)}) %collective-permute-start.20) | collective-permute-done | bytes 221216 | tf_op jit(solution)/shard_map/ppermute | solution.py:27
  165.9 4.4 %collective-permute-done.21.rest_6_ = bf16[144,768]{1,0:T(8,128)(2,1)S(1)} collective-permute-done((bf16[144,768]{1,0:T(8,128)(2,1)S(1)}, bf16[144,768]{1,0:T(8,128)(2,1)S(1)}, u32[]{:S(2)}, u32[]{:S(2)}) %collective-permute-start.21) | collective-permute-done | bytes 221216 | tf_op jit(solution)/shard_map/ppermute | solution.py:27
  170.3 2.7 %collective-permute-done.19.rest_2_ = bf16[144,768]{1,0:T(8,128)(2,1)S(1)} collective-permute-done((bf16[144,768]{1,0:T(8,128)(2,1)S(1)}, bf16[144,768]{1,0:T(8,128)(2,1)S(1)}, u32[]{:S(2)}, u32[]{:S(2)}) %collective-permute-start.19) | collective-permute-done | bytes 221216 | tf_op jit(solution)/shard_map/ppermute | solution.py:27
  175.4 3.1 %collective-permute-start.26 = (bf16[144,768]{1,0:T(8,128)(2,1)S(1)}, bf16[144,768]{1,0:T(8,128)(2,1)S(1)}, u32[]{:S(2)}, u32[]{:S(2)}) collective-permute-start(bf16[144,768]{1,0:T(8,128)(2,1)S(1)} %collective-permute-done.21.rest_6_), channel_id=1, source_target_pairs={{0,14},{1,15},{2,0},{3,1},{4,2},{5,3},{6,4},{7,5},{8,6},{9,7},{10,... | collective-permute-start | bytes 663560 | tf_op jit(solution)/shard_map/ppermute | solution.py:27
  179.3 2.0 collective-permute-start.30
  181.7 4.7 %collective-permute-done.24.rest_3_ = bf16[144,768]{1,0:T(8,128)(2,1)S(1)} collective-permute-done((bf16[144,768]{1,0:T(8,128)(2,1)S(1)}, bf16[144,768]{1,0:T(8,128)(2,1)S(1)}, u32[]{:S(2)}, u32[]{:S(2)}) %collective-permute-start.24) | collective-permute-done | bytes 221216 | tf_op jit(solution)/shard_map/ppermute | solution.py:27
  186.5 1.9 collective-permute-done.28.rest_10_
  190.5 2.8 %collective-permute-done.32.rest_13_ = bf16[80,768]{1,0:T(8,128)(2,1)S(1)} collective-permute-done((bf16[80,768]{1,0:T(8,128)(2,1)S(1)}, bf16[80,768]{1,0:T(8,128)(2,1)S(1)}, u32[]{:S(2)}, u32[]{:S(2)}) %collective-permute-start.32) | collective-permute-done | bytes 122912 | tf_op jit(solution)/shard_map/ppermute | solution.py:27
  193.3 2.1 collective-permute-start.33
  195.4 3.6 %collective-permute-done.31.rest_11_ = bf16[80,768]{1,0:T(8,128)(2,1)S(1)} collective-permute-done((bf16[80,768]{1,0:T(8,128)(2,1)S(1)}, bf16[80,768]{1,0:T(8,128)(2,1)S(1)}, u32[]{:S(2)}, u32[]{:S(2)}) %collective-permute-start.31) | collective-permute-done | bytes 122912 | tf_op jit(solution)/shard_map/ppermute | solution.py:27
  199.0 3.8 %mix.1 = bf16[2,768,512]{2,1,0:T(8,128)(2,1)S(1)} custom-call(s32[5]{0:T(128)S(1)} %copy-done.2, bf16[1792,512]{1,0:T(8,128)(2,1)S(1)} %broadcast_select_fusion.mine_ref, bf16[1792,512]{1,0:T(8,128)(2,1)S(1)} %collective-permute-done.23.theirs_ref, bf16[144,768]{1,0:T(8,128)(2,1)S(1)} %activate.2.rest_0_, ...), custom_call_target="tpu_custom_call" | custom-call | flops 44040192 | bytes 100352 | tf_op jit(solution)/shard_map/mix/pallas_call | solution.py:217
  202.8 24.3 %all_to_all.15 = bf16[16,96,512]{2,1,0:T(8,128)(2,1)S(1)} all-to-all(bf16[16,96,512]{2,1,0:T(8,128)(2,1)S(1)} %bitcast.6), channel_id=1, replica_groups=mesh['xl'=2,'y'=4,'c'=2,'z'=8,'xh'=2] {'xh','y','xl'}, dimensions={0} | all-to-all | bytes 3145728 | tf_op jit(solution)/shard_map/all_to_all | solution.py:284
  (91 shorter events, 22.8 us)
Async XLA Ops:
  0.0 16.4 %collective-permute-start.5 = (bf16[96,512]{1,0:T(8,128)(2,1)}, bf16[96,512]{1,0:T(8,128)(2,1)S(1)}, u32[]{:S(2)}, u32[]{:S(2)}) collective-permute-start(bf16[96,512]{1,0:T(8,128)(2,1)} %rest_0_.1), channel_id=1, source_target_pairs={{0,12},{1,13},{2,14},{3,15},{4,0},{5,1},{6,2},{7,3},{8,4},{9,5},{1... | collective-permute-start | bytes 294920 | tf_op jit(solution)/shard_map/ppermute | solution.py:27
  6.3 16.0 %collective-permute-start.4 = (bf16[96,512]{1,0:T(8,128)(2,1)}, bf16[96,512]{1,0:T(8,128)(2,1)S(1)}, u32[]{:S(2)}, u32[]{:S(2)}) collective-permute-start(bf16[96,512]{1,0:T(8,128)(2,1)} %rest_0_.1), channel_id=1, source_target_pairs={{0,10},{1,11},{2,12},{3,13},{4,14},{5,15},{6,0},{7,1},{8,2},{9,3},... | collective-permute-start | bytes 294920 | tf_op jit(solution)/shard_map/ppermute | solution.py:27
  7.3 19.6 %collective-permute-start.3 = (bf16[96,512]{1,0:T(8,128)(2,1)}, bf16[96,512]{1,0:T(8,128)(2,1)S(1)}, u32[]{:S(2)}, u32[]{:S(2)}) collective-permute-start(bf16[96,512]{1,0:T(8,128)(2,1)} %rest_0_.1), channel_id=1, source_target_pairs={{0,8},{1,9},{2,10},{3,11},{4,12},{5,13},{6,14},{7,15},{8,0},{9,1},... | collective-permute-start | bytes 294920 | tf_op jit(solution)/shard_map/ppermute | solution.py:27
  11.8 15.1 %collective-permute-start.2 = (bf16[96,512]{1,0:T(8,128)(2,1)}, bf16[96,512]{1,0:T(8,128)(2,1)S(1)}, u32[]{:S(2)}, u32[]{:S(2)}) collective-permute-start(bf16[96,512]{1,0:T(8,128)(2,1)} %rest_0_.1), channel_id=1, source_target_pairs={{0,6},{1,7},{2,8},{3,9},{4,10},{5,11},{6,12},{7,13},{8,14},{9,15},... | collective-permute-start | bytes 294920 | tf_op jit(solution)/shard_map/ppermute | solution.py:27
  11.8 17.3 %collective-permute-start.1 = (bf16[96,512]{1,0:T(8,128)(2,1)}, bf16[96,512]{1,0:T(8,128)(2,1)S(1)}, u32[]{:S(2)}, u32[]{:S(2)}) collective-permute-start(bf16[96,512]{1,0:T(8,128)(2,1)} %rest_0_.1), channel_id=1, source_target_pairs={{0,4},{1,5},{2,6},{3,7},{4,8},{5,9},{6,10},{7,11},{8,12},{9,13},{1... | collective-permute-start | bytes 294920 | tf_op jit(solution)/shard_map/ppermute | solution.py:27
  16.4 13.3 %collective-permute-start = (bf16[96,512]{1,0:T(8,128)(2,1)}, bf16[96,512]{1,0:T(8,128)(2,1)S(1)}, u32[]{:S(2)}, u32[]{:S(2)}) collective-permute-start(bf16[96,512]{1,0:T(8,128)(2,1)} %rest_0_.1), channel_id=1, source_target_pairs={{0,2},{1,3},{2,4},{3,5},{4,6},{5,7},{6,8},{7,9},{8,10},{9,11},{10,... | collective-permute-start | bytes 294920 | tf_op jit(solution)/shard_map/ppermute | solution.py:27
  22.3 7.4 %collective-permute-start.6 = (bf16[96,512]{1,0:T(8,128)(2,1)}, bf16[96,512]{1,0:T(8,128)(2,1)S(1)}, u32[]{:S(2)}, u32[]{:S(2)}) collective-permute-start(bf16[96,512]{1,0:T(8,128)(2,1)} %rest_0_.1), channel_id=1, source_target_pairs={{0,14},{1,15},{2,0},{3,1},{4,2},{5,3},{6,4},{7,5},{8,6},{9,7},{10,... | collective-permute-start | bytes 294920 | tf_op jit(solution)/shard_map/ppermute | solution.py:27
  33.3 70.5 %all-to-all-start = ((bf16[8,288,512]{2,1,0:T(8,128)(2,1)}), bf16[8,288,512]{2,1,0:T(8,128)(2,1)S(1)}, u32[]{:S(2)}, u32[]{:S(2)}) async-start(bf16[8,288,512]{2,1,0:T(8,128)(2,1)} %get-tuple-element.40), calls=%async_computation | async-start | bytes 4718592 | tf_op jit(solution)/shard_map/all_to_all | solution.py:252
  37.8 19.4 %collective-permute-start.9 = (bf16[8,96,512]{2,1,0:T(8,128)(2,1)S(1)}, bf16[8,96,512]{2,1,0:T(8,128)(2,1)S(1)}, u32[]{:S(2)}, u32[]{:S(2)}) collective-permute-start(bf16[8,96,512]{2,1,0:T(8,128)(2,1)S(1)} %copy-done.4), channel_id=1, source_target_pairs={{0,96},{1,97},{2,98},{3,99},{4,100},{5,101},{6,102},{7,103},{8,104... | collective-permute-start | bytes 2359304 | tf_op jit(solution)/shard_map/ppermute | solution.py:27
  40.9 19.7 %collective-permute-start.8 = (bf16[8,96,512]{2,1,0:T(8,128)(2,1)S(1)}, bf16[8,96,512]{2,1,0:T(8,128)(2,1)S(1)}, u32[]{:S(2)}, u32[]{:S(2)}) collective-permute-start(bf16[8,96,512]{2,1,0:T(8,128)(2,1)S(1)} %copy-done.4), channel_id=1, source_target_pairs={{0,32},{1,33},{2,34},{3,35},{4,36},{5,37},{6,38},{7,39},{8,40},{9,... | collective-permute-start | bytes 2359304 | tf_op jit(solution)/shard_map/ppermute | solution.py:27
  40.9 19.7 %collective-permute-start.7 = (bf16[8,96,512]{2,1,0:T(8,128)(2,1)S(1)}, bf16[8,96,512]{2,1,0:T(8,128)(2,1)S(1)}, u32[]{:S(2)}, u32[]{:S(2)}) collective-permute-start(bf16[8,96,512]{2,1,0:T(8,128)(2,1)S(1)} %copy-done.4), channel_id=1, source_target_pairs={{0,128},{1,129},{2,130},{3,131},{4,132},{5,133},{6,134},{7,135},{8... | collective-permute-start | bytes 2359304 | tf_op jit(solution)/shard_map/ppermute | solution.py:27
  60.7 43.1 %collective-permute-start.14 = (bf16[1792,512]{1,0:T(8,128)(2,1)}, bf16[1792,512]{1,0:T(8,128)(2,1)}, u32[]{:S(2)}, u32[]{:S(2)}) collective-permute-start(bf16[1792,512]{1,0:T(8,128)(2,1)} %param.7), channel_id=1, source_target_pairs={{1,16},{3,18},{5,20},{7,22},{9,24},{11,26},{13,28},{15,30},{16,1},... | collective-permute-start | bytes 5505032 | tf_op jit(solution)/shard_map/ppermute | solution.py:27
  62.6 19.0 %collective-permute-start.10 = (bf16[8,96,512]{2,1,0:T(8,128)(2,1)S(1)}, bf16[8,96,512]{2,1,0:T(8,128)(2,1)S(1)}, u32[]{:S(2)}, u32[]{:S(2)}) collective-permute-start(bf16[8,96,512]{2,1,0:T(8,128)(2,1)S(1)} %collective-permute-done.7.rest_1_), channel_id=1, source_target_pairs={{0,96},{1,97},{2,98},{3,99},{4,100},{5,101},{6,102},{7,103},{8,104... | collective-permute-start | bytes 2359304 | tf_op jit(solution)/shard_map/ppermute | solution.py:27
  64.3 37.4 %collective-permute-start.13 = (bf16[8,96,512]{2,1,0:T(8,128)(2,1)S(1)}, bf16[8,96,512]{2,1,0:T(8,128)(2,1)S(1)}, u32[]{:S(2)}, u32[]{:S(2)}) collective-permute-start(bf16[8,96,512]{2,1,0:T(8,128)(2,1)S(1)} %collective-permute-done.7.rest_1_), channel_id=1, source_target_pairs={{0,32},{1,33},{2,34},{3,35},{4,36},{5,37},{6,38},{7,39},{8,40},{9,... | collective-permute-start | bytes 2359304 | tf_op jit(solution)/shard_map/ppermute | solution.py:27
  64.6 37.1 %collective-permute-start.11 = (bf16[8,96,512]{2,1,0:T(8,128)(2,1)S(1)}, bf16[8,96,512]{2,1,0:T(8,128)(2,1)S(1)}, u32[]{:S(2)}, u32[]{:S(2)}) collective-permute-start(bf16[8,96,512]{2,1,0:T(8,128)(2,1)S(1)} %collective-permute-done.8.rest_6_), channel_id=1, source_target_pairs={{0,32},{1,33},{2,34},{3,35},{4,36},{5,37},{6,38},{7,39},{8,40},{9,... | collective-permute-start | bytes 2359304 | tf_op jit(solution)/shard_map/ppermute | solution.py:27
  81.6 20.4 %collective-permute-start.12 = (bf16[8,96,512]{2,1,0:T(8,128)(2,1)S(1)}, bf16[8,96,512]{2,1,0:T(8,128)(2,1)S(1)}, u32[]{:S(2)}, u32[]{:S(2)}) collective-permute-start(bf16[8,96,512]{2,1,0:T(8,128)(2,1)S(1)} %collective-permute-done.10.rest_3_), channel_id=1, source_target_pairs={{0,96},{1,97},{2,98},{3,99},{4,100},{5,101},{6,102},{7,103},{8,104... | collective-permute-start | bytes 2359304 | tf_op jit(solution)/shard_map/ppermute | solution.py:27
  103.7 7.8 %collective-permute-start.15 = (bf16[8,288,512]{2,1,0:T(8,128)(2,1)S(1)}, bf16[8,288,512]{2,1,0:T(8,128)(2,1)}, u32[]{:S(2)}, u32[]{:S(2)}) collective-permute-start(bf16[8,288,512]{2,1,0:T(8,128)(2,1)S(1)} %all-to-all-done.own_ref), channel_id=1, source_target_pairs={{0,16},{1,17},{2,18},{3,19},{4,20},{5,21},{6,22},{7,23},{8,24},{9,... | collective-permute-start | bytes 7077896 | tf_op jit(solution)/shard_map/ppermute | solution.py:27
  104.7 41.5 %all-to-all-start.1 = ((bf16[8,160,512]{2,1,0:T(8,128)(2,1)}), bf16[8,160,512]{2,1,0:T(8,128)(2,1)}, u32[]{:S(2)}, u32[]{:S(2)}) async-start(bf16[8,160,512]{2,1,0:T(8,128)(2,1)} %get-tuple-element.57), calls=%async_computation.1 | async-start | bytes 2621440 | tf_op jit(solution)/shard_map/all_to_all | solution.py:266
  120.2 26.1 %collective-permute-start.16 = (f32[288,768]{1,0:T(8,128)}, f32[288,768]{1,0:T(8,128)S(1)}, u32[]{:S(2)}, u32[]{:S(2)}) collective-permute-start(f32[288,768]{1,0:T(8,128)} %get-tuple-element.56), channel_id=1, source_target_pairs={{0,1},{1,0},{2,3},{3,2},{4,5},{5,4},{6,7},{7,6},{8,9},{9,8},{10,11... | collective-permute-start | bytes 2654216 | tf_op jit(solution)/shard_map/ppermute | solution.py:27
  156.1 7.6 %collective-permute-start.20 = (bf16[144,768]{1,0:T(8,128)(2,1)S(1)}, bf16[144,768]{1,0:T(8,128)(2,1)S(1)}, u32[]{:S(2)}, u32[]{:S(2)}) collective-permute-start(bf16[144,768]{1,0:T(8,128)(2,1)S(1)} %activate.2.rest_0_), channel_id=1, source_target_pairs={{0,14},{1,15},{2,0},{3,1},{4,2},{5,3},{6,4},{7,5},{8,6},{9,7},{10,... | collective-permute-start | bytes 663560 | tf_op jit(solution)/shard_map/ppermute | solution.py:27
  156.2 9.0 %collective-permute-start.18 = (bf16[144,768]{1,0:T(8,128)(2,1)S(1)}, bf16[144,768]{1,0:T(8,128)(2,1)S(1)}, u32[]{:S(2)}, u32[]{:S(2)}) collective-permute-start(bf16[144,768]{1,0:T(8,128)(2,1)S(1)} %activate.2.rest_0_), channel_id=1, source_target_pairs={{0,2},{1,3},{2,4},{3,5},{4,6},{5,7},{6,8},{7,9},{8,10},{9,11},{10,... | collective-permute-start | bytes 663560 | tf_op jit(solution)/shard_map/ppermute | solution.py:27
  158.2 14.8 %collective-permute-start.22 = (f32[160,768]{1,0:T(8,128)}, f32[160,768]{1,0:T(8,128)S(1)}, u32[]{:S(2)}, u32[]{:S(2)}) collective-permute-start(f32[160,768]{1,0:T(8,128)} %get-tuple-element.61), channel_id=1, source_target_pairs={{0,1},{1,0},{2,3},{3,2},{4,5},{5,4},{6,7},{7,6},{8,9},{9,8},{10,11... | collective-permute-start | bytes 1474568 | tf_op jit(solution)/shard_map/ppermute | solution.py:27
  163.6 6.6 %collective-permute-start.21 = (bf16[144,768]{1,0:T(8,128)(2,1)S(1)}, bf16[144,768]{1,0:T(8,128)(2,1)S(1)}, u32[]{:S(2)}, u32[]{:S(2)}) collective-permute-start(bf16[144,768]{1,0:T(8,128)(2,1)S(1)} %collective-permute-done.20.rest_7_), channel_id=1, source_target_pairs={{0,14},{1,15},{2,0},{3,1},{4,2},{5,3},{6,4},{7,5},{8,6},{9,7},{10,... | collective-permute-start | bytes 663560 | tf_op jit(solution)/shard_map/ppermute | solution.py:27
  165.1 7.9 %collective-permute-start.19 = (bf16[144,768]{1,0:T(8,128)(2,1)S(1)}, bf16[144,768]{1,0:T(8,128)(2,1)S(1)}, u32[]{:S(2)}, u32[]{:S(2)}) collective-permute-start(bf16[144,768]{1,0:T(8,128)(2,1)S(1)} %collective-permute-done.18.rest_1_), channel_id=1, source_target_pairs={{0,2},{1,3},{2,4},{3,5},{4,6},{5,7},{6,8},{7,9},{8,10},{9,11},{10,... | collective-permute-start | bytes 663560 | tf_op jit(solution)/shard_map/ppermute | solution.py:27
  173.0 26.0 %collective-permute-start.23 = (bf16[1792,512]{1,0:T(8,128)(2,1)S(1)}, bf16[1792,512]{1,0:T(8,128)(2,1)S(1)}, u32[]{:S(2)}, u32[]{:S(2)}) collective-permute-start(bf16[1792,512]{1,0:T(8,128)(2,1)S(1)} %broadcast_select_fusion.mine_ref), channel_id=1, source_target_pairs={{0,16},{1,17},{2,18},{3,19},{4,20},{5,21},{6,22},{7,23},{8,24},{9,... | collective-permute-start | bytes 5505032 | tf_op jit(solution)/shard_map/ppermute | solution.py:27
  174.4 7.4 %collective-permute-start.27 = (bf16[80,768]{1,0:T(8,128)(2,1)S(1)}, bf16[80,768]{1,0:T(8,128)(2,1)S(1)}, u32[]{:S(2)}, u32[]{:S(2)}) collective-permute-start(bf16[80,768]{1,0:T(8,128)(2,1)S(1)} %activate.3.rest_8_), channel_id=1, source_target_pairs={{0,2},{1,3},{2,4},{3,5},{4,6},{5,7},{6,8},{7,9},{8,10},{9,11},{10,... | collective-permute-start | bytes 368648 | tf_op jit(solution)/shard_map/ppermute | solution.py:27
  175.2 11.2 %collective-permute-start.24 = (bf16[144,768]{1,0:T(8,128)(2,1)S(1)}, bf16[144,768]{1,0:T(8,128)(2,1)S(1)}, u32[]{:S(2)}, u32[]{:S(2)}) collective-permute-start(bf16[144,768]{1,0:T(8,128)(2,1)S(1)} %collective-permute-done.19.rest_2_), channel_id=1, source_target_pairs={{0,2},{1,3},{2,4},{3,5},{4,6},{5,7},{6,8},{7,9},{8,10},{9,11},{10,... | collective-permute-start | bytes 663560 | tf_op jit(solution)/shard_map/ppermute | solution.py:27
  175.4 11.1 %collective-permute-start.26 = (bf16[144,768]{1,0:T(8,128)(2,1)S(1)}, bf16[144,768]{1,0:T(8,128)(2,1)S(1)}, u32[]{:S(2)}, u32[]{:S(2)}) collective-permute-start(bf16[144,768]{1,0:T(8,128)(2,1)S(1)} %collective-permute-done.21.rest_6_), channel_id=1, source_target_pairs={{0,14},{1,15},{2,0},{3,1},{4,2},{5,3},{6,4},{7,5},{8,6},{9,7},{10,... | collective-permute-start | bytes 663560 | tf_op jit(solution)/shard_map/ppermute | solution.py:27
  179.3 7.2 %collective-permute-start.30 = (bf16[80,768]{1,0:T(8,128)(2,1)S(1)}, bf16[80,768]{1,0:T(8,128)(2,1)S(1)}, u32[]{:S(2)}, u32[]{:S(2)}) collective-permute-start(bf16[80,768]{1,0:T(8,128)(2,1)S(1)} %collective-permute-done.29.rest_15_), channel_id=1, source_target_pairs={{0,14},{1,15},{2,0},{3,1},{4,2},{5,3},{6,4},{7,5},{8,6},{9,7},{10,... | collective-permute-start | bytes 368648 | tf_op jit(solution)/shard_map/ppermute | solution.py:27
  181.7 6.7 %collective-permute-start.28 = (bf16[80,768]{1,0:T(8,128)(2,1)S(1)}, bf16[80,768]{1,0:T(8,128)(2,1)S(1)}, u32[]{:S(2)}, u32[]{:S(2)}) collective-permute-start(bf16[80,768]{1,0:T(8,128)(2,1)S(1)} %collective-permute-done.27.rest_9_), channel_id=1, source_target_pairs={{0,2},{1,3},{2,4},{3,5},{4,6},{5,7},{6,8},{7,9},{8,10},{9,11},{10,... | collective-permute-start | bytes 368648 | tf_op jit(solution)/shard_map/ppermute | solution.py:27
  189.3 9.7 %collective-permute-start.25 = (bf16[144,768]{1,0:T(8,128)(2,1)S(1)}, bf16[144,768]{1,0:T(8,128)(2,1)S(1)}, u32[]{:S(2)}, u32[]{:S(2)}) collective-permute-start(bf16[144,768]{1,0:T(8,128)(2,1)S(1)} %collective-permute-done.24.rest_3_), channel_id=1, source_target_pairs={{0,2},{1,3},{2,4},{3,5},{4,6},{5,7},{6,8},{7,9},{8,10},{9,11},{10,... | collective-permute-start | bytes 663560 | tf_op jit(solution)/shard_map/ppermute | solution.py:27
  190.4 8.5 %collective-permute-start.31 = (bf16[80,768]{1,0:T(8,128)(2,1)S(1)}, bf16[80,768]{1,0:T(8,128)(2,1)S(1)}, u32[]{:S(2)}, u32[]{:S(2)}) collective-permute-start(bf16[80,768]{1,0:T(8,128)(2,1)S(1)} %collective-permute-done.28.rest_10_), channel_id=1, source_target_pairs={{0,2},{1,3},{2,4},{3,5},{4,6},{5,7},{6,8},{7,9},{8,10},{9,11},{10,... | collective-permute-start | bytes 368648 | tf_op jit(solution)/shard_map/ppermute | solution.py:27
  (24 other events, 289.2 us)

commit v12 on v9

--- a/solution.py
+++ b/solution.py
@@ -270,7 +270,7 @@
     gots = [swap_xh(give) for give in gives]
     hiddens = [activate(keep, gots)]
 
-    weights[1], _ = together(weights[1], gots[0])
+    weights[1], _ = together(weights[1], hiddens[0])
     mine = jnp.where(c == xh, down_weight, moved)
 
     both = together(weights[1], swap_core(weights[1]), hiddens[0])

time: 220 us -> 221 us (level)
    ppermute x34, waiting for transfers between devices: 83.2 us -> 108 us  [send(): return lax.ppermute(value, AXES, pairs)]
    all_to_all x1, waiting for transfers between devices: 26 us -> 1.62 us  [shards(): weights.append(lax.all_to_all(ready, 'z', 0, 0, tiled=True))]
  transfers between devices with their start and end apart: 36 -> 36, of which waited for: 17 -> 18; matrix products, arithmetic and copies ran while one was open for 0% -> 0% of each run, Pallas kernels for 6% -> 6%
where the time goes in v12:
time: 221 us; the launch traced here: 220 us
  waiting for transfers between devices  110 us (50%)
  starting transfers between devices  54.8 us (25%)
  Pallas kernels  25.2 us (11%)
  blocking collectives  24.4 us (11%)
  local copies, waits for them, and re-layouts  4.88 us (2%)
    ppermute x34, waiting for transfers between devices, send(): return lax.ppermute(value, AXES, pairs)  108 us
    ppermute x34, starting transfers between devices, send(): return lax.ppermute(value, AXES, pairs)  44.3 us
    all_to_all x1, blocking collectives, shards(): got = lax.all_to_all(out, ('xh', 'y', 'xl'), 0, 0, tiled=True)  24.4 us
    pallas_call x2, Pallas kernels, project(): pl.pallas_call(body, in_specs=[SCALARS] + [pl.BlockSpec(memory_space=pl.A...  15 us
    all_to_all x1, starting transfers between devices, shards(): weights.append(lax.all_to_all(ready, 'z', 0, 0, tiled=True))  6.76 us
  transfers between devices with their start and end apart: 36, of which 18 were waited for; matrix products, arithmetic and copies ran while one was open for 0% of the time, Pallas kernels for 6%

profile of v12, /device:TPU:2, one launch (start us, length us, event | category | flops | bytes accessed | tf_op | source)
XLA Modules:
  0.0 220.2 jit_solution(2258748167104566063)
XLA Ops:
  0.0 6.3 %collective-permute-start.4 = (bf16[96,512]{1,0:T(8,128)(2,1)}, bf16[96,512]{1,0:T(8,128)(2,1)S(1)}, u32[]{:S(2)}, u32[]{:S(2)}) collective-permute-start(bf16[96,512]{1,0:T(8,128)(2,1)} %rest_0_.1), channel_id=1, source_target_pairs={{0,12},{1,13},{2,14},{3,15},{4,0},{5,1},{6,2},{7,3},{8,4},{9,5},{1... | collective-permute-start | bytes 294920 | tf_op jit(solution)/shard_map/ppermute | solution.py:27
  6.3 3.8 %collective-permute-start.3 = (bf16[96,512]{1,0:T(8,128)(2,1)}, bf16[96,512]{1,0:T(8,128)(2,1)S(1)}, u32[]{:S(2)}, u32[]{:S(2)}) collective-permute-start(bf16[96,512]{1,0:T(8,128)(2,1)} %rest_0_.1), channel_id=1, source_target_pairs={{0,8},{1,9},{2,10},{3,11},{4,12},{5,13},{6,14},{7,15},{8,0},{9,1},... | collective-permute-start | bytes 294920 | tf_op jit(solution)/shard_map/ppermute | solution.py:27
  11.1 2.2 %collective-permute-start.6 = (bf16[96,512]{1,0:T(8,128)(2,1)}, bf16[96,512]{1,0:T(8,128)(2,1)S(1)}, u32[]{:S(2)}, u32[]{:S(2)}) collective-permute-start(bf16[96,512]{1,0:T(8,128)(2,1)} %rest_0_.1), channel_id=1, source_target_pairs={{0,14},{1,15},{2,0},{3,1},{4,2},{5,3},{6,4},{7,5},{8,6},{9,7},{10,... | collective-permute-start | bytes 294920 | tf_op jit(solution)/shard_map/ppermute | solution.py:27
  13.5 4.0 %collective-permute-done.1.rest_2_ = bf16[96,512]{1,0:T(8,128)(2,1)S(1)} collective-permute-done((bf16[96,512]{1,0:T(8,128)(2,1)}, bf16[96,512]{1,0:T(8,128)(2,1)S(1)}, u32[]{:S(2)}, u32[]{:S(2)}) %collective-permute-start.1) | collective-permute-done | bytes 98336 | tf_op jit(solution)/shard_map/ppermute | solution.py:27
  17.5 2.9 %collective-permute-start.2 = (bf16[96,512]{1,0:T(8,128)(2,1)S(1)}, bf16[96,512]{1,0:T(8,128)(2,1)S(1)}, u32[]{:S(2)}, u32[]{:S(2)}) collective-permute-start(bf16[96,512]{1,0:T(8,128)(2,1)S(1)} %collective-permute-done.1.rest_2_), channel_id=1, source_target_pairs={{0,2},{1,3},{2,4},{3,5},{4,6},{5,7},{6,8},{7,9},{8,10},{9,11},{10,... | collective-permute-start | bytes 294920 | tf_op jit(solution)/shard_map/ppermute | solution.py:27
  20.5 3.9 %slice_units.1 = (bf16[8,288,512]{2,1,0:T(8,128)(2,1)}, bf16[8,160,512]{2,1,0:T(8,128)(2,1)}) custom-call(bf16[512,1792]{1,0:T(8,128)(2,1)} %g_ref.1, bf16[512,1792]{1,0:T(8,128)(2,1)} %u_ref.1), custom_call_target="tpu_custom_call" | custom-call | bytes 114688 | tf_op jit(solution)/shard_map/slice_units/pallas_call | solution.py:94
  26.4 2.2 %regroup.1.rest_0_ = bf16[8,96,512]{2,1,0:T(8,128)(2,1)} custom-call(s32[5]{0:T(128)} %stack.23.place_ref, bf16[96,512]{1,0:T(8,128)(2,1)} %rest_0_.1, bf16[96,512]{1,0:T(8,128)(2,1)} %copy-done.16, bf16[96,512]{1,0:T(8,128)(2,1)} %copy-done.14, bf16[96,512]{1,0:T(8,128)(2,1)} %copy-done.19, bf16[96,512]{1,0:T(8,128)(2,1)} %copy-done.15, ...), custom_call_target="tpu_custom_call" | custom-call | bytes 24576 | tf_op jit(solution)/shard_map/regroup/pallas_call | solution.py:71
  28.6 3.7 %all-to-all-start = ((bf16[8,288,512]{2,1,0:T(8,128)(2,1)}), bf16[8,288,512]{2,1,0:T(8,128)(2,1)S(1)}, u32[]{:S(2)}, u32[]{:S(2)}) async-start(bf16[8,288,512]{2,1,0:T(8,128)(2,1)} %get-tuple-element.40), calls=%async_computation | async-start | bytes 4718592 | tf_op jit(solution)/shard_map/all_to_all | solution.py:253
  32.4 3.1 %collective-permute-start.9 = (bf16[8,96,512]{2,1,0:T(8,128)(2,1)S(1)}, bf16[8,96,512]{2,1,0:T(8,128)(2,1)S(1)}, u32[]{:S(2)}, u32[]{:S(2)}) collective-permute-start(bf16[8,96,512]{2,1,0:T(8,128)(2,1)S(1)} %copy-done.4), channel_id=1, source_target_pairs={{0,96},{1,97},{2,98},{3,99},{4,100},{5,101},{6,102},{7,103},{8,104... | collective-permute-start | bytes 2359304 | tf_op jit(solution)/shard_map/ppermute | solution.py:27
  36.0 12.4 %collective-permute-done.9.rest_2_ = bf16[8,96,512]{2,1,0:T(8,128)(2,1)S(1)} collective-permute-done((bf16[8,96,512]{2,1,0:T(8,128)(2,1)S(1)}, bf16[8,96,512]{2,1,0:T(8,128)(2,1)S(1)}, u32[]{:S(2)}, u32[]{:S(2)}) %collective-permute-start.9) | collective-permute-done | bytes 786464 | tf_op jit(solution)/shard_map/ppermute | solution.py:27
  48.4 3.4 %collective-permute-done.8.rest_6_ = bf16[8,96,512]{2,1,0:T(8,128)(2,1)S(1)} collective-permute-done((bf16[8,96,512]{2,1,0:T(8,128)(2,1)S(1)}, bf16[8,96,512]{2,1,0:T(8,128)(2,1)S(1)}, u32[]{:S(2)}, u32[]{:S(2)}) %collective-permute-start.8) | collective-permute-done | bytes 786464 | tf_op jit(solution)/shard_map/ppermute | solution.py:27
  51.9 1.9 collective-permute-start.14
  55.8 17.0 %collective-permute-done.10.rest_3_ = bf16[8,96,512]{2,1,0:T(8,128)(2,1)S(1)} collective-permute-done((bf16[8,96,512]{2,1,0:T(8,128)(2,1)S(1)}, bf16[8,96,512]{2,1,0:T(8,128)(2,1)S(1)}, u32[]{:S(2)}, u32[]{:S(2)}) %collective-permute-start.10) | collective-permute-done | bytes 786464 | tf_op jit(solution)/shard_map/ppermute | solution.py:27
  72.8 2.9 %collective-permute-start.12 = (bf16[8,96,512]{2,1,0:T(8,128)(2,1)S(1)}, bf16[8,96,512]{2,1,0:T(8,128)(2,1)S(1)}, u32[]{:S(2)}, u32[]{:S(2)}) collective-permute-start(bf16[8,96,512]{2,1,0:T(8,128)(2,1)S(1)} %collective-permute-done.10.rest_3_), channel_id=1, source_target_pairs={{0,96},{1,97},{2,98},{3,99},{4,100},{5,101},{6,102},{7,103},{8,104... | collective-permute-start | bytes 2359304 | tf_op jit(solution)/shard_map/ppermute | solution.py:27
  75.7 17.2 %collective-permute-done.11.rest_4_ = bf16[8,96,512]{2,1,0:T(8,128)(2,1)S(1)} collective-permute-done((bf16[8,96,512]{2,1,0:T(8,128)(2,1)S(1)}, bf16[8,96,512]{2,1,0:T(8,128)(2,1)S(1)}, u32[]{:S(2)}, u32[]{:S(2)}) %collective-permute-start.11) | collective-permute-done | bytes 786464 | tf_op jit(solution)/shard_map/ppermute | solution.py:27
  95.9 6.8 %all-to-all-start.1 = ((bf16[8,160,512]{2,1,0:T(8,128)(2,1)}), bf16[8,160,512]{2,1,0:T(8,128)(2,1)}, u32[]{:S(2)}, u32[]{:S(2)}) async-start(bf16[8,160,512]{2,1,0:T(8,128)(2,1)} %get-tuple-element.57), calls=%async_computation.1 | async-start | bytes 2621440 | tf_op jit(solution)/shard_map/all_to_all | solution.py:267
  102.7 8.6 %project.2 = (f32[288,768]{1,0:T(8,128)}, f32[288,768]{1,0:T(8,128)}) custom-call(s32[5]{0:T(128)} %stack.23.place_ref, bf16[8,288,512]{2,1,0:T(8,128)(2,1)} %copy-done.3, bf16[8,288,512]{2,1,0:T(8,128)(2,1)} %collective-permute-done.15.other_ref, bf16[8,96,512]{2,1,0:T(8,128)(2,1)} %regroup.1.rest_0_, bf16[8,96,512]{2,1,0:T(8,128)(2,1)} %copy-done.7, ...), custom_call_target="tpu_custom_call" | custom-call | flops 56623104 | bytes 172032 | tf_op jit(solution)/shard_map/project/pallas_call | solution.py:154
  111.4 23.0 %collective-permute-done.16.rest_0_ = f32[288,768]{1,0:T(8,128)S(1)} collective-permute-done((f32[288,768]{1,0:T(8,128)}, f32[288,768]{1,0:T(8,128)S(1)}, u32[]{:S(2)}, u32[]{:S(2)}) %collective-permute-start.16) | collective-permute-done | bytes 884768 | tf_op jit(solution)/shard_map/ppermute | solution.py:27
  137.3 3.4 %collective-permute-done.17.other_ref = bf16[8,160,512]{2,1,0:T(8,128)(2,1)} collective-permute-done((bf16[8,160,512]{2,1,0:T(8,128)(2,1)}, bf16[8,160,512]{2,1,0:T(8,128)(2,1)}, u32[]{:S(2)}, u32[]{:S(2)}) %collective-permute-start.17) | collective-permute-done | bytes 1310752 | tf_op jit(solution)/shard_map/ppermute | solution.py:27
  140.7 6.5 %project.3 = (f32[160,768]{1,0:T(8,128)}, f32[160,768]{1,0:T(8,128)}) custom-call(s32[5]{0:T(128)} %stack.23.place_ref, bf16[8,160,512]{2,1,0:T(8,128)(2,1)} %all-to-all-done.1.own_ref, bf16[8,160,512]{2,1,0:T(8,128)(2,1)} %collective-permute-done.17.other_ref, bf16[8,96,512]{2,1,0:T(8,128)(2,1)} %regroup.1.rest_0_, bf16[8,96,512]{2,1,0:T(8,128)(2,1)} %copy-done.7, ...), custom_call_target="tpu_custom_call" | custom-call | flops 31457280 | bytes 139264 | tf_op jit(solution)/shard_map/project/pallas_call | solution.py:154
  149.3 5.4 %collective-permute-done.20.rest_7_ = bf16[144,768]{1,0:T(8,128)(2,1)S(1)} collective-permute-done((bf16[144,768]{1,0:T(8,128)(2,1)S(1)}, bf16[144,768]{1,0:T(8,128)(2,1)S(1)}, u32[]{:S(2)}, u32[]{:S(2)}) %collective-permute-start.20) | collective-permute-done | bytes 221216 | tf_op jit(solution)/shard_map/ppermute | solution.py:27
  154.7 2.6 %collective-permute-start.21 = (bf16[144,768]{1,0:T(8,128)(2,1)S(1)}, bf16[144,768]{1,0:T(8,128)(2,1)S(1)}, u32[]{:S(2)}, u32[]{:S(2)}) collective-permute-start(bf16[144,768]{1,0:T(8,128)(2,1)S(1)} %collective-permute-done.20.rest_7_), channel_id=1, source_target_pairs={{0,14},{1,15},{2,0},{3,1},{4,2},{5,3},{6,4},{7,5},{8,6},{9,7},{10,... | collective-permute-start | bytes 663560 | tf_op jit(solution)/shard_map/ppermute | solution.py:27
  157.6 3.9 %collective-permute-done.21.rest_6_ = bf16[144,768]{1,0:T(8,128)(2,1)S(1)} collective-permute-done((bf16[144,768]{1,0:T(8,128)(2,1)S(1)}, bf16[144,768]{1,0:T(8,128)(2,1)S(1)}, u32[]{:S(2)}, u32[]{:S(2)}) %collective-permute-start.21) | collective-permute-done | bytes 221216 | tf_op jit(solution)/shard_map/ppermute | solution.py:27
  161.5 3.4 %collective-permute-done.19.rest_2_ = bf16[144,768]{1,0:T(8,128)(2,1)S(1)} collective-permute-done((bf16[144,768]{1,0:T(8,128)(2,1)S(1)}, bf16[144,768]{1,0:T(8,128)(2,1)S(1)}, u32[]{:S(2)}, u32[]{:S(2)}) %collective-permute-start.19) | collective-permute-done | bytes 221216 | tf_op jit(solution)/shard_map/ppermute | solution.py:27
  167.2 3.2 %collective-permute-start.26 = (bf16[144,768]{1,0:T(8,128)(2,1)S(1)}, bf16[144,768]{1,0:T(8,128)(2,1)S(1)}, u32[]{:S(2)}, u32[]{:S(2)}) collective-permute-start(bf16[144,768]{1,0:T(8,128)(2,1)S(1)} %collective-permute-done.21.rest_6_), channel_id=1, source_target_pairs={{0,14},{1,15},{2,0},{3,1},{4,2},{5,3},{6,4},{7,5},{8,6},{9,7},{10,... | collective-permute-start | bytes 663560 | tf_op jit(solution)/shard_map/ppermute | solution.py:27
  171.2 2.2 %collective-permute-start.30 = (bf16[80,768]{1,0:T(8,128)(2,1)S(1)}, bf16[80,768]{1,0:T(8,128)(2,1)S(1)}, u32[]{:S(2)}, u32[]{:S(2)}) collective-permute-start(bf16[80,768]{1,0:T(8,128)(2,1)S(1)} %collective-permute-done.29.rest_15_), channel_id=1, source_target_pairs={{0,14},{1,15},{2,0},{3,1},{4,2},{5,3},{6,4},{7,5},{8,6},{9,7},{10,... | collective-permute-start | bytes 368648 | tf_op jit(solution)/shard_map/ppermute | solution.py:27
  173.9 4.7 %collective-permute-done.24.rest_3_ = bf16[144,768]{1,0:T(8,128)(2,1)S(1)} collective-permute-done((bf16[144,768]{1,0:T(8,128)(2,1)S(1)}, bf16[144,768]{1,0:T(8,128)(2,1)S(1)}, u32[]{:S(2)}, u32[]{:S(2)}) %collective-permute-start.24) | collective-permute-done | bytes 221216 | tf_op jit(solution)/shard_map/ppermute | solution.py:27
  178.6 1.9 collective-permute-done.28.rest_10_
  182.6 2.8 %collective-permute-done.32.rest_13_ = bf16[80,768]{1,0:T(8,128)(2,1)S(1)} collective-permute-done((bf16[80,768]{1,0:T(8,128)(2,1)S(1)}, bf16[80,768]{1,0:T(8,128)(2,1)S(1)}, u32[]{:S(2)}, u32[]{:S(2)}) %collective-permute-start.32) | collective-permute-done | bytes 122912 | tf_op jit(solution)/shard_map/ppermute | solution.py:27
  187.3 3.7 %collective-permute-done.31.rest_11_ = bf16[80,768]{1,0:T(8,128)(2,1)S(1)} collective-permute-done((bf16[80,768]{1,0:T(8,128)(2,1)S(1)}, bf16[80,768]{1,0:T(8,128)(2,1)S(1)}, u32[]{:S(2)}, u32[]{:S(2)}) %collective-permute-start.31) | collective-permute-done | bytes 122912 | tf_op jit(solution)/shard_map/ppermute | solution.py:27
  191.1 3.8 %mix.1 = bf16[2,768,512]{2,1,0:T(8,128)(2,1)S(1)} custom-call(s32[5]{0:T(128)S(1)} %copy-done.2, bf16[1792,512]{1,0:T(8,128)(2,1)S(1)} %broadcast_select_fusion.mine_ref, bf16[1792,512]{1,0:T(8,128)(2,1)S(1)} %collective-permute-done.23.theirs_ref, bf16[144,768]{1,0:T(8,128)(2,1)S(1)} %activate.2.rest_0_, ...), custom_call_target="tpu_custom_call" | custom-call | flops 44040192 | bytes 100352 | tf_op jit(solution)/shard_map/mix/pallas_call | solution.py:217
  194.9 24.4 %all_to_all.15 = bf16[16,96,512]{2,1,0:T(8,128)(2,1)S(1)} all-to-all(bf16[16,96,512]{2,1,0:T(8,128)(2,1)S(1)} %bitcast.6), channel_id=1, replica_groups=mesh['xl'=2,'y'=4,'c'=2,'z'=8,'xh'=2] {'xh','y','xl'}, dimensions={0} | all-to-all | bytes 3145728 | tf_op jit(solution)/shard_map/all_to_all | solution.py:285
  (91 shorter events, 22.5 us)
Async XLA Ops:
  0.0 13.4 %collective-permute-start.4 = (bf16[96,512]{1,0:T(8,128)(2,1)}, bf16[96,512]{1,0:T(8,128)(2,1)S(1)}, u32[]{:S(2)}, u32[]{:S(2)}) collective-permute-start(bf16[96,512]{1,0:T(8,128)(2,1)} %rest_0_.1), channel_id=1, source_target_pairs={{0,12},{1,13},{2,14},{3,15},{4,0},{5,1},{6,2},{7,3},{8,4},{9,5},{1... | collective-permute-start | bytes 294920 | tf_op jit(solution)/shard_map/ppermute | solution.py:27
  6.3 11.2 %collective-permute-start.1 = (bf16[96,512]{1,0:T(8,128)(2,1)}, bf16[96,512]{1,0:T(8,128)(2,1)S(1)}, u32[]{:S(2)}, u32[]{:S(2)}) collective-permute-start(bf16[96,512]{1,0:T(8,128)(2,1)} %rest_0_.1), channel_id=1, source_target_pairs={{0,4},{1,5},{2,6},{3,7},{4,8},{5,9},{6,10},{7,11},{8,12},{9,13},{1... | collective-permute-start | bytes 294920 | tf_op jit(solution)/shard_map/ppermute | solution.py:27
  6.3 18.7 %collective-permute-start.3 = (bf16[96,512]{1,0:T(8,128)(2,1)}, bf16[96,512]{1,0:T(8,128)(2,1)S(1)}, u32[]{:S(2)}, u32[]{:S(2)}) collective-permute-start(bf16[96,512]{1,0:T(8,128)(2,1)} %rest_0_.1), channel_id=1, source_target_pairs={{0,8},{1,9},{2,10},{3,11},{4,12},{5,13},{6,14},{7,15},{8,0},{9,1},... | collective-permute-start | bytes 294920 | tf_op jit(solution)/shard_map/ppermute | solution.py:27
  10.1 14.9 %collective-permute-start = (bf16[96,512]{1,0:T(8,128)(2,1)}, bf16[96,512]{1,0:T(8,128)(2,1)S(1)}, u32[]{:S(2)}, u32[]{:S(2)}) collective-permute-start(bf16[96,512]{1,0:T(8,128)(2,1)} %rest_0_.1), channel_id=1, source_target_pairs={{0,2},{1,3},{2,4},{3,5},{4,6},{5,7},{6,8},{7,9},{8,10},{9,11},{10,... | collective-permute-start | bytes 294920 | tf_op jit(solution)/shard_map/ppermute | solution.py:27
  11.1 13.9 %collective-permute-start.6 = (bf16[96,512]{1,0:T(8,128)(2,1)}, bf16[96,512]{1,0:T(8,128)(2,1)S(1)}, u32[]{:S(2)}, u32[]{:S(2)}) collective-permute-start(bf16[96,512]{1,0:T(8,128)(2,1)} %rest_0_.1), channel_id=1, source_target_pairs={{0,14},{1,15},{2,0},{3,1},{4,2},{5,3},{6,4},{7,5},{8,6},{9,7},{10,... | collective-permute-start | bytes 294920 | tf_op jit(solution)/shard_map/ppermute | solution.py:27
  13.4 11.7 %collective-permute-start.5 = (bf16[96,512]{1,0:T(8,128)(2,1)S(1)}, bf16[96,512]{1,0:T(8,128)(2,1)S(1)}, u32[]{:S(2)}, u32[]{:S(2)}) collective-permute-start(bf16[96,512]{1,0:T(8,128)(2,1)S(1)} %collective-permute-done.4.rest_6_), channel_id=1, source_target_pairs={{0,14},{1,15},{2,0},{3,1},{4,2},{5,3},{6,4},{7,5},{8,6},{9,7},{10,... | collective-permute-start | bytes 294920 | tf_op jit(solution)/shard_map/ppermute | solution.py:27
  17.5 7.5 %collective-permute-start.2 = (bf16[96,512]{1,0:T(8,128)(2,1)S(1)}, bf16[96,512]{1,0:T(8,128)(2,1)S(1)}, u32[]{:S(2)}, u32[]{:S(2)}) collective-permute-start(bf16[96,512]{1,0:T(8,128)(2,1)S(1)} %collective-permute-done.1.rest_2_), channel_id=1, source_target_pairs={{0,2},{1,3},{2,4},{3,5},{4,6},{5,7},{6,8},{7,9},{8,10},{9,11},{10,... | collective-permute-start | bytes 294920 | tf_op jit(solution)/shard_map/ppermute | solution.py:27
  28.6 66.3 %all-to-all-start = ((bf16[8,288,512]{2,1,0:T(8,128)(2,1)}), bf16[8,288,512]{2,1,0:T(8,128)(2,1)S(1)}, u32[]{:S(2)}, u32[]{:S(2)}) async-start(bf16[8,288,512]{2,1,0:T(8,128)(2,1)} %get-tuple-element.40), calls=%async_computation | async-start | bytes 4718592 | tf_op jit(solution)/shard_map/all_to_all | solution.py:253
  32.4 16.1 %collective-permute-start.9 = (bf16[8,96,512]{2,1,0:T(8,128)(2,1)S(1)}, bf16[8,96,512]{2,1,0:T(8,128)(2,1)S(1)}, u32[]{:S(2)}, u32[]{:S(2)}) collective-permute-start(bf16[8,96,512]{2,1,0:T(8,128)(2,1)S(1)} %copy-done.4), channel_id=1, source_target_pairs={{0,96},{1,97},{2,98},{3,99},{4,100},{5,101},{6,102},{7,103},{8,104... | collective-permute-start | bytes 2359304 | tf_op jit(solution)/shard_map/ppermute | solution.py:27
  35.5 16.4 %collective-permute-start.8 = (bf16[8,96,512]{2,1,0:T(8,128)(2,1)S(1)}, bf16[8,96,512]{2,1,0:T(8,128)(2,1)S(1)}, u32[]{:S(2)}, u32[]{:S(2)}) collective-permute-start(bf16[8,96,512]{2,1,0:T(8,128)(2,1)S(1)} %copy-done.4), channel_id=1, source_target_pairs={{0,32},{1,33},{2,34},{3,35},{4,36},{5,37},{6,38},{7,39},{8,40},{9,... | collective-permute-start | bytes 2359304 | tf_op jit(solution)/shard_map/ppermute | solution.py:27
  35.5 16.4 %collective-permute-start.7 = (bf16[8,96,512]{2,1,0:T(8,128)(2,1)S(1)}, bf16[8,96,512]{2,1,0:T(8,128)(2,1)S(1)}, u32[]{:S(2)}, u32[]{:S(2)}) collective-permute-start(bf16[8,96,512]{2,1,0:T(8,128)(2,1)S(1)} %copy-done.4), channel_id=1, source_target_pairs={{0,128},{1,129},{2,130},{3,131},{4,132},{5,133},{6,134},{7,135},{8... | collective-permute-start | bytes 2359304 | tf_op jit(solution)/shard_map/ppermute | solution.py:27
  51.9 43.1 %collective-permute-start.14 = (bf16[1792,512]{1,0:T(8,128)(2,1)}, bf16[1792,512]{1,0:T(8,128)(2,1)}, u32[]{:S(2)}, u32[]{:S(2)}) collective-permute-start(bf16[1792,512]{1,0:T(8,128)(2,1)} %param.7), channel_id=1, source_target_pairs={{1,16},{3,18},{5,20},{7,22},{9,24},{11,26},{13,28},{15,30},{16,1},... | collective-permute-start | bytes 5505032 | tf_op jit(solution)/shard_map/ppermute | solution.py:27
  53.8 19.0 %collective-permute-start.10 = (bf16[8,96,512]{2,1,0:T(8,128)(2,1)S(1)}, bf16[8,96,512]{2,1,0:T(8,128)(2,1)S(1)}, u32[]{:S(2)}, u32[]{:S(2)}) collective-permute-start(bf16[8,96,512]{2,1,0:T(8,128)(2,1)S(1)} %collective-permute-done.7.rest_1_), channel_id=1, source_target_pairs={{0,96},{1,97},{2,98},{3,99},{4,100},{5,101},{6,102},{7,103},{8,104... | collective-permute-start | bytes 2359304 | tf_op jit(solution)/shard_map/ppermute | solution.py:27
  55.5 37.4 %collective-permute-start.13 = (bf16[8,96,512]{2,1,0:T(8,128)(2,1)S(1)}, bf16[8,96,512]{2,1,0:T(8,128)(2,1)S(1)}, u32[]{:S(2)}, u32[]{:S(2)}) collective-permute-start(bf16[8,96,512]{2,1,0:T(8,128)(2,1)S(1)} %collective-permute-done.7.rest_1_), channel_id=1, source_target_pairs={{0,32},{1,33},{2,34},{3,35},{4,36},{5,37},{6,38},{7,39},{8,40},{9,... | collective-permute-start | bytes 2359304 | tf_op jit(solution)/shard_map/ppermute | solution.py:27
  55.8 37.1 %collective-permute-start.11 = (bf16[8,96,512]{2,1,0:T(8,128)(2,1)S(1)}, bf16[8,96,512]{2,1,0:T(8,128)(2,1)S(1)}, u32[]{:S(2)}, u32[]{:S(2)}) collective-permute-start(bf16[8,96,512]{2,1,0:T(8,128)(2,1)S(1)} %collective-permute-done.8.rest_6_), channel_id=1, source_target_pairs={{0,32},{1,33},{2,34},{3,35},{4,36},{5,37},{6,38},{7,39},{8,40},{9,... | collective-permute-start | bytes 2359304 | tf_op jit(solution)/shard_map/ppermute | solution.py:27
  72.8 20.4 %collective-permute-start.12 = (bf16[8,96,512]{2,1,0:T(8,128)(2,1)S(1)}, bf16[8,96,512]{2,1,0:T(8,128)(2,1)S(1)}, u32[]{:S(2)}, u32[]{:S(2)}) collective-permute-start(bf16[8,96,512]{2,1,0:T(8,128)(2,1)S(1)} %collective-permute-done.10.rest_3_), channel_id=1, source_target_pairs={{0,96},{1,97},{2,98},{3,99},{4,100},{5,101},{6,102},{7,103},{8,104... | collective-permute-start | bytes 2359304 | tf_op jit(solution)/shard_map/ppermute | solution.py:27
  94.9 7.7 %collective-permute-start.15 = (bf16[8,288,512]{2,1,0:T(8,128)(2,1)S(1)}, bf16[8,288,512]{2,1,0:T(8,128)(2,1)}, u32[]{:S(2)}, u32[]{:S(2)}) collective-permute-start(bf16[8,288,512]{2,1,0:T(8,128)(2,1)S(1)} %all-to-all-done.own_ref), channel_id=1, source_target_pairs={{0,16},{1,17},{2,18},{3,19},{4,20},{5,21},{6,22},{7,23},{8,24},{9,... | collective-permute-start | bytes 7077896 | tf_op jit(solution)/shard_map/ppermute | solution.py:27
  95.9 41.4 %all-to-all-start.1 = ((bf16[8,160,512]{2,1,0:T(8,128)(2,1)}), bf16[8,160,512]{2,1,0:T(8,128)(2,1)}, u32[]{:S(2)}, u32[]{:S(2)}) async-start(bf16[8,160,512]{2,1,0:T(8,128)(2,1)} %get-tuple-element.57), calls=%async_computation.1 | async-start | bytes 2621440 | tf_op jit(solution)/shard_map/all_to_all | solution.py:267
  111.3 23.1 %collective-permute-start.16 = (f32[288,768]{1,0:T(8,128)}, f32[288,768]{1,0:T(8,128)S(1)}, u32[]{:S(2)}, u32[]{:S(2)}) collective-permute-start(f32[288,768]{1,0:T(8,128)} %get-tuple-element.56), channel_id=1, source_target_pairs={{0,1},{1,0},{2,3},{3,2},{4,5},{5,4},{6,7},{7,6},{8,9},{9,8},{10,11... | collective-permute-start | bytes 2654216 | tf_op jit(solution)/shard_map/ppermute | solution.py:27
  147.2 7.5 %collective-permute-start.20 = (bf16[144,768]{1,0:T(8,128)(2,1)S(1)}, bf16[144,768]{1,0:T(8,128)(2,1)S(1)}, u32[]{:S(2)}, u32[]{:S(2)}) collective-permute-start(bf16[144,768]{1,0:T(8,128)(2,1)S(1)} %activate.2.rest_0_), channel_id=1, source_target_pairs={{0,14},{1,15},{2,0},{3,1},{4,2},{5,3},{6,4},{7,5},{8,6},{9,7},{10,... | collective-permute-start | bytes 663560 | tf_op jit(solution)/shard_map/ppermute | solution.py:27
  148.7 8.7 %collective-permute-start.18 = (bf16[144,768]{1,0:T(8,128)(2,1)S(1)}, bf16[144,768]{1,0:T(8,128)(2,1)S(1)}, u32[]{:S(2)}, u32[]{:S(2)}) collective-permute-start(bf16[144,768]{1,0:T(8,128)(2,1)S(1)} %activate.2.rest_0_), channel_id=1, source_target_pairs={{0,2},{1,3},{2,4},{3,5},{4,6},{5,7},{6,8},{7,9},{8,10},{9,11},{10,... | collective-permute-start | bytes 663560 | tf_op jit(solution)/shard_map/ppermute | solution.py:27
  149.3 15.6 %collective-permute-start.22 = (f32[160,768]{1,0:T(8,128)}, f32[160,768]{1,0:T(8,128)S(1)}, u32[]{:S(2)}, u32[]{:S(2)}) collective-permute-start(f32[160,768]{1,0:T(8,128)} %get-tuple-element.61), channel_id=1, source_target_pairs={{0,1},{1,0},{2,3},{3,2},{4,5},{5,4},{6,7},{7,6},{8,9},{9,8},{10,11... | collective-permute-start | bytes 1474568 | tf_op jit(solution)/shard_map/ppermute | solution.py:27
  154.7 6.8 %collective-permute-start.21 = (bf16[144,768]{1,0:T(8,128)(2,1)S(1)}, bf16[144,768]{1,0:T(8,128)(2,1)S(1)}, u32[]{:S(2)}, u32[]{:S(2)}) collective-permute-start(bf16[144,768]{1,0:T(8,128)(2,1)S(1)} %collective-permute-done.20.rest_7_), channel_id=1, source_target_pairs={{0,14},{1,15},{2,0},{3,1},{4,2},{5,3},{6,4},{7,5},{8,6},{9,7},{10,... | collective-permute-start | bytes 663560 | tf_op jit(solution)/shard_map/ppermute | solution.py:27
  157.4 7.6 %collective-permute-start.19 = (bf16[144,768]{1,0:T(8,128)(2,1)S(1)}, bf16[144,768]{1,0:T(8,128)(2,1)S(1)}, u32[]{:S(2)}, u32[]{:S(2)}) collective-permute-start(bf16[144,768]{1,0:T(8,128)(2,1)S(1)} %collective-permute-done.18.rest_1_), channel_id=1, source_target_pairs={{0,2},{1,3},{2,4},{3,5},{4,6},{5,7},{6,8},{7,9},{8,10},{9,11},{10,... | collective-permute-start | bytes 663560 | tf_op jit(solution)/shard_map/ppermute | solution.py:27
  164.9 26.1 %collective-permute-start.23 = (bf16[1792,512]{1,0:T(8,128)(2,1)S(1)}, bf16[1792,512]{1,0:T(8,128)(2,1)S(1)}, u32[]{:S(2)}, u32[]{:S(2)}) collective-permute-start(bf16[1792,512]{1,0:T(8,128)(2,1)S(1)} %broadcast_select_fusion.mine_ref), channel_id=1, source_target_pairs={{0,16},{1,17},{2,18},{3,19},{4,20},{5,21},{6,22},{7,23},{8,24},{9,... | collective-permute-start | bytes 5505032 | tf_op jit(solution)/shard_map/ppermute | solution.py:27
  166.5 7.4 %collective-permute-start.27 = (bf16[80,768]{1,0:T(8,128)(2,1)S(1)}, bf16[80,768]{1,0:T(8,128)(2,1)S(1)}, u32[]{:S(2)}, u32[]{:S(2)}) collective-permute-start(bf16[80,768]{1,0:T(8,128)(2,1)S(1)} %activate.3.rest_8_), channel_id=1, source_target_pairs={{0,2},{1,3},{2,4},{3,5},{4,6},{5,7},{6,8},{7,9},{8,10},{9,11},{10,... | collective-permute-start | bytes 368648 | tf_op jit(solution)/shard_map/ppermute | solution.py:27
  167.2 11.5 %collective-permute-start.24 = (bf16[144,768]{1,0:T(8,128)(2,1)S(1)}, bf16[144,768]{1,0:T(8,128)(2,1)S(1)}, u32[]{:S(2)}, u32[]{:S(2)}) collective-permute-start(bf16[144,768]{1,0:T(8,128)(2,1)S(1)} %collective-permute-done.19.rest_2_), channel_id=1, source_target_pairs={{0,2},{1,3},{2,4},{3,5},{4,6},{5,7},{6,8},{7,9},{8,10},{9,11},{10,... | collective-permute-start | bytes 663560 | tf_op jit(solution)/shard_map/ppermute | solution.py:27
  167.2 11.4 %collective-permute-start.26 = (bf16[144,768]{1,0:T(8,128)(2,1)S(1)}, bf16[144,768]{1,0:T(8,128)(2,1)S(1)}, u32[]{:S(2)}, u32[]{:S(2)}) collective-permute-start(bf16[144,768]{1,0:T(8,128)(2,1)S(1)} %collective-permute-done.21.rest_6_), channel_id=1, source_target_pairs={{0,14},{1,15},{2,0},{3,1},{4,2},{5,3},{6,4},{7,5},{8,6},{9,7},{10,... | collective-permute-start | bytes 663560 | tf_op jit(solution)/shard_map/ppermute | solution.py:27
  171.2 7.4 %collective-permute-start.30 = (bf16[80,768]{1,0:T(8,128)(2,1)S(1)}, bf16[80,768]{1,0:T(8,128)(2,1)S(1)}, u32[]{:S(2)}, u32[]{:S(2)}) collective-permute-start(bf16[80,768]{1,0:T(8,128)(2,1)S(1)} %collective-permute-done.29.rest_15_), channel_id=1, source_target_pairs={{0,14},{1,15},{2,0},{3,1},{4,2},{5,3},{6,4},{7,5},{8,6},{9,7},{10,... | collective-permute-start | bytes 368648 | tf_op jit(solution)/shard_map/ppermute | solution.py:27
  173.9 6.7 %collective-permute-start.28 = (bf16[80,768]{1,0:T(8,128)(2,1)S(1)}, bf16[80,768]{1,0:T(8,128)(2,1)S(1)}, u32[]{:S(2)}, u32[]{:S(2)}) collective-permute-start(bf16[80,768]{1,0:T(8,128)(2,1)S(1)} %collective-permute-done.27.rest_9_), channel_id=1, source_target_pairs={{0,2},{1,3},{2,4},{3,5},{4,6},{5,7},{6,8},{7,9},{8,10},{9,11},{10,... | collective-permute-start | bytes 368648 | tf_op jit(solution)/shard_map/ppermute | solution.py:27
  181.2 9.8 %collective-permute-start.25 = (bf16[144,768]{1,0:T(8,128)(2,1)S(1)}, bf16[144,768]{1,0:T(8,128)(2,1)S(1)}, u32[]{:S(2)}, u32[]{:S(2)}) collective-permute-start(bf16[144,768]{1,0:T(8,128)(2,1)S(1)} %collective-permute-done.24.rest_3_), channel_id=1, source_target_pairs={{0,2},{1,3},{2,4},{3,5},{4,6},{5,7},{6,8},{7,9},{8,10},{9,11},{10,... | collective-permute-start | bytes 663560 | tf_op jit(solution)/shard_map/ppermute | solution.py:27
  182.6 8.5 %collective-permute-start.31 = (bf16[80,768]{1,0:T(8,128)(2,1)S(1)}, bf16[80,768]{1,0:T(8,128)(2,1)S(1)}, u32[]{:S(2)}, u32[]{:S(2)}) collective-permute-start(bf16[80,768]{1,0:T(8,128)(2,1)S(1)} %collective-permute-done.28.rest_10_), channel_id=1, source_target_pairs={{0,2},{1,3},{2,4},{3,5},{4,6},{5,7},{6,8},{7,9},{8,10},{9,11},{10,... | collective-permute-start | bytes 368648 | tf_op jit(solution)/shard_map/ppermute | solution.py:27
  (24 other events, 293.3 us)
